TPU v7x, 256 devices: a whole 4x4x8 slice. The times are simulated.
256 devices in a mesh: dp: 32 (over x, z), tensor: 8 (over y, core).
Axes of the slice: x: 4, y: 4, z: 8, core: 2. Of those that a mesh axis runs over, the one named last changes fastest.
Arguments:
- hidden: bfloat16 [8192, 8192], P(('dp', 'tensor')), may hold values from -6 to 6
- cotangent: bfloat16 [8192, 2048], P('dp', 'tensor'), may hold values from -6 to 6
- frozen_key_value: bfloat16 [8192, 2048], P(None, 'tensor'), may hold values from -0.0625 to 0.0625
- adapter_down_factors: bfloat16 [8192, 2048], P('tensor'), may hold values from -0.0625 to 0.0625
- adapter_up_factors: bfloat16 [2048, 2048], P(None, 'tensor'), may hold values from -0.75 to 0.75
- down_master_copy: float32 [8192, 2048], P('tensor', 'dp'), may hold values from -0.0625 to 0.0625
- down_first_moment: float32 [8192, 2048], P('tensor', 'dp'), may hold values from -1.5 to 1.5
- down_second_moment: float32 [8192, 2048], P('tensor', 'dp'), may hold values from 0.001 to 0.05
- up_master_copy: float32 [2048, 2048], P('dp', 'tensor'), may hold values from -0.75 to 0.75
- up_first_moment: float32 [2048, 2048], P('dp', 'tensor'), may hold values from -0.3125 to 0.3125
- up_second_moment: float32 [2048, 2048], P('dp', 'tensor'), may hold values from 1e-05 to 0.001
- adapter_of_token: int32 [8192, 1], P('dp'), may hold values from 0 to 31; in each aligned block of 256 rows (0 to 255, 256 to 511, ...) at most 16 rows name the same one
- adapter_rank_bucket: int32 [32], replicated, may hold values from 0 to 3
- adapter_owner_slot: int32 [32], replicated, may hold values from 0 to 31, each once
- live_token_counts: int32 [32], replicated, may hold values from 64 to 256, as said below
Outputs:
- hidden_gradient: bfloat16 [8192, 8192], P(('dp', 'tensor'))
- new_down_master: float32 [8192, 2048], P('tensor', 'dp')
- new_down_moment: float32 [8192, 2048], P('tensor', 'dp')
- new_down_second: float32 [8192, 2048], P('tensor', 'dp')
- new_up_master: float32 [2048, 2048], P('dp', 'tensor')
- new_up_moment: float32 [2048, 2048], P('dp', 'tensor')
- new_up_second: float32 [2048, 2048], P('dp', 'tensor')
Inputs may be any that keep to these rules, and one draw needn't show every extreme that they name: `adapter_of_token`: in the rows of one index of dp (aligned blocks of 256 rows) no adapter is named by more than 16 rows, and some adapter reaches 16; every adapter is named somewhere. `adapter_owner_slot`: each slot once. `live_token_counts`: some shard is full.
All inputs are finite; a program needn't handle non-finite values.
Results may differ from a plain program's by a relative error of at most 0.0034.
Values may be sent and summed in bfloat16 or wider, within the bound.
No kernel may reach another device: no remote copies, remote signals or barrier semaphores. Data moves between devices by JAX's collectives and lax.ppermute only.
A program may use at most 128 MiB of HBM per device.

v0:
```python
import jax
import jax.numpy as jnp
from jax import lax
from jax.sharding import PartitionSpec as P

RMIN = 8
PADDED_RANK = 64


adapter_alpha_scale = 16.0
beta_one = 0.9
beta_two = 0.999
adam_eps = 1e-08
learn_rate = 0.0002
weight_decay = 0.1
first_fix = 0.9999734386011124
second_fix = 0.09520785288629038


def adapter_tables(adapter_of_token, adapter_rank_bucket, adapter_owner_slot):
    adapter = adapter_of_token[:, 0]
    idents = jnp.arange(adapter_owner_slot.shape[0], dtype=jnp.int32)
    slot_hit = (adapter[:, None] == idents[None, :]).astype(jnp.int32)
    slot_of = jnp.sum(slot_hit * adapter_owner_slot[None, :], axis=1)
    bucket = jnp.sum(slot_hit * adapter_rank_bucket[None, :], axis=1)
    steps_up = (
        1
        + (bucket >= 1).astype(jnp.int32)
        + 2 * (bucket >= 2).astype(jnp.int32)
        + 4 * (bucket >= 3).astype(jnp.int32)
    )
    return (slot_of, RMIN * steps_up)


def adamw(master, moment, second, grad):
    new_moment = beta_one * moment + (1.0 - beta_one) * grad
    new_second = beta_two * second + (1.0 - beta_two) * grad * grad
    update = new_moment / first_fix / (jnp.sqrt(new_second / second_fix) + adam_eps)
    new_master = master - learn_rate * (update + weight_decay * master)
    return (new_master, new_moment, new_second)


def contract_helper(left, right, left_dim, right_dim):
    return lax.dot_general(
        left, right, (((left_dim,), (right_dim,)), ((), ())), preferred_element_type=jnp.float32
    )


def local(
    hidden,
    cotangent,
    frozen_key_value,
    adapter_down_factors,
    adapter_up_factors,
    down_master_copy,
    down_first_moment,
    down_second_moment,
    up_master_copy,
    up_first_moment,
    up_second_moment,
    adapter_of_token,
    adapter_rank_bucket,
    adapter_owner_slot,
    live_token_counts,
):
    n_tensor = lax.axis_size("tensor")
    token_row_block = cotangent.shape[0]
    width = hidden.shape[1]
    shard_columns = width // n_tensor
    slot_count_total = adapter_owner_slot.shape[0]
    tensor_position = lax.axis_index("tensor")
    gathered = lax.all_gather(hidden, "tensor", axis=0, tiled=True)
    hidden_columns = lax.dynamic_slice_in_dim(
        gathered, tensor_position * shard_columns, shard_columns, 1
    )
    row_limit = lax.dynamic_index_in_dim(live_token_counts, lax.axis_index("dp"), 0, keepdims=False)
    is_valid = jnp.arange(token_row_block, dtype=jnp.int32) < row_limit
    masked_cotangent = jnp.where(is_valid[:, None], cotangent, jnp.zeros_like(cotangent))
    slot_of, rank_lookup = adapter_tables(adapter_of_token, adapter_rank_bucket, adapter_owner_slot)
    idents = jnp.arange(slot_count_total, dtype=jnp.int32)
    slot_hit = (slot_of[:, None] == idents[None, :]).astype(jnp.float32)
    down_partial = jnp.dot(
        hidden_columns, adapter_down_factors, preferred_element_type=jnp.float32
    ).reshape(token_row_block, slot_count_total, PADDED_RANK)
    up_partial = contract_helper(masked_cotangent, adapter_up_factors, 1, 1).reshape(
        token_row_block, slot_count_total, PADDED_RANK
    )
    down_own = jnp.einsum("tsk,ts->tk", down_partial, slot_hit)
    up_own = jnp.einsum("tsk,ts->tk", up_partial, slot_hit)
    down_sum, up_sum = lax.psum((down_own, up_own), "tensor")
    kept_cols = jnp.arange(PADDED_RANK, dtype=jnp.int32)[None, :] < rank_lookup[:, None]
    alpha_rank_ratio = (adapter_alpha_scale / rank_lookup.astype(jnp.float32))[:, None]
    factor = jnp.where(kept_cols, alpha_rank_ratio, jnp.zeros_like(alpha_rank_ratio))
    down_weight = (down_sum * factor).astype(jnp.bfloat16)
    up_weight = (up_sum * factor).astype(jnp.bfloat16)
    hit_half = slot_hit.astype(jnp.bfloat16)
    positioned_up_factors = (up_weight[:, None, :] * hit_half[:, :, None]).reshape(
        token_row_block, slot_count_total * PADDED_RANK
    )
    adapter_extra_output = contract_helper(positioned_up_factors, adapter_down_factors, 1, 1)
    frozen_input_term = contract_helper(masked_cotangent, frozen_key_value, 1, 1)
    current_block = lax.dynamic_slice_in_dim(
        frozen_input_term, tensor_position * shard_columns, shard_columns, 1
    )
    frozen_input_term = lax.dynamic_update_slice_in_dim(
        frozen_input_term, current_block + adapter_extra_output, tensor_position * shard_columns, 1
    )
    reduced = lax.psum_scatter(frozen_input_term, "tensor", scatter_dimension=0, tiled=True)
    hidden_gradient = reduced.astype(jnp.bfloat16)
    placed_down = (down_weight[:, None, :] * hit_half[:, :, None]).reshape(
        token_row_block, slot_count_total * PADDED_RANK
    )
    grad_all_down = contract_helper(hidden_columns, positioned_up_factors, 0, 0)
    grad_all_up = contract_helper(placed_down, masked_cotangent, 0, 0)
    grad_down, grad_up = (
        lax.psum_scatter(grad_all_down, "dp", scatter_dimension=1, tiled=True),
        lax.psum_scatter(grad_all_up, "dp", scatter_dimension=0, tiled=True),
    )
    grad_down = grad_down / token_row_block
    grad_up = grad_up / token_row_block
    new_dm, new_dmo, new_ds = adamw(
        down_master_copy, down_first_moment, down_second_moment, grad_down
    )
    new_um, new_umo, new_us = adamw(up_master_copy, up_first_moment, up_second_moment, grad_up)
    return (hidden_gradient, new_dm, new_dmo, new_ds, new_um, new_umo, new_us)


def solution(mesh):
    return jax.shard_map(
        local,
        mesh=mesh,
        in_specs=(
            P(("dp", "tensor"), None),
            P("dp", "tensor"),
            P(None, "tensor"),
            P("tensor", None),
            P(None, "tensor"),
            P("tensor", "dp"),
            P("tensor", "dp"),
            P("tensor", "dp"),
            P("dp", "tensor"),
            P("dp", "tensor"),
            P("dp", "tensor"),
            P("dp", None),
            P(),
            P(),
            P(),
        ),
        out_specs=(
            P(("dp", "tensor"), None),
            P("tensor", "dp"),
            P("tensor", "dp"),
            P("tensor", "dp"),
            P("dp", "tensor"),
            P("dp", "tensor"),
            P("dp", "tensor"),
        ),
        check_vma=False,
    )
```

profile of v0, /device:TPU:32, one launch (start us, length us, event | category | flops | bytes accessed | tf_op | source)
XLA Modules:
  0.0 632.7 jit_solution(17289739096166033977)
XLA Ops:
  7.2 0.0 copy-start
  7.2 0.0 all-gather.2.cloned.1.call-start
  7.2 0.7 all-gather.2.cloned.1.call-update
  7.9 0.0 all-reduce.3.cloned.1.call-start
  8.0 1.2 dynamic_slice.10
  9.2 0.6 iota_compare_fusion.3
  9.9 0.8 select_reduce_fusion
  10.7 0.0 copy-done
  10.7 1.4 fusion.16
  12.1 35.1 %all-gather.2.cloned.1.call-done = bf16[256,8192]{1,0:T(8,128)(2,1)} async-done(((bf16[32,8192]{1,0:T(8,128)(2,1)}), bf16[256,8192]{1,0:T(8,128)(2,1)}) %all-gather.2.cloned.1.call-update) | async-done | bytes 4194320 | tf_op jit(solution)/shard_map/all_gather | solution.py:72
  47.2 4.1 fusion.1
  51.3 0.0 copy-start.1
  51.4 1.1 multiply_reduce_fusion
  52.5 0.0 all-reduce.3.cloned.1.call-update
  52.5 0.0 reduce-scatter.8.cloned.1.call-start
  52.5 64.6 %all-reduce.3.cloned.1.call-done = (f32[256,64]{0,1:T(8,128)}, f32[256,64]{0,1:T(8,128)}) async-done(((f32[256,64]{0,1:T(8,128)}, f32[256,64]{0,1:T(8,128)}), (f32[256,64]{0,1:T(8,128)}, f32[256,64]{0,1:T(8,128)})) %all-reduce.3.cloned.1.call-update) | async-done | bytes 131088 | tf_op jit(solution)/shard_map/psum | solution.py:90
  117.2 0.9 fusion.6
  118.0 0.1 broadcast_multiply_fusion
  118.2 0.0 copy-done.1
  118.2 1.8 fusion.15
  120.0 0.0 reduce-scatter.8.cloned.1.call-update
  120.1 0.0 reduce-scatter.4.cloned.1.call-start
  120.1 0.0 copy-start.8
  120.1 6.9 %fusion.17 = f32[256,8192]{1,0:T(8,128)} fusion(bf16[8192,256]{1,0:T(8,128)(2,1)} %param.17, bf16[256,256]{1,0:T(8,128)(2,1)S(1)} %copy-done.1, pred[256]{0:T(512)(128)(4,1)S(1)} %iota_compare_fusion.3), kind=kOutput, calls=%fused_computation.41 | convolution fusion | flops 1073807360 | bytes 12714240 | tf_op jit(solution)/shard_map/dot_general | solution.py:44
  127.0 0.0 copy-done.8
  127.0 3.6 fusion
  130.6 0.0 reduce-scatter.4.cloned.1.call-update
  130.6 0.0 reduce-scatter.6.cloned.1.call-start
  130.7 5.5 fusion.3
  136.2 0.0 copy-start.5
  136.2 0.0 copy-start.6
  136.2 0.0 copy-start.7
  136.2 0.0 copy-start.2
  136.2 0.0 copy-start.3
  136.2 0.0 copy-start.4
  136.2 0.0 reduce-scatter.6.cloned.1.call-update
  136.3 199.6 %reduce-scatter.8.cloned.1.call-done = f32[64,256]{1,0:T(8,128)} async-done(((f32[2048,256]{1,0:T(8,128)}), f32[64,256]{1,0:T(8,128)}) %reduce-scatter.8.cloned.1.call-update) | async-done | bytes 65552 | tf_op jit(solution)/shard_map/reduce_scatter | solution.py:117
  335.9 0.0 copy-done.5
  335.9 0.0 copy-done.6
  335.9 0.0 copy-done.7
  335.9 1.5 multiply_subtract_fusion.1
  337.4 55.1 %reduce-scatter.4.cloned.1.call-done = f32[32,8192]{1,0:T(8,128)} async-done(((f32[256,8192]{1,0:T(8,128)}), f32[32,8192]{1,0:T(8,128)}) %reduce-scatter.4.cloned.1.call-update) | async-done | bytes 1048592 | tf_op jit(solution)/shard_map/reduce_scatter | solution.py:108
  392.6 2.1 convert_element_type.48
  394.6 229.6 %reduce-scatter.6.cloned.1.call-done = f32[1024,64]{0,1:T(8,128)} async-done(((f32[1024,2048]{0,1:T(8,128)}), f32[1024,64]{0,1:T(8,128)}) %reduce-scatter.6.cloned.1.call-update) | async-done | bytes 262160 | tf_op jit(solution)/shard_map/reduce_scatter | solution.py:116
  624.3 0.0 copy-done.2
  624.3 0.0 copy-done.3
  624.3 0.0 copy-done.4
  624.3 1.9 multiply_subtract_fusion
  (2 shorter events, 0.0 us)
Async XLA Ops:
  7.2 3.5 copy-start
  7.2 40.1 %all-gather.2.cloned.1.call-start = ((), (), s32[]{:S(2)}) async-start(), calls=%async_computation.4 | async-start | bytes 4718592 | tf_op jit(solution)/shard_map/all_gather | solution.py:72
  7.9 109.2 %all-reduce.3.cloned.1.call-start = ((), (), s32[]{:S(2)}) async-start(), calls=%async_computation.7 | async-start | bytes 262144 | tf_op jit(solution)/shard_map/psum | solution.py:90
  51.3 66.9 %copy-start.1 = (bf16[256,256]{1,0:T(8,128)(2,1)S(1)}, bf16[256,256]{1,0:T(8,128)(2,1)}, u32[]{:S(2)}) copy-start(bf16[256,256]{1,0:T(8,128)(2,1)} %param.16) | copy-start | bytes 393220
  52.5 283.4 %reduce-scatter.8.cloned.1.call-start = ((), (), s32[]{:S(2)}) async-start(), calls=%async_computation.6 | async-start | bytes 2162688 | tf_op jit(solution)/shard_map/reduce_scatter | solution.py:117
  120.1 272.5 %reduce-scatter.4.cloned.1.call-start = ((), (), s32[]{:S(2)}) async-start(), calls=%async_computation.3 | async-start | bytes 9437184 | tf_op jit(solution)/shard_map/reduce_scatter | solution.py:108
  120.1 6.9 %copy-start.8 = (bf16[1024,2048]{1,0:T(8,128)(2,1)S(1)}, bf16[1024,2048]{1,0:T(8,128)(2,1)}, u32[]{:S(2)}) copy-start(bf16[1024,2048]{1,0:T(8,128)(2,1)} %param.18) | copy-start | bytes 12582916
  130.6 493.6 %reduce-scatter.6.cloned.1.call-start = ((), (), s32[]{:S(2)}) async-start(), calls=%async_computation.5 | async-start | bytes 8650752 | tf_op jit(solution)/shard_map/reduce_scatter | solution.py:116
  136.2 199.7 %copy-start.5 = (f32[64,256]{1,0:T(8,128)S(1)}, f32[64,256]{1,0:T(8,128)}, u32[]{:S(2)}) copy-start(f32[64,256]{1,0:T(8,128)} %param.23) | copy-start | bytes 196612
  136.2 199.7 %copy-start.6 = (f32[64,256]{1,0:T(8,128)S(1)}, f32[64,256]{1,0:T(8,128)}, u32[]{:S(2)}) copy-start(f32[64,256]{1,0:T(8,128)} %param.24) | copy-start | bytes 196612
  136.2 199.7 %copy-start.7 = (f32[64,256]{1,0:T(8,128)S(1)}, f32[64,256]{1,0:T(8,128)}, u32[]{:S(2)}) copy-start(f32[64,256]{1,0:T(8,128)} %param.25) | copy-start | bytes 196612
  136.2 488.0 %copy-start.2 = (f32[1024,64]{0,1:T(8,128)S(1)}, f32[1024,64]{0,1:T(8,128)}, u32[]{:S(2)}) copy-start(f32[1024,64]{0,1:T(8,128)} %param.20) | copy-start | bytes 786436
  136.2 488.0 %copy-start.3 = (f32[1024,64]{0,1:T(8,128)S(1)}, f32[1024,64]{0,1:T(8,128)}, u32[]{:S(2)}) copy-start(f32[1024,64]{0,1:T(8,128)} %param.21) | copy-start | bytes 786436
  136.2 488.0 %copy-start.4 = (f32[1024,64]{0,1:T(8,128)S(1)}, f32[1024,64]{0,1:T(8,128)}, u32[]{:S(2)}) copy-start(f32[1024,64]{0,1:T(8,128)} %param.22) | copy-start | bytes 786436
Sparse Core Ops, SparseCore 0:
  9.9 37.3 all-gather.1
  52.6 64.5 all-reduce.2
  121.5 214.3 reduce-scatter.7
  338.3 54.2 reduce-scatter.3
  396.4 227.7 reduce-scatter.5
where the time goes:
time: 634 us; the launch traced here: 633 us
  waiting for transfers between devices  585 us (92%)
  matrix products  23.4 us (4%)
  between operations  13.9 us (2%)
  other arithmetic  9.13 us (1%)
    reduce_scatter x1, waiting for transfers between devices, local(): lax.psum_scatter(grad_all_down, 'dp', scatter_dimension=1, tiled=True)  230 us
    reduce_scatter x1, waiting for transfers between devices, local(): lax.psum_scatter(grad_all_up, 'dp', scatter_dimension=0, tiled=True)  200 us
    psum x1, waiting for transfers between devices, local(): down_sum, up_sum = lax.psum((down_own, up_own), 'tensor')  64.6 us
    reduce_scatter x1, waiting for transfers between devices, local(): lax.psum_scatter(frozen_input_term, 'tensor', scatter_dimension=0, tiled=...  55.1 us
    all_gather x1, waiting for transfers between devices, local(): gathered = lax.all_gather(hidden, 'tensor', axis=0, tiled=True)  35.1 us
    dot_general x5, matrix products, contract_helper(): lax.dot_general(left, right, (((left_dim,), (right_dim,)), ((), ())), pre...  19.3 us
  transfers between devices with their start and end apart: 5, of which 5 were waited for; matrix products, arithmetic and copies ran while one was open for 4% of the time, Pallas kernels for 0%

commit v1 on v0

v1 whole, which is shorter than its diff:
```python
import jax
import jax.numpy as jnp
from jax import lax
from jax.sharding import PartitionSpec as P

RMIN = 8
PADDED_RANK = 64
CAP = 16


adapter_alpha_scale = 16.0
beta_one = 0.9
beta_two = 0.999
adam_eps = 1e-08
learn_rate = 0.0002
weight_decay = 0.1
first_fix = 0.9999734386011124
second_fix = 0.09520785288629038


def adapter_tables(adapter_of_token, adapter_rank_bucket, adapter_owner_slot):
    adapter = adapter_of_token[:, 0]
    idents = jnp.arange(adapter_owner_slot.shape[0], dtype=jnp.int32)
    slot_hit = (adapter[:, None] == idents[None, :]).astype(jnp.int32)
    slot_of = jnp.sum(slot_hit * adapter_owner_slot[None, :], axis=1)
    bucket = jnp.sum(slot_hit * adapter_rank_bucket[None, :], axis=1)
    steps_up = (
        1
        + (bucket >= 1).astype(jnp.int32)
        + 2 * (bucket >= 2).astype(jnp.int32)
        + 4 * (bucket >= 3).astype(jnp.int32)
    )
    return (slot_of, RMIN * steps_up)


def adamw(master, moment, second, grad):
    new_moment = beta_one * moment + (1.0 - beta_one) * grad
    new_second = beta_two * second + (1.0 - beta_two) * grad * grad
    update = new_moment / first_fix / (jnp.sqrt(new_second / second_fix) + adam_eps)
    new_master = master - learn_rate * (update + weight_decay * master)
    return (new_master, new_moment, new_second)


def contract_helper(left, right, left_dim, right_dim):
    return lax.dot_general(
        left, right, (((left_dim,), (right_dim,)), ((), ())), preferred_element_type=jnp.float32
    )


def swap(value, mask, count):
    return lax.ppermute(value, "tensor", [(i, i ^ mask) for i in range(count)])


def sum_over_tensor(value, count):
    mask = 1
    while mask < count:
        value = value + swap(value, mask, count)
        mask *= 2
    return value


def local(
    hidden,
    cotangent,
    frozen_key_value,
    adapter_down_factors,
    adapter_up_factors,
    down_master_copy,
    down_first_moment,
    down_second_moment,
    up_master_copy,
    up_first_moment,
    up_second_moment,
    adapter_of_token,
    adapter_rank_bucket,
    adapter_owner_slot,
    live_token_counts,
):
    n_tensor = lax.axis_size("tensor")
    n_chip = n_tensor // 2
    tokens = cotangent.shape[0]
    width = hidden.shape[1]
    rows_own = hidden.shape[0]
    columns = width // n_tensor
    n_slot = adapter_owner_slot.shape[0]
    position = lax.axis_index("tensor")
    chip, core = position // 2, position % 2

    blocks = hidden.reshape(rows_own, n_tensor, columns).transpose(1, 0, 2)
    hidden_columns = lax.all_to_all(blocks, "tensor", 0, 0, tiled=True).reshape(tokens, columns)

    row_limit = lax.dynamic_index_in_dim(live_token_counts, lax.axis_index("dp"), 0, keepdims=False)
    is_valid = jnp.arange(tokens, dtype=jnp.int32) < row_limit
    masked_cotangent = jnp.where(is_valid[:, None], cotangent, jnp.zeros_like(cotangent))
    slot_of, rank_lookup = adapter_tables(adapter_of_token, adapter_rank_bucket, adapter_owner_slot)
    idents = jnp.arange(n_slot, dtype=jnp.int32)
    slot_hit = (slot_of[:, None] == idents[None, :]).astype(jnp.float32)
    hit_half = slot_hit.astype(jnp.bfloat16)
    kept_cols = jnp.arange(PADDED_RANK, dtype=jnp.int32)[None, :] < rank_lookup[:, None]
    alpha_rank_ratio = (adapter_alpha_scale / rank_lookup.astype(jnp.float32))[:, None]
    factor = jnp.where(kept_cols, alpha_rank_ratio, jnp.zeros_like(alpha_rank_ratio))

    order = jnp.arange(tokens, dtype=jnp.int32)
    earlier = (slot_of[:, None] == slot_of[None, :]) & (order[:, None] < order[None, :])
    rank_in_slot = jnp.sum(earlier.astype(jnp.int32), axis=0)
    packed_row = slot_of * CAP + rank_in_slot
    pack = (
        jnp.arange(n_slot * CAP, dtype=jnp.int32)[:, None] == packed_row[None, :]
    ).astype(jnp.bfloat16)

    by_core = masked_cotangent.reshape(n_chip, 2, rows_own, cotangent.shape[1])
    theirs = lax.dynamic_index_in_dim(by_core, 1 - core, 1, keepdims=False).reshape(
        tokens // 2, -1
    )
    ours = lax.dynamic_index_in_dim(by_core, core, 1, keepdims=False).reshape(tokens // 2, -1)
    frozen_theirs = contract_helper(theirs, frozen_key_value, 1, 1)
    frozen_from_pair = swap(frozen_theirs, 1, n_tensor)
    frozen_ours = contract_helper(ours, frozen_key_value, 1, 1)

    up_partial = contract_helper(masked_cotangent, adapter_up_factors, 1, 1).reshape(
        tokens, n_slot, PADDED_RANK
    )
    up_own = jnp.einsum("tsk,ts->tk", up_partial, slot_hit)
    up_weight = (sum_over_tensor(up_own, n_tensor) * factor).astype(jnp.bfloat16)
    positioned_up = (up_weight[:, None, :] * hit_half[:, :, None]).reshape(
        tokens, n_slot * PADDED_RANK
    )
    extra = contract_helper(positioned_up, adapter_down_factors, 1, 1)
    extra_by_core = extra.reshape(n_chip, 2, rows_own, columns)
    extra_theirs = lax.dynamic_index_in_dim(extra_by_core, 1 - core, 1, keepdims=False).reshape(
        tokens // 2, columns
    )
    extra_ours = lax.dynamic_index_in_dim(extra_by_core, core, 1, keepdims=False).reshape(
        tokens // 2, columns
    )
    extra_from_pair = swap(extra_theirs, 1, n_tensor)
    extra_low = jnp.where(core == 0, extra_ours, extra_from_pair)
    extra_high = jnp.where(core == 0, extra_from_pair, extra_ours)
    extra_pair = jnp.concatenate([extra_low, extra_high], axis=1)
    chip_hit = (jnp.arange(n_chip, dtype=jnp.int32) == chip)[None, :, None]
    pair_sum = (frozen_ours + frozen_from_pair).reshape(tokens // 2, n_chip, 2 * columns)
    pair_sum = pair_sum + jnp.where(chip_hit, extra_pair[:, None, :], 0.0)
    pair_sum = pair_sum.reshape(n_chip, rows_own, width)
    total = lax.dynamic_index_in_dim(pair_sum, chip, 0, keepdims=False)
    for step in (1, n_chip - 1, 2):
        out_block = lax.dynamic_index_in_dim(
            pair_sum, (chip + step) % n_chip, 0, keepdims=False
        ).astype(jnp.bfloat16)
        arrived = lax.ppermute(
            out_block, "tensor", [(i, (i + 2 * step) % n_tensor) for i in range(n_tensor)]
        )
        total = total + arrived.astype(jnp.float32)
    hidden_gradient = total.astype(jnp.bfloat16)

    rows = jnp.concatenate([hidden_columns, masked_cotangent], axis=1)
    packed = jnp.dot(pack, rows, preferred_element_type=jnp.float32).astype(jnp.bfloat16)
    owned = lax.all_to_all(
        packed.reshape(n_slot, CAP, -1), "dp", 0, 0, tiled=True
    ).reshape(n_slot * CAP, -1)

    down_partial = jnp.dot(
        hidden_columns, adapter_down_factors, preferred_element_type=jnp.float32
    ).reshape(tokens, n_slot, PADDED_RANK)
    down_own = jnp.einsum("tsk,ts->tk", down_partial, slot_hit)
    down_weight = (sum_over_tensor(down_own, n_tensor) * factor).astype(jnp.bfloat16)
    weights = jnp.concatenate([down_weight, up_weight], axis=1)
    packed_weights = jnp.dot(pack, weights, preferred_element_type=jnp.float32).astype(
        jnp.bfloat16
    )
    owned_weights = lax.all_to_all(
        packed_weights.reshape(n_slot, CAP, -1), "dp", 0, 0, tiled=True
    ).reshape(n_slot * CAP, -1)

    grad_down = contract_helper(owned[:, :columns], owned_weights[:, PADDED_RANK:], 0, 0) / tokens
    grad_up = contract_helper(owned_weights[:, :PADDED_RANK], owned[:, columns:], 0, 0) / tokens
    new_dm, new_dmo, new_ds = adamw(
        down_master_copy, down_first_moment, down_second_moment, grad_down
    )
    new_um, new_umo, new_us = adamw(up_master_copy, up_first_moment, up_second_moment, grad_up)
    return (hidden_gradient, new_dm, new_dmo, new_ds, new_um, new_umo, new_us)


def solution(mesh):
    return jax.shard_map(
        local,
        mesh=mesh,
        in_specs=(
            P(("dp", "tensor"), None),
            P("dp", "tensor"),
            P(None, "tensor"),
            P("tensor", None),
            P(None, "tensor"),
            P("tensor", "dp"),
            P("tensor", "dp"),
            P("tensor", "dp"),
            P("dp", "tensor"),
            P("dp", "tensor"),
            P("dp", "tensor"),
            P("dp", None),
            P(),
            P(),
            P(),
        ),
        out_specs=(
            P(("dp", "tensor"), None),
            P("tensor", "dp"),
            P("tensor", "dp"),
            P("tensor", "dp"),
            P("dp", "tensor"),
            P("dp", "tensor"),
            P("dp", "tensor"),
        ),
        check_vma=False,
    )
```

time: 634 us -> 149 us (0.24)
  waiting for transfers between devices: 585 us -> 31 us
  starting transfers between devices: 0.2 us -> 38.8 us
  local copies, waits for them, and re-layouts: 1.29 us -> 33.1 us
  between operations: 13.9 us -> 0.95 us
  matrix products: 23.4 us -> 32 us
    reduce_scatter x3 -> x0, waiting for transfers between devices: 484 us -> none  [the longest x1 230 us: local(): lax.psum_scatter(grad_all_down, 'dp', scatter_dimension=1, tiled=True)]
    psum x1 -> x0, waiting for transfers between devices: 64.6 us -> none  [local(): down_sum, up_sum = lax.psum((down_own, up_own), 'tensor')]
    all_gather x1 -> x0, waiting for transfers between devices: 35.1 us -> none  [local(): gathered = lax.all_gather(hidden, 'tensor', axis=0, tiled=True)]
    all_to_all x0 -> x3, starting transfers between devices: none -> 25.5 us  [the longest x1 11.2 us: local(): lax.all_to_all(packed_weights.reshape(n_slot, CAP, -1), 'dp', 0, 0, tiled...]
    all_to_all x0 -> x3, waiting for transfers between devices: none -> 22.5 us  [the longest x1 22.5 us: local(): lax.all_to_all(packed.reshape(n_slot, CAP, -1), 'dp', 0, 0, tiled=True)]
    ppermute x0 -> x11, starting transfers between devices: none -> 13.3 us  [the longest x8 8.75 us: swap(): return lax.ppermute(value, 'tensor', [(i, i ^ mask) for i in range(count)])]
    unnamed x18 -> x20, local copies, waits for them, and re-layouts: 0.05 us -> 9.43 us
    broadcast_in_dim x0 -> x2, local copies, waits for them, and re-layouts: none -> 9.2 us  [local(): pair_sum = pair_sum + jnp.where(chip_hit, extra_pair[:, None, :], 0.0)]
  transfers between devices with their start and end apart: 5 -> 14, of which waited for: 5 -> 4; matrix products, arithmetic and copies ran while one was open for 4% -> 42% of each run, Pallas kernels for 0% -> 0%
where the time goes in v1:
time: 149 us; the launch traced here: 148 us
  starting transfers between devices  38.8 us (26%)
  local copies, waits for them, and re-layouts  33.1 us (22%)
  matrix products  32 us (21%)
  waiting for transfers between devices  31 us (21%)
  other arithmetic  11.9 us (8%)
    all_to_all x1, waiting for transfers between devices, local(): lax.all_to_all(packed.reshape(n_slot, CAP, -1), 'dp', 0, 0, tiled=True)  22.5 us
    dot_general x6, matrix products, contract_helper(): lax.dot_general(left, right, (((left_dim,), (right_dim,)), ((), ())), pre...  21.4 us
    all_to_all x1, starting transfers between devices, local(): lax.all_to_all(packed_weights.reshape(n_slot, CAP, -1), 'dp', 0, 0, tiled...  11.2 us
    all_to_all x1, starting transfers between devices, local(): lax.all_to_all(packed.reshape(n_slot, CAP, -1), 'dp', 0, 0, tiled=True)  9.78 us
    unnamed x20, local copies, waits for them, and re-layouts  9.43 us
    broadcast_in_dim x2, local copies, waits for them, and re-layouts, local(): pair_sum = pair_sum + jnp.where(chip_hit, extra_pair[:, None, :], 0.0)  9.2 us
    ppermute x8, starting transfers between devices, swap(): return lax.ppermute(value, 'tensor', [(i, i ^ mask) for i in range(count)])  8.75 us
    ppermute x8, waiting for transfers between devices, swap(): return lax.ppermute(value, 'tensor', [(i, i ^ mask) for i in range(count)])  8.48 us
  transfers between devices with their start and end apart: 14, of which 4 were waited for; matrix products, arithmetic and copies ran while one was open for 42% of the time, Pallas kernels for 0%

profile of v1, /device:TPU:32, one launch (start us, length us, event | category | flops | bytes accessed | tf_op | source)
XLA Modules:
  0.0 147.8 jit_solution(12647807481504113741)
XLA Ops:
  0.7 1.3 dynamic_slice.31
  2.0 0.6 iota_compare_fusion.7
  2.7 1.0 broadcast_select_fusion
  3.7 5.8 %fusion.37 = f32[128,8192]{1,0:T(8,128)} fusion(bf16[128,256]{1,0:T(8,128)(2,1)S(1)} %bitcast.75, bf16[8192,256]{1,0:T(8,128)(2,1)} %param.17), kind=kOutput, calls=%fused_computation.78 | convolution fusion | flops 536870912 | bytes 8454144 | tf_op jit(solution)/shard_map/dot_general | solution.py:45
  9.5 0.3 copy.41
  9.8 1.1 copy.31
  10.9 4.6 %all-to-all-start = ((bf16[8,32,1024]{2,1,0:T(8,128)(2,1)}), bf16[8,32,1024]{2,1,0:T(8,128)(2,1)S(1)}, u32[]{:S(2)}, u32[]{:S(2)}) async-start(bf16[8,32,1024]{2,1,0:T(8,128)(2,1)} %copy.31), calls=%async_computation | async-start | bytes 1048576 | tf_op jit(solution)/shard_map/all_to_all | solution.py:90
  15.5 0.5 fusion.38
  16.2 3.8 %copy.34 = bf16[256,32,64]{2,1,0:T(8,128)(2,1)} copy(bf16[256,32,64]{0,2,1:T(8,128)(2,1)S(1)} %bitcast.65) | data formatting | bytes 2097152 | tf_op jit(solution)/shard_map/reshape | solution.py:120
  20.0 2.9 %fusion.15 = f32[256,1,64]{2,1,0:T(1,128)} fusion(bf16[256,32,64]{2,1,0:T(8,128)(2,1)} %copy.34, pred[256,32,1]{1,0,2:T(32,128)(4,1)S(1)} %get-tuple-element.28), kind=kOutput, calls=%fused_computation.28 | convolution fusion | flops 1048576 | bytes 1122304 | tf_op jit(solution)/shard_map/tsk,ts->tk/dot_general | solution.py:123
  22.9 0.5 collective-permute-start.1
  23.4 6.3 %copy.32 = bf16[1024,2048]{0,1:T(8,128)(2,1)} copy(bf16[1024,2048]{1,0:T(8,128)(2,1)} %param.18) | data formatting | bytes 8388608 | tf_op args[3]
  29.7 0.8 copy-done.3
  30.5 4.5 %fusion.39 = bf16[256,32,64]{0,2,1:T(8,128)(2,1)} fusion(bf16[256,1024,1]{1,0,2:T(8,128)(2,1)S(1)} %bitcast.72, bf16[32,64,1024]{2,1,0:T(8,128)(2,1)} %bitcast.66), kind=kOutput, calls=%fused_computation.80 | convolution fusion | flops 1073741824 | bytes 5767168 | tf_op jit(solution)/shard_map/dot_general | solution.py:161
  35.0 3.9 %copy.38 = bf16[256,32,64]{2,1,0:T(8,128)(2,1)S(1)} copy(bf16[256,32,64]{0,2,1:T(8,128)(2,1)} %fusion.39) | data formatting | bytes 2097152 | tf_op jit(solution)/shard_map/dot_general | solution.py:161
  38.9 0.7 fusion.13
  39.8 1.0 add.157
  40.8 2.1 %collective-permute-start.2 = (f32[256,64]{1,0:T(8,128)S(1)}, f32[256,64]{1,0:T(8,128)S(1)}, u32[]{:S(2)}, u32[]{:S(2)}) collective-permute-start(f32[256,64]{1,0:T(8,128)S(1)} %add.157), channel_id=1, source_target_pairs={{0,2},{1,3},{2,0},{3,1},{4,6},{5,7},{6,4},{7,5},{8,10},{9,11},{10,... | collective-permute-start | bytes 196616 | tf_op jit(solution)/shard_map/ppermute | solution.py:51
  42.9 0.1 collective-permute-start.9
  43.0 4.1 %collective-permute-done.2 = f32[256,64]{1,0:T(8,128)S(1)} collective-permute-done((f32[256,64]{1,0:T(8,128)S(1)}, f32[256,64]{1,0:T(8,128)S(1)}, u32[]{:S(2)}, u32[]{:S(2)}) %collective-permute-start.2) | collective-permute-done | bytes 65568 | tf_op jit(solution)/shard_map/ppermute | solution.py:51
  47.2 3.6 %collective-permute-start.3 = (f32[256,64]{1,0:T(8,128)S(1)}, f32[256,64]{1,0:T(8,128)S(1)}, u32[]{:S(2)}, u32[]{:S(2)}) collective-permute-start(f32[256,64]{1,0:T(8,128)S(1)} %add.158), channel_id=1, source_target_pairs={{0,4},{1,5},{2,6},{3,7},{4,0},{5,1},{6,2},{7,3},{8,12},{9,13},{10,... | collective-permute-start | bytes 196616 | tf_op jit(solution)/shard_map/ppermute | solution.py:51
  50.8 2.3 %collective-permute-start.10 = (f32[256,64]{1,0:T(8,128)S(1)}, f32[256,64]{1,0:T(8,128)S(1)}, u32[]{:S(2)}, u32[]{:S(2)}) collective-permute-start(f32[256,64]{1,0:T(8,128)S(1)} %add.179), channel_id=1, source_target_pairs={{0,4},{1,5},{2,6},{3,7},{4,0},{5,1},{6,2},{7,3},{8,12},{9,13},{10,... | collective-permute-start | bytes 196616 | tf_op jit(solution)/shard_map/ppermute | solution.py:51
  53.1 0.1 convert_reduce_fusion
  53.2 2.2 %collective-permute-done.3 = f32[256,64]{1,0:T(8,128)S(1)} collective-permute-done((f32[256,64]{1,0:T(8,128)S(1)}, f32[256,64]{1,0:T(8,128)S(1)}, u32[]{:S(2)}, u32[]{:S(2)}) %collective-permute-start.3) | collective-permute-done | bytes 65568 | tf_op jit(solution)/shard_map/ppermute | solution.py:51
  55.5 2.1 %collective-permute-done.10 = f32[256,64]{1,0:T(8,128)S(1)} collective-permute-done((f32[256,64]{1,0:T(8,128)S(1)}, f32[256,64]{1,0:T(8,128)S(1)}, u32[]{:S(2)}, u32[]{:S(2)}) %collective-permute-start.10) | collective-permute-done | bytes 65568 | tf_op jit(solution)/shard_map/ppermute | solution.py:51
  57.6 0.1 fusion.23
  57.7 1.8 %broadcast_multiply_fusion = bf16[256,32,64]{2,1,0:T(8,128)(2,1)S(1)} fusion(bf16[256,32]{1,0:T(8,128)(2,1)S(1)} %get-tuple-element.29, bf16[256,64]{1,0:T(8,128)(2,1)S(1)} %get-tuple-element.27), kind=kLoop, calls=%fused_computation.16 | loop fusion | flops 524288 | bytes 1097728 | tf_op jit(solution)/shard_map/mul | solution.py:125
  59.5 2.4 %mul.155 = bf16[4,2,32,2048]{3,2,1,0:T(8,128)(2,1)} reshape(bf16[256,32,64]{2,1,0:T(8,128)(2,1)S(1)} %broadcast_multiply_fusion) | data formatting | bytes 2097152 | tf_op jit(solution)/shard_map/mul | solution.py:125
  61.9 3.8 %fusion = f32[4,2,32,1024]{3,2,1,0:T(8,128)S(1)} fusion(bf16[4,2,32,2048]{3,2,1,0:T(8,128)(2,1)} %mul.155, bf16[1024,2048]{1,0:T(8,128)(2,1)} %param.18), kind=kOutput, calls=%fused_computation.1 | convolution fusion | flops 1073741824 | bytes 6291456 | tf_op jit(solution)/shard_map/dot_general | solution.py:45
  65.8 0.9 constant_dynamic-slice_fusion.1
  66.7 1.6 %convolution_convert_fusion = bf16[512,1280]{1,0:T(8,128)(2,1)} fusion(bf16[256,256]{1,0:T(8,128)(2,1)S(1)} %broadcast_select_fusion, bf16[256,1024]{1,0:T(8,128)(2,1)S(1)} %bitcast.73, s32[256]{0:T(256)S(1)} %multiply_add_fusion.4), kind=kOutput, calls=%fused_computation.4 | convolution fusion | flops 337641472 | bytes 1967104 | tf_op jit(solution)/shard_map/dot_general | solution.py:156
  68.3 1.0 convolution_convert_fusion.1
  69.3 11.2 %all-to-all-start.2 = ((bf16[32,16,128]{2,1,0:T(8,128)(2,1)}), bf16[32,16,128]{2,1,0:T(8,128)(2,1)S(1)}, u32[]{:S(2)}, u32[]{:S(2)}) async-start(bf16[32,16,128]{2,1,0:T(8,128)(2,1)} %bitcast.27), calls=%async_computation.2 | async-start | bytes 262144 | tf_op jit(solution)/shard_map/all_to_all | solution.py:170
  80.5 0.1 bitcast_select_fusion.1
  80.7 3.1 %broadcast_in_dim.80 = f32[128,4,2048]{2,1,0:T(4,128)} broadcast(f32[128,2048]{1,0:T(8,128)S(1)} %pad_maximum_fusion), dimensions={0,2} | broadcast | bytes 5242880 | tf_op jit(solution)/shard_map/jit(_where)/broadcast_in_dim | solution.py:142
  83.9 6.1 %broadcast_in_dim.81 = f32[4,32,8192]{2,1,0:T(8,128)} reshape(f32[128,4,2048]{2,1,0:T(4,128)} %broadcast_in_dim.80) | data formatting | bytes 8388608 | tf_op jit(solution)/shard_map/jit(_where)/broadcast_in_dim | solution.py:142
  89.9 7.0 %convolution_add_fusion = f32[128,8192]{1,0:T(8,128)} fusion(f32[128,8192]{1,0:T(8,128)} %collective-permute-done, bf16[128,256]{1,0:T(8,128)(2,1)S(1)} %bitcast.74, bf16[8192,256]{1,0:T(8,128)(2,1)} %param.17), kind=kOutput, calls=%fused_computation | convolution fusion | flops 537919488 | bytes 12648448 | tf_op jit(solution)/shard_map/dot_general | solution.py:45
  96.9 9.8 %all-to-all-start.1 = ((bf16[32,16,1280]{2,1,0:T(8,128)(2,1)}), bf16[32,16,1280]{2,1,0:T(8,128)(2,1)S(1)}, u32[]{:S(2)}, u32[]{:S(2)}) async-start(bf16[32,16,1280]{2,1,0:T(8,128)(2,1)} %bitcast.20), calls=%async_computation.1 | async-start | bytes 2621440 | tf_op jit(solution)/shard_map/all_to_all | solution.py:157
  106.7 4.0 %select_add_fusion = f32[4,32,8192]{2,1,0:T(8,128)S(1)} fusion(f32[4,32,8192]{2,1,0:T(8,128)} %bitcast.64, f32[4,32,8192]{2,1,0:T(8,128)} %broadcast_in_dim.81, pred[8192]{0:T(1024)(128)(4,1)S(1)} %bitcast.80), kind=kLoop, calls=%fused_computation.3 | loop fusion | flops 2097152 | bytes 12591104 | tf_op jit(solution)/shard_map/add | solution.py:142
  110.8 1.9 %copy-done.1 = f32[4,32,8192]{2,1,0:T(8,128)} copy-done((f32[4,32,8192]{2,1,0:T(8,128)}, f32[4,32,8192]{2,1,0:T(8,128)S(1)}, u32[]{:S(2)}) %copy-start.1) | copy-done | bytes 4194328
  112.7 1.0 fusion.10
  113.7 2.5 %collective-permute-start.7 = (bf16[32,8192]{1,0:T(8,128)(2,1)}, bf16[32,8192]{1,0:T(8,128)(2,1)}, u32[]{:S(2)}, u32[]{:S(2)}) collective-permute-start(bf16[32,8192]{1,0:T(8,128)(2,1)} %get-tuple-element.18), channel_id=1, source_target_pairs={{0,4},{1,5},{2,6},{3,7},{4,0},{5,1},{6,2},{7,3},{8,12},{9,13},{10,... | collective-permute-start | bytes 1572872 | tf_op jit(solution)/shard_map/ppermute | solution.py:149
  116.2 1.2 collective-permute-start.6
  117.4 0.8 collective-permute-start.5
  118.2 22.5 %all-to-all-done.1 = bf16[32,16,1280]{2,1,0:T(8,128)(2,1)S(1)} async-done(((bf16[32,16,1280]{2,1,0:T(8,128)(2,1)}), bf16[32,16,1280]{2,1,0:T(8,128)(2,1)S(1)}, u32[]{:S(2)}, u32[]{:S(2)}) %all-to-all-start.1) | async-done | bytes 1310752 | tf_op jit(solution)/shard_map/all_to_all | solution.py:157
  140.7 1.8 %multiply_subtract_fusion.1 = (f32[64,256]{1,0:T(8,128)}, f32[64,256]{1,0:T(8,128)}, f32[64,256]{1,0:T(8,128)}) fusion(f32[64,256]{1,0:T(8,128)} %param.23, f32[64,256]{1,0:T(8,128)} %param.24, f32[64,256]{1,0:T(8,128)} %param.25, bf16[512,1280]{1,0:T(8,128)(2,1)S(1)} %bitcast.68, bf16[512,128]{1,0:T(8,128)(2,1)S(1)} %bitcast.78), kind=kOutput, calls=%fused_computation.54 | convolution fusion | flops 17039360 | bytes 786432 | tf_op jit(solution)/shard_map/dot_general | solution.py:45
  142.5 2.5 %multiply_subtract_fusion = (f32[1024,64]{0,1:T(8,128)}, f32[1024,64]{0,1:T(8,128)}, f32[1024,64]{0,1:T(8,128)}) fusion(f32[1024,64]{0,1:T(8,128)} %param.20, f32[1024,64]{0,1:T(8,128)} %param.21, f32[1024,64]{0,1:T(8,128)} %param.22, bf16[512,128]{1,0:T(8,128)(2,1)S(1)} %bitcast.79, bf16[512,1280]{1,0:T(8,128)(2,1)S(1)} %bitcast.69), kind=kOutput, calls=%fused_computation.32 | convolution fusion | flops 68157440 | bytes 2752512 | tf_op jit(solution)/shard_map/dot_general | solution.py:45
  145.1 2.7 %fusion.6 = bf16[32,8192]{1,0:T(8,128)(2,1)} fusion(bf16[32,8192]{1,0:T(8,128)(2,1)} %collective-permute-done.7, bf16[32,8192]{1,0:T(8,128)(2,1)} %collective-permute-done.6, bf16[32,8192]{1,0:T(8,128)(2,1)} %collective-permute-done.5, f32[4,32,8192]{2,1,0:T(8,128)} %copy-done.1, s32[]{:T(128)S(6)} %select_n.86), kind=kLoop, calls=%fused_computation.12 | loop fusion | flops 1835008 | bytes 3145732 | tf_op jit(solution)/shard_map/convert_element_type | solution.py:153
  (39 shorter events, 0.6 us)
Async XLA Ops:
  0.6 14.8 %copy-start = (bf16[2048,256]{1,0:T(8,128)(2,1)S(1)}, bf16[2048,256]{1,0:T(8,128)(2,1)}, u32[]{:S(2)}) copy-start(bf16[2048,256]{1,0:T(8,128)(2,1)} %param.19) | copy-start | bytes 3145732
  3.7 5.8 %copy-start.2 = (bf16[32,8192]{1,0:T(8,128)(2,1)S(1)}, bf16[32,8192]{1,0:T(8,128)(2,1)}, u32[]{:S(2)}) copy-start(bf16[32,8192]{1,0:T(8,128)(2,1)} %param.15) | copy-start | bytes 1572868
  9.5 6.5 %copy-start.5 = (s32[256,1]{0,1:T(1,128)S(1)}, s32[256,1]{0,1:T(1,128)}, u32[]{:S(2)}) copy-start(s32[256,1]{0,1:T(1,128)} %param.26) | copy-start | bytes 3076
  9.5 6.5 %copy-start.6 = (s32[32]{0:T(128)S(1)}, s32[32]{0:T(128)}, u32[]{:S(2)}) copy-start(s32[32]{0:T(128)} %param.27) | copy-start | bytes 388
  9.5 6.5 %copy-start.7 = (s32[32]{0:T(128)S(1)}, s32[32]{0:T(128)}, u32[]{:S(2)}) copy-start(s32[32]{0:T(128)} %param.28) | copy-start | bytes 388
  9.5 80.5 %collective-permute-start = (f32[128,8192]{1,0:T(8,128)}, f32[128,8192]{1,0:T(8,128)}, u32[]{:S(2)}, u32[]{:S(2)}) collective-permute-start(f32[128,8192]{1,0:T(8,128)} %fusion.37), channel_id=1, source_target_pairs={{0,1},{1,0},{2,3},{3,2},{4,5},{5,4},{6,7},{7,6},{8,9},{9,8},{10,11... | collective-permute-start | bytes 12582920 | tf_op jit(solution)/shard_map/ppermute | solution.py:51
  10.9 18.8 %all-to-all-start = ((bf16[8,32,1024]{2,1,0:T(8,128)(2,1)}), bf16[8,32,1024]{2,1,0:T(8,128)(2,1)S(1)}, u32[]{:S(2)}, u32[]{:S(2)}) async-start(bf16[8,32,1024]{2,1,0:T(8,128)(2,1)} %copy.31), calls=%async_computation | async-start | bytes 1048576 | tf_op jit(solution)/shard_map/all_to_all | solution.py:90
  22.9 16.9 %collective-permute-start.1 = (f32[256,64]{1,0:T(8,128)}, f32[256,64]{1,0:T(8,128)}, u32[]{:S(2)}, u32[]{:S(2)}) collective-permute-start(f32[256,64]{1,0:T(8,128)} %bitcast.9), channel_id=1, source_target_pairs={{0,1},{1,0},{2,3},{3,2},{4,5},{5,4},{6,7},{7,6},{8,9},{9,8},{10,11... | collective-permute-start | bytes 196616 | tf_op jit(solution)/shard_map/ppermute | solution.py:51
  29.7 0.8 copy-start.3
  39.6 3.3 %collective-permute-start.8 = (f32[256,64]{1,0:T(8,128)S(1)}, f32[256,64]{1,0:T(8,128)S(1)}, u32[]{:S(2)}, u32[]{:S(2)}) collective-permute-start(f32[256,64]{1,0:T(8,128)S(1)} %bitcast.76), channel_id=1, source_target_pairs={{0,1},{1,0},{2,3},{3,2},{4,5},{5,4},{6,7},{7,6},{8,9},{9,8},{10,11... | collective-permute-start | bytes 196616 | tf_op jit(solution)/shard_map/ppermute | solution.py:51
  40.8 6.4 %collective-permute-start.2 = (f32[256,64]{1,0:T(8,128)S(1)}, f32[256,64]{1,0:T(8,128)S(1)}, u32[]{:S(2)}, u32[]{:S(2)}) collective-permute-start(f32[256,64]{1,0:T(8,128)S(1)} %add.157), channel_id=1, source_target_pairs={{0,2},{1,3},{2,0},{3,1},{4,6},{5,7},{6,4},{7,5},{8,10},{9,11},{10,... | collective-permute-start | bytes 196616 | tf_op jit(solution)/shard_map/ppermute | solution.py:51
  42.9 7.9 %collective-permute-start.9 = (f32[256,64]{1,0:T(8,128)S(1)}, f32[256,64]{1,0:T(8,128)S(1)}, u32[]{:S(2)}, u32[]{:S(2)}) collective-permute-start(f32[256,64]{1,0:T(8,128)S(1)} %add.178), channel_id=1, source_target_pairs={{0,2},{1,3},{2,0},{3,1},{4,6},{5,7},{6,4},{7,5},{8,10},{9,11},{10,... | collective-permute-start | bytes 196616 | tf_op jit(solution)/shard_map/ppermute | solution.py:51
  47.2 8.3 %collective-permute-start.3 = (f32[256,64]{1,0:T(8,128)S(1)}, f32[256,64]{1,0:T(8,128)S(1)}, u32[]{:S(2)}, u32[]{:S(2)}) collective-permute-start(f32[256,64]{1,0:T(8,128)S(1)} %add.158), channel_id=1, source_target_pairs={{0,4},{1,5},{2,6},{3,7},{4,0},{5,1},{6,2},{7,3},{8,12},{9,13},{10,... | collective-permute-start | bytes 196616 | tf_op jit(solution)/shard_map/ppermute | solution.py:51
  50.8 6.7 %collective-permute-start.10 = (f32[256,64]{1,0:T(8,128)S(1)}, f32[256,64]{1,0:T(8,128)S(1)}, u32[]{:S(2)}, u32[]{:S(2)}) collective-permute-start(f32[256,64]{1,0:T(8,128)S(1)} %add.179), channel_id=1, source_target_pairs={{0,4},{1,5},{2,6},{3,7},{4,0},{5,1},{6,2},{7,3},{8,12},{9,13},{10,... | collective-permute-start | bytes 196616 | tf_op jit(solution)/shard_map/ppermute | solution.py:51
  61.9 4.8 %copy-start.4 = (bf16[8,32,1024]{2,1,0:T(8,128)(2,1)S(1)}, bf16[8,32,1024]{2,1,0:T(8,128)(2,1)}, u32[]{:S(2)}) copy-start(bf16[8,32,1024]{2,1,0:T(8,128)(2,1)} %copy-done.3) | copy-start | bytes 1572868
  66.7 13.8 %collective-permute-start.4 = (f32[128,1024]{1,0:T(8,128)}, f32[128,1024]{1,0:T(8,128)S(1)}, u32[]{:S(2)}, u32[]{:S(2)}) collective-permute-start(f32[128,1024]{1,0:T(8,128)} %bitcast.13), channel_id=1, source_target_pairs={{0,1},{1,0},{2,3},{3,2},{4,5},{5,4},{6,7},{7,6},{8,9},{9,8},{10,11... | collective-permute-start | bytes 1572872 | tf_op jit(solution)/shard_map/ppermute | solution.py:51
  69.3 27.6 %all-to-all-start.2 = ((bf16[32,16,128]{2,1,0:T(8,128)(2,1)}), bf16[32,16,128]{2,1,0:T(8,128)(2,1)S(1)}, u32[]{:S(2)}, u32[]{:S(2)}) async-start(bf16[32,16,128]{2,1,0:T(8,128)(2,1)} %bitcast.27), calls=%async_computation.2 | async-start | bytes 262144 | tf_op jit(solution)/shard_map/all_to_all | solution.py:170
  96.9 43.8 %all-to-all-start.1 = ((bf16[32,16,1280]{2,1,0:T(8,128)(2,1)}), bf16[32,16,1280]{2,1,0:T(8,128)(2,1)S(1)}, u32[]{:S(2)}, u32[]{:S(2)}) async-start(bf16[32,16,1280]{2,1,0:T(8,128)(2,1)} %bitcast.20), calls=%async_computation.1 | async-start | bytes 2621440 | tf_op jit(solution)/shard_map/all_to_all | solution.py:157
  110.8 1.9 %copy-start.1 = (f32[4,32,8192]{2,1,0:T(8,128)}, f32[4,32,8192]{2,1,0:T(8,128)S(1)}, u32[]{:S(2)}) copy-start(f32[4,32,8192]{2,1,0:T(8,128)S(1)} %select_add_fusion) | copy-start | bytes 12582916
  113.7 31.4 %collective-permute-start.7 = (bf16[32,8192]{1,0:T(8,128)(2,1)}, bf16[32,8192]{1,0:T(8,128)(2,1)}, u32[]{:S(2)}, u32[]{:S(2)}) collective-permute-start(bf16[32,8192]{1,0:T(8,128)(2,1)} %get-tuple-element.18), channel_id=1, source_target_pairs={{0,4},{1,5},{2,6},{3,7},{4,0},{5,1},{6,2},{7,3},{8,12},{9,13},{10,... | collective-permute-start | bytes 1572872 | tf_op jit(solution)/shard_map/ppermute | solution.py:149
  116.2 28.9 %collective-permute-start.6 = (bf16[32,8192]{1,0:T(8,128)(2,1)S(1)}, bf16[32,8192]{1,0:T(8,128)(2,1)}, u32[]{:S(2)}, u32[]{:S(2)}) collective-permute-start(bf16[32,8192]{1,0:T(8,128)(2,1)S(1)} %get-tuple-element.19), channel_id=1, source_target_pairs={{0,6},{1,7},{2,0},{3,1},{4,2},{5,3},{6,4},{7,5},{8,14},{9,15},{10,... | collective-permute-start | bytes 1572872 | tf_op jit(solution)/shard_map/ppermute | solution.py:149
  117.4 27.7 %collective-permute-start.5 = (bf16[32,8192]{1,0:T(8,128)(2,1)S(1)}, bf16[32,8192]{1,0:T(8,128)(2,1)}, u32[]{:S(2)}, u32[]{:S(2)}) collective-permute-start(bf16[32,8192]{1,0:T(8,128)(2,1)S(1)} %get-tuple-element.17), channel_id=1, source_target_pairs={{0,2},{1,3},{2,4},{3,5},{4,6},{5,7},{6,0},{7,1},{8,10},{9,11},{10,... | collective-permute-start | bytes 1572872 | tf_op jit(solution)/shard_map/ppermute | solution.py:149

commit v2 on v1

v2 whole, which is shorter than its diff:
```python
import functools

import jax
import jax.numpy as jnp
from jax import lax
from jax.experimental import pallas as pl
from jax.experimental.pallas import tpu as pltpu
from jax.sharding import PartitionSpec as P

RMIN = 8
PADDED_RANK = 64
CAP = 16


adapter_alpha_scale = 16.0
beta_one = 0.9
beta_two = 0.999
adam_eps = 1e-08
learn_rate = 0.0002
weight_decay = 0.1
first_fix = 0.9999734386011124
second_fix = 0.09520785288629038


def adamw(master, moment, second, grad):
    new_moment = beta_one * moment + (1.0 - beta_one) * grad
    new_second = beta_two * second + (1.0 - beta_two) * grad * grad
    update = new_moment / first_fix / (jnp.sqrt(new_second / second_fix) + adam_eps)
    new_master = master - learn_rate * (update + weight_decay * master)
    return (new_master, new_moment, new_second)


def contract_helper(left, right, left_dim, right_dim):
    return lax.dot_general(
        left, right, (((left_dim,), (right_dim,)), ((), ())), preferred_element_type=jnp.float32
    )


def swap(value, mask, count):
    return lax.ppermute(value, "tensor", [(i, i ^ mask) for i in range(count)])


def sum_over_tensor(value, count):
    mask = 1
    while mask < count:
        value = value + swap(value, mask, count)
        mask *= 2
    return value


VMEM_LIMIT = 60 * 1024 * 1024
VMEM = pltpu.MemorySpace.VMEM
SMEM = pltpu.MemorySpace.SMEM
NT = (((1,), (1,)), ((), ()))
NN = (((1,), (0,)), ((), ()))


def call(kernel, out_shape, flops, moved, **options):
    return pl.pallas_call(
        kernel,
        out_shape=out_shape,
        compiler_params=pltpu.CompilerParams(vmem_limit_bytes=VMEM_LIMIT),
        cost_estimate=pl.CostEstimate(flops=flops, bytes_accessed=moved, transcendentals=0),
        **options,
    )


def whole(shape, memory_space=None):
    zeros = (0,) * len(shape)
    return pl.BlockSpec(shape, lambda *_: zeros, memory_space=memory_space)


def dot(left, right, dims):
    return lax.dot_general(left, right, dims, preferred_element_type=jnp.float32)


def lane_slot(shape, first):
    return (lax.broadcasted_iota(jnp.int32, shape, 1) // PADDED_RANK + first).astype(jnp.float32)


def prep_kernel(rows_own, live_ref, bucket_ref, owner_ref, adapter_ref, cot_ref, up_ref,
                masked_ref, turned_ref, slot_ref, factor_ref, place_ref, up_own_ref):
    tokens = cot_ref.shape[0]
    n_chip = tokens // rows_own // 2
    position = lax.axis_index("tensor")
    chip, core = position // 2, position % 2
    live = live_ref[lax.axis_index("dp")]
    token = lax.broadcasted_iota(jnp.int32, (tokens, 1), 0)
    masked = jnp.where(token < live, cot_ref[...].astype(jnp.float32), 0.0).astype(jnp.bfloat16)
    masked_ref[...] = masked
    for step in range(n_chip):
        block = (chip + step) % n_chip * 2
        for out, k in ((0, core), (tokens // 2, 1 - core)):
            start = pl.multiple_of((block + k) * rows_own, rows_own)
            ids = start + lax.broadcasted_iota(jnp.int32, (rows_own, 1), 0)
            rows = cot_ref[pl.ds(start, rows_own), :].astype(jnp.float32)
            turned_ref[pl.ds(out + step * rows_own, rows_own), :] = jnp.where(
                ids < live, rows, 0.0
            ).astype(jnp.bfloat16)
    adapter = adapter_ref[...]
    slot = jnp.zeros_like(adapter)
    rank = jnp.zeros_like(adapter)
    for a in range(owner_ref.shape[0]):
        hit = adapter == a
        slot = jnp.where(hit, owner_ref[a], slot)
        rank = jnp.where(hit, lax.shift_left(RMIN, bucket_ref[a]), rank)
    slot_row = slot.astype(jnp.float32)
    rank_row = rank.astype(jnp.float32)
    down = lax.broadcasted_iota(jnp.int32, (tokens, tokens), 0)
    across = lax.broadcasted_iota(jnp.int32, (tokens, tokens), 1)
    diagonal = down == across
    slot_col = jnp.sum(jnp.where(diagonal, slot_row, 0.0), axis=1, keepdims=True)
    rank_col = jnp.sum(jnp.where(diagonal, rank_row, 0.0), axis=1, keepdims=True)
    earlier = jnp.where((slot_col == slot_row) & (down < across), 1.0, 0.0)
    place = slot_row * CAP + jnp.sum(earlier, axis=0, keepdims=True)
    place_ref[...] = place.astype(jnp.int32)
    lanes = factor_ref.shape[1]
    slot_wide = jnp.broadcast_to(slot_col, (tokens, lanes))
    slot_ref[...] = slot_wide
    kept = lax.broadcasted_iota(jnp.int32, (tokens, lanes), 1) % PADDED_RANK
    factor_ref[...] = jnp.where(
        kept.astype(jnp.float32) < rank_col, adapter_alpha_scale / rank_col, 0.0
    )
    chunk = 256
    acc = jnp.zeros((tokens, chunk), jnp.float32)
    for c in range(up_ref.shape[0] // chunk):
        part = dot(masked, up_ref[pl.ds(c * chunk, chunk), :], NT)
        hit = slot_col == lane_slot((1, chunk), c * chunk // PADDED_RANK)
        acc = acc + jnp.where(hit, part, 0.0)
    acc = acc[:, :128] + acc[:, 128:]
    up_own_ref[...] = acc[:, :PADDED_RANK] + acc[:, PADDED_RANK:]


def prep(rows_own, live, bucket, owner, adapter_row, cotangent, up_factors):
    tokens, kv = cotangent.shape
    shapes = (
        jax.ShapeDtypeStruct((tokens, kv), jnp.bfloat16),
        jax.ShapeDtypeStruct((tokens, kv), jnp.bfloat16),
        jax.ShapeDtypeStruct((tokens, 128), jnp.float32),
        jax.ShapeDtypeStruct((tokens, 128), jnp.float32),
        jax.ShapeDtypeStruct((1, tokens), jnp.int32),
        jax.ShapeDtypeStruct((tokens, PADDED_RANK), jnp.float32),
    )
    return call(
        functools.partial(prep_kernel, rows_own),
        shapes,
        2 * tokens * kv * up_factors.shape[0],
        up_factors.size * 2,
        grid=(1,),
        in_specs=[whole(v.shape, SMEM) for v in (live, bucket, owner)]
        + [whole(v.shape) for v in (adapter_row, cotangent, up_factors)],
        out_specs=tuple(whole(v.shape) for v in shapes),
        name="prep",
    )(live, bucket, owner, adapter_row, cotangent, up_factors)


def frozen_kernel(turned_ref, frozen_ref, ours_ref, theirs_ref):
    half = ours_ref.shape[0]
    both = dot(turned_ref[...], frozen_ref[...], NT)
    ours_ref[...] = both[:half, :]
    theirs_ref[...] = both[half:, :]


def frozen_term(turned, frozen, part, width):
    tokens, kv = turned.shape
    chunk = width // 2
    half = jax.ShapeDtypeStruct((tokens // 2, width), jnp.float32)
    block = pl.BlockSpec((tokens // 2, chunk), lambda i: (0, i))
    return call(
        frozen_kernel,
        (half, half),
        2 * tokens * kv * width,
        2 * kv * width + 4 * tokens * width,
        grid=(2,),
        in_specs=[whole(turned.shape), pl.BlockSpec((chunk, kv), lambda i: (2 * part + i, 0))],
        out_specs=(block, block),
        name="frozen_term",
    )(turned, frozen)


def pack_kernel(place_ref, hidden_ref, masked_ref, out_ref):
    rows, tokens = out_ref.shape[0], place_ref.shape[1]
    down = lax.broadcasted_iota(jnp.int32, (rows, tokens), 0)
    pick = jnp.where(down == place_ref[...], 1.0, 0.0).astype(jnp.bfloat16)
    width = hidden_ref.shape[1]
    out_ref[:, :width] = dot(pick, hidden_ref[...], NN).astype(jnp.bfloat16)
    out_ref[:, width:] = dot(pick, masked_ref[...], NN).astype(jnp.bfloat16)


def pack_rows(place, hidden_columns, masked, rows):
    columns = hidden_columns.shape[1] + masked.shape[1]
    return call(
        pack_kernel,
        jax.ShapeDtypeStruct((rows, columns), jnp.bfloat16),
        2 * rows * columns * hidden_columns.shape[0],
        4 * rows * columns,
        grid=(1,),
        in_specs=[whole(v.shape) for v in (place, hidden_columns, masked)],
        out_specs=whole((rows, columns)),
        name="pack",
    )(place, hidden_columns, masked)


def down_kernel(hidden_ref, factors_ref, slot_ref, out_ref, acc_ref):
    step = pl.program_id(0)
    chunk = factors_ref.shape[1]
    slots = chunk // PADDED_RANK

    @pl.when(step == 0)
    def _():
        acc_ref[...] = jnp.zeros_like(acc_ref)

    part = dot(hidden_ref[...], factors_ref[...], NN)
    first = (step * slots).astype(jnp.float32)
    acc = acc_ref[...]
    for c in range(chunk // 128):
        hit = slot_ref[...] == lane_slot((1, 128), 2 * c) + first
        acc = acc + jnp.where(hit, part[:, c * 128 : (c + 1) * 128], 0.0)
    acc_ref[...] = acc

    @pl.when(step == pl.num_programs(0) - 1)
    def _():
        out_ref[...] = acc[:, :PADDED_RANK] + acc[:, PADDED_RANK:]


def down_low_rank(hidden_columns, factors, slot_wide):
    tokens, columns = hidden_columns.shape
    chunk = 512
    return call(
        down_kernel,
        jax.ShapeDtypeStruct((tokens, PADDED_RANK), jnp.float32),
        2 * tokens * factors.size,
        2 * factors.size,
        grid=(factors.shape[1] // chunk,),
        in_specs=[
            pl.BlockSpec((tokens, columns), lambda i: (0, 0)),
            pl.BlockSpec((columns, chunk), lambda i: (0, i)),
            pl.BlockSpec((tokens, 128), lambda i: (0, 0)),
        ],
        out_specs=pl.BlockSpec((tokens, PADDED_RANK), lambda i: (0, 0)),
        scratch_shapes=[pltpu.VMEM((tokens, 128), jnp.float32)],
        name="down_low_rank",
    )(hidden_columns, factors, slot_wide)


def extra_kernel(rows_own, weight_ref, slot_ref, factors_ref, ours_ref, theirs_ref, acc_ref):
    step = pl.program_id(0)
    chunk = factors_ref.shape[1]
    tokens = weight_ref.shape[0]
    n_chip = tokens // rows_own // 2

    @pl.when(step == 0)
    def _():
        acc_ref[...] = jnp.zeros_like(acc_ref)

    weight = weight_ref[...].astype(jnp.float32)
    double = jnp.concatenate([weight, weight], axis=1)
    first = (step * (chunk // PADDED_RANK)).astype(jnp.float32)
    pieces = []
    for c in range(chunk // 128):
        hit = slot_ref[...] == lane_slot((1, 128), 2 * c) + first
        pieces.append(jnp.where(hit, double, 0.0).astype(jnp.bfloat16))
    placed = jnp.concatenate(pieces, axis=1)
    acc_ref[...] += dot(placed, factors_ref[...], NT)

    @pl.when(step == pl.num_programs(0) - 1)
    def _():
        position = lax.axis_index("tensor")
        chip, core = position // 2, position % 2
        for turn in range(n_chip):
            block = (chip + turn) % n_chip * 2
            for out, k in ((ours_ref, core), (theirs_ref, 1 - core)):
                start = pl.multiple_of((block + k) * rows_own, rows_own)
                out[pl.ds(turn * rows_own, rows_own), :] = acc_ref[pl.ds(start, rows_own), :]


def extra_term(rows_own, up_weight, slot_wide, factors):
    tokens = up_weight.shape[0]
    columns = factors.shape[0]
    chunk = 512
    half = jax.ShapeDtypeStruct((tokens // 2, columns), jnp.float32)
    half_spec = pl.BlockSpec((tokens // 2, columns), lambda i: (0, 0))
    return call(
        functools.partial(extra_kernel, rows_own),
        (half, half),
        2 * tokens * factors.size,
        2 * factors.size,
        grid=(factors.shape[1] // chunk,),
        in_specs=[
            pl.BlockSpec((tokens, PADDED_RANK), lambda i: (0, 0)),
            pl.BlockSpec((tokens, 128), lambda i: (0, 0)),
            pl.BlockSpec((columns, chunk), lambda i: (0, i)),
        ],
        out_specs=(half_spec, half_spec),
        scratch_shapes=[pltpu.VMEM((tokens, columns), jnp.float32)],
        name="extra_term",
    )(up_weight, slot_wide, factors)


def pair_kernel(rows_own, parts, extra_ours_ref, extra_pair_ref, *refs):
    ours_refs, pair_refs, own_ref, out_refs = (
        refs[:parts],
        refs[parts : 2 * parts],
        refs[2 * parts],
        refs[2 * parts + 1 :],
    )
    step = pl.program_id(0)
    position = lax.axis_index("tensor")
    chip, core = position // 2, position % 2

    def write(value):
        own_ref[...] = value[:rows_own, :]
        for i, out in enumerate(out_refs):
            out[...] = value[(i + 1) * rows_own : (i + 2) * rows_own, :].astype(jnp.bfloat16)

    for part in range(parts):
        here = step // 2 == part

        @pl.when(here & (chip != part))
        def _():
            write(ours_refs[part][...] + pair_refs[part][...])

        @pl.when(here & (chip == part) & (step % 2 == core))
        def _():
            write(ours_refs[part][...] + pair_refs[part][...] + extra_ours_ref[...])

        @pl.when(here & (chip == part) & (step % 2 != core))
        def _():
            write(ours_refs[part][...] + pair_refs[part][...] + extra_pair_ref[...])


def pair_sum(rows_own, ours, from_pair, extra_ours, extra_pair):
    parts = len(ours)
    half, width = ours[0].shape
    columns = extra_ours.shape[1]
    sent = jax.ShapeDtypeStruct((rows_own, parts * width), jnp.bfloat16)
    out_block = pl.BlockSpec((rows_own, columns), lambda i: (0, i))
    in_blocks = [
        pl.BlockSpec((half, columns), lambda i, q=q: (0, jnp.clip(i - 2 * q, 0, 1)))
        for q in range(parts)
    ]
    n_out = half // rows_own - 1
    return call(
        functools.partial(pair_kernel, rows_own, parts),
        (jax.ShapeDtypeStruct((rows_own, parts * width), jnp.float32),) + (sent,) * n_out,
        2 * half * width * parts,
        12 * half * width * parts,
        grid=(2 * parts,),
        in_specs=[whole(extra_ours.shape), whole(extra_pair.shape)] + in_blocks + in_blocks,
        out_specs=(out_block,) * (n_out + 1),
        name="pair_sum",
    )(extra_ours, extra_pair, *ours, *from_pair)


def local(
    hidden,
    cotangent,
    frozen_key_value,
    adapter_down_factors,
    adapter_up_factors,
    down_master_copy,
    down_first_moment,
    down_second_moment,
    up_master_copy,
    up_first_moment,
    up_second_moment,
    adapter_of_token,
    adapter_rank_bucket,
    adapter_owner_slot,
    live_token_counts,
):
    n_tensor = lax.axis_size("tensor")
    n_chip = n_tensor // 2
    tokens = cotangent.shape[0]
    rows_own, width = hidden.shape
    columns = width // n_tensor
    n_slot = adapter_owner_slot.shape[0]

    blocks = hidden.reshape(rows_own, n_tensor, columns).transpose(1, 0, 2)
    hidden_columns = lax.all_to_all(blocks, "tensor", 0, 0, tiled=True).reshape(tokens, columns)

    masked, turned, slot_wide, factor_wide, place, up_own = prep(
        rows_own,
        live_token_counts,
        adapter_rank_bucket,
        adapter_owner_slot,
        adapter_of_token.reshape(1, tokens),
        cotangent,
        adapter_up_factors,
    )
    factor = factor_wide[:, :PADDED_RANK]

    frozen_ours, from_pair = [], []
    for part in range(n_chip):
        mine, theirs = frozen_term(turned, frozen_key_value, part, 2 * columns)
        frozen_ours.append(mine)
        from_pair.append(swap(theirs, 1, n_tensor))

    packed = pack_rows(place, hidden_columns, masked, n_slot * CAP)
    owned = lax.all_to_all(
        packed.reshape(n_slot, CAP, -1), "dp", 0, 0, tiled=True
    ).reshape(n_slot * CAP, -1)

    up_weight = (sum_over_tensor(up_own, n_tensor) * factor).astype(jnp.bfloat16)
    extra_ours, extra_theirs = extra_term(rows_own, up_weight, slot_wide, adapter_down_factors)
    extra_pair = swap(extra_theirs, 1, n_tensor)
    total, *sent = pair_sum(
        rows_own, frozen_ours, from_pair, extra_ours, extra_pair
    )
    for step in range(1, n_chip):
        arrived = lax.ppermute(
            sent[step - 1], "tensor", [(i, (i + 2 * step) % n_tensor) for i in range(n_tensor)]
        )
        total = total + arrived.astype(jnp.float32)
    hidden_gradient = total.astype(jnp.bfloat16)

    down_own = down_low_rank(hidden_columns, adapter_down_factors, slot_wide)
    down_weight = (sum_over_tensor(down_own, n_tensor) * factor).astype(jnp.bfloat16)
    weights = jnp.concatenate([down_weight, up_weight], axis=1)
    pick = (
        jnp.arange(n_slot * CAP, dtype=jnp.int32)[:, None] == place
    ).astype(jnp.bfloat16)
    packed_weights = jnp.dot(pick, weights, preferred_element_type=jnp.float32).astype(
        jnp.bfloat16
    )
    owned, packed_weights = lax.optimization_barrier((owned, packed_weights))
    owned_weights = lax.all_to_all(
        packed_weights.reshape(n_slot, CAP, -1), "dp", 0, 0, tiled=True
    ).reshape(n_slot * CAP, -1)

    grad_down = contract_helper(owned[:, :columns], owned_weights[:, PADDED_RANK:], 0, 0) / tokens
    grad_up = contract_helper(owned_weights[:, :PADDED_RANK], owned[:, columns:], 0, 0) / tokens
    new_dm, new_dmo, new_ds = adamw(
        down_master_copy, down_first_moment, down_second_moment, grad_down
    )
    new_um, new_umo, new_us = adamw(up_master_copy, up_first_moment, up_second_moment, grad_up)
    return (hidden_gradient, new_dm, new_dmo, new_ds, new_um, new_umo, new_us)


def solution(mesh):
    return jax.shard_map(
        local,
        mesh=mesh,
        in_specs=(
            P(("dp", "tensor"), None),
            P("dp", "tensor"),
            P(None, "tensor"),
            P("tensor", None),
            P(None, "tensor"),
            P("tensor", "dp"),
            P("tensor", "dp"),
            P("tensor", "dp"),
            P("dp", "tensor"),
            P("dp", "tensor"),
            P("dp", "tensor"),
            P("dp", None),
            P(),
            P(),
            P(),
        ),
        out_specs=(
            P(("dp", "tensor"), None),
            P("tensor", "dp"),
            P("tensor", "dp"),
            P("tensor", "dp"),
            P("dp", "tensor"),
            P("dp", "tensor"),
            P("dp", "tensor"),
        ),
        check_vma=False,
    )
```

time: 149 us -> 118 us (0.79)
  Pallas kernels: 0 us -> 34.8 us
  local copies, waits for them, and re-layouts: 33.1 us -> 3.56 us
  matrix products: 32 us -> 4.32 us
  other arithmetic: 11.9 us -> 3.94 us
  starting transfers between devices: 38.8 us -> 37.2 us
  waiting for transfers between devices: 31 us -> 32.5 us
    pallas_call x0 -> x9, Pallas kernels: none -> 34.8 us  [the longest x4 11 us: frozen_term(): call(frozen_kernel, (half, half), 2 * tokens * kv * width, 2 * kv * width...]
    all_to_all x1, waiting for transfers between devices: 22.5 us -> 0.01 us  [local(): lax.all_to_all(packed.reshape(n_slot, CAP, -1), 'dp', 0, 0, tiled=True)]
    dot_general x6 -> x2, matrix products: 21.4 us -> 3.35 us  [contract_helper(): lax.dot_general(left, right, (((left_dim,), (right_dim,)), ((), ())), pre...]
    ppermute x3, waiting for transfers between devices: 0.01 us -> 12.5 us  [local(): lax.ppermute(sent[step - 1], 'tensor', [(i, (i + 2 * step) % n_tensor) fo...]
    dot_general x5 -> x1, matrix products: 10.6 us -> 0.97 us  [local(): jnp.dot(pick, weights, preferred_element_type=jnp.float32)]
    broadcast_in_dim x2 -> x0, local copies, waits for them, and re-layouts: 9.2 us -> none  [local(): pair_sum = pair_sum + jnp.where(chip_hit, extra_pair[:, None, :], 0.0)]
    all_to_all x1, waiting for transfers between devices: 0.01 us -> 7.79 us  [local(): lax.all_to_all(blocks, 'tensor', 0, 0, tiled=True).reshape(tokens, columns)]
    unnamed x20 -> x26, local copies, waits for them, and re-layouts: 9.43 us -> 1.68 us
  transfers between devices with their start and end apart: 14 -> 17, of which waited for: 4 -> 7; matrix products, arithmetic and copies ran while one was open for 42% -> 4% of each run, Pallas kernels for 0% -> 27%
where the time goes in v2:
time: 118 us; the launch traced here: 117 us
  starting transfers between devices  37.2 us (32%)
  Pallas kernels  34.8 us (29%)
  waiting for transfers between devices  32.5 us (28%)
  matrix products  4.32 us (4%)
  other arithmetic  3.94 us (3%)
  local copies, waits for them, and re-layouts  3.56 us (3%)
    ppermute x3, waiting for transfers between devices, local(): lax.ppermute(sent[step - 1], 'tensor', [(i, (i + 2 * step) % n_tensor) fo...  12.5 us
    ppermute x11, waiting for transfers between devices, swap(): return lax.ppermute(value, 'tensor', [(i, i ^ mask) for i in range(count)])  12.2 us
    all_to_all x1, starting transfers between devices, local(): lax.all_to_all(packed.reshape(n_slot, CAP, -1), 'dp', 0, 0, tiled=True)  11.3 us
    pallas_call x4, Pallas kernels, frozen_term(): call(frozen_kernel, (half, half), 2 * tokens * kv * width, 2 * kv * width...  11 us
    all_to_all x1, starting transfers between devices, local(): lax.all_to_all(packed_weights.reshape(n_slot, CAP, -1), 'dp', 0, 0, tiled...  9.79 us
    pallas_call x1, Pallas kernels, pair_sum(): call(functools.partial(pair_kernel, rows_own, parts), (jax.ShapeDtypeStru...  8.59 us
    all_to_all x1, waiting for transfers between devices, local(): lax.all_to_all(blocks, 'tensor', 0, 0, tiled=True).reshape(tokens, columns)  7.79 us
    ppermute x11, starting transfers between devices, swap(): return lax.ppermute(value, 'tensor', [(i, i ^ mask) for i in range(count)])  7.45 us
  transfers between devices with their start and end apart: 17, of which 7 were waited for; matrix products, arithmetic and copies ran while one was open for 4% of the time, Pallas kernels for 27%

profile of v2, /device:TPU:32, one launch (start us, length us, event | category | flops | bytes accessed | tf_op | source)
XLA Modules:
  0.0 117.2 jit_solution(12382400830021963702)
XLA Ops:
  0.6 1.9 %copy.25 = bf16[4,8,8,1024]{3,2,0,1:T(8,128)(2,1)} copy(bf16[4,8,8,1024]{3,2,1,0:T(8,128)(2,1)} %bitcast.19) | data formatting | bytes 1048576 | tf_op jit(solution)/shard_map/reshape | solution.py:379
  2.5 4.5 %all-to-all-start = ((bf16[8,32,1024]{2,1,0:T(8,128)(2,1)}), bf16[8,32,1024]{2,1,0:T(8,128)(2,1)S(1)}, u32[]{:S(2)}, u32[]{:S(2)}) async-start(bf16[8,32,1024]{2,1,0:T(8,128)(2,1)} %bitcast.13), calls=%async_computation | async-start | bytes 1048576 | tf_op jit(solution)/shard_map/all_to_all | solution.py:380
  7.0 2.6 %prep.1 = (bf16[256,256]{1,0:T(8,128)(2,1)}, bf16[256,256]{1,0:T(8,128)(2,1)}, f32[256,128]{1,0:T(8,128)}, f32[256,128]{1,0:T(8,128)}, s32[1,256]{1,0:T(1,128)}, /*index=5*/f32[256,64]{1,0:T(8,128)}) custom-call(s32[32]{0:T(128)} %live_ref.1, s32[32]{0:T(128)} %bucket_ref.1, s32[32]{0:T(128)} %owner_ref.1, s32[1,256]{1,0:T(1,128)} %bitcast.23, ...), custom_call_target="tpu_custom_call" | custom-call | flops 268435456 | bytes 1048576 | tf_op jit(solution)/shard_map/prep/pallas_call | solution.py:144
  9.5 7.8 %all-to-all-done = bf16[8,32,1024]{2,1,0:T(8,128)(2,1)S(1)} async-done(((bf16[8,32,1024]{2,1,0:T(8,128)(2,1)}), bf16[8,32,1024]{2,1,0:T(8,128)(2,1)S(1)}, u32[]{:S(2)}, u32[]{:S(2)}) %all-to-all-start) | async-done | bytes 524320 | tf_op jit(solution)/shard_map/all_to_all | solution.py:380
  17.3 0.8 copy-done
  18.1 2.7 %pack.1 = bf16[512,1280]{1,0:T(8,128)(2,1)} custom-call(s32[1,256]{1,0:T(1,128)} %get-tuple-element.47.place_ref, bf16[256,1024]{1,0:T(8,128)(2,1)} %bitcast.15, bf16[256,256]{1,0:T(8,128)(2,1)} %get-tuple-element.48.masked_ref), custom_call_target="tpu_custom_call" | custom-call | flops 335544320 | bytes 2621440 | tf_op jit(solution)/shard_map/pack/pallas_call | solution.py:192
  20.8 11.3 %all-to-all-start.1 = ((bf16[32,16,1280]{2,1,0:T(8,128)(2,1)}), bf16[32,16,1280]{2,1,0:T(8,128)(2,1)S(1)}, u32[]{:S(2)}, u32[]{:S(2)}) async-start(bf16[32,16,1280]{2,1,0:T(8,128)(2,1)} %bitcast.14), calls=%async_computation.1 | async-start | bytes 2621440 | tf_op jit(solution)/shard_map/all_to_all | solution.py:400
  32.2 0.1 collective-permute-start
  32.3 4.8 %down_low_rank.1 = f32[256,64]{1,0:T(8,128)} custom-call(bf16[256,1024]{1,0:T(8,128)(2,1)} %bitcast.16, bf16[1024,2048]{1,0:T(8,128)(2,1)} %factors_ref.3, f32[256,128]{1,0:T(8,128)} %get-tuple-element.31.slot_ref), custom_call_target="tpu_custom_call" | custom-call | flops 1073741824 | bytes 4194304 | tf_op jit(solution)/shard_map/down_low_rank/pallas_call | solution.py:229
  37.1 0.5 collective-permute-start.11
  37.5 2.8 %frozen_term.4 = (f32[128,2048]{1,0:T(8,128)}, f32[128,2048]{1,0:T(8,128)}) custom-call(bf16[256,256]{1,0:T(8,128)(2,1)} %get-tuple-element.34.turned_ref, bf16[8192,256]{1,0:T(8,128)(2,1)} %frozen_ref.7), custom_call_target="tpu_custom_call" | custom-call | flops 268435456 | bytes 3145728 | tf_op jit(solution)/shard_map/frozen_term/pallas_call | solution.py:169
  40.3 0.0 collective-permute-start.4
  40.3 0.0 collective-permute-done
  40.4 0.7 collective-permute-start.1
  41.0 2.7 %frozen_term.5 = (f32[128,2048]{1,0:T(8,128)}, f32[128,2048]{1,0:T(8,128)}) custom-call(bf16[256,256]{1,0:T(8,128)(2,1)} %get-tuple-element.34.turned_ref, bf16[8192,256]{1,0:T(8,128)(2,1)} %frozen_ref.7), custom_call_target="tpu_custom_call" | custom-call | flops 268435456 | bytes 3145728 | tf_op jit(solution)/shard_map/frozen_term/pallas_call | solution.py:169
  43.7 0.2 collective-permute-start.5
  43.9 2.8 %frozen_term.6 = (f32[128,2048]{1,0:T(8,128)}, f32[128,2048]{1,0:T(8,128)}) custom-call(bf16[256,256]{1,0:T(8,128)(2,1)} %get-tuple-element.34.turned_ref, bf16[8192,256]{1,0:T(8,128)(2,1)} %frozen_ref.7), custom_call_target="tpu_custom_call" | custom-call | flops 268435456 | bytes 3145728 | tf_op jit(solution)/shard_map/frozen_term/pallas_call | solution.py:169
  46.7 0.3 collective-permute-start.6
  47.0 0.0 collective-permute-done.11
  47.0 1.5 %collective-permute-start.12 = (f32[256,64]{1,0:T(8,128)S(1)}, f32[256,64]{1,0:T(8,128)S(1)}, u32[]{:S(2)}, u32[]{:S(2)}) collective-permute-start(f32[256,64]{1,0:T(8,128)S(1)} %add.63), channel_id=1, source_target_pairs={{0,2},{1,3},{2,0},{3,1},{4,6},{5,7},{6,4},{7,5},{8,10},{9,11},{10,... | collective-permute-start | bytes 196616 | tf_op jit(solution)/shard_map/ppermute | solution.py:40
  48.6 2.7 %frozen_term.7 = (f32[128,2048]{1,0:T(8,128)}, f32[128,2048]{1,0:T(8,128)}) custom-call(bf16[256,256]{1,0:T(8,128)(2,1)} %get-tuple-element.34.turned_ref, bf16[8192,256]{1,0:T(8,128)(2,1)} %frozen_ref.7), custom_call_target="tpu_custom_call" | custom-call | flops 268435456 | bytes 3145728 | tf_op jit(solution)/shard_map/frozen_term/pallas_call | solution.py:169
  51.3 0.0 collective-permute-start.7
  51.4 1.4 %collective-permute-done.12 = f32[256,64]{1,0:T(8,128)S(1)} collective-permute-done((f32[256,64]{1,0:T(8,128)S(1)}, f32[256,64]{1,0:T(8,128)S(1)}, u32[]{:S(2)}, u32[]{:S(2)}) %collective-permute-start.12) | collective-permute-done | bytes 65568 | tf_op jit(solution)/shard_map/ppermute | solution.py:40
  52.7 2.1 %collective-permute-start.2 = (f32[256,64]{1,0:T(8,128)S(1)}, f32[256,64]{1,0:T(8,128)S(1)}, u32[]{:S(2)}, u32[]{:S(2)}) collective-permute-start(f32[256,64]{1,0:T(8,128)S(1)} %add.58), channel_id=1, source_target_pairs={{0,4},{1,5},{2,6},{3,7},{4,0},{5,1},{6,2},{7,3},{8,12},{9,13},{10,... | collective-permute-start | bytes 196616 | tf_op jit(solution)/shard_map/ppermute | solution.py:40
  54.8 4.4 %collective-permute-done.2 = f32[256,64]{1,0:T(8,128)S(1)} collective-permute-done((f32[256,64]{1,0:T(8,128)S(1)}, f32[256,64]{1,0:T(8,128)S(1)}, u32[]{:S(2)}, u32[]{:S(2)}) %collective-permute-start.2) | collective-permute-done | bytes 65568 | tf_op jit(solution)/shard_map/ppermute | solution.py:40
  59.2 2.1 %collective-permute-start.13 = (f32[256,64]{1,0:T(8,128)S(1)}, f32[256,64]{1,0:T(8,128)S(1)}, u32[]{:S(2)}, u32[]{:S(2)}) collective-permute-start(f32[256,64]{1,0:T(8,128)S(1)} %add.64), channel_id=1, source_target_pairs={{0,4},{1,5},{2,6},{3,7},{4,0},{5,1},{6,2},{7,3},{8,12},{9,13},{10,... | collective-permute-start | bytes 196616 | tf_op jit(solution)/shard_map/ppermute | solution.py:40
  61.3 4.4 %collective-permute-done.13 = f32[256,64]{1,0:T(8,128)S(1)} collective-permute-done((f32[256,64]{1,0:T(8,128)S(1)}, f32[256,64]{1,0:T(8,128)S(1)}, u32[]{:S(2)}, u32[]{:S(2)}) %collective-permute-start.13) | collective-permute-done | bytes 65568 | tf_op jit(solution)/shard_map/ppermute | solution.py:40
  65.7 1.6 %multiply_convert_fusion = (bf16[256,64]{1,0:T(8,128)(2,1)S(1)}, bf16[256,64]{1,0:T(8,128)(2,1)}) fusion(f32[256,64]{1,0:T(8,128)S(1)} %add.64, f32[256,64]{1,0:T(8,128)S(1)} %collective-permute-done.13, f32[256,128]{1,0:T(8,128)} %get-tuple-element.30, f32[256,64]{1,0:T(8,128)S(1)} %add.58, f32[256,64]{1,0:T(8,128)S(1)} %collective-permute-done.2), kind=kLoop, calls=%fused_computation.14 | loop fusion | flops 98304 | bytes 393216 | tf_op jit(solution)/shard_map/convert_element_type | solution.py:418
  67.3 5.2 %extra_term.1 = (f32[128,1024]{1,0:T(8,128)}, f32[128,1024]{1,0:T(8,128)}) custom-call(bf16[256,64]{1,0:T(8,128)(2,1)} %get-tuple-element.58.weight_ref, f32[256,128]{1,0:T(8,128)} %get-tuple-element.31.slot_ref, bf16[1024,2048]{1,0:T(8,128)(2,1)} %factors_ref.3), custom_call_target="tpu_custom_call" | custom-call | flops 1073741824 | bytes 4194304 | tf_op jit(solution)/shard_map/extra_term/pallas_call | solution.py:283
  72.5 0.0 collective-permute-done.5.refs_5_
  72.5 2.1 %collective-permute-done.3.extra_pair_ref = f32[128,1024]{1,0:T(8,128)S(1)} collective-permute-done((f32[128,1024]{1,0:T(8,128)}, f32[128,1024]{1,0:T(8,128)S(1)}, u32[]{:S(2)}, u32[]{:S(2)}) %collective-permute-start.3) | collective-permute-done | bytes 524320 | tf_op jit(solution)/shard_map/ppermute | solution.py:40
  74.6 0.8 copy-done.3
  75.4 8.6 %pair_sum.1 = (f32[32,8192]{1,0:T(8,128)}, bf16[32,8192]{1,0:T(8,128)(2,1)}, bf16[32,8192]{1,0:T(8,128)(2,1)}, bf16[32,8192]{1,0:T(8,128)(2,1)}) custom-call(f32[128,1024]{1,0:T(8,128)} %get-tuple-element.32.extra_ours_ref, f32[128,1024]{1,0:T(8,128)} %copy-done.3, f32[128,2048]{1,0:T(8,128)} %get-tuple-element.35.refs_0_, ...), custom_call_target="tpu_custom_call" | custom-call | flops 2097152 | bytes 12582912 | tf_op jit(solution)/shard_map/pair_sum/pallas_call | solution.py:343
  84.0 1.1 collective-permute-start.10
  85.1 1.0 collective-permute-start.8
  86.1 2.1 %collective-permute-start.9 = (bf16[32,8192]{1,0:T(8,128)(2,1)}, bf16[32,8192]{1,0:T(8,128)(2,1)S(1)}, u32[]{:S(2)}, u32[]{:S(2)}) collective-permute-start(bf16[32,8192]{1,0:T(8,128)(2,1)} %get-tuple-element.45), channel_id=1, source_target_pairs={{0,4},{1,5},{2,6},{3,7},{4,0},{5,1},{6,2},{7,3},{8,12},{9,13},{10,... | collective-permute-start | bytes 1572872 | tf_op jit(solution)/shard_map/ppermute | solution.py:411
  88.2 1.0 convolution_convert_fusion
  89.1 0.0 all-to-all-done.1
  89.2 9.8 %all-to-all-start.2 = ((bf16[32,16,128]{2,1,0:T(8,128)(2,1)}), bf16[32,16,128]{2,1,0:T(8,128)(2,1)S(1)}, u32[]{:S(2)}, u32[]{:S(2)}) async-start(bf16[32,16,128]{2,1,0:T(8,128)(2,1)} %bitcast.6), calls=%async_computation.2 | async-start | bytes 262144 | tf_op jit(solution)/shard_map/all_to_all | solution.py:427
  98.9 0.1 collective-permute-done.10
  99.1 12.4 %collective-permute-done.8 = bf16[32,8192]{1,0:T(8,128)(2,1)S(1)} collective-permute-done((bf16[32,8192]{1,0:T(8,128)(2,1)}, bf16[32,8192]{1,0:T(8,128)(2,1)S(1)}, u32[]{:S(2)}, u32[]{:S(2)}) %collective-permute-start.8) | collective-permute-done | bytes 524320 | tf_op jit(solution)/shard_map/ppermute | solution.py:411
  111.4 0.0 collective-permute-done.9
  111.5 2.3 %add_convert_fusion = bf16[32,8192]{1,0:T(8,128)(2,1)} fusion(bf16[32,8192]{1,0:T(8,128)(2,1)S(1)} %collective-permute-done.10, bf16[32,8192]{1,0:T(8,128)(2,1)S(1)} %collective-permute-done.9, f32[32,8192]{1,0:T(8,128)} %get-tuple-element.43, bf16[32,8192]{1,0:T(8,128)(2,1)S(1)} %collective-permute-done.8), kind=kLoop, calls=%fused_computation.3 | loop fusion | flops 1835008 | bytes 3145728 | tf_op jit(solution)/shard_map/convert_element_type | solution.py:415
  113.8 0.0 copy-start.10
  113.8 0.0 copy-start.11
  113.8 0.0 copy-start.12
  113.8 2.4 %multiply_subtract_fusion = (f32[1024,64]{0,1:T(8,128)}, f32[1024,64]{0,1:T(8,128)}, f32[1024,64]{0,1:T(8,128)}) fusion(f32[1024,64]{0,1:T(8,128)S(1)} %copy-done.8, f32[1024,64]{0,1:T(8,128)S(1)} %copy-done.9, f32[1024,64]{0,1:T(8,128)} %param.22, bf16[512,128]{1,0:T(8,128)(2,1)S(1)} %bitcast.20, bf16[512,1280]{1,0:T(8,128)(2,1)S(1)} %bitcast.17), kind=kOutput, calls=%fused_computation.8 | convolution fusion | flops 68157440 | bytes 2752512 | tf_op jit(solution)/shard_map/dot_general | solution.py:34
  116.2 0.9 multiply_subtract_fusion.1
  (31 shorter events, 0.1 us)
Async XLA Ops:
  2.5 14.8 %all-to-all-start = ((bf16[8,32,1024]{2,1,0:T(8,128)(2,1)}), bf16[8,32,1024]{2,1,0:T(8,128)(2,1)S(1)}, u32[]{:S(2)}, u32[]{:S(2)}) async-start(bf16[8,32,1024]{2,1,0:T(8,128)(2,1)} %bitcast.13), calls=%async_computation | async-start | bytes 1048576 | tf_op jit(solution)/shard_map/all_to_all | solution.py:380
  17.3 0.8 copy-start
  20.8 11.3 %copy-start.6 = (f32[256,64]{1,0:T(8,128)S(1)}, f32[256,64]{1,0:T(8,128)}, u32[]{:S(2)}) copy-start(f32[256,64]{1,0:T(8,128)} %get-tuple-element.29) | copy-start | bytes 196612
  20.8 68.3 %all-to-all-start.1 = ((bf16[32,16,1280]{2,1,0:T(8,128)(2,1)}), bf16[32,16,1280]{2,1,0:T(8,128)(2,1)S(1)}, u32[]{:S(2)}, u32[]{:S(2)}) async-start(bf16[32,16,1280]{2,1,0:T(8,128)(2,1)} %bitcast.14), calls=%async_computation.1 | async-start | bytes 2621440 | tf_op jit(solution)/shard_map/all_to_all | solution.py:400
  32.2 8.2 %collective-permute-start = (f32[256,64]{1,0:T(8,128)S(1)}, f32[256,64]{1,0:T(8,128)S(1)}, u32[]{:S(2)}, u32[]{:S(2)}) collective-permute-start(f32[256,64]{1,0:T(8,128)S(1)} %copy-done.6), channel_id=1, source_target_pairs={{0,1},{1,0},{2,3},{3,2},{4,5},{5,4},{6,7},{7,6},{8,9},{9,8},{10,11... | collective-permute-start | bytes 196616 | tf_op jit(solution)/shard_map/ppermute | solution.py:40
  37.1 10.0 %collective-permute-start.11 = (f32[256,64]{1,0:T(8,128)}, f32[256,64]{1,0:T(8,128)S(1)}, u32[]{:S(2)}, u32[]{:S(2)}) collective-permute-start(f32[256,64]{1,0:T(8,128)} %down_low_rank.1), channel_id=1, source_target_pairs={{0,1},{1,0},{2,3},{3,2},{4,5},{5,4},{6,7},{7,6},{8,9},{9,8},{10,11... | collective-permute-start | bytes 196616 | tf_op jit(solution)/shard_map/ppermute | solution.py:40
  40.3 32.1 %collective-permute-start.4 = (f32[128,2048]{1,0:T(8,128)}, f32[128,2048]{1,0:T(8,128)S(1)}, u32[]{:S(2)}, u32[]{:S(2)}) collective-permute-start(f32[128,2048]{1,0:T(8,128)} %get-tuple-element.39), channel_id=1, source_target_pairs={{0,1},{1,0},{2,3},{3,2},{4,5},{5,4},{6,7},{7,6},{8,9},{9,8},{10,11... | collective-permute-start | bytes 3145736 | tf_op jit(solution)/shard_map/ppermute | solution.py:40
  40.4 11.0 %collective-permute-start.1 = (f32[256,64]{1,0:T(8,128)S(1)}, f32[256,64]{1,0:T(8,128)S(1)}, u32[]{:S(2)}, u32[]{:S(2)}) collective-permute-start(f32[256,64]{1,0:T(8,128)S(1)} %add.57), channel_id=1, source_target_pairs={{0,2},{1,3},{2,0},{3,1},{4,6},{5,7},{6,4},{7,5},{8,10},{9,11},{10,... | collective-permute-start | bytes 196616 | tf_op jit(solution)/shard_map/ppermute | solution.py:40
  43.7 3.3 %copy-start.4 = (f32[256,64]{1,0:T(8,128)S(1)}, f32[256,64]{1,0:T(8,128)}, u32[]{:S(2)}) copy-start(f32[256,64]{1,0:T(8,128)} %down_low_rank.1) | copy-start | bytes 196612
  43.7 28.7 %collective-permute-start.5 = (f32[128,2048]{1,0:T(8,128)}, f32[128,2048]{1,0:T(8,128)S(1)}, u32[]{:S(2)}, u32[]{:S(2)}) collective-permute-start(f32[128,2048]{1,0:T(8,128)} %get-tuple-element.40), channel_id=1, source_target_pairs={{0,1},{1,0},{2,3},{3,2},{4,5},{5,4},{6,7},{7,6},{8,9},{9,8},{10,11... | collective-permute-start | bytes 3145736 | tf_op jit(solution)/shard_map/ppermute | solution.py:40
  46.7 25.8 %collective-permute-start.6 = (f32[128,2048]{1,0:T(8,128)}, f32[128,2048]{1,0:T(8,128)}, u32[]{:S(2)}, u32[]{:S(2)}) collective-permute-start(f32[128,2048]{1,0:T(8,128)} %get-tuple-element.41), channel_id=1, source_target_pairs={{0,1},{1,0},{2,3},{3,2},{4,5},{5,4},{6,7},{7,6},{8,9},{9,8},{10,11... | collective-permute-start | bytes 3145736 | tf_op jit(solution)/shard_map/ppermute | solution.py:40
  47.0 5.7 %collective-permute-start.12 = (f32[256,64]{1,0:T(8,128)S(1)}, f32[256,64]{1,0:T(8,128)S(1)}, u32[]{:S(2)}, u32[]{:S(2)}) collective-permute-start(f32[256,64]{1,0:T(8,128)S(1)} %add.63), channel_id=1, source_target_pairs={{0,2},{1,3},{2,0},{3,1},{4,6},{5,7},{6,4},{7,5},{8,10},{9,11},{10,... | collective-permute-start | bytes 196616 | tf_op jit(solution)/shard_map/ppermute | solution.py:40
  51.3 21.2 %collective-permute-start.7 = (f32[128,2048]{1,0:T(8,128)}, f32[128,2048]{1,0:T(8,128)}, u32[]{:S(2)}, u32[]{:S(2)}) collective-permute-start(f32[128,2048]{1,0:T(8,128)} %get-tuple-element.42), channel_id=1, source_target_pairs={{0,1},{1,0},{2,3},{3,2},{4,5},{5,4},{6,7},{7,6},{8,9},{9,8},{10,11... | collective-permute-start | bytes 3145736 | tf_op jit(solution)/shard_map/ppermute | solution.py:40
  52.7 6.5 %collective-permute-start.2 = (f32[256,64]{1,0:T(8,128)S(1)}, f32[256,64]{1,0:T(8,128)S(1)}, u32[]{:S(2)}, u32[]{:S(2)}) collective-permute-start(f32[256,64]{1,0:T(8,128)S(1)} %add.58), channel_id=1, source_target_pairs={{0,4},{1,5},{2,6},{3,7},{4,0},{5,1},{6,2},{7,3},{8,12},{9,13},{10,... | collective-permute-start | bytes 196616 | tf_op jit(solution)/shard_map/ppermute | solution.py:40
  59.2 6.5 %collective-permute-start.13 = (f32[256,64]{1,0:T(8,128)S(1)}, f32[256,64]{1,0:T(8,128)S(1)}, u32[]{:S(2)}, u32[]{:S(2)}) collective-permute-start(f32[256,64]{1,0:T(8,128)S(1)} %add.64), channel_id=1, source_target_pairs={{0,4},{1,5},{2,6},{3,7},{4,0},{5,1},{6,2},{7,3},{8,12},{9,13},{10,... | collective-permute-start | bytes 196616 | tf_op jit(solution)/shard_map/ppermute | solution.py:40
  72.4 2.1 %collective-permute-start.3 = (f32[128,1024]{1,0:T(8,128)}, f32[128,1024]{1,0:T(8,128)S(1)}, u32[]{:S(2)}, u32[]{:S(2)}) collective-permute-start(f32[128,1024]{1,0:T(8,128)} %get-tuple-element.33), channel_id=1, source_target_pairs={{0,1},{1,0},{2,3},{3,2},{4,5},{5,4},{6,7},{7,6},{8,9},{9,8},{10,11... | collective-permute-start | bytes 1572872 | tf_op jit(solution)/shard_map/ppermute | solution.py:40
  72.4 2.1 %copy-start.1 = (f32[128,2048]{1,0:T(8,128)}, f32[128,2048]{1,0:T(8,128)S(1)}, u32[]{:S(2)}) copy-start(f32[128,2048]{1,0:T(8,128)S(1)} %collective-permute-done.4.refs_4_) | copy-start | bytes 3145732
  72.5 2.1 %copy-start.2 = (f32[128,2048]{1,0:T(8,128)}, f32[128,2048]{1,0:T(8,128)S(1)}, u32[]{:S(2)}) copy-start(f32[128,2048]{1,0:T(8,128)S(1)} %collective-permute-done.5.refs_5_) | copy-start | bytes 3145732
  74.6 0.8 copy-start.3
  75.4 12.8 %copy-start.5 = (bf16[256,64]{1,0:T(8,128)(2,1)S(1)}, bf16[256,64]{1,0:T(8,128)(2,1)}, u32[]{:S(2)}) copy-start(bf16[256,64]{1,0:T(8,128)(2,1)} %get-tuple-element.58.weight_ref) | copy-start | bytes 98308
  75.4 12.8 %copy-start.7 = (s32[1,256]{1,0:T(1,128)S(1)}, s32[1,256]{1,0:T(1,128)}, u32[]{:S(2)}) copy-start(s32[1,256]{1,0:T(1,128)} %get-tuple-element.47.place_ref) | copy-start | bytes 3076
  84.0 15.1 %collective-permute-start.10 = (bf16[32,8192]{1,0:T(8,128)(2,1)}, bf16[32,8192]{1,0:T(8,128)(2,1)S(1)}, u32[]{:S(2)}, u32[]{:S(2)}) collective-permute-start(bf16[32,8192]{1,0:T(8,128)(2,1)} %get-tuple-element.46), channel_id=1, source_target_pairs={{0,6},{1,7},{2,0},{3,1},{4,2},{5,3},{6,4},{7,5},{8,14},{9,15},{10,... | collective-permute-start | bytes 1572872 | tf_op jit(solution)/shard_map/ppermute | solution.py:411
  85.1 26.3 %collective-permute-start.8 = (bf16[32,8192]{1,0:T(8,128)(2,1)}, bf16[32,8192]{1,0:T(8,128)(2,1)S(1)}, u32[]{:S(2)}, u32[]{:S(2)}) collective-permute-start(bf16[32,8192]{1,0:T(8,128)(2,1)} %get-tuple-element.44), channel_id=1, source_target_pairs={{0,2},{1,3},{2,4},{3,5},{4,6},{5,7},{6,0},{7,1},{8,10},{9,11},{10,... | collective-permute-start | bytes 1572872 | tf_op jit(solution)/shard_map/ppermute | solution.py:411
  86.1 25.3 %collective-permute-start.9 = (bf16[32,8192]{1,0:T(8,128)(2,1)}, bf16[32,8192]{1,0:T(8,128)(2,1)S(1)}, u32[]{:S(2)}, u32[]{:S(2)}) collective-permute-start(bf16[32,8192]{1,0:T(8,128)(2,1)} %get-tuple-element.45), channel_id=1, source_target_pairs={{0,4},{1,5},{2,6},{3,7},{4,0},{5,1},{6,2},{7,3},{8,12},{9,13},{10,... | collective-permute-start | bytes 1572872 | tf_op jit(solution)/shard_map/ppermute | solution.py:411
  89.2 24.6 %all-to-all-start.2 = ((bf16[32,16,128]{2,1,0:T(8,128)(2,1)}), bf16[32,16,128]{2,1,0:T(8,128)(2,1)S(1)}, u32[]{:S(2)}, u32[]{:S(2)}) async-start(bf16[32,16,128]{2,1,0:T(8,128)(2,1)} %bitcast.6), calls=%async_computation.2 | async-start | bytes 262144 | tf_op jit(solution)/shard_map/all_to_all | solution.py:427
  111.4 2.3 %copy-start.8 = (f32[1024,64]{0,1:T(8,128)S(1)}, f32[1024,64]{0,1:T(8,128)}, u32[]{:S(2)}) copy-start(f32[1024,64]{0,1:T(8,128)} %param.20) | copy-start | bytes 786436
  111.4 2.3 %copy-start.9 = (f32[1024,64]{0,1:T(8,128)S(1)}, f32[1024,64]{0,1:T(8,128)}, u32[]{:S(2)}) copy-start(f32[1024,64]{0,1:T(8,128)} %param.21) | copy-start | bytes 786436
  113.8 2.5 %copy-start.10 = (f32[64,256]{1,0:T(8,128)S(1)}, f32[64,256]{1,0:T(8,128)}, u32[]{:S(2)}) copy-start(f32[64,256]{1,0:T(8,128)} %param.23) | copy-start | bytes 196612
  113.8 2.5 %copy-start.11 = (f32[64,256]{1,0:T(8,128)S(1)}, f32[64,256]{1,0:T(8,128)}, u32[]{:S(2)}) copy-start(f32[64,256]{1,0:T(8,128)} %param.24) | copy-start | bytes 196612
  113.8 2.5 %copy-start.12 = (f32[64,256]{1,0:T(8,128)S(1)}, f32[64,256]{1,0:T(8,128)}, u32[]{:S(2)}) copy-start(f32[64,256]{1,0:T(8,128)} %param.25) | copy-start | bytes 196612

commit v3 on v2

--- a/solution.py
+++ b/solution.py
@@ -40,16 +40,15 @@
     return lax.ppermute(value, "tensor", [(i, i ^ mask) for i in range(count)])
 
 
-def sum_over_tensor(value, count):
-    mask = 1
+def sum_over_tensor(value, count, mask=1):
     while mask < count:
-        value = value + swap(value, mask, count)
+        value = value + swap(value, mask, lax.axis_size("tensor"))
         mask *= 2
     return value
 
 
 VMEM_LIMIT = 60 * 1024 * 1024
-VMEM = pltpu.MemorySpace.VMEM
+HBM = pltpu.MemorySpace.HBM
 SMEM = pltpu.MemorySpace.SMEM
 NT = (((1,), (1,)), ((), ()))
 NN = (((1,), (0,)), ((), ()))
@@ -154,202 +153,202 @@
     )(live, bucket, owner, adapter_row, cotangent, up_factors)
 
 
-def frozen_kernel(turned_ref, frozen_ref, ours_ref, theirs_ref):
+def frozen_kernel(turned_ref, frozen_ref, ours_ref, *theirs_refs):
+    step = pl.program_id(0)
     half = ours_ref.shape[0]
+    per_part = pl.num_programs(0) // len(theirs_refs)
     both = dot(turned_ref[...], frozen_ref[...], NT)
     ours_ref[...] = both[:half, :]
-    theirs_ref[...] = both[half:, :]
-
-
-def frozen_term(turned, frozen, part, width):
+    for part, out in enumerate(theirs_refs):
+
+        @pl.when(step // per_part == part)
+        def _():
+            out[...] = both[half:, :]
+
+
+def part_blocks(rows, chunk, parts, per_part):
+    return [
+        pl.BlockSpec((rows, chunk), lambda i, q=q: (0, jnp.clip(i - q * per_part, 0, per_part - 1)))
+        for q in range(parts)
+    ]
+
+
+def frozen_term(turned, frozen, parts):
     tokens, kv = turned.shape
-    chunk = width // 2
-    half = jax.ShapeDtypeStruct((tokens // 2, width), jnp.float32)
-    block = pl.BlockSpec((tokens // 2, chunk), lambda i: (0, i))
+    width = frozen.shape[0]
+    chunk = 1024
+    steps = width // chunk
+    theirs = jax.ShapeDtypeStruct((tokens // 2, width // parts), jnp.float32)
     return call(
         frozen_kernel,
-        (half, half),
+        (jax.ShapeDtypeStruct((tokens // 2, width), jnp.float32),) + (theirs,) * parts,
         2 * tokens * kv * width,
         2 * kv * width + 4 * tokens * width,
-        grid=(2,),
-        in_specs=[whole(turned.shape), pl.BlockSpec((chunk, kv), lambda i: (2 * part + i, 0))],
-        out_specs=(block, block),
+        grid=(steps,),
+        in_specs=[whole(turned.shape), pl.BlockSpec((chunk, kv), lambda i: (i, 0))],
+        out_specs=(
+            pl.BlockSpec((tokens // 2, chunk), lambda i: (0, i)),
+            *part_blocks(tokens // 2, chunk, parts, steps // parts),
+        ),
         name="frozen_term",
     )(turned, frozen)
 
 
-def pack_kernel(place_ref, hidden_ref, masked_ref, out_ref):
-    rows, tokens = out_ref.shape[0], place_ref.shape[1]
-    down = lax.broadcasted_iota(jnp.int32, (rows, tokens), 0)
-    pick = jnp.where(down == place_ref[...], 1.0, 0.0).astype(jnp.bfloat16)
-    width = hidden_ref.shape[1]
-    out_ref[:, :width] = dot(pick, hidden_ref[...], NN).astype(jnp.bfloat16)
-    out_ref[:, width:] = dot(pick, masked_ref[...], NN).astype(jnp.bfloat16)
+def pack_kernel(place_ref, hidden_ref, masked_ref, out_ref, pick_ref):
+    step = pl.program_id(0)
+    last = pl.num_programs(0) - 1
+
+    @pl.when(step == 0)
+    def _():
+        down = lax.broadcasted_iota(jnp.int32, pick_ref.shape, 0)
+        pick_ref[...] = jnp.where(down == place_ref[...], 1.0, 0.0).astype(jnp.bfloat16)
+
+    @pl.when(step < last)
+    def _():
+        out_ref[...] = dot(pick_ref[...], hidden_ref[...], NN).astype(jnp.bfloat16)
+
+    @pl.when(step == last)
+    def _():
+        out_ref[...] = dot(pick_ref[...], masked_ref[...], NN).astype(jnp.bfloat16)
 
 
 def pack_rows(place, hidden_columns, masked, rows):
-    columns = hidden_columns.shape[1] + masked.shape[1]
+    tokens, chunk = masked.shape
+    columns = hidden_columns.shape[1] + chunk
+    steps = columns // chunk
     return call(
         pack_kernel,
         jax.ShapeDtypeStruct((rows, columns), jnp.bfloat16),
-        2 * rows * columns * hidden_columns.shape[0],
-        4 * rows * columns,
-        grid=(1,),
-        in_specs=[whole(v.shape) for v in (place, hidden_columns, masked)],
-        out_specs=whole((rows, columns)),
+        2 * rows * columns * tokens,
+        2 * (rows + tokens) * columns,
+        grid=(steps,),
+        in_specs=[
+            whole(place.shape),
+            pl.BlockSpec((tokens, chunk), lambda i: (0, jnp.minimum(i, steps - 2))),
+            whole(masked.shape),
+        ],
+        out_specs=pl.BlockSpec((rows, chunk), lambda i: (0, i)),
+        scratch_shapes=[pltpu.VMEM((rows, tokens), jnp.bfloat16)],
         name="pack",
     )(place, hidden_columns, masked)
 
 
-def down_kernel(hidden_ref, factors_ref, slot_ref, out_ref, acc_ref):
-    step = pl.program_id(0)
-    chunk = factors_ref.shape[1]
-    slots = chunk // PADDED_RANK
-
-    @pl.when(step == 0)
-    def _():
-        acc_ref[...] = jnp.zeros_like(acc_ref)
-
-    part = dot(hidden_ref[...], factors_ref[...], NN)
-    first = (step * slots).astype(jnp.float32)
-    acc = acc_ref[...]
-    for c in range(chunk // 128):
-        hit = slot_ref[...] == lane_slot((1, 128), 2 * c) + first
-        acc = acc + jnp.where(hit, part[:, c * 128 : (c + 1) * 128], 0.0)
-    acc_ref[...] = acc
-
-    @pl.when(step == pl.num_programs(0) - 1)
-    def _():
-        out_ref[...] = acc[:, :PADDED_RANK] + acc[:, PADDED_RANK:]
-
-
-def down_low_rank(hidden_columns, factors, slot_wide):
-    tokens, columns = hidden_columns.shape
-    chunk = 512
-    return call(
-        down_kernel,
-        jax.ShapeDtypeStruct((tokens, PADDED_RANK), jnp.float32),
-        2 * tokens * factors.size,
-        2 * factors.size,
-        grid=(factors.shape[1] // chunk,),
-        in_specs=[
-            pl.BlockSpec((tokens, columns), lambda i: (0, 0)),
-            pl.BlockSpec((columns, chunk), lambda i: (0, i)),
-            pl.BlockSpec((tokens, 128), lambda i: (0, 0)),
-        ],
-        out_specs=pl.BlockSpec((tokens, PADDED_RANK), lambda i: (0, 0)),
-        scratch_shapes=[pltpu.VMEM((tokens, 128), jnp.float32)],
-        name="down_low_rank",
-    )(hidden_columns, factors, slot_wide)
-
-
-def extra_kernel(rows_own, weight_ref, slot_ref, factors_ref, ours_ref, theirs_ref, acc_ref):
-    step = pl.program_id(0)
-    chunk = factors_ref.shape[1]
-    tokens = weight_ref.shape[0]
+def factors_kernel(rows_own, hidden_ref, weight_ref, slot_ref, factors_ref, down_ref, ours_ref,
+                   theirs_ref, held_ref, extra_ref, sems):
+    parts, columns, chunk = held_ref.shape
+    tokens = hidden_ref.shape[0]
     n_chip = tokens // rows_own // 2
-
-    @pl.when(step == 0)
-    def _():
-        acc_ref[...] = jnp.zeros_like(acc_ref)
-
+    copies = [
+        pltpu.make_async_copy(
+            factors_ref.at[:, pl.ds(c * chunk, chunk)], held_ref.at[c], sems.at[c]
+        )
+        for c in range(parts)
+    ]
+    for copy in copies:
+        copy.start()
+    slot = slot_ref[...]
     weight = weight_ref[...].astype(jnp.float32)
     double = jnp.concatenate([weight, weight], axis=1)
-    first = (step * (chunk // PADDED_RANK)).astype(jnp.float32)
-    pieces = []
-    for c in range(chunk // 128):
-        hit = slot_ref[...] == lane_slot((1, 128), 2 * c) + first
-        pieces.append(jnp.where(hit, double, 0.0).astype(jnp.bfloat16))
-    placed = jnp.concatenate(pieces, axis=1)
-    acc_ref[...] += dot(placed, factors_ref[...], NT)
-
-    @pl.when(step == pl.num_programs(0) - 1)
-    def _():
-        position = lax.axis_index("tensor")
-        chip, core = position // 2, position % 2
-        for turn in range(n_chip):
-            block = (chip + turn) % n_chip * 2
-            for out, k in ((ours_ref, core), (theirs_ref, 1 - core)):
-                start = pl.multiple_of((block + k) * rows_own, rows_own)
-                out[pl.ds(turn * rows_own, rows_own), :] = acc_ref[pl.ds(start, rows_own), :]
-
-
-def extra_term(rows_own, up_weight, slot_wide, factors):
-    tokens = up_weight.shape[0]
-    columns = factors.shape[0]
-    chunk = 512
-    half = jax.ShapeDtypeStruct((tokens // 2, columns), jnp.float32)
-    half_spec = pl.BlockSpec((tokens // 2, columns), lambda i: (0, 0))
-    return call(
-        functools.partial(extra_kernel, rows_own),
-        (half, half),
-        2 * tokens * factors.size,
-        2 * factors.size,
-        grid=(factors.shape[1] // chunk,),
-        in_specs=[
-            pl.BlockSpec((tokens, PADDED_RANK), lambda i: (0, 0)),
-            pl.BlockSpec((tokens, 128), lambda i: (0, 0)),
-            pl.BlockSpec((columns, chunk), lambda i: (0, i)),
-        ],
-        out_specs=(half_spec, half_spec),
-        scratch_shapes=[pltpu.VMEM((tokens, columns), jnp.float32)],
-        name="extra_term",
-    )(up_weight, slot_wide, factors)
-
-
-def pair_kernel(rows_own, parts, extra_ours_ref, extra_pair_ref, *refs):
-    ours_refs, pair_refs, own_ref, out_refs = (
-        refs[:parts],
-        refs[parts : 2 * parts],
-        refs[2 * parts],
-        refs[2 * parts + 1 :],
-    )
-    step = pl.program_id(0)
+    acc = jnp.zeros((tokens, 128), jnp.float32)
+    for c in range(parts):
+        copies[c].wait()
+        factors = held_ref[c]
+        product = dot(hidden_ref[...], factors, NN)
+        pieces = []
+        for d in range(chunk // 128):
+            hit = slot == lane_slot((1, 128), (c * chunk + d * 128) // PADDED_RANK)
+            acc = acc + jnp.where(hit, product[:, d * 128 : (d + 1) * 128], 0.0)
+            pieces.append(jnp.where(hit, double, 0.0).astype(jnp.bfloat16))
+        term = dot(jnp.concatenate(pieces, axis=1), factors, NT)
+        if c == 0:
+            extra_ref[...] = term
+        else:
+            extra_ref[...] += term
+    down_ref[...] = acc[:, :PADDED_RANK] + acc[:, PADDED_RANK:]
     position = lax.axis_index("tensor")
     chip, core = position // 2, position % 2
+    for turn in range(n_chip):
+        block = (chip + turn) % n_chip * 2
+        for out, k in ((ours_ref, core), (theirs_ref, 1 - core)):
+            start = pl.multiple_of((block + k) * rows_own, rows_own)
+            out[pl.ds(turn * rows_own, rows_own), :] = extra_ref[pl.ds(start, rows_own), :]
+
+
+def factor_products(rows_own, hidden_columns, up_weight, slot_wide, factors):
+    tokens, columns = hidden_columns.shape
+    chunk = 256
+    parts = factors.shape[1] // chunk
+    half = jax.ShapeDtypeStruct((tokens // 2, columns), jnp.float32)
+    shapes = (jax.ShapeDtypeStruct((tokens, PADDED_RANK), jnp.float32), half, half)
+    return call(
+        functools.partial(factors_kernel, rows_own),
+        shapes,
+        4 * tokens * factors.size,
+        2 * factors.size,
+        grid=(1,),
+        in_specs=[whole(v.shape) for v in (hidden_columns, up_weight, slot_wide)]
+        + [pl.BlockSpec(memory_space=HBM)],
+        out_specs=tuple(whole(v.shape) for v in shapes),
+        scratch_shapes=[
+            pltpu.VMEM((parts, columns, chunk), jnp.bfloat16),
+            pltpu.VMEM((tokens, columns), jnp.float32),
+            pltpu.SemaphoreType.DMA((parts,)),
+        ],
+        name="factor_products",
+    )(hidden_columns, up_weight, slot_wide, factors)
+
+
+def pair_kernel(rows_own, parts, extra_ours_ref, extra_pair_ref, ours_ref, *refs):
+    pair_refs, own_ref, out_refs = refs[:parts], refs[parts], refs[parts + 1 :]
+    step = pl.program_id(0)
+    per_part = pl.num_programs(0) // parts
+    position = lax.axis_index("tensor")
+    chip, core = position // 2, position % 2
+    total = ours_ref[...]
+    for part in range(parts):
+        total = jnp.where(step // per_part == part, total + pair_refs[part][...], total)
 
     def write(value):
         own_ref[...] = value[:rows_own, :]
         for i, out in enumerate(out_refs):
             out[...] = value[(i + 1) * rows_own : (i + 2) * rows_own, :].astype(jnp.bfloat16)
 
-    for part in range(parts):
-        here = step // 2 == part
-
-        @pl.when(here & (chip != part))
-        def _():
-            write(ours_refs[part][...] + pair_refs[part][...])
-
-        @pl.when(here & (chip == part) & (step % 2 == core))
-        def _():
-            write(ours_refs[part][...] + pair_refs[part][...] + extra_ours_ref[...])
-
-        @pl.when(here & (chip == part) & (step % 2 != core))
-        def _():
-            write(ours_refs[part][...] + pair_refs[part][...] + extra_pair_ref[...])
+    @pl.when(step // 2 != chip)
+    def _():
+        write(total)
+
+    @pl.when((step // 2 == chip) & (step % 2 == core))
+    def _():
+        write(total + extra_ours_ref[...])
+
+    @pl.when((step // 2 == chip) & (step % 2 != core))
+    def _():
+        write(total + extra_pair_ref[...])
 
 
 def pair_sum(rows_own, ours, from_pair, extra_ours, extra_pair):
-    parts = len(ours)
-    half, width = ours[0].shape
+    parts = len(from_pair)
+    half, width = ours.shape
     columns = extra_ours.shape[1]
-    sent = jax.ShapeDtypeStruct((rows_own, parts * width), jnp.bfloat16)
+    steps = width // columns
+    sent = jax.ShapeDtypeStruct((rows_own, width), jnp.bfloat16)
     out_block = pl.BlockSpec((rows_own, columns), lambda i: (0, i))
-    in_blocks = [
-        pl.BlockSpec((half, columns), lambda i, q=q: (0, jnp.clip(i - 2 * q, 0, 1)))
-        for q in range(parts)
-    ]
     n_out = half // rows_own - 1
     return call(
         functools.partial(pair_kernel, rows_own, parts),
-        (jax.ShapeDtypeStruct((rows_own, parts * width), jnp.float32),) + (sent,) * n_out,
-        2 * half * width * parts,
-        12 * half * width * parts,
-        grid=(2 * parts,),
-        in_specs=[whole(extra_ours.shape), whole(extra_pair.shape)] + in_blocks + in_blocks,
+        (jax.ShapeDtypeStruct((rows_own, width), jnp.float32),) + (sent,) * n_out,
+        2 * half * width,
+        10 * half * width,
+        grid=(steps,),
+        in_specs=[
+            whole(extra_ours.shape),
+            whole(extra_pair.shape),
+            pl.BlockSpec((half, columns), lambda i: (0, i)),
+            *part_blocks(half, columns, parts, steps // parts),
+        ],
         out_specs=(out_block,) * (n_out + 1),
         name="pair_sum",
-    )(extra_ours, extra_pair, *ours, *from_pair)
+    )(extra_ours, extra_pair, ours, *from_pair)
 
 
 def local(
@@ -390,19 +389,22 @@
     )
     factor = factor_wide[:, :PADDED_RANK]
 
-    frozen_ours, from_pair = [], []
-    for part in range(n_chip):
-        mine, theirs = frozen_term(turned, frozen_key_value, part, 2 * columns)
-        frozen_ours.append(mine)
-        from_pair.append(swap(theirs, 1, n_tensor))
+    frozen_ours, *frozen_theirs = frozen_term(turned, frozen_key_value, 2)
+    up_own = sum_over_tensor(up_own, n_tensor // 2)
+    place, up_own, frozen_ours, frozen_theirs = lax.optimization_barrier(
+        (place, up_own, frozen_ours, frozen_theirs)
+    )
+    from_pair = [swap(theirs, 1, n_tensor) for theirs in frozen_theirs]
 
     packed = pack_rows(place, hidden_columns, masked, n_slot * CAP)
     owned = lax.all_to_all(
         packed.reshape(n_slot, CAP, -1), "dp", 0, 0, tiled=True
     ).reshape(n_slot * CAP, -1)
 
-    up_weight = (sum_over_tensor(up_own, n_tensor) * factor).astype(jnp.bfloat16)
-    extra_ours, extra_theirs = extra_term(rows_own, up_weight, slot_wide, adapter_down_factors)
+    up_weight = (sum_over_tensor(up_own, n_tensor, n_tensor // 2) * factor).astype(jnp.bfloat16)
+    down_own, extra_ours, extra_theirs = factor_products(
+        rows_own, hidden_columns, up_weight, slot_wide, adapter_down_factors
+    )
     extra_pair = swap(extra_theirs, 1, n_tensor)
     total, *sent = pair_sum(
         rows_own, frozen_ours, from_pair, extra_ours, extra_pair
@@ -414,7 +416,6 @@
         total = total + arrived.astype(jnp.float32)
     hidden_gradient = total.astype(jnp.bfloat16)
 
-    down_own = down_low_rank(hidden_columns, adapter_down_factors, slot_wide)
     down_weight = (sum_over_tensor(down_own, n_tensor) * factor).astype(jnp.bfloat16)
     weights = jnp.concatenate([down_weight, up_weight], axis=1)
     pick = (

time: 118 us -> 110 us (0.932)
  waiting for transfers between devices: 32.5 us -> 23.9 us
  Pallas kernels: 34.8 us -> 30.5 us
  starting transfers between devices: 37.2 us -> 38.7 us
    all_to_all x1, waiting for transfers between devices: 7.79 us -> 0.01 us  [local(): lax.all_to_all(blocks, 'tensor', 0, 0, tiled=True).reshape(tokens, columns)]
    pallas_call x6 -> x2, Pallas kernels: 21 us -> 15.3 us  [the longest x1 8.63 us: frozen_term(): call(frozen_kernel, (jax.ShapeDtypeStruct((tokens // 2, width), jnp.float...]
    ppermute x11 -> x9, starting transfers between devices: 7.45 us -> 9.47 us  [swap(): return lax.ppermute(value, 'tensor', [(i, i ^ mask) for i in range(count)])]
    add x4, other arithmetic: 0.06 us -> 1.87 us  [sum_over_tensor(): value = value + swap(value, mask, lax.axis_size('tensor'))]
    convert_element_type x1, other arithmetic: 1.58 us -> 0.02 us  [local(): (sum_over_tensor(down_own, n_tensor) * factor).astype(jnp.bfloat16)]
    pallas_call x1, Pallas kernels: 2.71 us -> 4.24 us  [pack_rows(): call(pack_kernel, jax.ShapeDtypeStruct((rows, columns), jnp.bfloat16), 2...]
    ppermute x11 -> x9, waiting for transfers between devices: 12.2 us -> 12.1 us  [swap(): return lax.ppermute(value, 'tensor', [(i, i ^ mask) for i in range(count)])]
  transfers between devices with their start and end apart: 17 -> 15, of which waited for: 7 -> 6; matrix products, arithmetic and copies ran while one was open for 4% -> 5% of each run, Pallas kernels for 27% -> 28%
where the time goes in v3:
time: 110 us; the launch traced here: 108 us
  starting transfers between devices  38.7 us (35%)
  Pallas kernels  30.5 us (28%)
  waiting for transfers between devices  23.9 us (22%)
  matrix products  5.49 us (5%)
  other arithmetic  4.78 us (4%)
  local copies, waits for them, and re-layouts  4.22 us (4%)
    ppermute x9, waiting for transfers between devices, swap(): return lax.ppermute(value, 'tensor', [(i, i ^ mask) for i in range(count)])  12.1 us
    ppermute x3, waiting for transfers between devices, local(): lax.ppermute(sent[step - 1], 'tensor', [(i, (i + 2 * step) % n_tensor) fo...  11.8 us
    all_to_all x1, starting transfers between devices, local(): lax.all_to_all(packed.reshape(n_slot, CAP, -1), 'dp', 0, 0, tiled=True)  11.2 us
    all_to_all x1, starting transfers between devices, local(): lax.all_to_all(packed_weights.reshape(n_slot, CAP, -1), 'dp', 0, 0, tiled...  9.94 us
    ppermute x9, starting transfers between devices, swap(): return lax.ppermute(value, 'tensor', [(i, i ^ mask) for i in range(count)])  9.47 us
    pallas_call x1, Pallas kernels, frozen_term(): call(frozen_kernel, (jax.ShapeDtypeStruct((tokens // 2, width), jnp.float...  8.63 us
    pallas_call x1, Pallas kernels, pair_sum(): call(functools.partial(pair_kernel, rows_own, parts), (jax.ShapeDtypeStru...  8.33 us
    pallas_call x1, Pallas kernels, factor_products(): call(functools.partial(factors_kernel, rows_own), shapes, 4 * tokens * fa...  6.7 us
  transfers between devices with their start and end apart: 15, of which 6 were waited for; matrix products, arithmetic and copies ran while one was open for 5% of the time, Pallas kernels for 28%

profile of v3, /device:TPU:32, one launch (start us, length us, event | category | flops | bytes accessed | tf_op | source)
XLA Modules:
  0.0 108.3 jit_solution(6331454037913372590)
XLA Ops:
  0.6 1.9 %copy.25 = bf16[4,8,8,1024]{3,2,0,1:T(8,128)(2,1)} copy(bf16[4,8,8,1024]{3,2,1,0:T(8,128)(2,1)} %bitcast.17) | data formatting | bytes 1048576 | tf_op jit(solution)/shard_map/reshape | solution.py:378
  2.5 4.5 %all-to-all-start = ((bf16[8,32,1024]{2,1,0:T(8,128)(2,1)}), bf16[8,32,1024]{2,1,0:T(8,128)(2,1)S(1)}, u32[]{:S(2)}, u32[]{:S(2)}) async-start(bf16[8,32,1024]{2,1,0:T(8,128)(2,1)} %bitcast.13), calls=%async_computation | async-start | bytes 1048576 | tf_op jit(solution)/shard_map/all_to_all | solution.py:379
  7.0 2.6 %prep.1 = (bf16[256,256]{1,0:T(8,128)(2,1)}, bf16[256,256]{1,0:T(8,128)(2,1)}, f32[256,128]{1,0:T(8,128)}, f32[256,128]{1,0:T(8,128)}, s32[1,256]{1,0:T(1,128)}, /*index=5*/f32[256,64]{1,0:T(8,128)}) custom-call(s32[32]{0:T(128)} %live_ref.1, s32[32]{0:T(128)} %bucket_ref.1, s32[32]{0:T(128)} %owner_ref.1, s32[1,256]{1,0:T(1,128)} %bitcast.21, ...), custom_call_target="tpu_custom_call" | custom-call | flops 268435456 | bytes 1048576 | tf_op jit(solution)/shard_map/prep/pallas_call | solution.py:143
  9.5 0.5 collective-permute-start
  10.0 1.2 %collective-permute-done = f32[256,64]{1,0:T(8,128)S(1)} collective-permute-done((f32[256,64]{1,0:T(8,128)}, f32[256,64]{1,0:T(8,128)S(1)}, u32[]{:S(2)}, u32[]{:S(2)}) %collective-permute-start) | collective-permute-done | bytes 65568 | tf_op jit(solution)/shard_map/ppermute | solution.py:40
  11.2 0.9 add.57
  12.2 2.0 %collective-permute-start.1 = (f32[256,64]{1,0:T(8,128)S(1)}, f32[256,64]{1,0:T(8,128)S(1)}, u32[]{:S(2)}, u32[]{:S(2)}) collective-permute-start(f32[256,64]{1,0:T(8,128)S(1)} %add.57), channel_id=1, source_target_pairs={{0,2},{1,3},{2,0},{3,1},{4,6},{5,7},{6,4},{7,5},{8,10},{9,11},{10,... | collective-permute-start | bytes 196616 | tf_op jit(solution)/shard_map/ppermute | solution.py:40
  14.1 8.6 %frozen_term.1 = (f32[128,8192]{1,0:T(8,128)}, f32[128,4096]{1,0:T(8,128)}, f32[128,4096]{1,0:T(8,128)}) custom-call(bf16[256,256]{1,0:T(8,128)(2,1)} %get-tuple-element.32.turned_ref, bf16[8192,256]{1,0:T(8,128)(2,1)} %frozen_ref.1), custom_call_target="tpu_custom_call" | custom-call | flops 1073741824 | bytes 12582912 | tf_op jit(solution)/shard_map/frozen_term/pallas_call | solution.py:182
  22.8 0.0 collective-permute-done.1
  22.8 0.1 collective-permute-start.4
  22.9 0.5 collective-permute-start.5
  23.4 0.0 all-to-all-done
  23.4 0.8 copy-done
  24.2 4.2 %pack.1 = bf16[512,1280]{1,0:T(8,128)(2,1)} custom-call(s32[1,256]{1,0:T(1,128)} %get-tuple-element.48.place_ref, bf16[256,1024]{1,0:T(8,128)(2,1)} %bitcast.15, bf16[256,256]{1,0:T(8,128)(2,1)} %get-tuple-element.49.masked_ref), custom_call_target="tpu_custom_call" | custom-call | flops 335544320 | bytes 1966080 | tf_op jit(solution)/shard_map/pack/pallas_call | solution.py:219
  28.4 11.2 %all-to-all-start.1 = ((bf16[32,16,1280]{2,1,0:T(8,128)(2,1)}), bf16[32,16,1280]{2,1,0:T(8,128)(2,1)}, u32[]{:S(2)}, u32[]{:S(2)}) async-start(bf16[32,16,1280]{2,1,0:T(8,128)(2,1)} %bitcast.14), calls=%async_computation.1 | async-start | bytes 2621440 | tf_op jit(solution)/shard_map/all_to_all | solution.py:400
  39.7 2.8 %collective-permute-start.2 = (f32[256,64]{1,0:T(8,128)S(1)}, f32[256,64]{1,0:T(8,128)S(1)}, u32[]{:S(2)}, u32[]{:S(2)}) collective-permute-start(f32[256,64]{1,0:T(8,128)S(1)} %add.58), channel_id=1, source_target_pairs={{0,4},{1,5},{2,6},{3,7},{4,0},{5,1},{6,2},{7,3},{8,12},{9,13},{10,... | collective-permute-start | bytes 196616 | tf_op jit(solution)/shard_map/ppermute | solution.py:40
  42.4 3.8 %collective-permute-done.2 = f32[256,64]{1,0:T(8,128)S(1)} collective-permute-done((f32[256,64]{1,0:T(8,128)S(1)}, f32[256,64]{1,0:T(8,128)S(1)}, u32[]{:S(2)}, u32[]{:S(2)}) %collective-permute-start.2) | collective-permute-done | bytes 65568 | tf_op jit(solution)/shard_map/ppermute | solution.py:40
  46.2 0.7 multiply_convert_fusion.1.weight_ref
  46.9 6.7 %factor_products.1 = (f32[256,64]{1,0:T(8,128)}, f32[128,1024]{1,0:T(8,128)}, f32[128,1024]{1,0:T(8,128)}) custom-call(bf16[256,1024]{1,0:T(8,128)(2,1)} %bitcast.16, bf16[256,64]{1,0:T(8,128)(2,1)} %multiply_convert_fusion.1.weight_ref, f32[256,128]{1,0:T(8,128)} %get-tuple-element.38.slot_ref, bf16[1024,2048]{1,0:T(8,128)(2,1)} %factors_ref.1), custom_call_target="tpu_custom_call" | custom-call | flops 2147483648 | bytes 4194304 | tf_op jit(solution)/shard_map/factor_products/pallas_call | solution.py:283
  53.6 0.1 collective-permute-start.3
  53.7 0.5 collective-permute-start.9
  54.2 1.8 %collective-permute-done.9 = f32[256,64]{1,0:T(8,128)S(1)} collective-permute-done((f32[256,64]{1,0:T(8,128)}, f32[256,64]{1,0:T(8,128)S(1)}, u32[]{:S(2)}, u32[]{:S(2)}) %collective-permute-start.9) | collective-permute-done | bytes 65568 | tf_op jit(solution)/shard_map/ppermute | solution.py:40
  56.0 0.9 add.63
  56.9 0.3 collective-permute-start.10
  57.2 5.3 %collective-permute-done.10 = f32[256,64]{1,0:T(8,128)S(1)} collective-permute-done((f32[256,64]{1,0:T(8,128)S(1)}, f32[256,64]{1,0:T(8,128)S(1)}, u32[]{:S(2)}, u32[]{:S(2)}) %collective-permute-start.10) | collective-permute-done | bytes 65568 | tf_op jit(solution)/shard_map/ppermute | solution.py:40
  62.5 2.8 %collective-permute-start.11 = (f32[256,64]{1,0:T(8,128)S(1)}, f32[256,64]{1,0:T(8,128)S(1)}, u32[]{:S(2)}, u32[]{:S(2)}) collective-permute-start(f32[256,64]{1,0:T(8,128)S(1)} %add.64), channel_id=1, source_target_pairs={{0,4},{1,5},{2,6},{3,7},{4,0},{5,1},{6,2},{7,3},{8,12},{9,13},{10,... | collective-permute-start | bytes 196616 | tf_op jit(solution)/shard_map/ppermute | solution.py:40
  65.3 0.0 collective-permute-done.3.extra_pair_ref
  65.3 0.0 collective-permute-done.4.refs_0_
  65.3 0.0 collective-permute-done.5.refs_1_
  65.3 0.8 copy-done.2
  66.1 0.7 copy-done.1
  66.9 8.3 %pair_sum.1 = (f32[32,8192]{1,0:T(8,128)}, bf16[32,8192]{1,0:T(8,128)(2,1)}, bf16[32,8192]{1,0:T(8,128)(2,1)}, bf16[32,8192]{1,0:T(8,128)(2,1)}) custom-call(f32[128,1024]{1,0:T(8,128)} %get-tuple-element.39.extra_ours_ref, f32[128,1024]{1,0:T(8,128)} %copy-done.2, f32[128,8192]{1,0:T(8,128)} %get-tuple-element.41.ours_ref, f32[128,4096]{1,0:T(8,128)} %copy-done.1, ...), custom_call_target="tpu_custom_call" | custom-call | flops 2097152 | bytes 10485760 | tf_op jit(solution)/shard_map/pair_sum/pallas_call | solution.py:337
  75.2 0.0 copy-start.11
  75.2 0.3 collective-permute-start.6
  75.5 1.5 %collective-permute-start.7 = (bf16[32,8192]{1,0:T(8,128)(2,1)}, bf16[32,8192]{1,0:T(8,128)(2,1)S(1)}, u32[]{:S(2)}, u32[]{:S(2)}) collective-permute-start(bf16[32,8192]{1,0:T(8,128)(2,1)} %get-tuple-element.46), channel_id=1, source_target_pairs={{0,4},{1,5},{2,6},{3,7},{4,0},{5,1},{6,2},{7,3},{8,12},{9,13},{10,... | collective-permute-start | bytes 1572872 | tf_op jit(solution)/shard_map/ppermute | solution.py:413
  77.0 1.7 %collective-permute-start.8 = (bf16[32,8192]{1,0:T(8,128)(2,1)}, bf16[32,8192]{1,0:T(8,128)(2,1)S(1)}, u32[]{:S(2)}, u32[]{:S(2)}) collective-permute-start(bf16[32,8192]{1,0:T(8,128)(2,1)} %get-tuple-element.47), channel_id=1, source_target_pairs={{0,6},{1,7},{2,0},{3,1},{4,2},{5,3},{6,4},{7,5},{8,14},{9,15},{10,... | collective-permute-start | bytes 1572872 | tf_op jit(solution)/shard_map/ppermute | solution.py:413
  78.8 0.0 collective-permute-done.11
  78.8 0.0 copy-done.4
  78.8 1.0 convolution_convert_fusion
  79.8 0.0 all-to-all-done.1
  79.8 9.9 %all-to-all-start.2 = ((bf16[32,16,128]{2,1,0:T(8,128)(2,1)}), bf16[32,16,128]{2,1,0:T(8,128)(2,1)S(1)}, u32[]{:S(2)}, u32[]{:S(2)}) async-start(bf16[32,16,128]{2,1,0:T(8,128)(2,1)} %bitcast.6), calls=%async_computation.2 | async-start | bytes 262144 | tf_op jit(solution)/shard_map/all_to_all | solution.py:428
  89.7 11.2 %collective-permute-done.6 = bf16[32,8192]{1,0:T(8,128)(2,1)S(1)} collective-permute-done((bf16[32,8192]{1,0:T(8,128)(2,1)}, bf16[32,8192]{1,0:T(8,128)(2,1)S(1)}, u32[]{:S(2)}, u32[]{:S(2)}) %collective-permute-start.6) | collective-permute-done | bytes 524320 | tf_op jit(solution)/shard_map/ppermute | solution.py:413
  100.9 0.0 collective-permute-done.7
  100.9 0.6 collective-permute-done.8
  101.5 2.2 %add_convert_fusion = bf16[32,8192]{1,0:T(8,128)(2,1)} fusion(bf16[32,8192]{1,0:T(8,128)(2,1)S(1)} %collective-permute-done.8, bf16[32,8192]{1,0:T(8,128)(2,1)S(1)} %collective-permute-done.7, f32[32,8192]{1,0:T(8,128)} %get-tuple-element.44, bf16[32,8192]{1,0:T(8,128)(2,1)S(1)} %collective-permute-done.6), kind=kLoop, calls=%fused_computation.3 | loop fusion | flops 1835008 | bytes 3145728 | tf_op jit(solution)/shard_map/convert_element_type | solution.py:417
  103.8 0.0 all-to-all-done.2
  103.8 1.9 %multiply_subtract_fusion.1 = (f32[64,256]{1,0:T(8,128)}, f32[64,256]{1,0:T(8,128)}, f32[64,256]{1,0:T(8,128)}) fusion(f32[64,256]{1,0:T(8,128)S(1)} %copy-done.9, f32[64,256]{1,0:T(8,128)S(1)} %copy-done.10, f32[64,256]{1,0:T(8,128)S(1)} %copy-done.11, bf16[512,1280]{1,0:T(8,128)(2,1)} %bitcast.4, bf16[512,128]{1,0:T(8,128)(2,1)S(1)} %bitcast.18), kind=kOutput, calls=%fused_computation.19 | convolution fusion | flops 17039360 | bytes 786432 | tf_op jit(solution)/shard_map/dot_general | solution.py:34
  105.7 2.7 %multiply_subtract_fusion = (f32[1024,64]{0,1:T(8,128)}, f32[1024,64]{0,1:T(8,128)}, f32[1024,64]{0,1:T(8,128)}) fusion(f32[1024,64]{0,1:T(8,128)S(1)} %copy-done.6, f32[1024,64]{0,1:T(8,128)S(1)} %copy-done.7, f32[1024,64]{0,1:T(8,128)S(1)} %copy-done.8, bf16[512,128]{1,0:T(8,128)(2,1)S(1)} %bitcast.19, bf16[512,1280]{1,0:T(8,128)(2,1)} %bitcast.4), kind=kOutput, calls=%fused_computation.8 | convolution fusion | flops 68157440 | bytes 2752512 | tf_op jit(solution)/shard_map/dot_general | solution.py:34
  (22 shorter events, 0.1 us)
Async XLA Ops:
  2.5 20.9 %all-to-all-start = ((bf16[8,32,1024]{2,1,0:T(8,128)(2,1)}), bf16[8,32,1024]{2,1,0:T(8,128)(2,1)S(1)}, u32[]{:S(2)}, u32[]{:S(2)}) async-start(bf16[8,32,1024]{2,1,0:T(8,128)(2,1)} %bitcast.13), calls=%async_computation | async-start | bytes 1048576 | tf_op jit(solution)/shard_map/all_to_all | solution.py:379
  9.5 1.7 %collective-permute-start = (f32[256,64]{1,0:T(8,128)}, f32[256,64]{1,0:T(8,128)S(1)}, u32[]{:S(2)}, u32[]{:S(2)}) collective-permute-start(f32[256,64]{1,0:T(8,128)} %get-tuple-element.31), channel_id=1, source_target_pairs={{0,1},{1,0},{2,3},{3,2},{4,5},{5,4},{6,7},{7,6},{8,9},{9,8},{10,11... | collective-permute-start | bytes 196616 | tf_op jit(solution)/shard_map/ppermute | solution.py:40
  12.2 10.6 %collective-permute-start.1 = (f32[256,64]{1,0:T(8,128)S(1)}, f32[256,64]{1,0:T(8,128)S(1)}, u32[]{:S(2)}, u32[]{:S(2)}) collective-permute-start(f32[256,64]{1,0:T(8,128)S(1)} %add.57), channel_id=1, source_target_pairs={{0,2},{1,3},{2,0},{3,1},{4,6},{5,7},{6,4},{7,5},{8,10},{9,11},{10,... | collective-permute-start | bytes 196616 | tf_op jit(solution)/shard_map/ppermute | solution.py:40
  22.8 42.5 %collective-permute-start.4 = (f32[128,4096]{1,0:T(8,128)}, f32[128,4096]{1,0:T(8,128)S(1)}, u32[]{:S(2)}, u32[]{:S(2)}) collective-permute-start(f32[128,4096]{1,0:T(8,128)} %get-tuple-element.42), channel_id=1, source_target_pairs={{0,1},{1,0},{2,3},{3,2},{4,5},{5,4},{6,7},{7,6},{8,9},{9,8},{10,11... | collective-permute-start | bytes 6291464 | tf_op jit(solution)/shard_map/ppermute | solution.py:40
  22.9 42.4 %collective-permute-start.5 = (f32[128,4096]{1,0:T(8,128)}, f32[128,4096]{1,0:T(8,128)}, u32[]{:S(2)}, u32[]{:S(2)}) collective-permute-start(f32[128,4096]{1,0:T(8,128)} %get-tuple-element.43), channel_id=1, source_target_pairs={{0,1},{1,0},{2,3},{3,2},{4,5},{5,4},{6,7},{7,6},{8,9},{9,8},{10,11... | collective-permute-start | bytes 6291464 | tf_op jit(solution)/shard_map/ppermute | solution.py:40
  23.4 0.8 copy-start
  24.2 22.0 %copy-start.3 = (f32[256,128]{1,0:T(8,128)S(1)}, f32[256,128]{1,0:T(8,128)}, u32[]{:S(2)}) copy-start(f32[256,128]{1,0:T(8,128)} %get-tuple-element.37) | copy-start | bytes 393220
  28.4 51.4 %all-to-all-start.1 = ((bf16[32,16,1280]{2,1,0:T(8,128)(2,1)}), bf16[32,16,1280]{2,1,0:T(8,128)(2,1)}, u32[]{:S(2)}, u32[]{:S(2)}) async-start(bf16[32,16,1280]{2,1,0:T(8,128)(2,1)} %bitcast.14), calls=%async_computation.1 | async-start | bytes 2621440 | tf_op jit(solution)/shard_map/all_to_all | solution.py:400
  39.7 6.6 %collective-permute-start.2 = (f32[256,64]{1,0:T(8,128)S(1)}, f32[256,64]{1,0:T(8,128)S(1)}, u32[]{:S(2)}, u32[]{:S(2)}) collective-permute-start(f32[256,64]{1,0:T(8,128)S(1)} %add.58), channel_id=1, source_target_pairs={{0,4},{1,5},{2,6},{3,7},{4,0},{5,1},{6,2},{7,3},{8,12},{9,13},{10,... | collective-permute-start | bytes 196616 | tf_op jit(solution)/shard_map/ppermute | solution.py:40
  53.6 11.7 %collective-permute-start.3 = (f32[128,1024]{1,0:T(8,128)}, f32[128,1024]{1,0:T(8,128)S(1)}, u32[]{:S(2)}, u32[]{:S(2)}) collective-permute-start(f32[128,1024]{1,0:T(8,128)} %get-tuple-element.40), channel_id=1, source_target_pairs={{0,1},{1,0},{2,3},{3,2},{4,5},{5,4},{6,7},{7,6},{8,9},{9,8},{10,11... | collective-permute-start | bytes 1572872 | tf_op jit(solution)/shard_map/ppermute | solution.py:40
  53.7 2.3 %collective-permute-start.9 = (f32[256,64]{1,0:T(8,128)}, f32[256,64]{1,0:T(8,128)S(1)}, u32[]{:S(2)}, u32[]{:S(2)}) collective-permute-start(f32[256,64]{1,0:T(8,128)} %get-tuple-element.50), channel_id=1, source_target_pairs={{0,1},{1,0},{2,3},{3,2},{4,5},{5,4},{6,7},{7,6},{8,9},{9,8},{10,11... | collective-permute-start | bytes 196616 | tf_op jit(solution)/shard_map/ppermute | solution.py:40
  56.9 5.6 %collective-permute-start.10 = (f32[256,64]{1,0:T(8,128)S(1)}, f32[256,64]{1,0:T(8,128)S(1)}, u32[]{:S(2)}, u32[]{:S(2)}) collective-permute-start(f32[256,64]{1,0:T(8,128)S(1)} %add.63), channel_id=1, source_target_pairs={{0,2},{1,3},{2,0},{3,1},{4,6},{5,7},{6,4},{7,5},{8,10},{9,11},{10,... | collective-permute-start | bytes 196616 | tf_op jit(solution)/shard_map/ppermute | solution.py:40
  62.5 16.2 %collective-permute-start.11 = (f32[256,64]{1,0:T(8,128)S(1)}, f32[256,64]{1,0:T(8,128)S(1)}, u32[]{:S(2)}, u32[]{:S(2)}) collective-permute-start(f32[256,64]{1,0:T(8,128)S(1)} %add.64), channel_id=1, source_target_pairs={{0,4},{1,5},{2,6},{3,7},{4,0},{5,1},{6,2},{7,3},{8,12},{9,13},{10,... | collective-permute-start | bytes 196616 | tf_op jit(solution)/shard_map/ppermute | solution.py:40
  65.3 0.8 copy-start.2
  65.3 1.5 %copy-start.1 = (f32[128,4096]{1,0:T(8,128)}, f32[128,4096]{1,0:T(8,128)S(1)}, u32[]{:S(2)}) copy-start(f32[128,4096]{1,0:T(8,128)S(1)} %collective-permute-done.4.refs_0_) | copy-start | bytes 6291460
  66.8 12.0 %copy-start.4 = (bf16[256,64]{1,0:T(8,128)(2,1)S(1)}, bf16[256,64]{1,0:T(8,128)(2,1)}, u32[]{:S(2)}) copy-start(bf16[256,64]{1,0:T(8,128)(2,1)} %multiply_convert_fusion.1.weight_ref) | copy-start | bytes 98308
  66.8 12.0 %copy-start.5 = (s32[1,256]{1,0:T(1,128)S(1)}, s32[1,256]{1,0:T(1,128)}, u32[]{:S(2)}) copy-start(s32[1,256]{1,0:T(1,128)} %get-tuple-element.48.place_ref) | copy-start | bytes 3076
  75.2 28.6 %copy-start.9 = (f32[64,256]{1,0:T(8,128)S(1)}, f32[64,256]{1,0:T(8,128)}, u32[]{:S(2)}) copy-start(f32[64,256]{1,0:T(8,128)} %param.23) | copy-start | bytes 196612
  75.2 28.6 %copy-start.10 = (f32[64,256]{1,0:T(8,128)S(1)}, f32[64,256]{1,0:T(8,128)}, u32[]{:S(2)}) copy-start(f32[64,256]{1,0:T(8,128)} %param.24) | copy-start | bytes 196612
  75.2 28.6 %copy-start.11 = (f32[64,256]{1,0:T(8,128)S(1)}, f32[64,256]{1,0:T(8,128)}, u32[]{:S(2)}) copy-start(f32[64,256]{1,0:T(8,128)} %param.25) | copy-start | bytes 196612
  75.2 25.7 %collective-permute-start.6 = (bf16[32,8192]{1,0:T(8,128)(2,1)}, bf16[32,8192]{1,0:T(8,128)(2,1)S(1)}, u32[]{:S(2)}, u32[]{:S(2)}) collective-permute-start(bf16[32,8192]{1,0:T(8,128)(2,1)} %get-tuple-element.45), channel_id=1, source_target_pairs={{0,2},{1,3},{2,4},{3,5},{4,6},{5,7},{6,0},{7,1},{8,10},{9,11},{10,... | collective-permute-start | bytes 1572872 | tf_op jit(solution)/shard_map/ppermute | solution.py:413
  75.5 25.4 %collective-permute-start.7 = (bf16[32,8192]{1,0:T(8,128)(2,1)}, bf16[32,8192]{1,0:T(8,128)(2,1)S(1)}, u32[]{:S(2)}, u32[]{:S(2)}) collective-permute-start(bf16[32,8192]{1,0:T(8,128)(2,1)} %get-tuple-element.46), channel_id=1, source_target_pairs={{0,4},{1,5},{2,6},{3,7},{4,0},{5,1},{6,2},{7,3},{8,12},{9,13},{10,... | collective-permute-start | bytes 1572872 | tf_op jit(solution)/shard_map/ppermute | solution.py:413
  77.0 24.5 %collective-permute-start.8 = (bf16[32,8192]{1,0:T(8,128)(2,1)}, bf16[32,8192]{1,0:T(8,128)(2,1)S(1)}, u32[]{:S(2)}, u32[]{:S(2)}) collective-permute-start(bf16[32,8192]{1,0:T(8,128)(2,1)} %get-tuple-element.47), channel_id=1, source_target_pairs={{0,6},{1,7},{2,0},{3,1},{4,2},{5,3},{6,4},{7,5},{8,14},{9,15},{10,... | collective-permute-start | bytes 1572872 | tf_op jit(solution)/shard_map/ppermute | solution.py:413
  79.8 25.9 %copy-start.6 = (f32[1024,64]{0,1:T(8,128)S(1)}, f32[1024,64]{0,1:T(8,128)}, u32[]{:S(2)}) copy-start(f32[1024,64]{0,1:T(8,128)} %param.20) | copy-start | bytes 786436
  79.8 25.9 %copy-start.7 = (f32[1024,64]{0,1:T(8,128)S(1)}, f32[1024,64]{0,1:T(8,128)}, u32[]{:S(2)}) copy-start(f32[1024,64]{0,1:T(8,128)} %param.21) | copy-start | bytes 786436
  79.8 25.9 %copy-start.8 = (f32[1024,64]{0,1:T(8,128)S(1)}, f32[1024,64]{0,1:T(8,128)}, u32[]{:S(2)}) copy-start(f32[1024,64]{0,1:T(8,128)} %param.22) | copy-start | bytes 786436
  79.8 24.0 %all-to-all-start.2 = ((bf16[32,16,128]{2,1,0:T(8,128)(2,1)}), bf16[32,16,128]{2,1,0:T(8,128)(2,1)S(1)}, u32[]{:S(2)}, u32[]{:S(2)}) async-start(bf16[32,16,128]{2,1,0:T(8,128)(2,1)} %bitcast.6), calls=%async_computation.2 | async-start | bytes 262144 | tf_op jit(solution)/shard_map/all_to_all | solution.py:428

commit v4 on v3

--- a/solution.py
+++ b/solution.py
@@ -40,41 +40,51 @@
     return lax.ppermute(value, "tensor", [(i, i ^ mask) for i in range(count)])
 
 
-def sum_over_tensor(value, count, mask=1):
-    while mask < count:
-        value = value + swap(value, mask, lax.axis_size("tensor"))
-        mask *= 2
-    return value
-
-
-VMEM_LIMIT = 60 * 1024 * 1024
+def sum_over_chips(value, count):
+    near = value + swap(value, 2, count)
+    far = swap(value, 4, count) + swap(value, 6, count)
+    return near + far
+
+
+VMEM_LIMIT = 16 * 1024 * 1024
+VMEM_MOST = 57 * 1024 * 1024
+SMEM_SPEC = pl.BlockSpec(memory_space=pltpu.MemorySpace.SMEM)
 HBM = pltpu.MemorySpace.HBM
-SMEM = pltpu.MemorySpace.SMEM
 NT = (((1,), (1,)), ((), ()))
 NN = (((1,), (0,)), ((), ()))
 
 
-def call(kernel, out_shape, flops, moved, **options):
+def call(kernel, out_shape, flops, moved, limit=VMEM_LIMIT, **options):
     return pl.pallas_call(
         kernel,
         out_shape=out_shape,
-        compiler_params=pltpu.CompilerParams(vmem_limit_bytes=VMEM_LIMIT),
+        compiler_params=pltpu.CompilerParams(vmem_limit_bytes=limit),
         cost_estimate=pl.CostEstimate(flops=flops, bytes_accessed=moved, transcendentals=0),
         **options,
     )
 
 
-def whole(shape, memory_space=None):
-    zeros = (0,) * len(shape)
-    return pl.BlockSpec(shape, lambda *_: zeros, memory_space=memory_space)
-
-
 def dot(left, right, dims):
     return lax.dot_general(left, right, dims, preferred_element_type=jnp.float32)
 
 
 def lane_slot(shape, first):
     return (lax.broadcasted_iota(jnp.int32, shape, 1) // PADDED_RANK + first).astype(jnp.float32)
+
+
+def fetch(sources, targets, sems):
+    copies = [
+        pltpu.make_async_copy(source, target, sems.at[i])
+        for i, (source, target) in enumerate(zip(sources, targets, strict=True))
+    ]
+    for copy in copies:
+        copy.start()
+    return copies
+
+
+def row_parts(ref, parts):
+    rows = ref.shape[0] // parts
+    return [ref.at[pl.ds(i * rows, rows), :] for i in range(parts)]
 
 
 def prep_kernel(rows_own, live_ref, bucket_ref, owner_ref, adapter_ref, cot_ref, up_ref,
@@ -145,90 +155,62 @@
         shapes,
         2 * tokens * kv * up_factors.shape[0],
         up_factors.size * 2,
-        grid=(1,),
-        in_specs=[whole(v.shape, SMEM) for v in (live, bucket, owner)]
-        + [whole(v.shape) for v in (adapter_row, cotangent, up_factors)],
-        out_specs=tuple(whole(v.shape) for v in shapes),
+        in_specs=[SMEM_SPEC] * 3
+        + [pl.BlockSpec(v.shape) for v in (adapter_row, cotangent, up_factors)],
         name="prep",
     )(live, bucket, owner, adapter_row, cotangent, up_factors)
 
 
-def frozen_kernel(turned_ref, frozen_ref, ours_ref, *theirs_refs):
-    step = pl.program_id(0)
-    half = ours_ref.shape[0]
-    per_part = pl.num_programs(0) // len(theirs_refs)
-    both = dot(turned_ref[...], frozen_ref[...], NT)
-    ours_ref[...] = both[:half, :]
-    for part, out in enumerate(theirs_refs):
-
-        @pl.when(step // per_part == part)
-        def _():
-            out[...] = both[half:, :]
-
-
-def part_blocks(rows, chunk, parts, per_part):
-    return [
-        pl.BlockSpec((rows, chunk), lambda i, q=q: (0, jnp.clip(i - q * per_part, 0, per_part - 1)))
-        for q in range(parts)
-    ]
+def frozen_kernel(turned_ref, frozen_any, *refs):
+    outs, (frozen_ref, sems) = refs[:-2], refs[-2:]
+    steps = sems.shape[0]
+    half = outs[0].shape[0]
+    chunk = frozen_ref.shape[0] // steps
+    per_part = steps // len(outs)
+    copies = fetch(row_parts(frozen_any, steps), row_parts(frozen_ref, steps), sems)
+    theirs = turned_ref[half:, :]
+    for c in range(steps):
+        copies[c].wait()
+        first = c % per_part * chunk
+        outs[c // per_part][:, first : first + chunk] = dot(
+            theirs, frozen_ref[c * chunk : (c + 1) * chunk, :], NT
+        )
 
 
 def frozen_term(turned, frozen, parts):
     tokens, kv = turned.shape
     width = frozen.shape[0]
-    chunk = 1024
-    steps = width // chunk
-    theirs = jax.ShapeDtypeStruct((tokens // 2, width // parts), jnp.float32)
     return call(
         frozen_kernel,
-        (jax.ShapeDtypeStruct((tokens // 2, width), jnp.float32),) + (theirs,) * parts,
-        2 * tokens * kv * width,
-        2 * kv * width + 4 * tokens * width,
-        grid=(steps,),
-        in_specs=[whole(turned.shape), pl.BlockSpec((chunk, kv), lambda i: (i, 0))],
-        out_specs=(
-            pl.BlockSpec((tokens // 2, chunk), lambda i: (0, i)),
-            *part_blocks(tokens // 2, chunk, parts, steps // parts),
-        ),
+        (jax.ShapeDtypeStruct((tokens // 2, width // parts), jnp.float32),) * parts,
+        tokens * kv * width,
+        2 * kv * width + 2 * tokens * width,
+        VMEM_MOST,
+        in_specs=[pl.BlockSpec(turned.shape), pl.BlockSpec(memory_space=HBM)],
+        scratch_shapes=[
+            pltpu.VMEM(frozen.shape, frozen.dtype),
+            pltpu.SemaphoreType.DMA((8,)),
+        ],
         name="frozen_term",
     )(turned, frozen)
 
 
-def pack_kernel(place_ref, hidden_ref, masked_ref, out_ref, pick_ref):
-    step = pl.program_id(0)
-    last = pl.num_programs(0) - 1
-
-    @pl.when(step == 0)
-    def _():
-        down = lax.broadcasted_iota(jnp.int32, pick_ref.shape, 0)
-        pick_ref[...] = jnp.where(down == place_ref[...], 1.0, 0.0).astype(jnp.bfloat16)
-
-    @pl.when(step < last)
-    def _():
-        out_ref[...] = dot(pick_ref[...], hidden_ref[...], NN).astype(jnp.bfloat16)
-
-    @pl.when(step == last)
-    def _():
-        out_ref[...] = dot(pick_ref[...], masked_ref[...], NN).astype(jnp.bfloat16)
+def pack_kernel(place_ref, hidden_ref, masked_ref, out_ref):
+    rows, tokens = out_ref.shape[0], place_ref.shape[1]
+    down = lax.broadcasted_iota(jnp.int32, (rows, tokens), 0)
+    pick = jnp.where(down == place_ref[...], 1.0, 0.0).astype(jnp.bfloat16)
+    width = hidden_ref.shape[1]
+    out_ref[:, :width] = dot(pick, hidden_ref[...], NN).astype(jnp.bfloat16)
+    out_ref[:, width:] = dot(pick, masked_ref[...], NN).astype(jnp.bfloat16)
 
 
 def pack_rows(place, hidden_columns, masked, rows):
-    tokens, chunk = masked.shape
-    columns = hidden_columns.shape[1] + chunk
-    steps = columns // chunk
+    tokens, columns = masked.shape[0], hidden_columns.shape[1] + masked.shape[1]
     return call(
         pack_kernel,
         jax.ShapeDtypeStruct((rows, columns), jnp.bfloat16),
         2 * rows * columns * tokens,
         2 * (rows + tokens) * columns,
-        grid=(steps,),
-        in_specs=[
-            whole(place.shape),
-            pl.BlockSpec((tokens, chunk), lambda i: (0, jnp.minimum(i, steps - 2))),
-            whole(masked.shape),
-        ],
-        out_specs=pl.BlockSpec((rows, chunk), lambda i: (0, i)),
-        scratch_shapes=[pltpu.VMEM((rows, tokens), jnp.bfloat16)],
         name="pack",
     )(place, hidden_columns, masked)
 
@@ -285,10 +267,9 @@
         shapes,
         4 * tokens * factors.size,
         2 * factors.size,
-        grid=(1,),
-        in_specs=[whole(v.shape) for v in (hidden_columns, up_weight, slot_wide)]
+        VMEM_MOST,
+        in_specs=[pl.BlockSpec(v.shape) for v in (hidden_columns, up_weight, slot_wide)]
         + [pl.BlockSpec(memory_space=HBM)],
-        out_specs=tuple(whole(v.shape) for v in shapes),
         scratch_shapes=[
             pltpu.VMEM((parts, columns, chunk), jnp.bfloat16),
             pltpu.VMEM((tokens, columns), jnp.float32),
@@ -298,57 +279,50 @@
     )(hidden_columns, up_weight, slot_wide, factors)
 
 
-def pair_kernel(rows_own, parts, extra_ours_ref, extra_pair_ref, ours_ref, *refs):
-    pair_refs, own_ref, out_refs = refs[:parts], refs[parts], refs[parts + 1 :]
-    step = pl.program_id(0)
-    per_part = pl.num_programs(0) // parts
+def pair_kernel(rows_own, parts, turned_ref, extra_ours_ref, extra_pair_ref, frozen_any, *refs):
+    pair_refs, outs, (frozen_ref, sems) = refs[:parts], refs[parts:-2], refs[-2:]
+    steps = sems.shape[0]
+    half, columns = extra_ours_ref.shape
+    per_part = steps // parts
+    copies = fetch(row_parts(frozen_any, steps), row_parts(frozen_ref, steps), sems)
     position = lax.axis_index("tensor")
     chip, core = position // 2, position % 2
-    total = ours_ref[...]
-    for part in range(parts):
-        total = jnp.where(step // per_part == part, total + pair_refs[part][...], total)
-
-    def write(value):
-        own_ref[...] = value[:rows_own, :]
-        for i, out in enumerate(out_refs):
-            out[...] = value[(i + 1) * rows_own : (i + 2) * rows_own, :].astype(jnp.bfloat16)
-
-    @pl.when(step // 2 != chip)
-    def _():
-        write(total)
-
-    @pl.when((step // 2 == chip) & (step % 2 == core))
-    def _():
-        write(total + extra_ours_ref[...])
-
-    @pl.when((step // 2 == chip) & (step % 2 != core))
-    def _():
-        write(total + extra_pair_ref[...])
-
-
-def pair_sum(rows_own, ours, from_pair, extra_ours, extra_pair):
+    ours = turned_ref[:half, :]
+    low = jnp.where(core == 0, extra_ours_ref[...], extra_pair_ref[...])
+    high = jnp.where(core == 0, extra_pair_ref[...], extra_ours_ref[...])
+    for c in range(steps):
+        copies[c].wait()
+        at = slice(c * columns, (c + 1) * columns)
+        first = c % per_part * columns
+        total = dot(ours, frozen_ref[at, :], NT)
+        total = total + pair_refs[c // per_part][:, first : first + columns]
+        total = total + jnp.where(chip == c // 2, low if c % 2 == 0 else high, 0.0)
+        outs[0][:, at] = total[:rows_own, :]
+        for i, out in enumerate(outs[1:]):
+            out[:, at] = total[(i + 1) * rows_own : (i + 2) * rows_own, :].astype(jnp.bfloat16)
+
+
+def pair_sum(rows_own, turned, frozen, from_pair, extra_ours, extra_pair):
     parts = len(from_pair)
-    half, width = ours.shape
-    columns = extra_ours.shape[1]
-    steps = width // columns
+    half, columns = extra_ours.shape
+    width, kv = frozen.shape
     sent = jax.ShapeDtypeStruct((rows_own, width), jnp.bfloat16)
-    out_block = pl.BlockSpec((rows_own, columns), lambda i: (0, i))
     n_out = half // rows_own - 1
     return call(
         functools.partial(pair_kernel, rows_own, parts),
         (jax.ShapeDtypeStruct((rows_own, width), jnp.float32),) + (sent,) * n_out,
-        2 * half * width,
-        10 * half * width,
-        grid=(steps,),
-        in_specs=[
-            whole(extra_ours.shape),
-            whole(extra_pair.shape),
-            pl.BlockSpec((half, columns), lambda i: (0, i)),
-            *part_blocks(half, columns, parts, steps // parts),
+        2 * half * width * kv,
+        2 * kv * width + 6 * half * width,
+        VMEM_MOST,
+        in_specs=[pl.BlockSpec(v.shape) for v in (turned, extra_ours, extra_pair)]
+        + [pl.BlockSpec(memory_space=HBM)]
+        + [pl.BlockSpec(v.shape) for v in from_pair],
+        scratch_shapes=[
+            pltpu.VMEM(frozen.shape, frozen.dtype),
+            pltpu.SemaphoreType.DMA((width // columns,)),
         ],
-        out_specs=(out_block,) * (n_out + 1),
         name="pair_sum",
-    )(extra_ours, extra_pair, ours, *from_pair)
+    )(turned, extra_ours, extra_pair, frozen, *from_pair)
 
 
 def local(
@@ -389,26 +363,28 @@
     )
     factor = factor_wide[:, :PADDED_RANK]
 
-    frozen_ours, *frozen_theirs = frozen_term(turned, frozen_key_value, 2)
-    up_own = sum_over_tensor(up_own, n_tensor // 2)
-    place, up_own, frozen_ours, frozen_theirs = lax.optimization_barrier(
-        (place, up_own, frozen_ours, frozen_theirs)
-    )
+    frozen_theirs = frozen_term(turned, frozen_key_value, 2)
+    up_own = up_own + swap(up_own, 1, n_tensor)
+    place, up_own, frozen_theirs = lax.optimization_barrier((place, up_own, frozen_theirs))
     from_pair = [swap(theirs, 1, n_tensor) for theirs in frozen_theirs]
+    up_sum = sum_over_chips(up_own, n_tensor)
 
     packed = pack_rows(place, hidden_columns, masked, n_slot * CAP)
+    packed, up_sum = lax.optimization_barrier((packed, up_sum))
     owned = lax.all_to_all(
         packed.reshape(n_slot, CAP, -1), "dp", 0, 0, tiled=True
     ).reshape(n_slot * CAP, -1)
 
-    up_weight = (sum_over_tensor(up_own, n_tensor, n_tensor // 2) * factor).astype(jnp.bfloat16)
+    up_weight = (up_sum * factor).astype(jnp.bfloat16)
     down_own, extra_ours, extra_theirs = factor_products(
         rows_own, hidden_columns, up_weight, slot_wide, adapter_down_factors
     )
     extra_pair = swap(extra_theirs, 1, n_tensor)
     total, *sent = pair_sum(
-        rows_own, frozen_ours, from_pair, extra_ours, extra_pair
-    )
+        rows_own, turned, frozen_key_value, from_pair, extra_ours, extra_pair
+    )
+    down_own = down_own + swap(down_own, 1, n_tensor)
+    down_own, total, sent = lax.optimization_barrier((down_own, total, sent))
     for step in range(1, n_chip):
         arrived = lax.ppermute(
             sent[step - 1], "tensor", [(i, (i + 2 * step) % n_tensor) for i in range(n_tensor)]
@@ -416,7 +392,7 @@
         total = total + arrived.astype(jnp.float32)
     hidden_gradient = total.astype(jnp.bfloat16)
 
-    down_weight = (sum_over_tensor(down_own, n_tensor) * factor).astype(jnp.bfloat16)
+    down_weight = (sum_over_chips(down_own, n_tensor) * factor).astype(jnp.bfloat16)
     weights = jnp.concatenate([down_weight, up_weight], axis=1)
     pick = (
         jnp.arange(n_slot * CAP, dtype=jnp.int32)[:, None] == place

time: 110 us -> 101 us (0.918); the launches traced: 108 us -> 100 us
  Pallas kernels: 30.5 us -> 23.4 us
  starting transfers between devices: 38.7 us -> 42.4 us
  waiting for transfers between devices: 23.9 us -> 20.6 us
    ppermute x3, starting transfers between devices: 3.56 us -> 7.25 us  [local(): lax.ppermute(sent[step - 1], 'tensor', [(i, (i + 2 * step) % n_tensor) fo...]
    ppermute x9 -> x11, waiting for transfers between devices: 12.1 us -> 8.92 us  [swap(): return lax.ppermute(value, 'tensor', [(i, i ^ mask) for i in range(count)])]
    pallas_call x1, Pallas kernels: 4.24 us -> 1.6 us  [pack_rows(): call(pack_kernel, jax.ShapeDtypeStruct((rows, columns), jnp.bfloat16), 2...]
    pallas_call x1, Pallas kernels: 8.63 us -> 6.22 us  [frozen_term(): call(frozen_kernel, (jax.ShapeDtypeStruct((tokens // 2, width // parts),...]
    pallas_call x1, Pallas kernels: 2.56 us -> 1.13 us  [prep(): call(functools.partial(prep_kernel, rows_own), shapes, 2 * tokens * kv *...]
    ppermute x9 -> x11, starting transfers between devices: 9.47 us -> 9.95 us  [swap(): return lax.ppermute(value, 'tensor', [(i, i ^ mask) for i in range(count)])]
    unnamed x24 -> x26, local copies, waits for them, and re-layouts: 2.34 us -> 2.11 us
  transfers between devices with their start and end apart: 15 -> 17, of which waited for: 6 -> 6; matrix products, arithmetic and copies ran while one was open for 5% -> 5% of each run, Pallas kernels for 28% -> 23%
where the time goes in v4:
time: 101 us; the launch traced here: 100 us
  starting transfers between devices  42.4 us (42%)
  Pallas kernels  23.4 us (23%)
  waiting for transfers between devices  20.6 us (20%)
  matrix products  5.17 us (5%)
  local copies, waits for them, and re-layouts  4.09 us (4%)
  other arithmetic  3.92 us (4%)
    ppermute x3, waiting for transfers between devices, local(): lax.ppermute(sent[step - 1], 'tensor', [(i, (i + 2 * step) % n_tensor) fo...  11.3 us
    all_to_all x1, starting transfers between devices, local(): lax.all_to_all(packed.reshape(n_slot, CAP, -1), 'dp', 0, 0, tiled=True)  11.2 us
    ppermute x11, starting transfers between devices, swap(): return lax.ppermute(value, 'tensor', [(i, i ^ mask) for i in range(count)])  9.95 us
    all_to_all x1, starting transfers between devices, local(): lax.all_to_all(packed_weights.reshape(n_slot, CAP, -1), 'dp', 0, 0, tiled...  9.57 us
    ppermute x11, waiting for transfers between devices, swap(): return lax.ppermute(value, 'tensor', [(i, i ^ mask) for i in range(count)])  8.92 us
    pallas_call x1, Pallas kernels, pair_sum(): call(functools.partial(pair_kernel, rows_own, parts), (jax.ShapeDtypeStru...  7.72 us
    ppermute x3, starting transfers between devices, local(): lax.ppermute(sent[step - 1], 'tensor', [(i, (i + 2 * step) % n_tensor) fo...  7.25 us
    pallas_call x1, Pallas kernels, factor_products(): call(functools.partial(factors_kernel, rows_own), shapes, 4 * tokens * fa...  6.7 us
  transfers between devices with their start and end apart: 17, of which 6 were waited for; matrix products, arithmetic and copies ran while one was open for 5% of the time, Pallas kernels for 23%

profile of v4, /device:TPU:32, one launch (start us, length us, event | category | flops | bytes accessed | tf_op | source)
XLA Modules:
  0.0 100.4 jit_solution(3274023294455365919)
XLA Ops:
  0.7 2.0 %copy.25 = bf16[4,8,8,1024]{3,2,0,1:T(8,128)(2,1)} copy(bf16[4,8,8,1024]{3,2,1,0:T(8,128)(2,1)} %bitcast.20) | data formatting | bytes 1048576 | tf_op jit(solution)/shard_map/reshape | solution.py:352
  2.7 4.5 %all-to-all-start = ((bf16[8,32,1024]{2,1,0:T(8,128)(2,1)}), bf16[8,32,1024]{2,1,0:T(8,128)(2,1)S(1)}, u32[]{:S(2)}, u32[]{:S(2)}) async-start(bf16[8,32,1024]{2,1,0:T(8,128)(2,1)} %bitcast.13), calls=%async_computation | async-start | bytes 1048576 | tf_op jit(solution)/shard_map/all_to_all | solution.py:353
  7.2 1.1 %prep.1 = (bf16[256,256]{1,0:T(8,128)(2,1)S(1)}, bf16[256,256]{1,0:T(8,128)(2,1)S(1)}, f32[256,128]{1,0:T(8,128)S(1)}, f32[256,128]{1,0:T(8,128)S(1)}, s32[1,256]{1,0:T(1,128)S(1)}, /*index=5*/f32[256,64]{1,0:T(8,128)S(1)}) custom-call(s32[32]{0:T(128)S(1)} %copy-done.5, s32[32]{0:T(128)S(1)} %copy-done.6, s32[32]{0:T(128)S(1)} %copy-done.7, ...), custom_call_target="tpu_custom_call" | custom-call | flops 268435456 | bytes 1048576 | tf_op jit(solution)/shard_map/prep/pallas_call | solution.py:153
  8.3 0.0 copy-start.2
  8.3 0.6 copy-done.2
  9.0 0.7 copy-done.8
  9.6 0.5 collective-permute-start
  10.1 6.2 %frozen_term.1 = (f32[128,4096]{1,0:T(8,128)}, f32[128,4096]{1,0:T(8,128)}) custom-call(bf16[256,256]{1,0:T(8,128)(2,1)} %copy-done.2, bf16[8192,256]{1,0:T(8,128)(2,1)} %frozen_any.3), custom_call_target="tpu_custom_call" | custom-call | flops 536870912 | bytes 8388608 | tf_op jit(solution)/shard_map/frozen_term/pallas_call | solution.py:183
  16.4 3.0 %collective-permute-start.3 = (f32[256,64]{1,0:T(8,128)S(1)}, f32[256,64]{1,0:T(8,128)S(1)}, u32[]{:S(2)}, u32[]{:S(2)}) collective-permute-start(f32[256,64]{1,0:T(8,128)S(1)} %add.63), channel_id=1, source_target_pairs={{0,6},{1,7},{2,4},{3,5},{4,2},{5,3},{6,0},{7,1},{8,14},{9,15},{10,... | collective-permute-start | bytes 196616 | tf_op jit(solution)/shard_map/ppermute | solution.py:40
  19.4 0.9 collective-permute-start.2
  20.2 0.3 collective-permute-start.1
  20.6 0.5 collective-permute-start.7
  21.1 4.4 %collective-permute-done.3 = f32[256,64]{1,0:T(8,128)S(1)} collective-permute-done((f32[256,64]{1,0:T(8,128)S(1)}, f32[256,64]{1,0:T(8,128)S(1)}, u32[]{:S(2)}, u32[]{:S(2)}) %collective-permute-start.3) | collective-permute-done | bytes 65568 | tf_op jit(solution)/shard_map/ppermute | solution.py:40
  25.4 1.8 %collective-permute-done.2 = f32[256,64]{1,0:T(8,128)S(1)} collective-permute-done((f32[256,64]{1,0:T(8,128)S(1)}, f32[256,64]{1,0:T(8,128)S(1)}, u32[]{:S(2)}, u32[]{:S(2)}) %collective-permute-start.2) | collective-permute-done | bytes 65568 | tf_op jit(solution)/shard_map/ppermute | solution.py:40
  27.3 0.0 all-to-all-done
  27.3 0.0 copy-start
  27.3 1.6 %pack.1 = bf16[512,1280]{1,0:T(8,128)(2,1)} custom-call(s32[1,256]{1,0:T(1,128)S(1)} %get-tuple-element.40.place_ref, bf16[256,1024]{1,0:T(8,128)(2,1)S(1)} %bitcast.14, bf16[256,256]{1,0:T(8,128)(2,1)S(1)} %get-tuple-element.41.masked_ref), custom_call_target="tpu_custom_call" | custom-call | flops 335544320 | bytes 1966080 | tf_op jit(solution)/shard_map/pack/pallas_call | solution.py:209
  28.9 11.2 %all-to-all-start.1 = ((bf16[32,16,1280]{2,1,0:T(8,128)(2,1)}), bf16[32,16,1280]{2,1,0:T(8,128)(2,1)S(1)}, u32[]{:S(2)}, u32[]{:S(2)}) async-start(bf16[32,16,1280]{2,1,0:T(8,128)(2,1)} %bitcast.3), calls=%async_computation.1 | async-start | bytes 2621440 | tf_op jit(solution)/shard_map/all_to_all | solution.py:374
  40.1 0.6 multiply_convert_fusion.1.weight_ref
  40.7 6.7 %factor_products.1 = (f32[256,64]{1,0:T(8,128)}, f32[128,1024]{1,0:T(8,128)}, f32[128,1024]{1,0:T(8,128)}) custom-call(bf16[256,1024]{1,0:T(8,128)(2,1)} %bitcast.15, bf16[256,64]{1,0:T(8,128)(2,1)} %multiply_convert_fusion.1.weight_ref, f32[256,128]{1,0:T(8,128)} %copy-done.8, bf16[1024,2048]{1,0:T(8,128)(2,1)} %factors_ref.1), custom_call_target="tpu_custom_call" | custom-call | flops 2147483648 | bytes 4194304 | tf_op jit(solution)/shard_map/factor_products/pallas_call | solution.py:265
  47.4 0.1 collective-permute-start.5
  47.5 0.5 collective-permute-start.4
  48.0 1.8 %collective-permute-done.4 = f32[256,64]{1,0:T(8,128)S(1)} collective-permute-done((f32[256,64]{1,0:T(8,128)}, f32[256,64]{1,0:T(8,128)S(1)}, u32[]{:S(2)}, u32[]{:S(2)}) %collective-permute-start.4) | collective-permute-done | bytes 65568 | tf_op jit(solution)/shard_map/ppermute | solution.py:40
  49.8 0.9 add.67
  50.8 0.0 collective-permute-done.5.extra_pair_ref
  50.8 0.0 copy-start.9
  50.8 0.0 collective-permute-done.6.refs_0_
  50.8 0.0 collective-permute-done.7.refs_1_
  50.8 0.8 copy-done.9
  51.6 7.7 %pair_sum.1 = (f32[32,8192]{1,0:T(8,128)}, bf16[32,8192]{1,0:T(8,128)(2,1)}, bf16[32,8192]{1,0:T(8,128)(2,1)}, bf16[32,8192]{1,0:T(8,128)(2,1)}) custom-call(bf16[256,256]{1,0:T(8,128)(2,1)} %copy-done.2, f32[128,1024]{1,0:T(8,128)} %get-tuple-element.47.extra_ours_ref, f32[128,1024]{1,0:T(8,128)} %copy-done.9, bf16[8192,256]{1,0:T(8,128)(2,1)} %frozen_any.3, ...), custom_call_target="tpu_custom_call" | custom-call | flops 536870912 | bytes 10485760 | tf_op jit(solution)/shard_map/pair_sum/pallas_call | solution.py:311
  59.3 2.6 %collective-permute-start.13 = (f32[256,64]{1,0:T(8,128)S(1)}, f32[256,64]{1,0:T(8,128)S(1)}, u32[]{:S(2)}, u32[]{:S(2)}) collective-permute-start(f32[256,64]{1,0:T(8,128)S(1)} %add.67), channel_id=1, source_target_pairs={{0,6},{1,7},{2,4},{3,5},{4,2},{5,3},{6,0},{7,1},{8,14},{9,15},{10,... | collective-permute-start | bytes 196616 | tf_op jit(solution)/shard_map/ppermute | solution.py:40
  61.9 0.9 collective-permute-start.12
  62.8 0.7 collective-permute-start.11
  63.5 1.3 %collective-permute-start.8 = (bf16[32,8192]{1,0:T(8,128)(2,1)}, bf16[32,8192]{1,0:T(8,128)(2,1)S(1)}, u32[]{:S(2)}, u32[]{:S(2)}) collective-permute-start(bf16[32,8192]{1,0:T(8,128)(2,1)} %get-tuple-element.56), channel_id=1, source_target_pairs={{0,2},{1,3},{2,4},{3,5},{4,6},{5,7},{6,0},{7,1},{8,10},{9,11},{10,... | collective-permute-start | bytes 1572872 | tf_op jit(solution)/shard_map/ppermute | solution.py:389
  64.8 2.6 %collective-permute-start.9 = (bf16[32,8192]{1,0:T(8,128)(2,1)}, bf16[32,8192]{1,0:T(8,128)(2,1)S(1)}, u32[]{:S(2)}, u32[]{:S(2)}) collective-permute-start(bf16[32,8192]{1,0:T(8,128)(2,1)} %get-tuple-element.57), channel_id=1, source_target_pairs={{0,4},{1,5},{2,6},{3,7},{4,0},{5,1},{6,2},{7,3},{8,12},{9,13},{10,... | collective-permute-start | bytes 1572872 | tf_op jit(solution)/shard_map/ppermute | solution.py:389
  67.4 1.0 collective-permute-done.13
  68.4 3.3 %collective-permute-start.10 = (bf16[32,8192]{1,0:T(8,128)(2,1)}, bf16[32,8192]{1,0:T(8,128)(2,1)S(1)}, u32[]{:S(2)}, u32[]{:S(2)}) collective-permute-start(bf16[32,8192]{1,0:T(8,128)(2,1)} %get-tuple-element.58), channel_id=1, source_target_pairs={{0,6},{1,7},{2,0},{3,1},{4,2},{5,3},{6,4},{7,5},{8,14},{9,15},{10,... | collective-permute-start | bytes 1572872 | tf_op jit(solution)/shard_map/ppermute | solution.py:389
  71.7 0.0 collective-permute-done.12
  71.7 0.0 collective-permute-done.11
  71.7 1.0 convolution_convert_fusion
  72.7 0.3 all-to-all-done.1
  73.1 9.6 %all-to-all-start.2 = ((bf16[32,16,128]{2,1,0:T(8,128)(2,1)}), bf16[32,16,128]{2,1,0:T(8,128)(2,1)S(1)}, u32[]{:S(2)}, u32[]{:S(2)}) async-start(bf16[32,16,128]{2,1,0:T(8,128)(2,1)} %bitcast.6), calls=%async_computation.2 | async-start | bytes 262144 | tf_op jit(solution)/shard_map/all_to_all | solution.py:404
  82.6 0.0 collective-permute-done.8
  82.7 11.3 %collective-permute-done.9 = bf16[32,8192]{1,0:T(8,128)(2,1)S(1)} collective-permute-done((bf16[32,8192]{1,0:T(8,128)(2,1)}, bf16[32,8192]{1,0:T(8,128)(2,1)S(1)}, u32[]{:S(2)}, u32[]{:S(2)}) %collective-permute-start.9) | collective-permute-done | bytes 524320 | tf_op jit(solution)/shard_map/ppermute | solution.py:389
  93.9 2.3 %add_convert_fusion = bf16[32,8192]{1,0:T(8,128)(2,1)} fusion(bf16[32,8192]{1,0:T(8,128)(2,1)S(1)} %collective-permute-done.10, bf16[32,8192]{1,0:T(8,128)(2,1)S(1)} %collective-permute-done.9, f32[32,8192]{1,0:T(8,128)} %get-tuple-element.55, bf16[32,8192]{1,0:T(8,128)(2,1)S(1)} %collective-permute-done.8), kind=kLoop, calls=%fused_computation.3 | loop fusion | flops 1835008 | bytes 3145728 | tf_op jit(solution)/shard_map/convert_element_type | solution.py:393
  96.2 0.0 all-to-all-done.2
  96.2 1.8 %multiply_subtract_fusion.1 = (f32[64,256]{1,0:T(8,128)}, f32[64,256]{1,0:T(8,128)}, f32[64,256]{1,0:T(8,128)}) fusion(f32[64,256]{1,0:T(8,128)} %param.23, f32[64,256]{1,0:T(8,128)} %param.24, f32[64,256]{1,0:T(8,128)} %param.25, bf16[512,1280]{1,0:T(8,128)(2,1)S(1)} %bitcast.18, bf16[512,128]{1,0:T(8,128)(2,1)S(1)} %bitcast.21), kind=kOutput, calls=%fused_computation.20 | convolution fusion | flops 17039360 | bytes 786432 | tf_op jit(solution)/shard_map/dot_general | solution.py:34
  98.0 2.4 %multiply_subtract_fusion = (f32[1024,64]{0,1:T(8,128)}, f32[1024,64]{0,1:T(8,128)}, f32[1024,64]{0,1:T(8,128)}) fusion(f32[1024,64]{0,1:T(8,128)S(1)} %copy-done.11, f32[1024,64]{0,1:T(8,128)S(1)} %copy-done.12, f32[1024,64]{0,1:T(8,128)} %param.22, bf16[512,128]{1,0:T(8,128)(2,1)S(1)} %bitcast.22, bf16[512,1280]{1,0:T(8,128)(2,1)S(1)} %bitcast.19), kind=kOutput, calls=%fused_computation.8 | convolution fusion | flops 68157440 | bytes 2752512 | tf_op jit(solution)/shard_map/dot_general | solution.py:34
  (27 shorter events, 0.1 us)
Async XLA Ops:
  0.6 6.5 %copy-start.5 = (s32[32]{0:T(128)S(1)}, s32[32]{0:T(128)}, u32[]{:S(2)}) copy-start(s32[32]{0:T(128)} %live_ref.1) | copy-start | bytes 388
  0.6 6.5 %copy-start.7 = (s32[32]{0:T(128)S(1)}, s32[32]{0:T(128)}, u32[]{:S(2)}) copy-start(s32[32]{0:T(128)} %owner_ref.1) | copy-start | bytes 388
  0.7 6.5 %copy-start.6 = (s32[32]{0:T(128)S(1)}, s32[32]{0:T(128)}, u32[]{:S(2)}) copy-start(s32[32]{0:T(128)} %bucket_ref.1) | copy-start | bytes 388
  0.7 6.5 %copy-start.4 = (s32[256,1]{0,1:T(1,128)S(1)}, s32[256,1]{0,1:T(1,128)}, u32[]{:S(2)}) copy-start(s32[256,1]{0,1:T(1,128)} %param.26) | copy-start | bytes 3076
  0.7 6.5 %copy-start.1 = (bf16[2048,256]{1,0:T(8,128)(2,1)S(1)}, bf16[2048,256]{1,0:T(8,128)(2,1)}, u32[]{:S(2)}) copy-start(bf16[2048,256]{1,0:T(8,128)(2,1)} %up_ref.1) | copy-start | bytes 3145732
  0.7 6.5 %copy-start.3 = (bf16[256,256]{1,0:T(8,128)(2,1)S(1)}, bf16[256,256]{1,0:T(8,128)(2,1)}, u32[]{:S(2)}) copy-start(bf16[256,256]{1,0:T(8,128)(2,1)} %cot_ref.1) | copy-start | bytes 393220
  2.7 24.6 %all-to-all-start = ((bf16[8,32,1024]{2,1,0:T(8,128)(2,1)}), bf16[8,32,1024]{2,1,0:T(8,128)(2,1)S(1)}, u32[]{:S(2)}, u32[]{:S(2)}) async-start(bf16[8,32,1024]{2,1,0:T(8,128)(2,1)} %bitcast.13), calls=%async_computation | async-start | bytes 1048576 | tf_op jit(solution)/shard_map/all_to_all | solution.py:353
  8.3 0.7 copy-start.2
  9.0 0.7 copy-start.8
  9.6 6.7 %collective-permute-start = (f32[256,64]{1,0:T(8,128)S(1)}, f32[256,64]{1,0:T(8,128)S(1)}, u32[]{:S(2)}, u32[]{:S(2)}) collective-permute-start(f32[256,64]{1,0:T(8,128)S(1)} %get-tuple-element.36), channel_id=1, source_target_pairs={{0,1},{1,0},{2,3},{3,2},{4,5},{5,4},{6,7},{7,6},{8,9},{9,8},{10,11... | collective-permute-start | bytes 196616 | tf_op jit(solution)/shard_map/ppermute | solution.py:40
  16.4 9.0 %collective-permute-start.3 = (f32[256,64]{1,0:T(8,128)S(1)}, f32[256,64]{1,0:T(8,128)S(1)}, u32[]{:S(2)}, u32[]{:S(2)}) collective-permute-start(f32[256,64]{1,0:T(8,128)S(1)} %add.63), channel_id=1, source_target_pairs={{0,6},{1,7},{2,4},{3,5},{4,2},{5,3},{6,0},{7,1},{8,14},{9,15},{10,... | collective-permute-start | bytes 196616 | tf_op jit(solution)/shard_map/ppermute | solution.py:40
  19.4 7.9 %collective-permute-start.2 = (f32[256,64]{1,0:T(8,128)S(1)}, f32[256,64]{1,0:T(8,128)S(1)}, u32[]{:S(2)}, u32[]{:S(2)}) collective-permute-start(f32[256,64]{1,0:T(8,128)S(1)} %add.63), channel_id=1, source_target_pairs={{0,4},{1,5},{2,6},{3,7},{4,0},{5,1},{6,2},{7,3},{8,12},{9,13},{10,... | collective-permute-start | bytes 196616 | tf_op jit(solution)/shard_map/ppermute | solution.py:40
  20.2 7.0 %collective-permute-start.1 = (f32[256,64]{1,0:T(8,128)S(1)}, f32[256,64]{1,0:T(8,128)S(1)}, u32[]{:S(2)}, u32[]{:S(2)}) collective-permute-start(f32[256,64]{1,0:T(8,128)S(1)} %add.63), channel_id=1, source_target_pairs={{0,2},{1,3},{2,0},{3,1},{4,6},{5,7},{6,4},{7,5},{8,10},{9,11},{10,... | collective-permute-start | bytes 196616 | tf_op jit(solution)/shard_map/ppermute | solution.py:40
  20.6 30.2 %collective-permute-start.6 = (f32[128,4096]{1,0:T(8,128)}, f32[128,4096]{1,0:T(8,128)}, u32[]{:S(2)}, u32[]{:S(2)}) collective-permute-start(f32[128,4096]{1,0:T(8,128)} %get-tuple-element.49), channel_id=1, source_target_pairs={{0,1},{1,0},{2,3},{3,2},{4,5},{5,4},{6,7},{7,6},{8,9},{9,8},{10,11... | collective-permute-start | bytes 6291464 | tf_op jit(solution)/shard_map/ppermute | solution.py:40
  20.6 30.2 %collective-permute-start.7 = (f32[128,4096]{1,0:T(8,128)}, f32[128,4096]{1,0:T(8,128)}, u32[]{:S(2)}, u32[]{:S(2)}) collective-permute-start(f32[128,4096]{1,0:T(8,128)} %get-tuple-element.50), channel_id=1, source_target_pairs={{0,1},{1,0},{2,3},{3,2},{4,5},{5,4},{6,7},{7,6},{8,9},{9,8},{10,11... | collective-permute-start | bytes 6291464 | tf_op jit(solution)/shard_map/ppermute | solution.py:40
  27.3 1.6 %copy-start = (bf16[8,32,1024]{2,1,0:T(8,128)(2,1)}, bf16[8,32,1024]{2,1,0:T(8,128)(2,1)S(1)}, u32[]{:S(2)}) copy-start(bf16[8,32,1024]{2,1,0:T(8,128)(2,1)S(1)} %all-to-all-done) | copy-start | bytes 1572868
  28.9 44.2 %all-to-all-start.1 = ((bf16[32,16,1280]{2,1,0:T(8,128)(2,1)}), bf16[32,16,1280]{2,1,0:T(8,128)(2,1)S(1)}, u32[]{:S(2)}, u32[]{:S(2)}) async-start(bf16[32,16,1280]{2,1,0:T(8,128)(2,1)} %bitcast.3), calls=%async_computation.1 | async-start | bytes 2621440 | tf_op jit(solution)/shard_map/all_to_all | solution.py:374
  47.4 3.3 %collective-permute-start.5 = (f32[128,1024]{1,0:T(8,128)}, f32[128,1024]{1,0:T(8,128)S(1)}, u32[]{:S(2)}, u32[]{:S(2)}) collective-permute-start(f32[128,1024]{1,0:T(8,128)} %get-tuple-element.48), channel_id=1, source_target_pairs={{0,1},{1,0},{2,3},{3,2},{4,5},{5,4},{6,7},{7,6},{8,9},{9,8},{10,11... | collective-permute-start | bytes 1572872 | tf_op jit(solution)/shard_map/ppermute | solution.py:40
  47.5 2.3 %collective-permute-start.4 = (f32[256,64]{1,0:T(8,128)}, f32[256,64]{1,0:T(8,128)S(1)}, u32[]{:S(2)}, u32[]{:S(2)}) collective-permute-start(f32[256,64]{1,0:T(8,128)} %get-tuple-element.46), channel_id=1, source_target_pairs={{0,1},{1,0},{2,3},{3,2},{4,5},{5,4},{6,7},{7,6},{8,9},{9,8},{10,11... | collective-permute-start | bytes 196616 | tf_op jit(solution)/shard_map/ppermute | solution.py:40
  50.8 0.8 copy-start.9
  51.6 20.2 %copy-start.10 = (bf16[256,64]{1,0:T(8,128)(2,1)S(1)}, bf16[256,64]{1,0:T(8,128)(2,1)}, u32[]{:S(2)}) copy-start(bf16[256,64]{1,0:T(8,128)(2,1)} %multiply_convert_fusion.1.weight_ref) | copy-start | bytes 98308
  59.3 9.1 %collective-permute-start.13 = (f32[256,64]{1,0:T(8,128)S(1)}, f32[256,64]{1,0:T(8,128)S(1)}, u32[]{:S(2)}, u32[]{:S(2)}) collective-permute-start(f32[256,64]{1,0:T(8,128)S(1)} %add.67), channel_id=1, source_target_pairs={{0,6},{1,7},{2,4},{3,5},{4,2},{5,3},{6,0},{7,1},{8,14},{9,15},{10,... | collective-permute-start | bytes 196616 | tf_op jit(solution)/shard_map/ppermute | solution.py:40
  61.9 9.8 %collective-permute-start.12 = (f32[256,64]{1,0:T(8,128)S(1)}, f32[256,64]{1,0:T(8,128)S(1)}, u32[]{:S(2)}, u32[]{:S(2)}) collective-permute-start(f32[256,64]{1,0:T(8,128)S(1)} %add.67), channel_id=1, source_target_pairs={{0,4},{1,5},{2,6},{3,7},{4,0},{5,1},{6,2},{7,3},{8,12},{9,13},{10,... | collective-permute-start | bytes 196616 | tf_op jit(solution)/shard_map/ppermute | solution.py:40
  62.8 8.9 %collective-permute-start.11 = (f32[256,64]{1,0:T(8,128)S(1)}, f32[256,64]{1,0:T(8,128)S(1)}, u32[]{:S(2)}, u32[]{:S(2)}) collective-permute-start(f32[256,64]{1,0:T(8,128)S(1)} %add.67), channel_id=1, source_target_pairs={{0,2},{1,3},{2,0},{3,1},{4,6},{5,7},{6,4},{7,5},{8,10},{9,11},{10,... | collective-permute-start | bytes 196616 | tf_op jit(solution)/shard_map/ppermute | solution.py:40
  63.5 19.2 %collective-permute-start.8 = (bf16[32,8192]{1,0:T(8,128)(2,1)}, bf16[32,8192]{1,0:T(8,128)(2,1)S(1)}, u32[]{:S(2)}, u32[]{:S(2)}) collective-permute-start(bf16[32,8192]{1,0:T(8,128)(2,1)} %get-tuple-element.56), channel_id=1, source_target_pairs={{0,2},{1,3},{2,4},{3,5},{4,6},{5,7},{6,0},{7,1},{8,10},{9,11},{10,... | collective-permute-start | bytes 1572872 | tf_op jit(solution)/shard_map/ppermute | solution.py:389
  64.8 29.2 %collective-permute-start.9 = (bf16[32,8192]{1,0:T(8,128)(2,1)}, bf16[32,8192]{1,0:T(8,128)(2,1)S(1)}, u32[]{:S(2)}, u32[]{:S(2)}) collective-permute-start(bf16[32,8192]{1,0:T(8,128)(2,1)} %get-tuple-element.57), channel_id=1, source_target_pairs={{0,4},{1,5},{2,6},{3,7},{4,0},{5,1},{6,2},{7,3},{8,12},{9,13},{10,... | collective-permute-start | bytes 1572872 | tf_op jit(solution)/shard_map/ppermute | solution.py:389
  68.4 25.6 %collective-permute-start.10 = (bf16[32,8192]{1,0:T(8,128)(2,1)}, bf16[32,8192]{1,0:T(8,128)(2,1)S(1)}, u32[]{:S(2)}, u32[]{:S(2)}) collective-permute-start(bf16[32,8192]{1,0:T(8,128)(2,1)} %get-tuple-element.58), channel_id=1, source_target_pairs={{0,6},{1,7},{2,0},{3,1},{4,2},{5,3},{6,4},{7,5},{8,14},{9,15},{10,... | collective-permute-start | bytes 1572872 | tf_op jit(solution)/shard_map/ppermute | solution.py:389
  73.1 25.0 %copy-start.11 = (f32[1024,64]{0,1:T(8,128)S(1)}, f32[1024,64]{0,1:T(8,128)}, u32[]{:S(2)}) copy-start(f32[1024,64]{0,1:T(8,128)} %param.20) | copy-start | bytes 786436
  73.1 25.0 %copy-start.12 = (f32[1024,64]{0,1:T(8,128)S(1)}, f32[1024,64]{0,1:T(8,128)}, u32[]{:S(2)}) copy-start(f32[1024,64]{0,1:T(8,128)} %param.21) | copy-start | bytes 786436
  73.1 23.2 %all-to-all-start.2 = ((bf16[32,16,128]{2,1,0:T(8,128)(2,1)}), bf16[32,16,128]{2,1,0:T(8,128)(2,1)S(1)}, u32[]{:S(2)}, u32[]{:S(2)}) async-start(bf16[32,16,128]{2,1,0:T(8,128)(2,1)} %bitcast.6), calls=%async_computation.2 | async-start | bytes 262144 | tf_op jit(solution)/shard_map/all_to_all | solution.py:404

commit v5 on v4

--- a/solution.py
+++ b/solution.py
@@ -47,7 +47,8 @@
 
 
 VMEM_LIMIT = 16 * 1024 * 1024
-VMEM_MOST = 57 * 1024 * 1024
+VMEM_MOST = 60 * 1024 * 1024
+VMEM_PAIR = 57 * 1024 * 1024
 SMEM_SPEC = pl.BlockSpec(memory_space=pltpu.MemorySpace.SMEM)
 HBM = pltpu.MemorySpace.HBM
 NT = (((1,), (1,)), ((), ()))
@@ -72,14 +73,20 @@
     return (lax.broadcasted_iota(jnp.int32, shape, 1) // PADDED_RANK + first).astype(jnp.float32)
 
 
-def fetch(sources, targets, sems):
-    copies = [
-        pltpu.make_async_copy(source, target, sems.at[i])
-        for i, (source, target) in enumerate(zip(sources, targets, strict=True))
-    ]
-    for copy in copies:
-        copy.start()
-    return copies
+class Stream:
+    def __init__(self, sources, targets, sems, depth=3):
+        self.copies = [
+            pltpu.make_async_copy(source, target, sems.at[i])
+            for i, (source, target) in enumerate(zip(sources, targets, strict=True))
+        ]
+        self.depth = depth
+        for copy in self.copies[:depth]:
+            copy.start()
+
+    def wait(self, c):
+        self.copies[c].wait()
+        if c + self.depth < len(self.copies):
+            self.copies[c + self.depth].start()
 
 
 def row_parts(ref, parts):
@@ -167,10 +174,10 @@
     half = outs[0].shape[0]
     chunk = frozen_ref.shape[0] // steps
     per_part = steps // len(outs)
-    copies = fetch(row_parts(frozen_any, steps), row_parts(frozen_ref, steps), sems)
+    stream = Stream(row_parts(frozen_any, steps), row_parts(frozen_ref, steps), sems)
     theirs = turned_ref[half:, :]
     for c in range(steps):
-        copies[c].wait()
+        stream.wait(c)
         first = c % per_part * chunk
         outs[c // per_part][:, first : first + chunk] = dot(
             theirs, frozen_ref[c * chunk : (c + 1) * chunk, :], NT
@@ -220,20 +227,17 @@
     parts, columns, chunk = held_ref.shape
     tokens = hidden_ref.shape[0]
     n_chip = tokens // rows_own // 2
-    copies = [
-        pltpu.make_async_copy(
-            factors_ref.at[:, pl.ds(c * chunk, chunk)], held_ref.at[c], sems.at[c]
-        )
-        for c in range(parts)
-    ]
-    for copy in copies:
-        copy.start()
+    stream = Stream(
+        [factors_ref.at[:, pl.ds(c * chunk, chunk)] for c in range(parts)],
+        [held_ref.at[c] for c in range(parts)],
+        sems,
+    )
     slot = slot_ref[...]
     weight = weight_ref[...].astype(jnp.float32)
     double = jnp.concatenate([weight, weight], axis=1)
     acc = jnp.zeros((tokens, 128), jnp.float32)
     for c in range(parts):
-        copies[c].wait()
+        stream.wait(c)
         factors = held_ref[c]
         product = dot(hidden_ref[...], factors, NN)
         pieces = []
@@ -284,14 +288,14 @@
     steps = sems.shape[0]
     half, columns = extra_ours_ref.shape
     per_part = steps // parts
-    copies = fetch(row_parts(frozen_any, steps), row_parts(frozen_ref, steps), sems)
+    stream = Stream(row_parts(frozen_any, steps), row_parts(frozen_ref, steps), sems)
     position = lax.axis_index("tensor")
     chip, core = position // 2, position % 2
     ours = turned_ref[:half, :]
     low = jnp.where(core == 0, extra_ours_ref[...], extra_pair_ref[...])
     high = jnp.where(core == 0, extra_pair_ref[...], extra_ours_ref[...])
     for c in range(steps):
-        copies[c].wait()
+        stream.wait(c)
         at = slice(c * columns, (c + 1) * columns)
         first = c % per_part * columns
         total = dot(ours, frozen_ref[at, :], NT)
@@ -313,7 +317,7 @@
         (jax.ShapeDtypeStruct((rows_own, width), jnp.float32),) + (sent,) * n_out,
         2 * half * width * kv,
         2 * kv * width + 6 * half * width,
-        VMEM_MOST,
+        VMEM_PAIR,
         in_specs=[pl.BlockSpec(v.shape) for v in (turned, extra_ours, extra_pair)]
         + [pl.BlockSpec(memory_space=HBM)]
         + [pl.BlockSpec(v.shape) for v in from_pair],
@@ -370,7 +374,6 @@
     up_sum = sum_over_chips(up_own, n_tensor)
 
     packed = pack_rows(place, hidden_columns, masked, n_slot * CAP)
-    packed, up_sum = lax.optimization_barrier((packed, up_sum))
     owned = lax.all_to_all(
         packed.reshape(n_slot, CAP, -1), "dp", 0, 0, tiled=True
     ).reshape(n_slot * CAP, -1)

time: 101 us -> 99.1 us (0.981); the launches traced: 100 us -> 97.3 us
  starting transfers between devices: 42.4 us -> 40 us
    ppermute x3, starting transfers between devices: 7.25 us -> 5.2 us  [local(): lax.ppermute(sent[step - 1], 'tensor', [(i, (i + 2 * step) % n_tensor) fo...]
    unnamed x26 -> x32, local copies, waits for them, and re-layouts: 2.11 us -> 1.48 us
  transfers between devices with their start and end apart: 17 -> 17, of which waited for: 6 -> 8; matrix products, arithmetic and copies ran while one was open for 5% -> 5% of each run, Pallas kernels for 23% -> 25%
where the time goes in v5:
time: 99.1 us; the launch traced here: 97.3 us
  starting transfers between devices  40 us (40%)
  Pallas kernels  24.1 us (24%)
  waiting for transfers between devices  20.6 us (21%)
  matrix products  4.32 us (4%)
  other arithmetic  3.93 us (4%)
  local copies, waits for them, and re-layouts  3.45 us (3%)
    all_to_all x1, starting transfers between devices, local(): lax.all_to_all(packed.reshape(n_slot, CAP, -1), 'dp', 0, 0, tiled=True)  11.2 us
    ppermute x3, waiting for transfers between devices, local(): lax.ppermute(sent[step - 1], 'tensor', [(i, (i + 2 * step) % n_tensor) fo...  11 us
    all_to_all x1, starting transfers between devices, local(): lax.all_to_all(packed_weights.reshape(n_slot, CAP, -1), 'dp', 0, 0, tiled...  9.79 us
    ppermute x11, starting transfers between devices, swap(): return lax.ppermute(value, 'tensor', [(i, i ^ mask) for i in range(count)])  9.35 us
    ppermute x11, waiting for transfers between devices, swap(): return lax.ppermute(value, 'tensor', [(i, i ^ mask) for i in range(count)])  8.87 us
    pallas_call x1, Pallas kernels, pair_sum(): call(functools.partial(pair_kernel, rows_own, parts), (jax.ShapeDtypeStru...  8.06 us
    pallas_call x1, Pallas kernels, factor_products(): call(functools.partial(factors_kernel, rows_own), shapes, 4 * tokens * fa...  6.7 us
    pallas_call x1, Pallas kernels, frozen_term(): call(frozen_kernel, (jax.ShapeDtypeStruct((tokens // 2, width // parts),...  6.62 us
  transfers between devices with their start and end apart: 17, of which 8 were waited for; matrix products, arithmetic and copies ran while one was open for 5% of the time, Pallas kernels for 25%

profile of v5, /device:TPU:32, one launch (start us, length us, event | category | flops | bytes accessed | tf_op | source)
XLA Modules:
  0.0 97.3 jit_solution(4695901630204239969)
XLA Ops:
  0.7 2.0 %copy.25 = bf16[4,8,8,1024]{3,2,0,1:T(8,128)(2,1)} copy(bf16[4,8,8,1024]{3,2,1,0:T(8,128)(2,1)} %bitcast.20) | data formatting | bytes 1048576 | tf_op jit(solution)/shard_map/reshape | solution.py:356
  2.7 4.5 %all-to-all-start = ((bf16[8,32,1024]{2,1,0:T(8,128)(2,1)}), bf16[8,32,1024]{2,1,0:T(8,128)(2,1)S(1)}, u32[]{:S(2)}, u32[]{:S(2)}) async-start(bf16[8,32,1024]{2,1,0:T(8,128)(2,1)} %bitcast.13), calls=%async_computation | async-start | bytes 1048576 | tf_op jit(solution)/shard_map/all_to_all | solution.py:357
  7.2 1.1 %prep.1 = (bf16[256,256]{1,0:T(8,128)(2,1)S(1)}, bf16[256,256]{1,0:T(8,128)(2,1)S(1)}, f32[256,128]{1,0:T(8,128)S(1)}, f32[256,128]{1,0:T(8,128)S(1)}, s32[1,256]{1,0:T(1,128)S(1)}, /*index=5*/f32[256,64]{1,0:T(8,128)S(1)}) custom-call(s32[32]{0:T(128)S(1)} %copy-done.5, s32[32]{0:T(128)S(1)} %copy-done.6, s32[32]{0:T(128)S(1)} %copy-done.7, ...), custom_call_target="tpu_custom_call" | custom-call | flops 268435456 | bytes 1048576 | tf_op jit(solution)/shard_map/prep/pallas_call | solution.py:160
  8.3 0.0 copy-start.2
  8.3 0.6 copy-done.2
  9.0 0.5 collective-permute-start
  9.5 6.6 %frozen_term.1 = (f32[128,4096]{1,0:T(8,128)}, f32[128,4096]{1,0:T(8,128)}) custom-call(bf16[256,256]{1,0:T(8,128)(2,1)} %copy-done.2, bf16[8192,256]{1,0:T(8,128)(2,1)} %frozen_any.3), custom_call_target="tpu_custom_call" | custom-call | flops 536870912 | bytes 8388608 | tf_op jit(solution)/shard_map/frozen_term/pallas_call | solution.py:190
  16.1 0.0 collective-permute-done
  16.1 0.1 collective-permute-start.6
  16.3 0.4 collective-permute-start.7
  16.7 0.7 all-to-all-done
  17.5 1.6 %pack.1 = bf16[512,1280]{1,0:T(8,128)(2,1)} custom-call(s32[1,256]{1,0:T(1,128)S(1)} %get-tuple-element.54.place_ref, bf16[256,1024]{1,0:T(8,128)(2,1)S(1)} %bitcast.14, bf16[256,256]{1,0:T(8,128)(2,1)S(1)} %get-tuple-element.55.masked_ref), custom_call_target="tpu_custom_call" | custom-call | flops 335544320 | bytes 1966080 | tf_op jit(solution)/shard_map/pack/pallas_call | solution.py:216
  19.1 11.2 %all-to-all-start.1 = ((bf16[32,16,1280]{2,1,0:T(8,128)(2,1)}), bf16[32,16,1280]{2,1,0:T(8,128)(2,1)S(1)}, u32[]{:S(2)}, u32[]{:S(2)}) async-start(bf16[32,16,1280]{2,1,0:T(8,128)(2,1)} %bitcast.3), calls=%async_computation.1 | async-start | bytes 2621440 | tf_op jit(solution)/shard_map/all_to_all | solution.py:377
  30.3 2.5 %collective-permute-start.2 = (f32[256,64]{1,0:T(8,128)S(1)}, f32[256,64]{1,0:T(8,128)S(1)}, u32[]{:S(2)}, u32[]{:S(2)}) collective-permute-start(f32[256,64]{1,0:T(8,128)S(1)} %add.63), channel_id=1, source_target_pairs={{0,4},{1,5},{2,6},{3,7},{4,0},{5,1},{6,2},{7,3},{8,12},{9,13},{10,... | collective-permute-start | bytes 196616 | tf_op jit(solution)/shard_map/ppermute | solution.py:40
  32.8 1.2 %collective-permute-start.3 = (f32[256,64]{1,0:T(8,128)S(1)}, f32[256,64]{1,0:T(8,128)S(1)}, u32[]{:S(2)}, u32[]{:S(2)}) collective-permute-start(f32[256,64]{1,0:T(8,128)S(1)} %add.63), channel_id=1, source_target_pairs={{0,6},{1,7},{2,4},{3,5},{4,2},{5,3},{6,0},{7,1},{8,14},{9,15},{10,... | collective-permute-start | bytes 196616 | tf_op jit(solution)/shard_map/ppermute | solution.py:40
  34.0 0.0 collective-permute-start.1
  34.0 2.9 %collective-permute-done.2 = f32[256,64]{1,0:T(8,128)S(1)} collective-permute-done((f32[256,64]{1,0:T(8,128)S(1)}, f32[256,64]{1,0:T(8,128)S(1)}, u32[]{:S(2)}, u32[]{:S(2)}) %collective-permute-start.2) | collective-permute-done | bytes 65568 | tf_op jit(solution)/shard_map/ppermute | solution.py:40
  36.9 2.7 %collective-permute-done.3 = f32[256,64]{1,0:T(8,128)S(1)} collective-permute-done((f32[256,64]{1,0:T(8,128)S(1)}, f32[256,64]{1,0:T(8,128)S(1)}, u32[]{:S(2)}, u32[]{:S(2)}) %collective-permute-start.3) | collective-permute-done | bytes 65568 | tf_op jit(solution)/shard_map/ppermute | solution.py:40
  39.6 0.0 collective-permute-done.1
  39.6 0.7 multiply_convert_fusion.1.weight_ref
  40.3 6.7 %factor_products.1 = (f32[256,64]{1,0:T(8,128)}, f32[128,1024]{1,0:T(8,128)}, f32[128,1024]{1,0:T(8,128)}) custom-call(bf16[256,1024]{1,0:T(8,128)(2,1)} %bitcast.15, bf16[256,64]{1,0:T(8,128)(2,1)} %multiply_convert_fusion.1.weight_ref, f32[256,128]{1,0:T(8,128)} %copy-done.8, bf16[1024,2048]{1,0:T(8,128)(2,1)} %factors_ref.1), custom_call_target="tpu_custom_call" | custom-call | flops 2147483648 | bytes 4194304 | tf_op jit(solution)/shard_map/factor_products/pallas_call | solution.py:269
  47.0 0.1 collective-permute-start.5
  47.1 0.5 collective-permute-start.4
  47.6 1.8 %collective-permute-done.4 = f32[256,64]{1,0:T(8,128)S(1)} collective-permute-done((f32[256,64]{1,0:T(8,128)}, f32[256,64]{1,0:T(8,128)S(1)}, u32[]{:S(2)}, u32[]{:S(2)}) %collective-permute-start.4) | collective-permute-done | bytes 65568 | tf_op jit(solution)/shard_map/ppermute | solution.py:40
  49.4 0.9 add.67
  50.4 0.0 copy-start.9
  50.4 0.0 collective-permute-done.6.refs_0_
  50.4 0.8 copy-done.9
  51.2 8.1 %pair_sum.1 = (f32[32,8192]{1,0:T(8,128)}, bf16[32,8192]{1,0:T(8,128)(2,1)}, bf16[32,8192]{1,0:T(8,128)(2,1)}, bf16[32,8192]{1,0:T(8,128)(2,1)}) custom-call(bf16[256,256]{1,0:T(8,128)(2,1)} %copy-done.2, f32[128,1024]{1,0:T(8,128)} %get-tuple-element.42.extra_ours_ref, f32[128,1024]{1,0:T(8,128)} %copy-done.9, bf16[8192,256]{1,0:T(8,128)(2,1)} %frozen_any.3, ...), custom_call_target="tpu_custom_call" | custom-call | flops 536870912 | bytes 10485760 | tf_op jit(solution)/shard_map/pair_sum/pallas_call | solution.py:315
  59.2 0.0 copy-start.11
  59.2 0.0 copy-start.12
  59.3 1.9 %collective-permute-start.12 = (f32[256,64]{1,0:T(8,128)S(1)}, f32[256,64]{1,0:T(8,128)S(1)}, u32[]{:S(2)}, u32[]{:S(2)}) collective-permute-start(f32[256,64]{1,0:T(8,128)S(1)} %add.67), channel_id=1, source_target_pairs={{0,4},{1,5},{2,6},{3,7},{4,0},{5,1},{6,2},{7,3},{8,12},{9,13},{10,... | collective-permute-start | bytes 196616 | tf_op jit(solution)/shard_map/ppermute | solution.py:40
  61.1 2.1 %collective-permute-start.13 = (f32[256,64]{1,0:T(8,128)S(1)}, f32[256,64]{1,0:T(8,128)S(1)}, u32[]{:S(2)}, u32[]{:S(2)}) collective-permute-start(f32[256,64]{1,0:T(8,128)S(1)} %add.67), channel_id=1, source_target_pairs={{0,6},{1,7},{2,4},{3,5},{4,2},{5,3},{6,0},{7,1},{8,14},{9,15},{10,... | collective-permute-start | bytes 196616 | tf_op jit(solution)/shard_map/ppermute | solution.py:40
  63.2 0.0 collective-permute-start.11
  63.2 2.0 %collective-permute-start.10 = (bf16[32,8192]{1,0:T(8,128)(2,1)}, bf16[32,8192]{1,0:T(8,128)(2,1)S(1)}, u32[]{:S(2)}, u32[]{:S(2)}) collective-permute-start(bf16[32,8192]{1,0:T(8,128)(2,1)} %get-tuple-element.53), channel_id=1, source_target_pairs={{0,6},{1,7},{2,0},{3,1},{4,2},{5,3},{6,4},{7,5},{8,14},{9,15},{10,... | collective-permute-start | bytes 1572872 | tf_op jit(solution)/shard_map/ppermute | solution.py:392
  65.2 2.1 %collective-permute-start.9 = (bf16[32,8192]{1,0:T(8,128)(2,1)}, bf16[32,8192]{1,0:T(8,128)(2,1)S(1)}, u32[]{:S(2)}, u32[]{:S(2)}) collective-permute-start(bf16[32,8192]{1,0:T(8,128)(2,1)} %get-tuple-element.52), channel_id=1, source_target_pairs={{0,4},{1,5},{2,6},{3,7},{4,0},{5,1},{6,2},{7,3},{8,12},{9,13},{10,... | collective-permute-start | bytes 1572872 | tf_op jit(solution)/shard_map/ppermute | solution.py:392
  67.3 0.0 collective-permute-done.12
  67.3 1.1 %collective-permute-start.8 = (bf16[32,8192]{1,0:T(8,128)(2,1)}, bf16[32,8192]{1,0:T(8,128)(2,1)S(1)}, u32[]{:S(2)}, u32[]{:S(2)}) collective-permute-start(bf16[32,8192]{1,0:T(8,128)(2,1)} %get-tuple-element.51), channel_id=1, source_target_pairs={{0,2},{1,3},{2,4},{3,5},{4,6},{5,7},{6,0},{7,1},{8,10},{9,11},{10,... | collective-permute-start | bytes 1572872 | tf_op jit(solution)/shard_map/ppermute | solution.py:392
  68.4 1.4 %collective-permute-done.13 = f32[256,64]{1,0:T(8,128)S(1)} collective-permute-done((f32[256,64]{1,0:T(8,128)S(1)}, f32[256,64]{1,0:T(8,128)S(1)}, u32[]{:S(2)}, u32[]{:S(2)}) %collective-permute-start.13) | collective-permute-done | bytes 65568 | tf_op jit(solution)/shard_map/ppermute | solution.py:40
  69.8 0.0 collective-permute-done.11
  69.9 1.0 convolution_convert_fusion
  70.9 9.8 %all-to-all-start.2 = ((bf16[32,16,128]{2,1,0:T(8,128)(2,1)}), bf16[32,16,128]{2,1,0:T(8,128)(2,1)S(1)}, u32[]{:S(2)}, u32[]{:S(2)}) async-start(bf16[32,16,128]{2,1,0:T(8,128)(2,1)} %bitcast.6), calls=%async_computation.2 | async-start | bytes 262144 | tf_op jit(solution)/shard_map/all_to_all | solution.py:407
  80.7 0.2 collective-permute-done.10
  80.9 1.0 collective-permute-done.9
  81.8 9.8 %collective-permute-done.8 = bf16[32,8192]{1,0:T(8,128)(2,1)S(1)} collective-permute-done((bf16[32,8192]{1,0:T(8,128)(2,1)}, bf16[32,8192]{1,0:T(8,128)(2,1)S(1)}, u32[]{:S(2)}, u32[]{:S(2)}) %collective-permute-start.8) | collective-permute-done | bytes 524320 | tf_op jit(solution)/shard_map/ppermute | solution.py:392
  91.7 2.3 %add_convert_fusion = bf16[32,8192]{1,0:T(8,128)(2,1)} fusion(bf16[32,8192]{1,0:T(8,128)(2,1)S(1)} %collective-permute-done.10, bf16[32,8192]{1,0:T(8,128)(2,1)S(1)} %collective-permute-done.9, f32[32,8192]{1,0:T(8,128)} %get-tuple-element.50, bf16[32,8192]{1,0:T(8,128)(2,1)S(1)} %collective-permute-done.8), kind=kLoop, calls=%fused_computation.3 | loop fusion | flops 1835008 | bytes 3145728 | tf_op jit(solution)/shard_map/convert_element_type | solution.py:396
  94.0 2.4 %multiply_subtract_fusion = (f32[1024,64]{0,1:T(8,128)}, f32[1024,64]{0,1:T(8,128)}, f32[1024,64]{0,1:T(8,128)}) fusion(f32[1024,64]{0,1:T(8,128)S(1)} %copy-done.11, f32[1024,64]{0,1:T(8,128)S(1)} %copy-done.12, f32[1024,64]{0,1:T(8,128)} %param.22, bf16[512,128]{1,0:T(8,128)(2,1)S(1)} %bitcast.21, bf16[512,1280]{1,0:T(8,128)(2,1)S(1)} %bitcast.18), kind=kOutput, calls=%fused_computation.8 | convolution fusion | flops 68157440 | bytes 2752512 | tf_op jit(solution)/shard_map/dot_general | solution.py:34
  96.4 0.9 multiply_subtract_fusion.1
  (32 shorter events, 0.1 us)
Async XLA Ops:
  0.6 6.5 %copy-start.5 = (s32[32]{0:T(128)S(1)}, s32[32]{0:T(128)}, u32[]{:S(2)}) copy-start(s32[32]{0:T(128)} %live_ref.1) | copy-start | bytes 388
  0.6 6.5 %copy-start.6 = (s32[32]{0:T(128)S(1)}, s32[32]{0:T(128)}, u32[]{:S(2)}) copy-start(s32[32]{0:T(128)} %bucket_ref.1) | copy-start | bytes 388
  0.7 6.5 %copy-start.7 = (s32[32]{0:T(128)S(1)}, s32[32]{0:T(128)}, u32[]{:S(2)}) copy-start(s32[32]{0:T(128)} %owner_ref.1) | copy-start | bytes 388
  0.7 6.5 %copy-start.4 = (s32[256,1]{0,1:T(1,128)S(1)}, s32[256,1]{0,1:T(1,128)}, u32[]{:S(2)}) copy-start(s32[256,1]{0,1:T(1,128)} %param.26) | copy-start | bytes 3076
  0.7 6.5 %copy-start.3 = (bf16[256,256]{1,0:T(8,128)(2,1)S(1)}, bf16[256,256]{1,0:T(8,128)(2,1)}, u32[]{:S(2)}) copy-start(bf16[256,256]{1,0:T(8,128)(2,1)} %cot_ref.1) | copy-start | bytes 393220
  0.7 6.5 %copy-start.1 = (bf16[2048,256]{1,0:T(8,128)(2,1)S(1)}, bf16[2048,256]{1,0:T(8,128)(2,1)}, u32[]{:S(2)}) copy-start(bf16[2048,256]{1,0:T(8,128)(2,1)} %up_ref.1) | copy-start | bytes 3145732
  2.7 14.8 %all-to-all-start = ((bf16[8,32,1024]{2,1,0:T(8,128)(2,1)}), bf16[8,32,1024]{2,1,0:T(8,128)(2,1)S(1)}, u32[]{:S(2)}, u32[]{:S(2)}) async-start(bf16[8,32,1024]{2,1,0:T(8,128)(2,1)} %bitcast.13), calls=%async_computation | async-start | bytes 1048576 | tf_op jit(solution)/shard_map/all_to_all | solution.py:357
  8.3 0.7 copy-start.2
  9.0 7.1 %copy-start.8 = (f32[256,128]{1,0:T(8,128)}, f32[256,128]{1,0:T(8,128)S(1)}, u32[]{:S(2)}) copy-start(f32[256,128]{1,0:T(8,128)S(1)} %get-tuple-element.40.slot_ref) | copy-start | bytes 393220
  9.0 7.1 %collective-permute-start = (f32[256,64]{1,0:T(8,128)S(1)}, f32[256,64]{1,0:T(8,128)S(1)}, u32[]{:S(2)}, u32[]{:S(2)}) collective-permute-start(f32[256,64]{1,0:T(8,128)S(1)} %get-tuple-element.34), channel_id=1, source_target_pairs={{0,1},{1,0},{2,3},{3,2},{4,5},{5,4},{6,7},{7,6},{8,9},{9,8},{10,11... | collective-permute-start | bytes 196616 | tf_op jit(solution)/shard_map/ppermute | solution.py:40
  16.1 34.2 %collective-permute-start.6 = (f32[128,4096]{1,0:T(8,128)}, f32[128,4096]{1,0:T(8,128)}, u32[]{:S(2)}, u32[]{:S(2)}) collective-permute-start(f32[128,4096]{1,0:T(8,128)} %get-tuple-element.44), channel_id=1, source_target_pairs={{0,1},{1,0},{2,3},{3,2},{4,5},{5,4},{6,7},{7,6},{8,9},{9,8},{10,11... | collective-permute-start | bytes 6291464 | tf_op jit(solution)/shard_map/ppermute | solution.py:40
  16.3 34.1 %collective-permute-start.7 = (f32[128,4096]{1,0:T(8,128)}, f32[128,4096]{1,0:T(8,128)}, u32[]{:S(2)}, u32[]{:S(2)}) collective-permute-start(f32[128,4096]{1,0:T(8,128)} %get-tuple-element.45), channel_id=1, source_target_pairs={{0,1},{1,0},{2,3},{3,2},{4,5},{5,4},{6,7},{7,6},{8,9},{9,8},{10,11... | collective-permute-start | bytes 6291464 | tf_op jit(solution)/shard_map/ppermute | solution.py:40
  17.5 1.6 %copy-start = (bf16[8,32,1024]{2,1,0:T(8,128)(2,1)}, bf16[8,32,1024]{2,1,0:T(8,128)(2,1)S(1)}, u32[]{:S(2)}) copy-start(bf16[8,32,1024]{2,1,0:T(8,128)(2,1)S(1)} %all-to-all-done) | copy-start | bytes 1572868
  19.1 51.8 %all-to-all-start.1 = ((bf16[32,16,1280]{2,1,0:T(8,128)(2,1)}), bf16[32,16,1280]{2,1,0:T(8,128)(2,1)S(1)}, u32[]{:S(2)}, u32[]{:S(2)}) async-start(bf16[32,16,1280]{2,1,0:T(8,128)(2,1)} %bitcast.3), calls=%async_computation.1 | async-start | bytes 2621440 | tf_op jit(solution)/shard_map/all_to_all | solution.py:377
  30.3 6.6 %collective-permute-start.2 = (f32[256,64]{1,0:T(8,128)S(1)}, f32[256,64]{1,0:T(8,128)S(1)}, u32[]{:S(2)}, u32[]{:S(2)}) collective-permute-start(f32[256,64]{1,0:T(8,128)S(1)} %add.63), channel_id=1, source_target_pairs={{0,4},{1,5},{2,6},{3,7},{4,0},{5,1},{6,2},{7,3},{8,12},{9,13},{10,... | collective-permute-start | bytes 196616 | tf_op jit(solution)/shard_map/ppermute | solution.py:40
  32.8 6.8 %collective-permute-start.3 = (f32[256,64]{1,0:T(8,128)S(1)}, f32[256,64]{1,0:T(8,128)S(1)}, u32[]{:S(2)}, u32[]{:S(2)}) collective-permute-start(f32[256,64]{1,0:T(8,128)S(1)} %add.63), channel_id=1, source_target_pairs={{0,6},{1,7},{2,4},{3,5},{4,2},{5,3},{6,0},{7,1},{8,14},{9,15},{10,... | collective-permute-start | bytes 196616 | tf_op jit(solution)/shard_map/ppermute | solution.py:40
  34.0 5.7 %collective-permute-start.1 = (f32[256,64]{1,0:T(8,128)S(1)}, f32[256,64]{1,0:T(8,128)S(1)}, u32[]{:S(2)}, u32[]{:S(2)}) collective-permute-start(f32[256,64]{1,0:T(8,128)S(1)} %add.63), channel_id=1, source_target_pairs={{0,2},{1,3},{2,0},{3,1},{4,6},{5,7},{6,4},{7,5},{8,10},{9,11},{10,... | collective-permute-start | bytes 196616 | tf_op jit(solution)/shard_map/ppermute | solution.py:40
  47.0 3.3 %collective-permute-start.5 = (f32[128,1024]{1,0:T(8,128)}, f32[128,1024]{1,0:T(8,128)S(1)}, u32[]{:S(2)}, u32[]{:S(2)}) collective-permute-start(f32[128,1024]{1,0:T(8,128)} %get-tuple-element.43), channel_id=1, source_target_pairs={{0,1},{1,0},{2,3},{3,2},{4,5},{5,4},{6,7},{7,6},{8,9},{9,8},{10,11... | collective-permute-start | bytes 1572872 | tf_op jit(solution)/shard_map/ppermute | solution.py:40
  47.1 2.3 %collective-permute-start.4 = (f32[256,64]{1,0:T(8,128)}, f32[256,64]{1,0:T(8,128)S(1)}, u32[]{:S(2)}, u32[]{:S(2)}) collective-permute-start(f32[256,64]{1,0:T(8,128)} %get-tuple-element.41), channel_id=1, source_target_pairs={{0,1},{1,0},{2,3},{3,2},{4,5},{5,4},{6,7},{7,6},{8,9},{9,8},{10,11... | collective-permute-start | bytes 196616 | tf_op jit(solution)/shard_map/ppermute | solution.py:40
  50.4 0.8 copy-start.9
  51.2 18.7 %copy-start.10 = (bf16[256,64]{1,0:T(8,128)(2,1)S(1)}, bf16[256,64]{1,0:T(8,128)(2,1)}, u32[]{:S(2)}) copy-start(bf16[256,64]{1,0:T(8,128)(2,1)} %multiply_convert_fusion.1.weight_ref) | copy-start | bytes 98308
  59.2 34.7 %copy-start.11 = (f32[1024,64]{0,1:T(8,128)S(1)}, f32[1024,64]{0,1:T(8,128)}, u32[]{:S(2)}) copy-start(f32[1024,64]{0,1:T(8,128)} %param.20) | copy-start | bytes 786436
  59.2 34.7 %copy-start.12 = (f32[1024,64]{0,1:T(8,128)S(1)}, f32[1024,64]{0,1:T(8,128)}, u32[]{:S(2)}) copy-start(f32[1024,64]{0,1:T(8,128)} %param.21) | copy-start | bytes 786436
  59.3 8.1 %collective-permute-start.12 = (f32[256,64]{1,0:T(8,128)S(1)}, f32[256,64]{1,0:T(8,128)S(1)}, u32[]{:S(2)}, u32[]{:S(2)}) collective-permute-start(f32[256,64]{1,0:T(8,128)S(1)} %add.67), channel_id=1, source_target_pairs={{0,4},{1,5},{2,6},{3,7},{4,0},{5,1},{6,2},{7,3},{8,12},{9,13},{10,... | collective-permute-start | bytes 196616 | tf_op jit(solution)/shard_map/ppermute | solution.py:40
  61.1 8.7 %collective-permute-start.13 = (f32[256,64]{1,0:T(8,128)S(1)}, f32[256,64]{1,0:T(8,128)S(1)}, u32[]{:S(2)}, u32[]{:S(2)}) collective-permute-start(f32[256,64]{1,0:T(8,128)S(1)} %add.67), channel_id=1, source_target_pairs={{0,6},{1,7},{2,4},{3,5},{4,2},{5,3},{6,0},{7,1},{8,14},{9,15},{10,... | collective-permute-start | bytes 196616 | tf_op jit(solution)/shard_map/ppermute | solution.py:40
  63.2 6.6 %collective-permute-start.11 = (f32[256,64]{1,0:T(8,128)S(1)}, f32[256,64]{1,0:T(8,128)S(1)}, u32[]{:S(2)}, u32[]{:S(2)}) collective-permute-start(f32[256,64]{1,0:T(8,128)S(1)} %add.67), channel_id=1, source_target_pairs={{0,2},{1,3},{2,0},{3,1},{4,6},{5,7},{6,4},{7,5},{8,10},{9,11},{10,... | collective-permute-start | bytes 196616 | tf_op jit(solution)/shard_map/ppermute | solution.py:40
  63.2 17.7 %collective-permute-start.10 = (bf16[32,8192]{1,0:T(8,128)(2,1)}, bf16[32,8192]{1,0:T(8,128)(2,1)S(1)}, u32[]{:S(2)}, u32[]{:S(2)}) collective-permute-start(bf16[32,8192]{1,0:T(8,128)(2,1)} %get-tuple-element.53), channel_id=1, source_target_pairs={{0,6},{1,7},{2,0},{3,1},{4,2},{5,3},{6,4},{7,5},{8,14},{9,15},{10,... | collective-permute-start | bytes 1572872 | tf_op jit(solution)/shard_map/ppermute | solution.py:392
  65.2 16.6 %collective-permute-start.9 = (bf16[32,8192]{1,0:T(8,128)(2,1)}, bf16[32,8192]{1,0:T(8,128)(2,1)S(1)}, u32[]{:S(2)}, u32[]{:S(2)}) collective-permute-start(bf16[32,8192]{1,0:T(8,128)(2,1)} %get-tuple-element.52), channel_id=1, source_target_pairs={{0,4},{1,5},{2,6},{3,7},{4,0},{5,1},{6,2},{7,3},{8,12},{9,13},{10,... | collective-permute-start | bytes 1572872 | tf_op jit(solution)/shard_map/ppermute | solution.py:392
  67.3 24.3 %collective-permute-start.8 = (bf16[32,8192]{1,0:T(8,128)(2,1)}, bf16[32,8192]{1,0:T(8,128)(2,1)S(1)}, u32[]{:S(2)}, u32[]{:S(2)}) collective-permute-start(bf16[32,8192]{1,0:T(8,128)(2,1)} %get-tuple-element.51), channel_id=1, source_target_pairs={{0,2},{1,3},{2,4},{3,5},{4,6},{5,7},{6,0},{7,1},{8,10},{9,11},{10,... | collective-permute-start | bytes 1572872 | tf_op jit(solution)/shard_map/ppermute | solution.py:392
  70.9 23.1 %all-to-all-start.2 = ((bf16[32,16,128]{2,1,0:T(8,128)(2,1)}), bf16[32,16,128]{2,1,0:T(8,128)(2,1)S(1)}, u32[]{:S(2)}, u32[]{:S(2)}) async-start(bf16[32,16,128]{2,1,0:T(8,128)(2,1)} %bitcast.6), calls=%async_computation.2 | async-start | bytes 262144 | tf_op jit(solution)/shard_map/all_to_all | solution.py:407
  93.9 2.5 %copy-start.13 = (f32[64,256]{1,0:T(8,128)S(1)}, f32[64,256]{1,0:T(8,128)}, u32[]{:S(2)}) copy-start(f32[64,256]{1,0:T(8,128)} %param.23) | copy-start | bytes 196612
  93.9 2.5 %copy-start.14 = (f32[64,256]{1,0:T(8,128)S(1)}, f32[64,256]{1,0:T(8,128)}, u32[]{:S(2)}) copy-start(f32[64,256]{1,0:T(8,128)} %param.24) | copy-start | bytes 196612
  94.0 2.5 %copy-start.15 = (f32[64,256]{1,0:T(8,128)S(1)}, f32[64,256]{1,0:T(8,128)}, u32[]{:S(2)}) copy-start(f32[64,256]{1,0:T(8,128)} %param.25) | copy-start | bytes 196612

commit v6 on v5

--- a/solution.py
+++ b/solution.py
@@ -48,7 +48,6 @@
 
 VMEM_LIMIT = 16 * 1024 * 1024
 VMEM_MOST = 60 * 1024 * 1024
-VMEM_PAIR = 57 * 1024 * 1024
 SMEM_SPEC = pl.BlockSpec(memory_space=pltpu.MemorySpace.SMEM)
 HBM = pltpu.MemorySpace.HBM
 NT = (((1,), (1,)), ((), ()))
@@ -202,55 +201,93 @@
     )(turned, frozen)
 
 
-def pack_kernel(place_ref, hidden_ref, masked_ref, out_ref):
+def pack_kernel(place_ref, *refs):
+    parts, out_ref = refs[:-1], refs[-1]
     rows, tokens = out_ref.shape[0], place_ref.shape[1]
     down = lax.broadcasted_iota(jnp.int32, (rows, tokens), 0)
     pick = jnp.where(down == place_ref[...], 1.0, 0.0).astype(jnp.bfloat16)
-    width = hidden_ref.shape[1]
-    out_ref[:, :width] = dot(pick, hidden_ref[...], NN).astype(jnp.bfloat16)
-    out_ref[:, width:] = dot(pick, masked_ref[...], NN).astype(jnp.bfloat16)
-
-
-def pack_rows(place, hidden_columns, masked, rows):
-    tokens, columns = masked.shape[0], hidden_columns.shape[1] + masked.shape[1]
+    first = 0
+    for part in parts:
+        width = part.shape[1]
+        out_ref[:, first : first + width] = dot(pick, part[...], NN).astype(jnp.bfloat16)
+        first += width
+
+
+def pack_rows(place, parts, rows):
+    tokens, columns = place.shape[1], sum(v.shape[1] for v in parts)
     return call(
         pack_kernel,
         jax.ShapeDtypeStruct((rows, columns), jnp.bfloat16),
         2 * rows * columns * tokens,
         2 * (rows + tokens) * columns,
         name="pack",
-    )(place, hidden_columns, masked)
-
-
-def factors_kernel(rows_own, hidden_ref, weight_ref, slot_ref, factors_ref, down_ref, ours_ref,
-                   theirs_ref, held_ref, extra_ref, sems):
-    parts, columns, chunk = held_ref.shape
-    tokens = hidden_ref.shape[0]
-    n_chip = tokens // rows_own // 2
-    stream = Stream(
-        [factors_ref.at[:, pl.ds(c * chunk, chunk)] for c in range(parts)],
+    )(place, *parts)
+
+
+def factor_stream(factors_any, held_ref, sems):
+    parts, _, chunk = held_ref.shape
+    return Stream(
+        [factors_any.at[:, pl.ds(c * chunk, chunk)] for c in range(parts)],
         [held_ref.at[c] for c in range(parts)],
         sems,
     )
+
+
+def down_kernel(hidden_ref, slot_ref, factors_any, out_ref, held_ref, sems):
+    parts, _, chunk = held_ref.shape
+    tokens = hidden_ref.shape[0]
+    stream = factor_stream(factors_any, held_ref, sems)
     slot = slot_ref[...]
-    weight = weight_ref[...].astype(jnp.float32)
-    double = jnp.concatenate([weight, weight], axis=1)
     acc = jnp.zeros((tokens, 128), jnp.float32)
     for c in range(parts):
         stream.wait(c)
-        factors = held_ref[c]
-        product = dot(hidden_ref[...], factors, NN)
+        product = dot(hidden_ref[...], held_ref[c], NN)
+        for d in range(chunk // 128):
+            hit = slot == lane_slot((1, 128), (c * chunk + d * 128) // PADDED_RANK)
+            acc = acc + jnp.where(hit, product[:, d * 128 : (d + 1) * 128], 0.0)
+    out_ref[...] = acc[:, :PADDED_RANK] + acc[:, PADDED_RANK:]
+
+
+def low_rank(hidden_columns, slot_wide, factors):
+    tokens, columns = hidden_columns.shape
+    chunk = 256
+    parts = factors.shape[1] // chunk
+    return call(
+        down_kernel,
+        jax.ShapeDtypeStruct((tokens, PADDED_RANK), jnp.float32),
+        2 * tokens * factors.size,
+        2 * factors.size,
+        VMEM_MOST,
+        in_specs=[pl.BlockSpec(v.shape) for v in (hidden_columns, slot_wide)]
+        + [pl.BlockSpec(memory_space=HBM)],
+        scratch_shapes=[
+            pltpu.VMEM((parts, columns, chunk), jnp.bfloat16),
+            pltpu.SemaphoreType.DMA((parts,)),
+        ],
+        name="low_rank",
+    )(hidden_columns, slot_wide, factors)
+
+
+def extra_kernel(rows_own, weight_ref, slot_ref, factors_any, ours_ref, theirs_ref, held_ref,
+                 extra_ref, sems):
+    parts, _, chunk = held_ref.shape
+    tokens = weight_ref.shape[0]
+    n_chip = tokens // rows_own // 2
+    stream = factor_stream(factors_any, held_ref, sems)
+    slot = slot_ref[...]
+    weight = weight_ref[:, PADDED_RANK:].astype(jnp.float32)
+    double = jnp.concatenate([weight, weight], axis=1)
+    for c in range(parts):
+        stream.wait(c)
         pieces = []
         for d in range(chunk // 128):
             hit = slot == lane_slot((1, 128), (c * chunk + d * 128) // PADDED_RANK)
-            acc = acc + jnp.where(hit, product[:, d * 128 : (d + 1) * 128], 0.0)
             pieces.append(jnp.where(hit, double, 0.0).astype(jnp.bfloat16))
-        term = dot(jnp.concatenate(pieces, axis=1), factors, NT)
+        term = dot(jnp.concatenate(pieces, axis=1), held_ref[c], NT)
         if c == 0:
             extra_ref[...] = term
         else:
             extra_ref[...] += term
-    down_ref[...] = acc[:, :PADDED_RANK] + acc[:, PADDED_RANK:]
     position = lax.axis_index("tensor")
     chip, core = position // 2, position % 2
     for turn in range(n_chip):
@@ -260,55 +297,50 @@
             out[pl.ds(turn * rows_own, rows_own), :] = extra_ref[pl.ds(start, rows_own), :]
 
 
-def factor_products(rows_own, hidden_columns, up_weight, slot_wide, factors):
-    tokens, columns = hidden_columns.shape
+def extra_term(rows_own, weights, slot_wide, factors):
+    tokens, columns = weights.shape[0], factors.shape[0]
     chunk = 256
     parts = factors.shape[1] // chunk
     half = jax.ShapeDtypeStruct((tokens // 2, columns), jnp.float32)
-    shapes = (jax.ShapeDtypeStruct((tokens, PADDED_RANK), jnp.float32), half, half)
-    return call(
-        functools.partial(factors_kernel, rows_own),
-        shapes,
-        4 * tokens * factors.size,
+    return call(
+        functools.partial(extra_kernel, rows_own),
+        (half, half),
+        2 * tokens * factors.size,
         2 * factors.size,
         VMEM_MOST,
-        in_specs=[pl.BlockSpec(v.shape) for v in (hidden_columns, up_weight, slot_wide)]
+        in_specs=[pl.BlockSpec(v.shape) for v in (weights, slot_wide)]
         + [pl.BlockSpec(memory_space=HBM)],
         scratch_shapes=[
             pltpu.VMEM((parts, columns, chunk), jnp.bfloat16),
             pltpu.VMEM((tokens, columns), jnp.float32),
             pltpu.SemaphoreType.DMA((parts,)),
         ],
-        name="factor_products",
-    )(hidden_columns, up_weight, slot_wide, factors)
-
-
-def pair_kernel(rows_own, parts, turned_ref, extra_ours_ref, extra_pair_ref, frozen_any, *refs):
+        name="extra_term",
+    )(weights, slot_wide, factors)
+
+
+def pair_kernel(rows_own, parts, turned_ref, frozen_any, *refs):
     pair_refs, outs, (frozen_ref, sems) = refs[:parts], refs[parts:-2], refs[-2:]
     steps = sems.shape[0]
-    half, columns = extra_ours_ref.shape
+    half = turned_ref.shape[0] // 2
+    columns = frozen_ref.shape[0] // steps
     per_part = steps // parts
     stream = Stream(row_parts(frozen_any, steps), row_parts(frozen_ref, steps), sems)
-    position = lax.axis_index("tensor")
-    chip, core = position // 2, position % 2
     ours = turned_ref[:half, :]
-    low = jnp.where(core == 0, extra_ours_ref[...], extra_pair_ref[...])
-    high = jnp.where(core == 0, extra_pair_ref[...], extra_ours_ref[...])
     for c in range(steps):
         stream.wait(c)
         at = slice(c * columns, (c + 1) * columns)
         first = c % per_part * columns
         total = dot(ours, frozen_ref[at, :], NT)
         total = total + pair_refs[c // per_part][:, first : first + columns]
-        total = total + jnp.where(chip == c // 2, low if c % 2 == 0 else high, 0.0)
         outs[0][:, at] = total[:rows_own, :]
         for i, out in enumerate(outs[1:]):
             out[:, at] = total[(i + 1) * rows_own : (i + 2) * rows_own, :].astype(jnp.bfloat16)
 
 
-def pair_sum(rows_own, turned, frozen, from_pair, extra_ours, extra_pair):
+def pair_sum(rows_own, turned, frozen, from_pair):
     parts = len(from_pair)
-    half, columns = extra_ours.shape
+    half = turned.shape[0] // 2
     width, kv = frozen.shape
     sent = jax.ShapeDtypeStruct((rows_own, width), jnp.bfloat16)
     n_out = half // rows_own - 1
@@ -317,16 +349,42 @@
         (jax.ShapeDtypeStruct((rows_own, width), jnp.float32),) + (sent,) * n_out,
         2 * half * width * kv,
         2 * kv * width + 6 * half * width,
-        VMEM_PAIR,
-        in_specs=[pl.BlockSpec(v.shape) for v in (turned, extra_ours, extra_pair)]
-        + [pl.BlockSpec(memory_space=HBM)]
+        VMEM_MOST,
+        in_specs=[pl.BlockSpec(turned.shape), pl.BlockSpec(memory_space=HBM)]
         + [pl.BlockSpec(v.shape) for v in from_pair],
         scratch_shapes=[
             pltpu.VMEM(frozen.shape, frozen.dtype),
-            pltpu.SemaphoreType.DMA((width // columns,)),
+            pltpu.SemaphoreType.DMA((8,)),
         ],
         name="pair_sum",
-    )(turned, extra_ours, extra_pair, frozen, *from_pair)
+    )(turned, frozen, *from_pair)
+
+
+def last_kernel(*refs):
+    count = (len(refs) - 1) // 2
+    frozen_refs, extra_refs, out_ref = refs[:count], refs[count:-1], refs[-1]
+    columns = extra_refs[0].shape[1]
+    chip = lax.axis_index("tensor") // 2
+    for step, extra_ref in enumerate(extra_refs):
+        block = (chip + count - step) % count
+        at = pl.ds(pl.multiple_of(block * columns, columns), columns)
+        total = extra_ref[...].astype(jnp.float32)
+        for frozen_ref in frozen_refs:
+            total = total + frozen_ref[:, at].astype(jnp.float32)
+        out_ref[:, at] = total.astype(jnp.bfloat16)
+
+
+def last_sum(frozen_terms, extra_terms):
+    size = frozen_terms[0].size
+    values = [*frozen_terms, *extra_terms]
+    return call(
+        last_kernel,
+        jax.ShapeDtypeStruct(frozen_terms[0].shape, jnp.bfloat16),
+        5 * size,
+        16 * size,
+        in_specs=[pl.BlockSpec(v.shape) for v in values],
+        name="last_sum",
+    )(*values)
 
 
 def local(
@@ -365,51 +423,55 @@
         cotangent,
         adapter_up_factors,
     )
-    factor = factor_wide[:, :PADDED_RANK]
-
-    frozen_theirs = frozen_term(turned, frozen_key_value, 2)
+
+    frozen_theirs = frozen_term(turned, frozen_key_value, 4)
     up_own = up_own + swap(up_own, 1, n_tensor)
-    place, up_own, frozen_theirs = lax.optimization_barrier((place, up_own, frozen_theirs))
+    slot_wide, up_own, frozen_theirs = lax.optimization_barrier(
+        (slot_wide, up_own, frozen_theirs)
+    )
     from_pair = [swap(theirs, 1, n_tensor) for theirs in frozen_theirs]
-    up_sum = sum_over_chips(up_own, n_tensor)
-
-    packed = pack_rows(place, hidden_columns, masked, n_slot * CAP)
+
+    own = low_rank(hidden_columns, slot_wide, adapter_down_factors)
+    own = jnp.concatenate([own + swap(own, 1, n_tensor), up_own], axis=1)
+    weights = (sum_over_chips(own, n_tensor) * factor_wide).astype(jnp.bfloat16)
+    total, *sent = pair_sum(rows_own, turned, frozen_key_value, from_pair)
+
+    packed = pack_rows(place, [hidden_columns, masked, weights], n_slot * CAP)
+    after = lax.optimization_barrier((weights, total, sent))
     owned = lax.all_to_all(
         packed.reshape(n_slot, CAP, -1), "dp", 0, 0, tiled=True
     ).reshape(n_slot * CAP, -1)
 
-    up_weight = (up_sum * factor).astype(jnp.bfloat16)
-    down_own, extra_ours, extra_theirs = factor_products(
-        rows_own, hidden_columns, up_weight, slot_wide, adapter_down_factors
-    )
+    def to_chips(sent):
+        return [
+            lax.ppermute(
+                value, "tensor", [(i, (i + 2 * step) % n_tensor) for i in range(n_tensor)]
+            )
+            for step, value in enumerate(sent, 1)
+        ]
+
+    weights, total, sent = after
+    arrived = to_chips(sent)
+    extra_ours, extra_theirs = extra_term(rows_own, weights, slot_wide, adapter_down_factors)
     extra_pair = swap(extra_theirs, 1, n_tensor)
-    total, *sent = pair_sum(
-        rows_own, turned, frozen_key_value, from_pair, extra_ours, extra_pair
-    )
-    down_own = down_own + swap(down_own, 1, n_tensor)
-    down_own, total, sent = lax.optimization_barrier((down_own, total, sent))
-    for step in range(1, n_chip):
-        arrived = lax.ppermute(
-            sent[step - 1], "tensor", [(i, (i + 2 * step) % n_tensor) for i in range(n_tensor)]
-        )
-        total = total + arrived.astype(jnp.float32)
-    hidden_gradient = total.astype(jnp.bfloat16)
-
-    down_weight = (sum_over_chips(down_own, n_tensor) * factor).astype(jnp.bfloat16)
-    weights = jnp.concatenate([down_weight, up_weight], axis=1)
-    pick = (
-        jnp.arange(n_slot * CAP, dtype=jnp.int32)[:, None] == place
-    ).astype(jnp.bfloat16)
-    packed_weights = jnp.dot(pick, weights, preferred_element_type=jnp.float32).astype(
-        jnp.bfloat16
-    )
-    owned, packed_weights = lax.optimization_barrier((owned, packed_weights))
-    owned_weights = lax.all_to_all(
-        packed_weights.reshape(n_slot, CAP, -1), "dp", 0, 0, tiled=True
-    ).reshape(n_slot * CAP, -1)
-
-    grad_down = contract_helper(owned[:, :columns], owned_weights[:, PADDED_RANK:], 0, 0) / tokens
-    grad_up = contract_helper(owned_weights[:, :PADDED_RANK], owned[:, columns:], 0, 0) / tokens
+    low_core = lax.axis_index("tensor") % 2 == 0
+    extra = jnp.concatenate(
+        [
+            jnp.where(low_core, extra_ours, extra_pair),
+            jnp.where(low_core, extra_pair, extra_ours),
+        ],
+        axis=1,
+    ).reshape(n_chip, rows_own, 2 * columns)
+    extra_sent = extra[1:].astype(jnp.bfloat16)
+    extra_arrived = to_chips([extra_sent[i] for i in range(n_chip - 1)])
+    hidden_gradient = last_sum([total, *arrived], [extra[0], *extra_arrived])
+
+    kv = cotangent.shape[1]
+    owned_hidden, owned_cot = owned[:, :columns], owned[:, columns : columns + kv]
+    owned_down = owned[:, columns + kv : columns + kv + PADDED_RANK]
+    owned_up = owned[:, columns + kv + PADDED_RANK :]
+    grad_down = contract_helper(owned_hidden, owned_up, 0, 0) / tokens
+    grad_up = contract_helper(owned_down, owned_cot, 0, 0) / tokens
     new_dm, new_dmo, new_ds = adamw(
         down_master_copy, down_first_moment, down_second_moment, grad_down
     )

time: 99.1 us -> 105 us (1.060)
  waiting for transfers between devices: 20.6 us -> 33.5 us
  starting transfers between devices: 40 us -> 29.2 us
  Pallas kernels: 24.1 us -> 30.5 us
  matrix products: 4.32 us -> 2.34 us
  local copies, waits for them, and re-layouts: 3.45 us -> 5.14 us
  other arithmetic: 3.93 us -> 2.26 us
    ppermute x3 -> x6, waiting for transfers between devices: 11 us -> 23.8 us  [to_chips(): lax.ppermute(value, 'tensor', [(i, (i + 2 * step) % n_tensor) for i in ra...]
    all_to_all x1 -> x0, starting transfers between devices: 9.79 us -> none  [local(): lax.all_to_all(packed_weights.reshape(n_slot, CAP, -1), 'dp', 0, 0, tiled...]
    pallas_call x1 -> x3, Pallas kernels: 6.7 us -> 13.3 us  [the longest x1 6.28 us: low_rank(): call(down_kernel, jax.ShapeDtypeStruct((tokens, PADDED_RANK), jnp.float32...]
    ppermute x11 -> x10, starting transfers between devices: 9.35 us -> 5.98 us  [swap(): return lax.ppermute(value, 'tensor', [(i, i ^ mask) for i in range(count)])]
    convert_element_type x3 -> x1, other arithmetic: 2.98 us -> 0.03 us  [local(): weights = (sum_over_chips(own, n_tensor) * factor_wide).astype(jnp.bfloat16)]
    ppermute x3 -> x6, starting transfers between devices: 5.2 us -> 7.56 us  [to_chips(): lax.ppermute(value, 'tensor', [(i, (i + 2 * step) % n_tensor) for i in ra...]
    unnamed x32 -> x44, local copies, waits for them, and re-layouts: 1.48 us -> 3.14 us
    select_n x0 -> x1, other arithmetic: none -> 1.11 us  [local(): jnp.where(low_core, extra_pair, extra_ours)]
  transfers between devices with their start and end apart: 17 -> 18, of which waited for: 8 -> 10; matrix products, arithmetic and copies ran while one was open for 5% -> 1% of each run, Pallas kernels for 25% -> 23%
where the time goes in v6:
time: 105 us; the launch traced here: 104 us
  waiting for transfers between devices  33.5 us (32%)
  Pallas kernels  30.5 us (29%)
  starting transfers between devices  29.2 us (28%)
  local copies, waits for them, and re-layouts  5.14 us (5%)
  matrix products  2.34 us (2%)
  other arithmetic  2.26 us (2%)
  between operations  1.06 us (1%)
    ppermute x6, waiting for transfers between devices, to_chips(): lax.ppermute(value, 'tensor', [(i, (i + 2 * step) % n_tensor) for i in ra...  23.8 us
    all_to_all x1, starting transfers between devices, local(): lax.all_to_all(packed.reshape(n_slot, CAP, -1), 'dp', 0, 0, tiled=True)  11.2 us
    ppermute x10, waiting for transfers between devices, swap(): return lax.ppermute(value, 'tensor', [(i, i ^ mask) for i in range(count)])  8.98 us
    pallas_call x1, Pallas kernels, pair_sum(): call(functools.partial(pair_kernel, rows_own, parts), (jax.ShapeDtypeStru...  7.68 us
    ppermute x6, starting transfers between devices, to_chips(): lax.ppermute(value, 'tensor', [(i, (i + 2 * step) % n_tensor) for i in ra...  7.56 us
    pallas_call x1, Pallas kernels, frozen_term(): call(frozen_kernel, (jax.ShapeDtypeStruct((tokens // 2, width // parts),...  6.59 us
    pallas_call x1, Pallas kernels, low_rank(): call(down_kernel, jax.ShapeDtypeStruct((tokens, PADDED_RANK), jnp.float32...  6.28 us
    ppermute x10, starting transfers between devices, swap(): return lax.ppermute(value, 'tensor', [(i, i ^ mask) for i in range(count)])  5.98 us
  transfers between devices with their start and end apart: 18, of which 10 were waited for; matrix products, arithmetic and copies ran while one was open for 1% of the time, Pallas kernels for 23%

profile of v6, /device:TPU:32, one launch (start us, length us, event | category | flops | bytes accessed | tf_op | source)
XLA Modules:
  0.0 104.0 jit_solution(16236192606923286705)
XLA Ops:
  0.7 2.0 %copy.25 = bf16[4,8,8,1024]{3,2,0,1:T(8,128)(2,1)} copy(bf16[4,8,8,1024]{3,2,1,0:T(8,128)(2,1)} %bitcast.16) | data formatting | bytes 1048576 | tf_op jit(solution)/shard_map/reshape | solution.py:414
  2.7 4.5 %all-to-all-start = ((bf16[8,32,1024]{2,1,0:T(8,128)(2,1)}), bf16[8,32,1024]{2,1,0:T(8,128)(2,1)S(1)}, u32[]{:S(2)}, u32[]{:S(2)}) async-start(bf16[8,32,1024]{2,1,0:T(8,128)(2,1)} %bitcast.10), calls=%async_computation | async-start | bytes 1048576 | tf_op jit(solution)/shard_map/all_to_all | solution.py:415
  7.2 1.1 %prep.1 = (bf16[256,256]{1,0:T(8,128)(2,1)S(1)}, bf16[256,256]{1,0:T(8,128)(2,1)S(1)}, f32[256,128]{1,0:T(8,128)S(1)}, f32[256,128]{1,0:T(8,128)S(1)}, s32[1,256]{1,0:T(1,128)S(1)}, /*index=5*/f32[256,64]{1,0:T(8,128)S(1)}) custom-call(s32[32]{0:T(128)S(1)} %copy-done.9, s32[32]{0:T(128)S(1)} %copy-done.10, s32[32]{0:T(128)S(1)} %copy-done.11, ...), custom_call_target="tpu_custom_call" | custom-call | flops 268435456 | bytes 1048576 | tf_op jit(solution)/shard_map/prep/pallas_call | solution.py:159
  8.3 0.6 copy-done.5
  9.0 0.7 copy-done.6
  9.6 0.5 collective-permute-start
  10.1 6.6 %frozen_term.1 = (f32[128,2048]{1,0:T(8,128)}, f32[128,2048]{1,0:T(8,128)}, f32[128,2048]{1,0:T(8,128)}, f32[128,2048]{1,0:T(8,128)}) custom-call(bf16[256,256]{1,0:T(8,128)(2,1)} %copy-done.5, bf16[8192,256]{1,0:T(8,128)(2,1)} %frozen_any.3), custom_call_target="tpu_custom_call" | custom-call | flops 536870912 | bytes 8388608 | tf_op jit(solution)/shard_map/frozen_term/pallas_call | solution.py:189
  16.8 0.7 all-to-all-done
  17.5 0.8 copy-done
  18.3 6.3 %low_rank.1 = f32[256,64]{1,0:T(8,128)} custom-call(bf16[256,1024]{1,0:T(8,128)(2,1)} %bitcast.11, f32[256,128]{1,0:T(8,128)} %copy-done.6, bf16[1024,2048]{1,0:T(8,128)(2,1)} %factors_any.3), custom_call_target="tpu_custom_call" | custom-call | flops 1073741824 | bytes 4194304 | tf_op jit(solution)/shard_map/low_rank/pallas_call | solution.py:255
  24.6 0.1 collective-permute-start.1
  24.7 1.5 %collective-permute-done.1 = f32[256,64]{1,0:T(8,128)S(1)} collective-permute-done((f32[256,64]{1,0:T(8,128)}, f32[256,64]{1,0:T(8,128)S(1)}, u32[]{:S(2)}, u32[]{:S(2)}) %collective-permute-start.1) | collective-permute-done | bytes 65568 | tf_op jit(solution)/shard_map/ppermute | solution.py:40
  26.2 0.9 add.50
  27.1 0.1 pad_maximum_fusion.1
  27.3 1.1 %collective-permute-start.2 = (f32[256,128]{1,0:T(8,128)S(1)}, f32[256,128]{1,0:T(8,128)S(1)}, u32[]{:S(2)}, u32[]{:S(2)}) collective-permute-start(f32[256,128]{1,0:T(8,128)S(1)} %pad_maximum_fusion.1), channel_id=1, source_target_pairs={{0,2},{1,3},{2,0},{3,1},{4,6},{5,7},{6,4},{7,5},{8,10},{9,11},{10,... | collective-permute-start | bytes 393224 | tf_op jit(solution)/shard_map/ppermute | solution.py:40
  28.3 2.7 %collective-permute-start.3 = (f32[256,128]{1,0:T(8,128)S(1)}, f32[256,128]{1,0:T(8,128)S(1)}, u32[]{:S(2)}, u32[]{:S(2)}) collective-permute-start(f32[256,128]{1,0:T(8,128)S(1)} %pad_maximum_fusion.1), channel_id=1, source_target_pairs={{0,4},{1,5},{2,6},{3,7},{4,0},{5,1},{6,2},{7,3},{8,12},{9,13},{10,... | collective-permute-start | bytes 393224 | tf_op jit(solution)/shard_map/ppermute | solution.py:40
  31.0 1.0 %collective-permute-start.4 = (f32[256,128]{1,0:T(8,128)S(1)}, f32[256,128]{1,0:T(8,128)S(1)}, u32[]{:S(2)}, u32[]{:S(2)}) collective-permute-start(f32[256,128]{1,0:T(8,128)S(1)} %pad_maximum_fusion.1), channel_id=1, source_target_pairs={{0,6},{1,7},{2,4},{3,5},{4,2},{5,3},{6,0},{7,1},{8,14},{9,15},{10,... | collective-permute-start | bytes 393224 | tf_op jit(solution)/shard_map/ppermute | solution.py:40
  32.0 0.5 collective-permute-start.6
  32.5 1.1 %collective-permute-done.2 = f32[256,128]{1,0:T(8,128)S(1)} collective-permute-done((f32[256,128]{1,0:T(8,128)S(1)}, f32[256,128]{1,0:T(8,128)S(1)}, u32[]{:S(2)}, u32[]{:S(2)}) %collective-permute-start.2) | collective-permute-done | bytes 131104 | tf_op jit(solution)/shard_map/ppermute | solution.py:40
  33.7 3.9 %collective-permute-done.3 = f32[256,128]{1,0:T(8,128)S(1)} collective-permute-done((f32[256,128]{1,0:T(8,128)S(1)}, f32[256,128]{1,0:T(8,128)S(1)}, u32[]{:S(2)}, u32[]{:S(2)}) %collective-permute-start.3) | collective-permute-done | bytes 131104 | tf_op jit(solution)/shard_map/ppermute | solution.py:40
  37.6 2.3 %collective-permute-done.4 = f32[256,128]{1,0:T(8,128)S(1)} collective-permute-done((f32[256,128]{1,0:T(8,128)S(1)}, f32[256,128]{1,0:T(8,128)S(1)}, u32[]{:S(2)}, u32[]{:S(2)}) %collective-permute-start.4) | collective-permute-done | bytes 131104 | tf_op jit(solution)/shard_map/ppermute | solution.py:40
  40.0 0.0 copy-start.4
  40.0 1.7 %pack.1 = bf16[512,1408]{1,0:T(8,128)(2,1)} custom-call(s32[1,256]{1,0:T(1,128)S(1)} %get-tuple-element.59.place_ref, bf16[256,1024]{1,0:T(8,128)(2,1)S(1)} %bitcast.12, bf16[256,256]{1,0:T(8,128)(2,1)S(1)} %get-tuple-element.60.refs_1_, bf16[256,128]{1,0:T(8,128)(2,1)S(1)} %multiply_convert_fusion.weight_ref.refs_2_), custom_call_target="tpu_custom_call" | custom-call | flops 369098752 | bytes 2162688 | tf_op jit(solution)/shard_map/pack/pallas_call | solution.py:218
  41.8 11.2 %all-to-all-start.1 = ((bf16[32,16,1408]{2,1,0:T(8,128)(2,1)}), bf16[32,16,1408]{2,1,0:T(8,128)(2,1)S(1)}, u32[]{:S(2)}, u32[]{:S(2)}) async-start(bf16[32,16,1408]{2,1,0:T(8,128)(2,1)} %bitcast.3), calls=%async_computation.1 | async-start | bytes 2883584 | tf_op jit(solution)/shard_map/all_to_all | solution.py:441
  53.0 0.9 copy-done.12
  54.0 7.7 %pair_sum.1 = (f32[32,8192]{1,0:T(8,128)}, bf16[32,8192]{1,0:T(8,128)(2,1)}, bf16[32,8192]{1,0:T(8,128)(2,1)}, bf16[32,8192]{1,0:T(8,128)(2,1)}) custom-call(bf16[256,256]{1,0:T(8,128)(2,1)} %copy-done.5, bf16[8192,256]{1,0:T(8,128)(2,1)} %frozen_any.3, f32[128,2048]{1,0:T(8,128)} %copy-done.12, f32[128,2048]{1,0:T(8,128)} %collective-permute-done.6.refs_1_, ...), custom_call_target="tpu_custom_call" | custom-call | flops 536870912 | bytes 10485760 | tf_op jit(solution)/shard_map/pair_sum/pallas_call | solution.py:347
  61.7 0.0 copy-start.13
  61.7 6.0 %extra_term.1 = (f32[128,1024]{1,0:T(8,128)}, f32[128,1024]{1,0:T(8,128)}) custom-call(bf16[256,128]{1,0:T(8,128)(2,1)} %copy-done.4, f32[256,128]{1,0:T(8,128)} %copy-done.6, bf16[1024,2048]{1,0:T(8,128)(2,1)} %factors_any.3), custom_call_target="tpu_custom_call" | custom-call | flops 1073741824 | bytes 4194304 | tf_op jit(solution)/shard_map/extra_term/pallas_call | solution.py:305
  67.7 0.1 collective-permute-start.12
  67.8 0.1 collective-permute-start.10
  67.9 1.9 %collective-permute-start.11 = (bf16[32,8192]{1,0:T(8,128)(2,1)S(1)}, bf16[32,8192]{1,0:T(8,128)(2,1)S(1)}, u32[]{:S(2)}, u32[]{:S(2)}) collective-permute-start(bf16[32,8192]{1,0:T(8,128)(2,1)S(1)} %copy-done.14), channel_id=1, source_target_pairs={{0,6},{1,7},{2,0},{3,1},{4,2},{5,3},{6,4},{7,5},{8,14},{9,15},{10,... | collective-permute-start | bytes 1572872 | tf_op jit(solution)/shard_map/ppermute | solution.py:447
  69.8 0.2 collective-permute-start.9
  70.0 1.1 %broadcast_select_fusion = (f32[128,1024]{1,0:T(8,128)S(1)}, f32[128,1024]{1,0:T(8,128)S(1)}) fusion(f32[128,1024]{1,0:T(8,128)S(1)} %collective-permute-done.12, f32[128,1024]{1,0:T(8,128)} %get-tuple-element.57, pred[]{:T(512)S(6)} %eq.5), kind=kLoop, calls=%fused_computation.13 | loop fusion | flops 262144 | bytes 2097153 | tf_op jit(solution)/shard_map/jit(_where)/select_n | solution.py:461
  71.1 0.1 fusion
  71.3 1.6 %collective-permute-start.13 = (bf16[32,2048]{1,0:T(8,128)(2,1)S(1)}, bf16[32,2048]{1,0:T(8,128)(2,1)S(1)}, u32[]{:S(2)}, u32[]{:S(2)}) collective-permute-start(bf16[32,2048]{1,0:T(8,128)(2,1)S(1)} %get-tuple-element.71), channel_id=1, source_target_pairs={{0,2},{1,3},{2,4},{3,5},{4,6},{5,7},{6,0},{7,1},{8,10},{9,11},{10,... | collective-permute-start | bytes 393224 | tf_op jit(solution)/shard_map/ppermute | solution.py:447
  72.9 3.0 %collective-permute-start.14 = (bf16[32,2048]{1,0:T(8,128)(2,1)S(1)}, bf16[32,2048]{1,0:T(8,128)(2,1)S(1)}, u32[]{:S(2)}, u32[]{:S(2)}) collective-permute-start(bf16[32,2048]{1,0:T(8,128)(2,1)S(1)} %get-tuple-element.70), channel_id=1, source_target_pairs={{0,4},{1,5},{2,6},{3,7},{4,0},{5,1},{6,2},{7,3},{8,12},{9,13},{10,... | collective-permute-start | bytes 393224 | tf_op jit(solution)/shard_map/ppermute | solution.py:447
  75.9 8.3 %collective-permute-done.10.refs_2_ = bf16[32,8192]{1,0:T(8,128)(2,1)S(1)} collective-permute-done((bf16[32,8192]{1,0:T(8,128)(2,1)S(1)}, bf16[32,8192]{1,0:T(8,128)(2,1)S(1)}, u32[]{:S(2)}, u32[]{:S(2)}) %collective-permute-start.10) | collective-permute-done | bytes 524320 | tf_op jit(solution)/shard_map/ppermute | solution.py:447
  84.2 0.7 collective-permute-start.15
  85.0 0.0 copy-start.18
  85.0 8.5 %collective-permute-done.11.refs_3_ = bf16[32,8192]{1,0:T(8,128)(2,1)S(1)} collective-permute-done((bf16[32,8192]{1,0:T(8,128)(2,1)S(1)}, bf16[32,8192]{1,0:T(8,128)(2,1)S(1)}, u32[]{:S(2)}, u32[]{:S(2)}) %collective-permute-start.11) | collective-permute-done | bytes 524320 | tf_op jit(solution)/shard_map/ppermute | solution.py:447
  93.5 1.4 %collective-permute-done.9.refs_1_ = bf16[32,8192]{1,0:T(8,128)(2,1)S(1)} collective-permute-done((bf16[32,8192]{1,0:T(8,128)(2,1)S(1)}, bf16[32,8192]{1,0:T(8,128)(2,1)S(1)}, u32[]{:S(2)}, u32[]{:S(2)}) %collective-permute-start.9) | collective-permute-done | bytes 524320 | tf_op jit(solution)/shard_map/ppermute | solution.py:447
  94.9 3.2 %collective-permute-done.13.refs_5_ = bf16[32,2048]{1,0:T(8,128)(2,1)S(1)} collective-permute-done((bf16[32,2048]{1,0:T(8,128)(2,1)S(1)}, bf16[32,2048]{1,0:T(8,128)(2,1)S(1)}, u32[]{:S(2)}, u32[]{:S(2)}) %collective-permute-start.13) | collective-permute-done | bytes 131104 | tf_op jit(solution)/shard_map/ppermute | solution.py:447
  98.2 2.3 %collective-permute-done.14.refs_6_ = bf16[32,2048]{1,0:T(8,128)(2,1)S(1)} collective-permute-done((bf16[32,2048]{1,0:T(8,128)(2,1)S(1)}, bf16[32,2048]{1,0:T(8,128)(2,1)S(1)}, u32[]{:S(2)}, u32[]{:S(2)}) %collective-permute-start.14) | collective-permute-done | bytes 131104 | tf_op jit(solution)/shard_map/ppermute | solution.py:447
  100.5 1.1 %last_sum.1 = bf16[32,8192]{1,0:T(8,128)(2,1)} custom-call(f32[32,8192]{1,0:T(8,128)S(1)} %copy-done.3, bf16[32,8192]{1,0:T(8,128)(2,1)S(1)} %collective-permute-done.9.refs_1_, bf16[32,8192]{1,0:T(8,128)(2,1)S(1)} %collective-permute-done.10.refs_2_, bf16[32,8192]{1,0:T(8,128)(2,1)S(1)} %collective-permute-done.11.refs_3_, f32[32,2048]{1,0:T(8,128)S(1)} %fusion.3.refs_4_, ...), custom_call_target="tpu_custom_call" | custom-call | flops 1310720 | bytes 4194304 | tf_op jit(solution)/shard_map/last_sum/pallas_call | solution.py:380
  101.6 0.0 copy-start.20
  101.6 0.0 copy-start.21
  101.6 1.4 %multiply_subtract_fusion = (f32[1024,64]{0,1:T(8,128)}, f32[1024,64]{0,1:T(8,128)}, f32[1024,64]{0,1:T(8,128)}) fusion(f32[1024,64]{0,1:T(8,128)S(1)} %copy-done.16, f32[1024,64]{0,1:T(8,128)S(1)} %copy-done.17, f32[1024,64]{0,1:T(8,128)S(1)} %copy-done.18, bf16[512,1408]{1,0:T(8,128)(2,1)S(1)} %bitcast.14), kind=kOutput, calls=%fused_computation.10 | convolution fusion | flops 68157440 | bytes 2752512 | tf_op jit(solution)/shard_map/dot_general | solution.py:34
  103.1 0.9 multiply_subtract_fusion.1
  (50 shorter events, 0.2 us)
Async XLA Ops:
  0.6 6.5 %copy-start.8 = (s32[256,1]{0,1:T(1,128)S(1)}, s32[256,1]{0,1:T(1,128)}, u32[]{:S(2)}) copy-start(s32[256,1]{0,1:T(1,128)} %param.26) | copy-start | bytes 3076
  0.6 6.5 %copy-start.7 = (bf16[256,256]{1,0:T(8,128)(2,1)S(1)}, bf16[256,256]{1,0:T(8,128)(2,1)}, u32[]{:S(2)}) copy-start(bf16[256,256]{1,0:T(8,128)(2,1)} %cot_ref.1) | copy-start | bytes 393220
  0.7 6.5 %copy-start.2 = (bf16[2048,256]{1,0:T(8,128)(2,1)S(1)}, bf16[2048,256]{1,0:T(8,128)(2,1)}, u32[]{:S(2)}) copy-start(bf16[2048,256]{1,0:T(8,128)(2,1)} %up_ref.1) | copy-start | bytes 3145732
  0.7 6.5 %copy-start.10 = (s32[32]{0:T(128)S(1)}, s32[32]{0:T(128)}, u32[]{:S(2)}) copy-start(s32[32]{0:T(128)} %bucket_ref.1) | copy-start | bytes 388
  0.7 6.5 %copy-start.11 = (s32[32]{0:T(128)S(1)}, s32[32]{0:T(128)}, u32[]{:S(2)}) copy-start(s32[32]{0:T(128)} %owner_ref.1) | copy-start | bytes 388
  0.7 6.5 %copy-start.9 = (s32[32]{0:T(128)S(1)}, s32[32]{0:T(128)}, u32[]{:S(2)}) copy-start(s32[32]{0:T(128)} %live_ref.1) | copy-start | bytes 388
  2.7 14.8 %all-to-all-start = ((bf16[8,32,1024]{2,1,0:T(8,128)(2,1)}), bf16[8,32,1024]{2,1,0:T(8,128)(2,1)S(1)}, u32[]{:S(2)}, u32[]{:S(2)}) async-start(bf16[8,32,1024]{2,1,0:T(8,128)(2,1)} %bitcast.10), calls=%async_computation | async-start | bytes 1048576 | tf_op jit(solution)/shard_map/all_to_all | solution.py:415
  8.3 0.7 copy-start.5
  9.0 0.7 copy-start.6
  9.6 7.1 %collective-permute-start = (f32[256,64]{1,0:T(8,128)S(1)}, f32[256,64]{1,0:T(8,128)S(1)}, u32[]{:S(2)}, u32[]{:S(2)}) collective-permute-start(f32[256,64]{1,0:T(8,128)S(1)} %get-tuple-element.35), channel_id=1, source_target_pairs={{0,1},{1,0},{2,3},{3,2},{4,5},{5,4},{6,7},{7,6},{8,9},{9,8},{10,11... | collective-permute-start | bytes 196616 | tf_op jit(solution)/shard_map/ppermute | solution.py:40
  17.5 0.8 copy-start
  24.6 15.5 %copy-start.1 = (bf16[8,32,1024]{2,1,0:T(8,128)(2,1)S(1)}, bf16[8,32,1024]{2,1,0:T(8,128)(2,1)}, u32[]{:S(2)}) copy-start(bf16[8,32,1024]{2,1,0:T(8,128)(2,1)} %copy-done) | copy-start | bytes 1572868
  24.6 1.6 %collective-permute-start.1 = (f32[256,64]{1,0:T(8,128)}, f32[256,64]{1,0:T(8,128)S(1)}, u32[]{:S(2)}, u32[]{:S(2)}) collective-permute-start(f32[256,64]{1,0:T(8,128)} %low_rank.1), channel_id=1, source_target_pairs={{0,1},{1,0},{2,3},{3,2},{4,5},{5,4},{6,7},{7,6},{8,9},{9,8},{10,11... | collective-permute-start | bytes 196616 | tf_op jit(solution)/shard_map/ppermute | solution.py:40
  27.3 6.4 %collective-permute-start.2 = (f32[256,128]{1,0:T(8,128)S(1)}, f32[256,128]{1,0:T(8,128)S(1)}, u32[]{:S(2)}, u32[]{:S(2)}) collective-permute-start(f32[256,128]{1,0:T(8,128)S(1)} %pad_maximum_fusion.1), channel_id=1, source_target_pairs={{0,2},{1,3},{2,0},{3,1},{4,6},{5,7},{6,4},{7,5},{8,10},{9,11},{10,... | collective-permute-start | bytes 393224 | tf_op jit(solution)/shard_map/ppermute | solution.py:40
  28.3 9.3 %collective-permute-start.3 = (f32[256,128]{1,0:T(8,128)S(1)}, f32[256,128]{1,0:T(8,128)S(1)}, u32[]{:S(2)}, u32[]{:S(2)}) collective-permute-start(f32[256,128]{1,0:T(8,128)S(1)} %pad_maximum_fusion.1), channel_id=1, source_target_pairs={{0,4},{1,5},{2,6},{3,7},{4,0},{5,1},{6,2},{7,3},{8,12},{9,13},{10,... | collective-permute-start | bytes 393224 | tf_op jit(solution)/shard_map/ppermute | solution.py:40
  31.0 9.0 %collective-permute-start.4 = (f32[256,128]{1,0:T(8,128)S(1)}, f32[256,128]{1,0:T(8,128)S(1)}, u32[]{:S(2)}, u32[]{:S(2)}) collective-permute-start(f32[256,128]{1,0:T(8,128)S(1)} %pad_maximum_fusion.1), channel_id=1, source_target_pairs={{0,6},{1,7},{2,4},{3,5},{4,2},{5,3},{6,0},{7,1},{8,14},{9,15},{10,... | collective-permute-start | bytes 393224 | tf_op jit(solution)/shard_map/ppermute | solution.py:40
  32.0 20.9 %collective-permute-start.5 = (f32[128,2048]{1,0:T(8,128)}, f32[128,2048]{1,0:T(8,128)S(1)}, u32[]{:S(2)}, u32[]{:S(2)}) collective-permute-start(f32[128,2048]{1,0:T(8,128)} %get-tuple-element.44), channel_id=1, source_target_pairs={{0,1},{1,0},{2,3},{3,2},{4,5},{5,4},{6,7},{7,6},{8,9},{9,8},{10,11... | collective-permute-start | bytes 3145736 | tf_op jit(solution)/shard_map/ppermute | solution.py:40
  32.0 20.9 %collective-permute-start.6 = (f32[128,2048]{1,0:T(8,128)}, f32[128,2048]{1,0:T(8,128)}, u32[]{:S(2)}, u32[]{:S(2)}) collective-permute-start(f32[128,2048]{1,0:T(8,128)} %get-tuple-element.45), channel_id=1, source_target_pairs={{0,1},{1,0},{2,3},{3,2},{4,5},{5,4},{6,7},{7,6},{8,9},{9,8},{10,11... | collective-permute-start | bytes 3145736 | tf_op jit(solution)/shard_map/ppermute | solution.py:40
  33.7 19.3 %collective-permute-start.7 = (f32[128,2048]{1,0:T(8,128)}, f32[128,2048]{1,0:T(8,128)}, u32[]{:S(2)}, u32[]{:S(2)}) collective-permute-start(f32[128,2048]{1,0:T(8,128)} %get-tuple-element.46), channel_id=1, source_target_pairs={{0,1},{1,0},{2,3},{3,2},{4,5},{5,4},{6,7},{7,6},{8,9},{9,8},{10,11... | collective-permute-start | bytes 3145736 | tf_op jit(solution)/shard_map/ppermute | solution.py:40
  37.6 15.4 %collective-permute-start.8 = (f32[128,2048]{1,0:T(8,128)}, f32[128,2048]{1,0:T(8,128)}, u32[]{:S(2)}, u32[]{:S(2)}) collective-permute-start(f32[128,2048]{1,0:T(8,128)} %get-tuple-element.47), channel_id=1, source_target_pairs={{0,1},{1,0},{2,3},{3,2},{4,5},{5,4},{6,7},{7,6},{8,9},{9,8},{10,11... | collective-permute-start | bytes 3145736 | tf_op jit(solution)/shard_map/ppermute | solution.py:40
  40.0 1.8 %copy-start.4 = (bf16[256,128]{1,0:T(8,128)(2,1)}, bf16[256,128]{1,0:T(8,128)(2,1)S(1)}, u32[]{:S(2)}) copy-start(bf16[256,128]{1,0:T(8,128)(2,1)S(1)} %multiply_convert_fusion.weight_ref.refs_2_) | copy-start | bytes 196612
  41.8 59.8 %all-to-all-start.1 = ((bf16[32,16,1408]{2,1,0:T(8,128)(2,1)}), bf16[32,16,1408]{2,1,0:T(8,128)(2,1)S(1)}, u32[]{:S(2)}, u32[]{:S(2)}) async-start(bf16[32,16,1408]{2,1,0:T(8,128)(2,1)} %bitcast.3), calls=%async_computation.1 | async-start | bytes 2883584 | tf_op jit(solution)/shard_map/all_to_all | solution.py:441
  53.0 1.0 copy-start.12
  61.7 6.1 %copy-start.15 = (bf16[32,8192]{1,0:T(8,128)(2,1)S(1)}, bf16[32,8192]{1,0:T(8,128)(2,1)}, u32[]{:S(2)}) copy-start(bf16[32,8192]{1,0:T(8,128)(2,1)} %get-tuple-element.54) | copy-start | bytes 1572868
  61.7 6.2 %copy-start.14 = (bf16[32,8192]{1,0:T(8,128)(2,1)S(1)}, bf16[32,8192]{1,0:T(8,128)(2,1)}, u32[]{:S(2)}) copy-start(bf16[32,8192]{1,0:T(8,128)(2,1)} %get-tuple-element.55) | copy-start | bytes 1572868
  61.7 8.2 %copy-start.13 = (bf16[32,8192]{1,0:T(8,128)(2,1)S(1)}, bf16[32,8192]{1,0:T(8,128)(2,1)}, u32[]{:S(2)}) copy-start(bf16[32,8192]{1,0:T(8,128)(2,1)} %get-tuple-element.53) | copy-start | bytes 1572868
  67.7 2.4 %collective-permute-start.12 = (f32[128,1024]{1,0:T(8,128)}, f32[128,1024]{1,0:T(8,128)S(1)}, u32[]{:S(2)}, u32[]{:S(2)}) collective-permute-start(f32[128,1024]{1,0:T(8,128)} %get-tuple-element.58), channel_id=1, source_target_pairs={{0,1},{1,0},{2,3},{3,2},{4,5},{5,4},{6,7},{7,6},{8,9},{9,8},{10,11... | collective-permute-start | bytes 1572872 | tf_op jit(solution)/shard_map/ppermute | solution.py:40
  67.8 16.4 %collective-permute-start.10 = (bf16[32,8192]{1,0:T(8,128)(2,1)S(1)}, bf16[32,8192]{1,0:T(8,128)(2,1)S(1)}, u32[]{:S(2)}, u32[]{:S(2)}) collective-permute-start(bf16[32,8192]{1,0:T(8,128)(2,1)S(1)} %copy-done.15), channel_id=1, source_target_pairs={{0,4},{1,5},{2,6},{3,7},{4,0},{5,1},{6,2},{7,3},{8,12},{9,13},{10,... | collective-permute-start | bytes 1572872 | tf_op jit(solution)/shard_map/ppermute | solution.py:447
  67.9 25.6 %collective-permute-start.11 = (bf16[32,8192]{1,0:T(8,128)(2,1)S(1)}, bf16[32,8192]{1,0:T(8,128)(2,1)S(1)}, u32[]{:S(2)}, u32[]{:S(2)}) collective-permute-start(bf16[32,8192]{1,0:T(8,128)(2,1)S(1)} %copy-done.14), channel_id=1, source_target_pairs={{0,6},{1,7},{2,0},{3,1},{4,2},{5,3},{6,4},{7,5},{8,14},{9,15},{10,... | collective-permute-start | bytes 1572872 | tf_op jit(solution)/shard_map/ppermute | solution.py:447
  69.8 25.1 %collective-permute-start.9 = (bf16[32,8192]{1,0:T(8,128)(2,1)S(1)}, bf16[32,8192]{1,0:T(8,128)(2,1)S(1)}, u32[]{:S(2)}, u32[]{:S(2)}) collective-permute-start(bf16[32,8192]{1,0:T(8,128)(2,1)S(1)} %copy-done.13), channel_id=1, source_target_pairs={{0,2},{1,3},{2,4},{3,5},{4,6},{5,7},{6,0},{7,1},{8,10},{9,11},{10,... | collective-permute-start | bytes 1572872 | tf_op jit(solution)/shard_map/ppermute | solution.py:447
  71.2 29.3 %copy-start.3 = (f32[32,8192]{1,0:T(8,128)S(1)}, f32[32,8192]{1,0:T(8,128)}, u32[]{:S(2)}) copy-start(f32[32,8192]{1,0:T(8,128)} %get-tuple-element.52.refs_0_) | copy-start | bytes 3145732
  71.3 26.9 %collective-permute-start.13 = (bf16[32,2048]{1,0:T(8,128)(2,1)S(1)}, bf16[32,2048]{1,0:T(8,128)(2,1)S(1)}, u32[]{:S(2)}, u32[]{:S(2)}) collective-permute-start(bf16[32,2048]{1,0:T(8,128)(2,1)S(1)} %get-tuple-element.71), channel_id=1, source_target_pairs={{0,2},{1,3},{2,4},{3,5},{4,6},{5,7},{6,0},{7,1},{8,10},{9,11},{10,... | collective-permute-start | bytes 393224 | tf_op jit(solution)/shard_map/ppermute | solution.py:447
  72.9 27.6 %collective-permute-start.14 = (bf16[32,2048]{1,0:T(8,128)(2,1)S(1)}, bf16[32,2048]{1,0:T(8,128)(2,1)S(1)}, u32[]{:S(2)}, u32[]{:S(2)}) collective-permute-start(bf16[32,2048]{1,0:T(8,128)(2,1)S(1)} %get-tuple-element.70), channel_id=1, source_target_pairs={{0,4},{1,5},{2,6},{3,7},{4,0},{5,1},{6,2},{7,3},{8,12},{9,13},{10,... | collective-permute-start | bytes 393224 | tf_op jit(solution)/shard_map/ppermute | solution.py:447
  84.2 16.3 %collective-permute-start.15 = (bf16[32,2048]{1,0:T(8,128)(2,1)S(1)}, bf16[32,2048]{1,0:T(8,128)(2,1)S(1)}, u32[]{:S(2)}, u32[]{:S(2)}) collective-permute-start(bf16[32,2048]{1,0:T(8,128)(2,1)S(1)} %get-tuple-element.69), channel_id=1, source_target_pairs={{0,6},{1,7},{2,0},{3,1},{4,2},{5,3},{6,4},{7,5},{8,14},{9,15},{10,... | collective-permute-start | bytes 393224 | tf_op jit(solution)/shard_map/ppermute | solution.py:447
  85.0 16.6 %copy-start.16 = (f32[1024,64]{0,1:T(8,128)S(1)}, f32[1024,64]{0,1:T(8,128)}, u32[]{:S(2)}) copy-start(f32[1024,64]{0,1:T(8,128)} %param.20) | copy-start | bytes 786436
  85.0 16.6 %copy-start.17 = (f32[1024,64]{0,1:T(8,128)S(1)}, f32[1024,64]{0,1:T(8,128)}, u32[]{:S(2)}) copy-start(f32[1024,64]{0,1:T(8,128)} %param.21) | copy-start | bytes 786436
  85.0 16.6 %copy-start.18 = (f32[1024,64]{0,1:T(8,128)S(1)}, f32[1024,64]{0,1:T(8,128)}, u32[]{:S(2)}) copy-start(f32[1024,64]{0,1:T(8,128)} %param.22) | copy-start | bytes 786436
  101.6 1.5 %copy-start.19 = (f32[64,256]{1,0:T(8,128)S(1)}, f32[64,256]{1,0:T(8,128)}, u32[]{:S(2)}) copy-start(f32[64,256]{1,0:T(8,128)} %param.23) | copy-start | bytes 196612
  101.6 1.5 %copy-start.20 = (f32[64,256]{1,0:T(8,128)S(1)}, f32[64,256]{1,0:T(8,128)}, u32[]{:S(2)}) copy-start(f32[64,256]{1,0:T(8,128)} %param.24) | copy-start | bytes 196612
  101.6 1.5 %copy-start.21 = (f32[64,256]{1,0:T(8,128)S(1)}, f32[64,256]{1,0:T(8,128)}, u32[]{:S(2)}) copy-start(f32[64,256]{1,0:T(8,128)} %param.25) | copy-start | bytes 196612

commit v7 on v6

--- a/solution.py
+++ b/solution.py
@@ -47,18 +47,17 @@
 
 
 VMEM_LIMIT = 16 * 1024 * 1024
-VMEM_MOST = 60 * 1024 * 1024
 SMEM_SPEC = pl.BlockSpec(memory_space=pltpu.MemorySpace.SMEM)
-HBM = pltpu.MemorySpace.HBM
+VMEM_SPEC = pl.BlockSpec(memory_space=pltpu.MemorySpace.VMEM)
 NT = (((1,), (1,)), ((), ()))
 NN = (((1,), (0,)), ((), ()))
 
 
-def call(kernel, out_shape, flops, moved, limit=VMEM_LIMIT, **options):
+def call(kernel, out_shape, flops, moved, **options):
     return pl.pallas_call(
         kernel,
         out_shape=out_shape,
-        compiler_params=pltpu.CompilerParams(vmem_limit_bytes=limit),
+        compiler_params=pltpu.CompilerParams(vmem_limit_bytes=VMEM_LIMIT),
         cost_estimate=pl.CostEstimate(flops=flops, bytes_accessed=moved, transcendentals=0),
         **options,
     )
@@ -70,27 +69,6 @@
 
 def lane_slot(shape, first):
     return (lax.broadcasted_iota(jnp.int32, shape, 1) // PADDED_RANK + first).astype(jnp.float32)
-
-
-class Stream:
-    def __init__(self, sources, targets, sems, depth=3):
-        self.copies = [
-            pltpu.make_async_copy(source, target, sems.at[i])
-            for i, (source, target) in enumerate(zip(sources, targets, strict=True))
-        ]
-        self.depth = depth
-        for copy in self.copies[:depth]:
-            copy.start()
-
-    def wait(self, c):
-        self.copies[c].wait()
-        if c + self.depth < len(self.copies):
-            self.copies[c + self.depth].start()
-
-
-def row_parts(ref, parts):
-    rows = ref.shape[0] // parts
-    return [ref.at[pl.ds(i * rows, rows), :] for i in range(parts)]
 
 
 def prep_kernel(rows_own, live_ref, bucket_ref, owner_ref, adapter_ref, cot_ref, up_ref,
@@ -161,25 +139,19 @@
         shapes,
         2 * tokens * kv * up_factors.shape[0],
         up_factors.size * 2,
-        in_specs=[SMEM_SPEC] * 3
-        + [pl.BlockSpec(v.shape) for v in (adapter_row, cotangent, up_factors)],
+        in_specs=[SMEM_SPEC] * 3 + [VMEM_SPEC] * 3,
+        out_specs=(VMEM_SPEC,) * len(shapes),
         name="prep",
     )(live, bucket, owner, adapter_row, cotangent, up_factors)
 
 
-def frozen_kernel(turned_ref, frozen_any, *refs):
-    outs, (frozen_ref, sems) = refs[:-2], refs[-2:]
-    steps = sems.shape[0]
-    half = outs[0].shape[0]
-    chunk = frozen_ref.shape[0] // steps
-    per_part = steps // len(outs)
-    stream = Stream(row_parts(frozen_any, steps), row_parts(frozen_ref, steps), sems)
-    theirs = turned_ref[half:, :]
-    for c in range(steps):
-        stream.wait(c)
-        first = c % per_part * chunk
-        outs[c // per_part][:, first : first + chunk] = dot(
-            theirs, frozen_ref[c * chunk : (c + 1) * chunk, :], NT
+def frozen_kernel(turned_ref, frozen_ref, *theirs_refs):
+    half, part_width = theirs_refs[0].shape
+    chunk = 512
+    for first in range(0, frozen_ref.shape[0], chunk):
+        at = first % part_width
+        theirs_refs[first // part_width][:, at : at + chunk] = dot(
+            turned_ref[half:, :], frozen_ref[first : first + chunk, :], NT
         )
 
 
@@ -191,12 +163,8 @@
         (jax.ShapeDtypeStruct((tokens // 2, width // parts), jnp.float32),) * parts,
         tokens * kv * width,
         2 * kv * width + 2 * tokens * width,
-        VMEM_MOST,
-        in_specs=[pl.BlockSpec(turned.shape), pl.BlockSpec(memory_space=HBM)],
-        scratch_shapes=[
-            pltpu.VMEM(frozen.shape, frozen.dtype),
-            pltpu.SemaphoreType.DMA((8,)),
-        ],
+        in_specs=[VMEM_SPEC] * 2,
+        out_specs=(VMEM_SPEC,) * parts,
         name="frozen_term",
     )(turned, frozen)
 
@@ -220,71 +188,55 @@
         jax.ShapeDtypeStruct((rows, columns), jnp.bfloat16),
         2 * rows * columns * tokens,
         2 * (rows + tokens) * columns,
+        in_specs=[VMEM_SPEC] * (len(parts) + 1),
+        out_specs=VMEM_SPEC,
         name="pack",
     )(place, *parts)
 
 
-def factor_stream(factors_any, held_ref, sems):
-    parts, _, chunk = held_ref.shape
-    return Stream(
-        [factors_any.at[:, pl.ds(c * chunk, chunk)] for c in range(parts)],
-        [held_ref.at[c] for c in range(parts)],
-        sems,
-    )
-
-
-def down_kernel(hidden_ref, slot_ref, factors_any, out_ref, held_ref, sems):
-    parts, _, chunk = held_ref.shape
-    tokens = hidden_ref.shape[0]
-    stream = factor_stream(factors_any, held_ref, sems)
+CHUNK = 256
+PARTS = 4
+
+
+def down_kernel(hidden_ref, slot_ref, up_own_ref, factors_ref, out_ref):
     slot = slot_ref[...]
-    acc = jnp.zeros((tokens, 128), jnp.float32)
-    for c in range(parts):
-        stream.wait(c)
-        product = dot(hidden_ref[...], held_ref[c], NN)
-        for d in range(chunk // 128):
-            hit = slot == lane_slot((1, 128), (c * chunk + d * 128) // PADDED_RANK)
-            acc = acc + jnp.where(hit, product[:, d * 128 : (d + 1) * 128], 0.0)
-    out_ref[...] = acc[:, :PADDED_RANK] + acc[:, PADDED_RANK:]
-
-
-def low_rank(hidden_columns, slot_wide, factors):
-    tokens, columns = hidden_columns.shape
-    chunk = 256
-    parts = factors.shape[1] // chunk
+    acc = jnp.zeros(slot.shape, jnp.float32)
+    for first in range(0, factors_ref.shape[1], CHUNK):
+        product = dot(hidden_ref[...], factors_ref[:, first : first + CHUNK], NN)
+        for d in range(0, CHUNK, 128):
+            hit = slot == lane_slot((1, 128), (first + d) // PADDED_RANK)
+            acc = acc + jnp.where(hit, product[:, d : d + 128], 0.0)
+    out_ref[:, :PADDED_RANK] = acc[:, :PADDED_RANK] + acc[:, PADDED_RANK:]
+    out_ref[:, PADDED_RANK:] = up_own_ref[...]
+
+
+def low_rank(hidden_columns, slot_wide, up_own, factors):
+    tokens = hidden_columns.shape[0]
     return call(
         down_kernel,
-        jax.ShapeDtypeStruct((tokens, PADDED_RANK), jnp.float32),
+        jax.ShapeDtypeStruct((tokens, 2 * PADDED_RANK), jnp.float32),
         2 * tokens * factors.size,
         2 * factors.size,
-        VMEM_MOST,
-        in_specs=[pl.BlockSpec(v.shape) for v in (hidden_columns, slot_wide)]
-        + [pl.BlockSpec(memory_space=HBM)],
-        scratch_shapes=[
-            pltpu.VMEM((parts, columns, chunk), jnp.bfloat16),
-            pltpu.SemaphoreType.DMA((parts,)),
-        ],
+        in_specs=[VMEM_SPEC] * 4,
+        out_specs=VMEM_SPEC,
         name="low_rank",
-    )(hidden_columns, slot_wide, factors)
-
-
-def extra_kernel(rows_own, weight_ref, slot_ref, factors_any, ours_ref, theirs_ref, held_ref,
-                 extra_ref, sems):
-    parts, _, chunk = held_ref.shape
+    )(hidden_columns, slot_wide, up_own, factors)
+
+
+def extra_kernel(rows_own, weight_ref, slot_ref, factors_ref, ours_ref, theirs_ref, extra_ref):
     tokens = weight_ref.shape[0]
     n_chip = tokens // rows_own // 2
-    stream = factor_stream(factors_any, held_ref, sems)
     slot = slot_ref[...]
     weight = weight_ref[:, PADDED_RANK:].astype(jnp.float32)
     double = jnp.concatenate([weight, weight], axis=1)
-    for c in range(parts):
-        stream.wait(c)
+    for first in range(0, factors_ref.shape[1], CHUNK):
         pieces = []
-        for d in range(chunk // 128):
-            hit = slot == lane_slot((1, 128), (c * chunk + d * 128) // PADDED_RANK)
+        for d in range(0, CHUNK, 128):
+            hit = slot == lane_slot((1, 128), (first + d) // PADDED_RANK)
             pieces.append(jnp.where(hit, double, 0.0).astype(jnp.bfloat16))
-        term = dot(jnp.concatenate(pieces, axis=1), held_ref[c], NT)
-        if c == 0:
+        placed = jnp.concatenate(pieces, axis=1)
+        term = dot(placed, factors_ref[:, first : first + CHUNK], NT)
+        if first == 0:
             extra_ref[...] = term
         else:
             extra_ref[...] += term
@@ -299,63 +251,47 @@
 
 def extra_term(rows_own, weights, slot_wide, factors):
     tokens, columns = weights.shape[0], factors.shape[0]
-    chunk = 256
-    parts = factors.shape[1] // chunk
     half = jax.ShapeDtypeStruct((tokens // 2, columns), jnp.float32)
     return call(
         functools.partial(extra_kernel, rows_own),
         (half, half),
         2 * tokens * factors.size,
         2 * factors.size,
-        VMEM_MOST,
-        in_specs=[pl.BlockSpec(v.shape) for v in (weights, slot_wide)]
-        + [pl.BlockSpec(memory_space=HBM)],
-        scratch_shapes=[
-            pltpu.VMEM((parts, columns, chunk), jnp.bfloat16),
-            pltpu.VMEM((tokens, columns), jnp.float32),
-            pltpu.SemaphoreType.DMA((parts,)),
-        ],
+        in_specs=[VMEM_SPEC] * 3,
+        out_specs=(VMEM_SPEC,) * 2,
+        scratch_shapes=[pltpu.VMEM((tokens, columns), jnp.float32)],
         name="extra_term",
     )(weights, slot_wide, factors)
 
 
-def pair_kernel(rows_own, parts, turned_ref, frozen_any, *refs):
-    pair_refs, outs, (frozen_ref, sems) = refs[:parts], refs[parts:-2], refs[-2:]
-    steps = sems.shape[0]
-    half = turned_ref.shape[0] // 2
-    columns = frozen_ref.shape[0] // steps
-    per_part = steps // parts
-    stream = Stream(row_parts(frozen_any, steps), row_parts(frozen_ref, steps), sems)
-    ours = turned_ref[:half, :]
-    for c in range(steps):
-        stream.wait(c)
-        at = slice(c * columns, (c + 1) * columns)
-        first = c % per_part * columns
-        total = dot(ours, frozen_ref[at, :], NT)
-        total = total + pair_refs[c // per_part][:, first : first + columns]
+def pair_kernel(rows_own, turned_ref, frozen_ref, *refs):
+    half, part_width = refs[0].shape
+    width = frozen_ref.shape[0]
+    parts = width // part_width
+    pair_refs, outs = refs[:parts], refs[parts:]
+    chunk = 512
+    for first in range(0, width, chunk):
+        at = slice(first, first + chunk)
+        inner = first % part_width
+        total = dot(turned_ref[:half, :], frozen_ref[at, :], NT)
+        total = total + pair_refs[first // part_width][:, inner : inner + chunk]
         outs[0][:, at] = total[:rows_own, :]
-        for i, out in enumerate(outs[1:]):
-            out[:, at] = total[(i + 1) * rows_own : (i + 2) * rows_own, :].astype(jnp.bfloat16)
+        for i, out in enumerate(outs[1:], 1):
+            out[:, at] = total[i * rows_own : (i + 1) * rows_own, :].astype(jnp.bfloat16)
 
 
 def pair_sum(rows_own, turned, frozen, from_pair):
-    parts = len(from_pair)
-    half = turned.shape[0] // 2
+    half = from_pair[0].shape[0]
     width, kv = frozen.shape
     sent = jax.ShapeDtypeStruct((rows_own, width), jnp.bfloat16)
     n_out = half // rows_own - 1
     return call(
-        functools.partial(pair_kernel, rows_own, parts),
+        functools.partial(pair_kernel, rows_own),
         (jax.ShapeDtypeStruct((rows_own, width), jnp.float32),) + (sent,) * n_out,
         2 * half * width * kv,
         2 * kv * width + 6 * half * width,
-        VMEM_MOST,
-        in_specs=[pl.BlockSpec(turned.shape), pl.BlockSpec(memory_space=HBM)]
-        + [pl.BlockSpec(v.shape) for v in from_pair],
-        scratch_shapes=[
-            pltpu.VMEM(frozen.shape, frozen.dtype),
-            pltpu.SemaphoreType.DMA((8,)),
-        ],
+        in_specs=[VMEM_SPEC] * (2 + len(from_pair)),
+        out_specs=(VMEM_SPEC,) * (n_out + 1),
         name="pair_sum",
     )(turned, frozen, *from_pair)
 
@@ -382,7 +318,8 @@
         jax.ShapeDtypeStruct(frozen_terms[0].shape, jnp.bfloat16),
         5 * size,
         16 * size,
-        in_specs=[pl.BlockSpec(v.shape) for v in values],
+        in_specs=[VMEM_SPEC] * len(values),
+        out_specs=VMEM_SPEC,
         name="last_sum",
     )(*values)
 
@@ -424,20 +361,20 @@
         adapter_up_factors,
     )
 
-    frozen_theirs = frozen_term(turned, frozen_key_value, 4)
-    up_own = up_own + swap(up_own, 1, n_tensor)
-    slot_wide, up_own, frozen_theirs = lax.optimization_barrier(
-        (slot_wide, up_own, frozen_theirs)
-    )
+    turned, hidden_columns = lax.optimization_barrier((turned, hidden_columns))
+    frozen_theirs = frozen_term(turned, frozen_key_value, PARTS)
+
+    own = low_rank(hidden_columns, slot_wide, up_own, adapter_down_factors)
+    own = own + swap(own, 1, n_tensor)
+    own, frozen_theirs = lax.optimization_barrier((own, frozen_theirs))
+    weights = (sum_over_chips(own, n_tensor) * factor_wide).astype(jnp.bfloat16)
+
     from_pair = [swap(theirs, 1, n_tensor) for theirs in frozen_theirs]
-
-    own = low_rank(hidden_columns, slot_wide, adapter_down_factors)
-    own = jnp.concatenate([own + swap(own, 1, n_tensor), up_own], axis=1)
-    weights = (sum_over_chips(own, n_tensor) * factor_wide).astype(jnp.bfloat16)
     total, *sent = pair_sum(rows_own, turned, frozen_key_value, from_pair)
 
     packed = pack_rows(place, [hidden_columns, masked, weights], n_slot * CAP)
-    after = lax.optimization_barrier((weights, total, sent))
+    packed, weights = lax.optimization_barrier((packed, weights))
+    weights, total, sent = lax.optimization_barrier((weights, total, sent))
     owned = lax.all_to_all(
         packed.reshape(n_slot, CAP, -1), "dp", 0, 0, tiled=True
     ).reshape(n_slot * CAP, -1)
@@ -450,7 +387,6 @@
             for step, value in enumerate(sent, 1)
         ]
 
-    weights, total, sent = after
     arrived = to_chips(sent)
     extra_ours, extra_theirs = extra_term(rows_own, weights, slot_wide, adapter_down_factors)
     extra_pair = swap(extra_theirs, 1, n_tensor)

time: 105 us -> 97.3 us (0.927)
  Pallas kernels: 30.5 us -> 12.7 us
  waiting for transfers between devices: 33.5 us -> 36.9 us
  local copies, waits for them, and re-layouts: 5.14 us -> 8.5 us
  starting transfers between devices: 29.2 us -> 31.8 us
  matrix products: 2.34 us -> 4.65 us
  other arithmetic: 2.26 us -> 0.24 us
    pallas_call x2, Pallas kernels: 14 us -> 4.51 us  [the longest x1 3.19 us: pair_sum(): call(functools.partial(pair_kernel, rows_own), (jax.ShapeDtypeStruct((row...]
    all_to_all x1, waiting for transfers between devices: 0.72 us -> 7.86 us  [local(): lax.all_to_all(blocks, 'tensor', 0, 0, tiled=True).reshape(tokens, columns)]
    pallas_call x1, Pallas kernels: 5.98 us -> 1.36 us  [extra_term(): call(functools.partial(extra_kernel, rows_own), (half, half), 2 * tokens...]
    pallas_call x1, Pallas kernels: 6.59 us -> 2.98 us  [frozen_term(): call(frozen_kernel, (jax.ShapeDtypeStruct((tokens // 2, width // parts),...]
    ppermute x10 -> x9, waiting for transfers between devices: 8.98 us -> 5.52 us  [swap(): return lax.ppermute(value, 'tensor', [(i, i ^ mask) for i in range(count)])]
    unnamed x44 -> x46, local copies, waits for them, and re-layouts: 3.14 us -> 6.5 us
    ppermute x6, starting transfers between devices: 7.56 us -> 10.6 us  [to_chips(): lax.ppermute(value, 'tensor', [(i, (i + 2 * step) % n_tensor) for i in ra...]
    dot_general x2, matrix products: 2.34 us -> 4.65 us  [contract_helper(): lax.dot_general(left, right, (((left_dim,), (right_dim,)), ((), ())), pre...]
  transfers between devices with their start and end apart: 18 -> 17, of which waited for: 10 -> 6; matrix products, arithmetic and copies ran while one was open for 1% -> 0% of each run, Pallas kernels for 23% -> 12%
where the time goes in v7:
time: 97.3 us; the launch traced here: 95.8 us
  waiting for transfers between devices  36.9 us (38%)
  starting transfers between devices  31.8 us (33%)
  Pallas kernels  12.7 us (13%)
  local copies, waits for them, and re-layouts  8.5 us (9%)
  matrix products  4.65 us (5%)
  between operations  1.04 us (1%)
    ppermute x6, waiting for transfers between devices, to_chips(): lax.ppermute(value, 'tensor', [(i, (i + 2 * step) % n_tensor) for i in ra...  23.5 us
    all_to_all x1, starting transfers between devices, local(): lax.all_to_all(packed.reshape(n_slot, CAP, -1), 'dp', 0, 0, tiled=True)  11.2 us
    ppermute x6, starting transfers between devices, to_chips(): lax.ppermute(value, 'tensor', [(i, (i + 2 * step) % n_tensor) for i in ra...  10.6 us
    all_to_all x1, waiting for transfers between devices, local(): lax.all_to_all(blocks, 'tensor', 0, 0, tiled=True).reshape(tokens, columns)  7.86 us
    unnamed x46, local copies, waits for them, and re-layouts  6.5 us
    ppermute x9, waiting for transfers between devices, swap(): return lax.ppermute(value, 'tensor', [(i, i ^ mask) for i in range(count)])  5.52 us
    ppermute x9, starting transfers between devices, swap(): return lax.ppermute(value, 'tensor', [(i, i ^ mask) for i in range(count)])  5.49 us
    dot_general x2, matrix products, contract_helper(): lax.dot_general(left, right, (((left_dim,), (right_dim,)), ((), ())), pre...  4.65 us
  transfers between devices with their start and end apart: 17, of which 6 were waited for; matrix products, arithmetic and copies ran while one was open for 0% of the time, Pallas kernels for 12%

profile of v7, /device:TPU:32, one launch (start us, length us, event | category | flops | bytes accessed | tf_op | source)
XLA Modules:
  0.0 95.8 jit_solution(15974902124128183122)
XLA Ops:
  0.7 2.0 %copy.25 = bf16[4,8,8,1024]{3,2,0,1:T(8,128)(2,1)} copy(bf16[4,8,8,1024]{3,2,1,0:T(8,128)(2,1)} %bitcast.14) | data formatting | bytes 1048576 | tf_op jit(solution)/shard_map/reshape | solution.py:351
  2.7 4.5 %all-to-all-start = ((bf16[8,32,1024]{2,1,0:T(8,128)(2,1)}), bf16[8,32,1024]{2,1,0:T(8,128)(2,1)S(1)}, u32[]{:S(2)}, u32[]{:S(2)}) async-start(bf16[8,32,1024]{2,1,0:T(8,128)(2,1)} %bitcast.10), calls=%async_computation | async-start | bytes 1048576 | tf_op jit(solution)/shard_map/all_to_all | solution.py:352
  7.2 1.1 %prep.1 = (bf16[256,256]{1,0:T(8,128)(2,1)S(1)}, bf16[256,256]{1,0:T(8,128)(2,1)S(1)}, f32[256,128]{1,0:T(8,128)S(1)}, f32[256,128]{1,0:T(8,128)S(1)}, s32[1,256]{1,0:T(1,128)S(1)}, /*index=5*/f32[256,64]{1,0:T(8,128)S(1)}) custom-call(s32[32]{0:T(128)S(1)} %copy-done.11, s32[32]{0:T(128)S(1)} %copy-done.12, s32[32]{0:T(128)S(1)} %copy-done.13, ...), custom_call_target="tpu_custom_call" | custom-call | flops 268435456 | bytes 1048576 | tf_op jit(solution)/shard_map/prep/pallas_call | solution.py:137
  8.3 0.0 copy-start.6
  8.3 0.6 copy-done.6
  9.0 0.7 copy-done.8
  9.6 7.9 %all-to-all-done = bf16[8,32,1024]{2,1,0:T(8,128)(2,1)S(1)} async-done(((bf16[8,32,1024]{2,1,0:T(8,128)(2,1)}), bf16[8,32,1024]{2,1,0:T(8,128)(2,1)S(1)}, u32[]{:S(2)}, u32[]{:S(2)}) %all-to-all-start) | async-done | bytes 524320 | tf_op jit(solution)/shard_map/all_to_all | solution.py:352
  17.5 2.2 %copy-done.2 = bf16[1024,2048]{1,0:T(8,128)(2,1)S(1)} copy-done((bf16[1024,2048]{1,0:T(8,128)(2,1)S(1)}, bf16[1024,2048]{1,0:T(8,128)(2,1)}, u32[]{:S(2)}) %copy-start.2) | copy-done | bytes 4194328
  19.7 1.3 %low_rank.1 = f32[256,128]{1,0:T(8,128)S(1)} custom-call(bf16[256,1024]{1,0:T(8,128)(2,1)S(1)} %bitcast.11, f32[256,128]{1,0:T(8,128)S(1)} %get-tuple-element.41.slot_ref, f32[256,64]{1,0:T(8,128)S(1)} %get-tuple-element.42.up_own_ref, bf16[1024,2048]{1,0:T(8,128)(2,1)S(1)} %copy-done.2), custom_call_target="tpu_custom_call" | custom-call | flops 1073741824 | bytes 4194304 | tf_op jit(solution)/shard_map/low_rank/pallas_call | solution.py:215
  21.0 0.0 copy-start.7
  21.0 0.0 copy-start.9
  21.0 0.1 collective-permute-start
  21.1 0.7 copy-done
  21.9 3.0 %frozen_term.1 = (f32[128,2048]{1,0:T(8,128)}, f32[128,2048]{1,0:T(8,128)}, f32[128,2048]{1,0:T(8,128)}, f32[128,2048]{1,0:T(8,128)}) custom-call(bf16[256,256]{1,0:T(8,128)(2,1)S(1)} %get-tuple-element.43.turned_ref, bf16[8192,256]{1,0:T(8,128)(2,1)S(1)} %copy-done), custom_call_target="tpu_custom_call" | custom-call | flops 536870912 | bytes 8388608 | tf_op jit(solution)/shard_map/frozen_term/pallas_call | solution.py:161
  24.9 0.7 collective-permute-start.1
  25.5 2.1 %collective-permute-start.2 = (f32[256,128]{1,0:T(8,128)S(1)}, f32[256,128]{1,0:T(8,128)S(1)}, u32[]{:S(2)}, u32[]{:S(2)}) collective-permute-start(f32[256,128]{1,0:T(8,128)S(1)} %add.46), channel_id=1, source_target_pairs={{0,4},{1,5},{2,6},{3,7},{4,0},{5,1},{6,2},{7,3},{8,12},{9,13},{10,... | collective-permute-start | bytes 393224 | tf_op jit(solution)/shard_map/ppermute | solution.py:40
  27.6 2.1 %collective-permute-start.3 = (f32[256,128]{1,0:T(8,128)S(1)}, f32[256,128]{1,0:T(8,128)S(1)}, u32[]{:S(2)}, u32[]{:S(2)}) collective-permute-start(f32[256,128]{1,0:T(8,128)S(1)} %add.46), channel_id=1, source_target_pairs={{0,6},{1,7},{2,4},{3,5},{4,2},{5,3},{6,0},{7,1},{8,14},{9,15},{10,... | collective-permute-start | bytes 393224 | tf_op jit(solution)/shard_map/ppermute | solution.py:40
  29.7 0.5 collective-permute-start.5
  30.2 1.2 %collective-permute-done.1 = f32[256,128]{1,0:T(8,128)S(1)} collective-permute-done((f32[256,128]{1,0:T(8,128)S(1)}, f32[256,128]{1,0:T(8,128)S(1)}, u32[]{:S(2)}, u32[]{:S(2)}) %collective-permute-start.1) | collective-permute-done | bytes 131104 | tf_op jit(solution)/shard_map/ppermute | solution.py:40
  31.3 2.3 %collective-permute-done.2 = f32[256,128]{1,0:T(8,128)S(1)} collective-permute-done((f32[256,128]{1,0:T(8,128)S(1)}, f32[256,128]{1,0:T(8,128)S(1)}, u32[]{:S(2)}, u32[]{:S(2)}) %collective-permute-start.2) | collective-permute-done | bytes 131104 | tf_op jit(solution)/shard_map/ppermute | solution.py:40
  33.6 2.0 %collective-permute-done.3 = f32[256,128]{1,0:T(8,128)S(1)} collective-permute-done((f32[256,128]{1,0:T(8,128)S(1)}, f32[256,128]{1,0:T(8,128)S(1)}, u32[]{:S(2)}, u32[]{:S(2)}) %collective-permute-start.3) | collective-permute-done | bytes 131104 | tf_op jit(solution)/shard_map/ppermute | solution.py:40
  35.7 0.1 multiply_convert_fusion.refs_2_.weight_ref
  35.7 1.7 %pack.1 = bf16[512,1408]{1,0:T(8,128)(2,1)} custom-call(s32[1,256]{1,0:T(1,128)S(1)} %get-tuple-element.37.place_ref, bf16[256,1024]{1,0:T(8,128)(2,1)S(1)} %bitcast.12, bf16[256,256]{1,0:T(8,128)(2,1)S(1)} %copy-done.9, bf16[256,128]{1,0:T(8,128)(2,1)S(1)} %multiply_convert_fusion.refs_2_.weight_ref), custom_call_target="tpu_custom_call" | custom-call | flops 369098752 | bytes 2162688 | tf_op jit(solution)/shard_map/pack/pallas_call | solution.py:186
  37.4 11.2 %all-to-all-start.1 = ((bf16[32,16,1408]{2,1,0:T(8,128)(2,1)}), bf16[32,16,1408]{2,1,0:T(8,128)(2,1)}, u32[]{:S(2)}, u32[]{:S(2)}) async-start(bf16[32,16,1408]{2,1,0:T(8,128)(2,1)} %bitcast.3), calls=%async_computation.1 | async-start | bytes 2883584 | tf_op jit(solution)/shard_map/all_to_all | solution.py:378
  48.7 0.0 copy-start.1
  48.7 2.2 %copy-done.1 = bf16[8192,256]{1,0:T(8,128)(2,1)S(1)} copy-done((bf16[8192,256]{1,0:T(8,128)(2,1)S(1)}, bf16[8192,256]{1,0:T(8,128)(2,1)}, u32[]{:S(2)}) %copy-start.1) | copy-done | bytes 4194328
  50.9 3.2 %pair_sum.1 = (f32[32,8192]{1,0:T(8,128)S(1)}, bf16[32,8192]{1,0:T(8,128)(2,1)S(1)}, bf16[32,8192]{1,0:T(8,128)(2,1)S(1)}, bf16[32,8192]{1,0:T(8,128)(2,1)S(1)}) custom-call(bf16[256,256]{1,0:T(8,128)(2,1)S(1)} %get-tuple-element.43.turned_ref, bf16[8192,256]{1,0:T(8,128)(2,1)S(1)} %copy-done.1, f32[128,2048]{1,0:T(8,128)S(1)} %collective-permute-done.4.refs_0_, ...), custom_call_target="tpu_custom_call" | custom-call | flops 536870912 | bytes 10485760 | tf_op jit(solution)/shard_map/pair_sum/pallas_call | solution.py:288
  54.1 0.0 copy-start.15
  54.1 1.4 %extra_term.1 = (f32[128,1024]{1,0:T(8,128)S(1)}, f32[128,1024]{1,0:T(8,128)S(1)}) custom-call(bf16[256,128]{1,0:T(8,128)(2,1)S(1)} %multiply_convert_fusion.refs_2_.weight_ref, f32[256,128]{1,0:T(8,128)S(1)} %get-tuple-element.41.slot_ref, bf16[1024,2048]{1,0:T(8,128)(2,1)S(1)} %copy-done.3), custom_call_target="tpu_custom_call" | custom-call | flops 1073741824 | bytes 4194304 | tf_op jit(solution)/shard_map/extra_term/pallas_call | solution.py:255
  55.5 0.1 collective-permute-start.11
  55.6 2.1 %collective-permute-start.10 = (bf16[32,8192]{1,0:T(8,128)(2,1)}, bf16[32,8192]{1,0:T(8,128)(2,1)S(1)}, u32[]{:S(2)}, u32[]{:S(2)}) collective-permute-start(bf16[32,8192]{1,0:T(8,128)(2,1)} %copy-done.16), channel_id=1, source_target_pairs={{0,6},{1,7},{2,0},{3,1},{4,2},{5,3},{6,4},{7,5},{8,14},{9,15},{10,... | collective-permute-start | bytes 1572872 | tf_op jit(solution)/shard_map/ppermute | solution.py:384
  57.8 1.7 %collective-permute-start.9 = (bf16[32,8192]{1,0:T(8,128)(2,1)}, bf16[32,8192]{1,0:T(8,128)(2,1)S(1)}, u32[]{:S(2)}, u32[]{:S(2)}) collective-permute-start(bf16[32,8192]{1,0:T(8,128)(2,1)} %copy-done.14), channel_id=1, source_target_pairs={{0,4},{1,5},{2,6},{3,7},{4,0},{5,1},{6,2},{7,3},{8,12},{9,13},{10,... | collective-permute-start | bytes 1572872 | tf_op jit(solution)/shard_map/ppermute | solution.py:384
  59.5 0.1 broadcast_select_fusion
  59.6 0.1 fusion
  59.7 2.4 %collective-permute-start.12 = (bf16[32,2048]{1,0:T(8,128)(2,1)S(1)}, bf16[32,2048]{1,0:T(8,128)(2,1)S(1)}, u32[]{:S(2)}, u32[]{:S(2)}) collective-permute-start(bf16[32,2048]{1,0:T(8,128)(2,1)S(1)} %get-tuple-element.77), channel_id=1, source_target_pairs={{0,2},{1,3},{2,4},{3,5},{4,6},{5,7},{6,0},{7,1},{8,10},{9,11},{10,... | collective-permute-start | bytes 393224 | tf_op jit(solution)/shard_map/ppermute | solution.py:384
  62.2 0.6 collective-permute-start.13
  62.8 21.1 %collective-permute-done.10.refs_3_ = bf16[32,8192]{1,0:T(8,128)(2,1)S(1)} collective-permute-done((bf16[32,8192]{1,0:T(8,128)(2,1)}, bf16[32,8192]{1,0:T(8,128)(2,1)S(1)}, u32[]{:S(2)}, u32[]{:S(2)}) %collective-permute-start.10) | collective-permute-done | bytes 524320 | tf_op jit(solution)/shard_map/ppermute | solution.py:384
  83.9 3.7 %collective-permute-start.14 = (bf16[32,2048]{1,0:T(8,128)(2,1)S(1)}, bf16[32,2048]{1,0:T(8,128)(2,1)S(1)}, u32[]{:S(2)}, u32[]{:S(2)}) collective-permute-start(bf16[32,2048]{1,0:T(8,128)(2,1)S(1)} %get-tuple-element.75), channel_id=1, source_target_pairs={{0,6},{1,7},{2,0},{3,1},{4,2},{5,3},{6,4},{7,5},{8,14},{9,15},{10,... | collective-permute-start | bytes 393224 | tf_op jit(solution)/shard_map/ppermute | solution.py:384
  87.5 0.0 copy-start.17
  87.5 0.0 copy-start.18
  87.6 0.0 copy-start.19
  87.6 2.5 %collective-permute-done.12.refs_5_ = bf16[32,2048]{1,0:T(8,128)(2,1)S(1)} collective-permute-done((bf16[32,2048]{1,0:T(8,128)(2,1)S(1)}, bf16[32,2048]{1,0:T(8,128)(2,1)S(1)}, u32[]{:S(2)}, u32[]{:S(2)}) %collective-permute-start.12) | collective-permute-done | bytes 131104 | tf_op jit(solution)/shard_map/ppermute | solution.py:384
  90.0 1.1 %last_sum.1 = bf16[32,8192]{1,0:T(8,128)(2,1)} custom-call(f32[32,8192]{1,0:T(8,128)S(1)} %get-tuple-element.59.refs_0_, bf16[32,8192]{1,0:T(8,128)(2,1)S(1)} %collective-permute-done.8.refs_1_, bf16[32,8192]{1,0:T(8,128)(2,1)S(1)} %collective-permute-done.9.refs_2_, bf16[32,8192]{1,0:T(8,128)(2,1)S(1)} %collective-permute-done.10.refs_3_, ...), custom_call_target="tpu_custom_call" | custom-call | flops 1310720 | bytes 4194304 | tf_op jit(solution)/shard_map/last_sum/pallas_call | solution.py:316
  91.1 0.0 copy-start.20
  91.2 0.0 copy-start.21
  91.2 0.0 copy-start.22
  91.2 2.7 %multiply_subtract_fusion = (f32[1024,64]{0,1:T(8,128)}, f32[1024,64]{0,1:T(8,128)}, f32[1024,64]{0,1:T(8,128)}) fusion(f32[1024,64]{0,1:T(8,128)S(1)} %copy-done.17, f32[1024,64]{0,1:T(8,128)S(1)} %copy-done.18, f32[1024,64]{0,1:T(8,128)S(1)} %copy-done.19, bf16[512,1408]{1,0:T(8,128)(2,1)} %bitcast.4), kind=kOutput, calls=%fused_computation.10 | convolution fusion | flops 68157440 | bytes 2752512 | tf_op jit(solution)/shard_map/dot_general | solution.py:34
  93.9 1.9 %multiply_subtract_fusion.1 = (f32[64,256]{1,0:T(8,128)}, f32[64,256]{1,0:T(8,128)}, f32[64,256]{1,0:T(8,128)}) fusion(f32[64,256]{1,0:T(8,128)S(1)} %copy-done.20, f32[64,256]{1,0:T(8,128)S(1)} %copy-done.21, f32[64,256]{1,0:T(8,128)S(1)} %copy-done.22, bf16[512,1408]{1,0:T(8,128)(2,1)} %bitcast.4), kind=kOutput, calls=%fused_computation.18 | convolution fusion | flops 17039360 | bytes 786432 | tf_op jit(solution)/shard_map/dot_general | solution.py:34
  (48 shorter events, 0.2 us)
Async XLA Ops:
  0.6 6.5 %copy-start.10 = (s32[256,1]{0,1:T(1,128)S(1)}, s32[256,1]{0,1:T(1,128)}, u32[]{:S(2)}) copy-start(s32[256,1]{0,1:T(1,128)} %param.26) | copy-start | bytes 3076
  0.6 6.5 %copy-start.5 = (bf16[256,256]{1,0:T(8,128)(2,1)S(1)}, bf16[256,256]{1,0:T(8,128)(2,1)}, u32[]{:S(2)}) copy-start(bf16[256,256]{1,0:T(8,128)(2,1)} %cot_ref.1) | copy-start | bytes 393220
  0.7 6.5 %copy-start.4 = (bf16[2048,256]{1,0:T(8,128)(2,1)S(1)}, bf16[2048,256]{1,0:T(8,128)(2,1)}, u32[]{:S(2)}) copy-start(bf16[2048,256]{1,0:T(8,128)(2,1)} %up_ref.1) | copy-start | bytes 3145732
  0.7 6.5 %copy-start.12 = (s32[32]{0:T(128)S(1)}, s32[32]{0:T(128)}, u32[]{:S(2)}) copy-start(s32[32]{0:T(128)} %bucket_ref.1) | copy-start | bytes 388
  0.7 6.5 %copy-start.13 = (s32[32]{0:T(128)S(1)}, s32[32]{0:T(128)}, u32[]{:S(2)}) copy-start(s32[32]{0:T(128)} %owner_ref.1) | copy-start | bytes 388
  0.7 6.5 %copy-start.11 = (s32[32]{0:T(128)S(1)}, s32[32]{0:T(128)}, u32[]{:S(2)}) copy-start(s32[32]{0:T(128)} %live_ref.1) | copy-start | bytes 388
  2.7 14.8 %all-to-all-start = ((bf16[8,32,1024]{2,1,0:T(8,128)(2,1)}), bf16[8,32,1024]{2,1,0:T(8,128)(2,1)S(1)}, u32[]{:S(2)}, u32[]{:S(2)}) async-start(bf16[8,32,1024]{2,1,0:T(8,128)(2,1)} %bitcast.10), calls=%async_computation | async-start | bytes 1048576 | tf_op jit(solution)/shard_map/all_to_all | solution.py:352
  8.3 0.7 copy-start.6
  9.0 0.7 copy-start.8
  17.5 2.2 %copy-start.2 = (bf16[1024,2048]{1,0:T(8,128)(2,1)S(1)}, bf16[1024,2048]{1,0:T(8,128)(2,1)}, u32[]{:S(2)}) copy-start(bf16[1024,2048]{1,0:T(8,128)(2,1)} %factors_ref.3) | copy-start | bytes 12582916
  19.7 2.2 %copy-start = (bf16[8192,256]{1,0:T(8,128)(2,1)S(1)}, bf16[8192,256]{1,0:T(8,128)(2,1)}, u32[]{:S(2)}) copy-start(bf16[8192,256]{1,0:T(8,128)(2,1)} %frozen_ref.3) | copy-start | bytes 12582916
  21.0 14.7 %copy-start.7 = (f32[256,128]{1,0:T(8,128)S(1)}, f32[256,128]{1,0:T(8,128)}, u32[]{:S(2)}) copy-start(f32[256,128]{1,0:T(8,128)} %copy-done.6) | copy-start | bytes 393220
  21.0 14.7 %copy-start.9 = (bf16[256,256]{1,0:T(8,128)(2,1)S(1)}, bf16[256,256]{1,0:T(8,128)(2,1)}, u32[]{:S(2)}) copy-start(bf16[256,256]{1,0:T(8,128)(2,1)} %copy-done.8) | copy-start | bytes 393220
  21.0 3.8 %collective-permute-start = (f32[256,128]{1,0:T(8,128)S(1)}, f32[256,128]{1,0:T(8,128)S(1)}, u32[]{:S(2)}, u32[]{:S(2)}) collective-permute-start(f32[256,128]{1,0:T(8,128)S(1)} %low_rank.1), channel_id=1, source_target_pairs={{0,1},{1,0},{2,3},{3,2},{4,5},{5,4},{6,7},{7,6},{8,9},{9,8},{10,11... | collective-permute-start | bytes 393224 | tf_op jit(solution)/shard_map/ppermute | solution.py:40
  24.9 6.5 %collective-permute-start.1 = (f32[256,128]{1,0:T(8,128)S(1)}, f32[256,128]{1,0:T(8,128)S(1)}, u32[]{:S(2)}, u32[]{:S(2)}) collective-permute-start(f32[256,128]{1,0:T(8,128)S(1)} %add.46), channel_id=1, source_target_pairs={{0,2},{1,3},{2,0},{3,1},{4,6},{5,7},{6,4},{7,5},{8,10},{9,11},{10,... | collective-permute-start | bytes 393224 | tf_op jit(solution)/shard_map/ppermute | solution.py:40
  25.5 8.1 %collective-permute-start.2 = (f32[256,128]{1,0:T(8,128)S(1)}, f32[256,128]{1,0:T(8,128)S(1)}, u32[]{:S(2)}, u32[]{:S(2)}) collective-permute-start(f32[256,128]{1,0:T(8,128)S(1)} %add.46), channel_id=1, source_target_pairs={{0,4},{1,5},{2,6},{3,7},{4,0},{5,1},{6,2},{7,3},{8,12},{9,13},{10,... | collective-permute-start | bytes 393224 | tf_op jit(solution)/shard_map/ppermute | solution.py:40
  27.6 8.1 %collective-permute-start.3 = (f32[256,128]{1,0:T(8,128)S(1)}, f32[256,128]{1,0:T(8,128)S(1)}, u32[]{:S(2)}, u32[]{:S(2)}) collective-permute-start(f32[256,128]{1,0:T(8,128)S(1)} %add.46), channel_id=1, source_target_pairs={{0,6},{1,7},{2,4},{3,5},{4,2},{5,3},{6,0},{7,1},{8,14},{9,15},{10,... | collective-permute-start | bytes 393224 | tf_op jit(solution)/shard_map/ppermute | solution.py:40
  29.7 19.0 %collective-permute-start.4 = (f32[128,2048]{1,0:T(8,128)}, f32[128,2048]{1,0:T(8,128)S(1)}, u32[]{:S(2)}, u32[]{:S(2)}) collective-permute-start(f32[128,2048]{1,0:T(8,128)} %get-tuple-element.51), channel_id=1, source_target_pairs={{0,1},{1,0},{2,3},{3,2},{4,5},{5,4},{6,7},{7,6},{8,9},{9,8},{10,11... | collective-permute-start | bytes 3145736 | tf_op jit(solution)/shard_map/ppermute | solution.py:40
  29.7 19.0 %collective-permute-start.5 = (f32[128,2048]{1,0:T(8,128)}, f32[128,2048]{1,0:T(8,128)S(1)}, u32[]{:S(2)}, u32[]{:S(2)}) collective-permute-start(f32[128,2048]{1,0:T(8,128)} %get-tuple-element.52), channel_id=1, source_target_pairs={{0,1},{1,0},{2,3},{3,2},{4,5},{5,4},{6,7},{7,6},{8,9},{9,8},{10,11... | collective-permute-start | bytes 3145736 | tf_op jit(solution)/shard_map/ppermute | solution.py:40
  31.3 17.3 %collective-permute-start.6 = (f32[128,2048]{1,0:T(8,128)}, f32[128,2048]{1,0:T(8,128)}, u32[]{:S(2)}, u32[]{:S(2)}) collective-permute-start(f32[128,2048]{1,0:T(8,128)} %get-tuple-element.53), channel_id=1, source_target_pairs={{0,1},{1,0},{2,3},{3,2},{4,5},{5,4},{6,7},{7,6},{8,9},{9,8},{10,11... | collective-permute-start | bytes 3145736 | tf_op jit(solution)/shard_map/ppermute | solution.py:40
  33.6 15.0 %collective-permute-start.7 = (f32[128,2048]{1,0:T(8,128)}, f32[128,2048]{1,0:T(8,128)}, u32[]{:S(2)}, u32[]{:S(2)}) collective-permute-start(f32[128,2048]{1,0:T(8,128)} %get-tuple-element.54), channel_id=1, source_target_pairs={{0,1},{1,0},{2,3},{3,2},{4,5},{5,4},{6,7},{7,6},{8,9},{9,8},{10,11... | collective-permute-start | bytes 3145736 | tf_op jit(solution)/shard_map/ppermute | solution.py:40
  37.4 53.7 %all-to-all-start.1 = ((bf16[32,16,1408]{2,1,0:T(8,128)(2,1)}), bf16[32,16,1408]{2,1,0:T(8,128)(2,1)}, u32[]{:S(2)}, u32[]{:S(2)}) async-start(bf16[32,16,1408]{2,1,0:T(8,128)(2,1)} %bitcast.3), calls=%async_computation.1 | async-start | bytes 2883584 | tf_op jit(solution)/shard_map/all_to_all | solution.py:378
  48.7 2.2 %copy-start.1 = (bf16[8192,256]{1,0:T(8,128)(2,1)S(1)}, bf16[8192,256]{1,0:T(8,128)(2,1)}, u32[]{:S(2)}) copy-start(bf16[8192,256]{1,0:T(8,128)(2,1)} %frozen_ref.3) | copy-start | bytes 12582916
  50.9 3.2 %copy-start.3 = (bf16[1024,2048]{1,0:T(8,128)(2,1)S(1)}, bf16[1024,2048]{1,0:T(8,128)(2,1)}, u32[]{:S(2)}) copy-start(bf16[1024,2048]{1,0:T(8,128)(2,1)} %factors_ref.3) | copy-start | bytes 12582916
  54.1 1.4 %copy-start.14 = (bf16[32,8192]{1,0:T(8,128)(2,1)}, bf16[32,8192]{1,0:T(8,128)(2,1)S(1)}, u32[]{:S(2)}) copy-start(bf16[32,8192]{1,0:T(8,128)(2,1)S(1)} %get-tuple-element.61) | copy-start | bytes 1572868
  54.1 1.4 %copy-start.15 = (bf16[32,8192]{1,0:T(8,128)(2,1)}, bf16[32,8192]{1,0:T(8,128)(2,1)S(1)}, u32[]{:S(2)}) copy-start(bf16[32,8192]{1,0:T(8,128)(2,1)S(1)} %get-tuple-element.60) | copy-start | bytes 1572868
  54.1 1.4 %copy-start.16 = (bf16[32,8192]{1,0:T(8,128)(2,1)}, bf16[32,8192]{1,0:T(8,128)(2,1)S(1)}, u32[]{:S(2)}) copy-start(bf16[32,8192]{1,0:T(8,128)(2,1)S(1)} %get-tuple-element.62) | copy-start | bytes 1572868
  55.5 4.0 %collective-permute-start.11 = (f32[128,1024]{1,0:T(8,128)S(1)}, f32[128,1024]{1,0:T(8,128)S(1)}, u32[]{:S(2)}, u32[]{:S(2)}) collective-permute-start(f32[128,1024]{1,0:T(8,128)S(1)} %get-tuple-element.65), channel_id=1, source_target_pairs={{0,1},{1,0},{2,3},{3,2},{4,5},{5,4},{6,7},{7,6},{8,9},{9,8},{10,11... | collective-permute-start | bytes 1572872 | tf_op jit(solution)/shard_map/ppermute | solution.py:40
  55.6 28.2 %collective-permute-start.10 = (bf16[32,8192]{1,0:T(8,128)(2,1)}, bf16[32,8192]{1,0:T(8,128)(2,1)S(1)}, u32[]{:S(2)}, u32[]{:S(2)}) collective-permute-start(bf16[32,8192]{1,0:T(8,128)(2,1)} %copy-done.16), channel_id=1, source_target_pairs={{0,6},{1,7},{2,0},{3,1},{4,2},{5,3},{6,4},{7,5},{8,14},{9,15},{10,... | collective-permute-start | bytes 1572872 | tf_op jit(solution)/shard_map/ppermute | solution.py:384
  57.8 29.8 %collective-permute-start.8 = (bf16[32,8192]{1,0:T(8,128)(2,1)}, bf16[32,8192]{1,0:T(8,128)(2,1)S(1)}, u32[]{:S(2)}, u32[]{:S(2)}) collective-permute-start(bf16[32,8192]{1,0:T(8,128)(2,1)} %copy-done.15), channel_id=1, source_target_pairs={{0,2},{1,3},{2,4},{3,5},{4,6},{5,7},{6,0},{7,1},{8,10},{9,11},{10,... | collective-permute-start | bytes 1572872 | tf_op jit(solution)/shard_map/ppermute | solution.py:384
  57.8 29.8 %collective-permute-start.9 = (bf16[32,8192]{1,0:T(8,128)(2,1)}, bf16[32,8192]{1,0:T(8,128)(2,1)S(1)}, u32[]{:S(2)}, u32[]{:S(2)}) collective-permute-start(bf16[32,8192]{1,0:T(8,128)(2,1)} %copy-done.14), channel_id=1, source_target_pairs={{0,4},{1,5},{2,6},{3,7},{4,0},{5,1},{6,2},{7,3},{8,12},{9,13},{10,... | collective-permute-start | bytes 1572872 | tf_op jit(solution)/shard_map/ppermute | solution.py:384
  59.7 30.3 %collective-permute-start.12 = (bf16[32,2048]{1,0:T(8,128)(2,1)S(1)}, bf16[32,2048]{1,0:T(8,128)(2,1)S(1)}, u32[]{:S(2)}, u32[]{:S(2)}) collective-permute-start(bf16[32,2048]{1,0:T(8,128)(2,1)S(1)} %get-tuple-element.77), channel_id=1, source_target_pairs={{0,2},{1,3},{2,4},{3,5},{4,6},{5,7},{6,0},{7,1},{8,10},{9,11},{10,... | collective-permute-start | bytes 393224 | tf_op jit(solution)/shard_map/ppermute | solution.py:384
  62.2 27.9 %collective-permute-start.13 = (bf16[32,2048]{1,0:T(8,128)(2,1)S(1)}, bf16[32,2048]{1,0:T(8,128)(2,1)S(1)}, u32[]{:S(2)}, u32[]{:S(2)}) collective-permute-start(bf16[32,2048]{1,0:T(8,128)(2,1)S(1)} %get-tuple-element.76), channel_id=1, source_target_pairs={{0,4},{1,5},{2,6},{3,7},{4,0},{5,1},{6,2},{7,3},{8,12},{9,13},{10,... | collective-permute-start | bytes 393224 | tf_op jit(solution)/shard_map/ppermute | solution.py:384
  83.9 6.2 %collective-permute-start.14 = (bf16[32,2048]{1,0:T(8,128)(2,1)S(1)}, bf16[32,2048]{1,0:T(8,128)(2,1)S(1)}, u32[]{:S(2)}, u32[]{:S(2)}) collective-permute-start(bf16[32,2048]{1,0:T(8,128)(2,1)S(1)} %get-tuple-element.75), channel_id=1, source_target_pairs={{0,6},{1,7},{2,0},{3,1},{4,2},{5,3},{6,4},{7,5},{8,14},{9,15},{10,... | collective-permute-start | bytes 393224 | tf_op jit(solution)/shard_map/ppermute | solution.py:384
  87.5 3.6 %copy-start.17 = (f32[1024,64]{0,1:T(8,128)S(1)}, f32[1024,64]{0,1:T(8,128)}, u32[]{:S(2)}) copy-start(f32[1024,64]{0,1:T(8,128)} %param.20) | copy-start | bytes 786436
  87.5 3.6 %copy-start.18 = (f32[1024,64]{0,1:T(8,128)S(1)}, f32[1024,64]{0,1:T(8,128)}, u32[]{:S(2)}) copy-start(f32[1024,64]{0,1:T(8,128)} %param.21) | copy-start | bytes 786436
  87.6 3.6 %copy-start.19 = (f32[1024,64]{0,1:T(8,128)S(1)}, f32[1024,64]{0,1:T(8,128)}, u32[]{:S(2)}) copy-start(f32[1024,64]{0,1:T(8,128)} %param.22) | copy-start | bytes 786436
  91.1 2.8 %copy-start.20 = (f32[64,256]{1,0:T(8,128)S(1)}, f32[64,256]{1,0:T(8,128)}, u32[]{:S(2)}) copy-start(f32[64,256]{1,0:T(8,128)} %param.23) | copy-start | bytes 196612
  91.2 2.7 %copy-start.21 = (f32[64,256]{1,0:T(8,128)S(1)}, f32[64,256]{1,0:T(8,128)}, u32[]{:S(2)}) copy-start(f32[64,256]{1,0:T(8,128)} %param.24) | copy-start | bytes 196612
  91.2 2.7 %copy-start.22 = (f32[64,256]{1,0:T(8,128)S(1)}, f32[64,256]{1,0:T(8,128)}, u32[]{:S(2)}) copy-start(f32[64,256]{1,0:T(8,128)} %param.25) | copy-start | bytes 196612

commit v8 on v7

--- a/solution.py
+++ b/solution.py
@@ -72,7 +72,7 @@
 
 
 def prep_kernel(rows_own, live_ref, bucket_ref, owner_ref, adapter_ref, cot_ref, up_ref,
-                masked_ref, turned_ref, slot_ref, factor_ref, place_ref, up_own_ref):
+                masked_ref, ours_ref, theirs_ref, slot_ref, factor_ref, place_ref, up_own_ref):
     tokens = cot_ref.shape[0]
     n_chip = tokens // rows_own // 2
     position = lax.axis_index("tensor")
@@ -83,13 +83,13 @@
     masked_ref[...] = masked
     for step in range(n_chip):
         block = (chip + step) % n_chip * 2
-        for out, k in ((0, core), (tokens // 2, 1 - core)):
+        for out, k in ((ours_ref, core), (theirs_ref, 1 - core)):
             start = pl.multiple_of((block + k) * rows_own, rows_own)
             ids = start + lax.broadcasted_iota(jnp.int32, (rows_own, 1), 0)
             rows = cot_ref[pl.ds(start, rows_own), :].astype(jnp.float32)
-            turned_ref[pl.ds(out + step * rows_own, rows_own), :] = jnp.where(
-                ids < live, rows, 0.0
-            ).astype(jnp.bfloat16)
+            out[pl.ds(step * rows_own, rows_own), :] = jnp.where(ids < live, rows, 0.0).astype(
+                jnp.bfloat16
+            )
     adapter = adapter_ref[...]
     slot = jnp.zeros_like(adapter)
     rank = jnp.zeros_like(adapter)
@@ -128,7 +128,8 @@
     tokens, kv = cotangent.shape
     shapes = (
         jax.ShapeDtypeStruct((tokens, kv), jnp.bfloat16),
-        jax.ShapeDtypeStruct((tokens, kv), jnp.bfloat16),
+        jax.ShapeDtypeStruct((tokens // 2, kv), jnp.bfloat16),
+        jax.ShapeDtypeStruct((tokens // 2, kv), jnp.bfloat16),
         jax.ShapeDtypeStruct((tokens, 128), jnp.float32),
         jax.ShapeDtypeStruct((tokens, 128), jnp.float32),
         jax.ShapeDtypeStruct((1, tokens), jnp.int32),
@@ -143,30 +144,6 @@
         out_specs=(VMEM_SPEC,) * len(shapes),
         name="prep",
     )(live, bucket, owner, adapter_row, cotangent, up_factors)
-
-
-def frozen_kernel(turned_ref, frozen_ref, *theirs_refs):
-    half, part_width = theirs_refs[0].shape
-    chunk = 512
-    for first in range(0, frozen_ref.shape[0], chunk):
-        at = first % part_width
-        theirs_refs[first // part_width][:, at : at + chunk] = dot(
-            turned_ref[half:, :], frozen_ref[first : first + chunk, :], NT
-        )
-
-
-def frozen_term(turned, frozen, parts):
-    tokens, kv = turned.shape
-    width = frozen.shape[0]
-    return call(
-        frozen_kernel,
-        (jax.ShapeDtypeStruct((tokens // 2, width // parts), jnp.float32),) * parts,
-        tokens * kv * width,
-        2 * kv * width + 2 * tokens * width,
-        in_specs=[VMEM_SPEC] * 2,
-        out_specs=(VMEM_SPEC,) * parts,
-        name="frozen_term",
-    )(turned, frozen)
 
 
 def pack_kernel(place_ref, *refs):
@@ -195,7 +172,6 @@
 
 
 CHUNK = 256
-PARTS = 4
 
 
 def down_kernel(hidden_ref, slot_ref, up_own_ref, factors_ref, out_ref):
@@ -264,64 +240,39 @@
     )(weights, slot_wide, factors)
 
 
-def pair_kernel(rows_own, turned_ref, frozen_ref, *refs):
-    half, part_width = refs[0].shape
+def pair_kernel(rows_own, rows_ref, pair_rows_ref, extra_ref, extra_pair_ref, frozen_ref,
+                pair_frozen_ref, *outs):
     width = frozen_ref.shape[0]
-    parts = width // part_width
-    pair_refs, outs = refs[:parts], refs[parts:]
-    chunk = 512
-    for first in range(0, width, chunk):
-        at = slice(first, first + chunk)
-        inner = first % part_width
-        total = dot(turned_ref[:half, :], frozen_ref[at, :], NT)
-        total = total + pair_refs[first // part_width][:, inner : inner + chunk]
+    columns = extra_ref.shape[1]
+    position = lax.axis_index("tensor")
+    chip, core = position // 2, position % 2
+    low = jnp.where(core == 0, extra_ref[...], extra_pair_ref[...])
+    high = jnp.where(core == 0, extra_pair_ref[...], extra_ref[...])
+    for block in range(width // columns):
+        at = slice(block * columns, (block + 1) * columns)
+        total = dot(rows_ref[...], frozen_ref[at, :], NT)
+        total = total + dot(pair_rows_ref[...], pair_frozen_ref[at, :], NT)
+        extra = low if block % 2 == 0 else high
+        total = total + jnp.where(chip == block // 2, extra, 0.0)
         outs[0][:, at] = total[:rows_own, :]
         for i, out in enumerate(outs[1:], 1):
             out[:, at] = total[i * rows_own : (i + 1) * rows_own, :].astype(jnp.bfloat16)
 
 
-def pair_sum(rows_own, turned, frozen, from_pair):
-    half = from_pair[0].shape[0]
-    width, kv = frozen.shape
+def pair_sum(rows_own, rows, pair_rows, extra, extra_pair, frozen, pair_frozen):
+    half, kv = rows.shape
+    width = frozen.shape[0]
     sent = jax.ShapeDtypeStruct((rows_own, width), jnp.bfloat16)
     n_out = half // rows_own - 1
     return call(
         functools.partial(pair_kernel, rows_own),
         (jax.ShapeDtypeStruct((rows_own, width), jnp.float32),) + (sent,) * n_out,
-        2 * half * width * kv,
-        2 * kv * width + 6 * half * width,
-        in_specs=[VMEM_SPEC] * (2 + len(from_pair)),
+        4 * half * width * kv,
+        4 * kv * width + 4 * half * width,
+        in_specs=[VMEM_SPEC] * 6,
         out_specs=(VMEM_SPEC,) * (n_out + 1),
         name="pair_sum",
-    )(turned, frozen, *from_pair)
-
-
-def last_kernel(*refs):
-    count = (len(refs) - 1) // 2
-    frozen_refs, extra_refs, out_ref = refs[:count], refs[count:-1], refs[-1]
-    columns = extra_refs[0].shape[1]
-    chip = lax.axis_index("tensor") // 2
-    for step, extra_ref in enumerate(extra_refs):
-        block = (chip + count - step) % count
-        at = pl.ds(pl.multiple_of(block * columns, columns), columns)
-        total = extra_ref[...].astype(jnp.float32)
-        for frozen_ref in frozen_refs:
-            total = total + frozen_ref[:, at].astype(jnp.float32)
-        out_ref[:, at] = total.astype(jnp.bfloat16)
-
-
-def last_sum(frozen_terms, extra_terms):
-    size = frozen_terms[0].size
-    values = [*frozen_terms, *extra_terms]
-    return call(
-        last_kernel,
-        jax.ShapeDtypeStruct(frozen_terms[0].shape, jnp.bfloat16),
-        5 * size,
-        16 * size,
-        in_specs=[VMEM_SPEC] * len(values),
-        out_specs=VMEM_SPEC,
-        name="last_sum",
-    )(*values)
+    )(rows, pair_rows, extra, extra_pair, frozen, pair_frozen)
 
 
 def local(
@@ -351,7 +302,7 @@
     blocks = hidden.reshape(rows_own, n_tensor, columns).transpose(1, 0, 2)
     hidden_columns = lax.all_to_all(blocks, "tensor", 0, 0, tiled=True).reshape(tokens, columns)
 
-    masked, turned, slot_wide, factor_wide, place, up_own = prep(
+    masked, rows, pair_rows, slot_wide, factor_wide, place, up_own = prep(
         rows_own,
         live_token_counts,
         adapter_rank_bucket,
@@ -361,46 +312,37 @@
         adapter_up_factors,
     )
 
-    turned, hidden_columns = lax.optimization_barrier((turned, hidden_columns))
-    frozen_theirs = frozen_term(turned, frozen_key_value, PARTS)
+    pair_rows = swap(pair_rows, 1, n_tensor)
+    pair_frozen = swap(frozen_key_value, 1, n_tensor)
 
     own = low_rank(hidden_columns, slot_wide, up_own, adapter_down_factors)
     own = own + swap(own, 1, n_tensor)
-    own, frozen_theirs = lax.optimization_barrier((own, frozen_theirs))
     weights = (sum_over_chips(own, n_tensor) * factor_wide).astype(jnp.bfloat16)
-
-    from_pair = [swap(theirs, 1, n_tensor) for theirs in frozen_theirs]
-    total, *sent = pair_sum(rows_own, turned, frozen_key_value, from_pair)
+    extra_ours, extra_theirs = extra_term(rows_own, weights, slot_wide, adapter_down_factors)
+    weights, extra_ours, extra_theirs = lax.optimization_barrier(
+        (weights, extra_ours, extra_theirs)
+    )
 
     packed = pack_rows(place, [hidden_columns, masked, weights], n_slot * CAP)
-    packed, weights = lax.optimization_barrier((packed, weights))
-    weights, total, sent = lax.optimization_barrier((weights, total, sent))
     owned = lax.all_to_all(
         packed.reshape(n_slot, CAP, -1), "dp", 0, 0, tiled=True
     ).reshape(n_slot * CAP, -1)
 
-    def to_chips(sent):
-        return [
-            lax.ppermute(
-                value, "tensor", [(i, (i + 2 * step) % n_tensor) for i in range(n_tensor)]
-            )
-            for step, value in enumerate(sent, 1)
-        ]
-
-    arrived = to_chips(sent)
-    extra_ours, extra_theirs = extra_term(rows_own, weights, slot_wide, adapter_down_factors)
-    extra_pair = swap(extra_theirs, 1, n_tensor)
-    low_core = lax.axis_index("tensor") % 2 == 0
-    extra = jnp.concatenate(
-        [
-            jnp.where(low_core, extra_ours, extra_pair),
-            jnp.where(low_core, extra_pair, extra_ours),
-        ],
-        axis=1,
-    ).reshape(n_chip, rows_own, 2 * columns)
-    extra_sent = extra[1:].astype(jnp.bfloat16)
-    extra_arrived = to_chips([extra_sent[i] for i in range(n_chip - 1)])
-    hidden_gradient = last_sum([total, *arrived], [extra[0], *extra_arrived])
+    total, *sent = pair_sum(
+        rows_own,
+        rows,
+        pair_rows,
+        extra_ours,
+        swap(extra_theirs, 1, n_tensor),
+        frozen_key_value,
+        pair_frozen,
+    )
+    for step, value in enumerate(sent, 1):
+        arrived = lax.ppermute(
+            value, "tensor", [(i, (i + 2 * step) % n_tensor) for i in range(n_tensor)]
+        )
+        total = total + arrived.astype(jnp.float32)
+    hidden_gradient = total.astype(jnp.bfloat16)
 
     kv = cotangent.shape[1]
     owned_hidden, owned_cot = owned[:, :columns], owned[:, columns : columns + kv]

time: 97.3 us -> 92.4 us (0.950); the launches traced: 95.8 us -> 92 us
  starting transfers between devices: 31.8 us -> 24.9 us
  waiting for transfers between devices: 36.9 us -> 42.2 us
  local copies, waits for them, and re-layouts: 8.5 us -> 6.39 us
  Pallas kernels: 12.7 us -> 10.6 us
  other arithmetic: 0.24 us -> 2.3 us
    all_to_all x1, waiting for transfers between devices: 0.01 us -> 23.5 us  [local(): lax.all_to_all(packed.reshape(n_slot, CAP, -1), 'dp', 0, 0, tiled=True)]
    ppermute x6 -> x3, waiting for transfers between devices: 23.5 us -> 0.01 us  [local(): lax.ppermute(value, 'tensor', [(i, (i + 2 * step) % n_tensor) for i in ra...]
    ppermute x6 -> x3, starting transfers between devices: 10.6 us -> 3.62 us  [local(): lax.ppermute(value, 'tensor', [(i, (i + 2 * step) % n_tensor) for i in ra...]
    pallas_call x2 -> x0, Pallas kernels: 4.06 us -> none  [the longest x1 2.98 us: frozen_term(): call(frozen_kernel, (jax.ShapeDtypeStruct((tokens // 2, width // parts),...]
    ppermute x9 -> x7, waiting for transfers between devices: 5.52 us -> 9.44 us  [swap(): return lax.ppermute(value, 'tensor', [(i, i ^ mask) for i in range(count)])]
    convert_element_type x0 -> x1, other arithmetic: none -> 2.25 us  [local(): hidden_gradient = total.astype(jnp.bfloat16)]
    unnamed x46 -> x22, local copies, waits for them, and re-layouts: 6.5 us -> 4.41 us
    pallas_call x1, Pallas kernels: 3.19 us -> 5.05 us  [pair_sum(): call(functools.partial(pair_kernel, rows_own), (jax.ShapeDtypeStruct((row...]
  transfers between devices with their start and end apart: 17 -> 12, of which waited for: 6 -> 7; matrix products, arithmetic and copies ran while one was open for 0% -> 7% of each run, Pallas kernels for 12% -> 12%
where the time goes in v8:
time: 92.4 us; the launch traced here: 92 us
  waiting for transfers between devices  42.2 us (46%)
  starting transfers between devices  24.9 us (27%)
  Pallas kernels  10.6 us (11%)
  local copies, waits for them, and re-layouts  6.39 us (7%)
  matrix products  4.83 us (5%)
  other arithmetic  2.3 us (2%)
    all_to_all x1, waiting for transfers between devices, local(): lax.all_to_all(packed.reshape(n_slot, CAP, -1), 'dp', 0, 0, tiled=True)  23.5 us
    all_to_all x1, starting transfers between devices, local(): lax.all_to_all(packed.reshape(n_slot, CAP, -1), 'dp', 0, 0, tiled=True)  11.2 us
    ppermute x7, waiting for transfers between devices, swap(): return lax.ppermute(value, 'tensor', [(i, i ^ mask) for i in range(count)])  9.44 us
    all_to_all x1, waiting for transfers between devices, local(): lax.all_to_all(blocks, 'tensor', 0, 0, tiled=True).reshape(tokens, columns)  9.16 us
    ppermute x7, starting transfers between devices, swap(): return lax.ppermute(value, 'tensor', [(i, i ^ mask) for i in range(count)])  5.56 us
    pallas_call x1, Pallas kernels, pair_sum(): call(functools.partial(pair_kernel, rows_own), (jax.ShapeDtypeStruct((row...  5.05 us
    dot_general x2, matrix products, contract_helper(): lax.dot_general(left, right, (((left_dim,), (right_dim,)), ((), ())), pre...  4.83 us
    all_to_all x1, starting transfers between devices, local(): lax.all_to_all(blocks, 'tensor', 0, 0, tiled=True).reshape(tokens, columns)  4.5 us
  transfers between devices with their start and end apart: 12, of which 7 were waited for; matrix products, arithmetic and copies ran while one was open for 7% of the time, Pallas kernels for 12%

profile of v8, /device:TPU:32, one launch (start us, length us, event | category | flops | bytes accessed | tf_op | source)
XLA Modules:
  0.0 92.0 jit_solution(2458597478609875126)
XLA Ops:
  0.6 0.0 copy-start.5
  0.6 0.0 copy-start.4
  0.7 0.0 copy-start.3
  0.7 0.0 copy-start.7
  0.7 0.0 copy-start.8
  0.7 0.0 copy-start.6
  0.7 0.1 collective-permute-start.6
  0.8 2.0 %copy.25 = bf16[4,8,8,1024]{3,2,0,1:T(8,128)(2,1)} copy(bf16[4,8,8,1024]{3,2,1,0:T(8,128)(2,1)} %bitcast.14) | data formatting | bytes 1048576 | tf_op jit(solution)/shard_map/reshape | solution.py:302
  2.8 4.5 %all-to-all-start = ((bf16[8,32,1024]{2,1,0:T(8,128)(2,1)}), bf16[8,32,1024]{2,1,0:T(8,128)(2,1)S(1)}, u32[]{:S(2)}, u32[]{:S(2)}) async-start(bf16[8,32,1024]{2,1,0:T(8,128)(2,1)} %bitcast.10), calls=%async_computation | async-start | bytes 1048576 | tf_op jit(solution)/shard_map/all_to_all | solution.py:303
  7.3 0.0 copy-done.5
  7.3 0.0 copy-done.4
  7.3 0.0 copy-done.3
  7.3 0.0 copy-done.7
  7.3 0.0 copy-done.8
  7.3 0.0 copy-done.6
  7.3 1.1 %prep.1 = (bf16[256,256]{1,0:T(8,128)(2,1)S(1)}, bf16[128,256]{1,0:T(8,128)(2,1)S(1)}, bf16[128,256]{1,0:T(8,128)(2,1)S(1)}, f32[256,128]{1,0:T(8,128)S(1)}, f32...) custom-call(s32[32]{0:T(128)S(1)} %copy-done.6, s32[32]{0:T(128)S(1)} %copy-done.7, ...), custom_call_target="tpu_custom_call" | custom-call | flops 268435456 | bytes 1048576 | tf_op jit(solution)/shard_map/prep/pallas_call | solution.py:138
  8.5 9.2 %all-to-all-done = bf16[8,32,1024]{2,1,0:T(8,128)(2,1)S(1)} async-done(((bf16[8,32,1024]{2,1,0:T(8,128)(2,1)}), bf16[8,32,1024]{2,1,0:T(8,128)(2,1)S(1)}, u32[]{:S(2)}, u32[]{:S(2)}) %all-to-all-start) | async-done | bytes 524320 | tf_op jit(solution)/shard_map/all_to_all | solution.py:303
  17.6 2.2 %copy-done = bf16[1024,2048]{1,0:T(8,128)(2,1)S(1)} copy-done((bf16[1024,2048]{1,0:T(8,128)(2,1)S(1)}, bf16[1024,2048]{1,0:T(8,128)(2,1)}, u32[]{:S(2)}) %copy-start) | copy-done | bytes 4194328
  19.8 1.3 %low_rank.1 = f32[256,128]{1,0:T(8,128)S(1)} custom-call(bf16[256,1024]{1,0:T(8,128)(2,1)S(1)} %bitcast.11, f32[256,128]{1,0:T(8,128)S(1)} %get-tuple-element.25.slot_ref, f32[256,64]{1,0:T(8,128)S(1)} %get-tuple-element.26.up_own_ref, bf16[1024,2048]{1,0:T(8,128)(2,1)S(1)} %copy-done), custom_call_target="tpu_custom_call" | custom-call | flops 1073741824 | bytes 4194304 | tf_op jit(solution)/shard_map/low_rank/pallas_call | solution.py:191
  21.2 0.1 collective-permute-start.1
  21.3 1.3 %collective-permute-done.1 = f32[256,128]{1,0:T(8,128)S(1)} collective-permute-done((f32[256,128]{1,0:T(8,128)S(1)}, f32[256,128]{1,0:T(8,128)S(1)}, u32[]{:S(2)}, u32[]{:S(2)}) %collective-permute-start.1) | collective-permute-done | bytes 131104 | tf_op jit(solution)/shard_map/ppermute | solution.py:40
  22.6 0.7 collective-permute-start.2
  23.3 2.1 %collective-permute-start.3 = (f32[256,128]{1,0:T(8,128)S(1)}, f32[256,128]{1,0:T(8,128)S(1)}, u32[]{:S(2)}, u32[]{:S(2)}) collective-permute-start(f32[256,128]{1,0:T(8,128)S(1)} %add.51), channel_id=1, source_target_pairs={{0,4},{1,5},{2,6},{3,7},{4,0},{5,1},{6,2},{7,3},{8,12},{9,13},{10,... | collective-permute-start | bytes 393224 | tf_op jit(solution)/shard_map/ppermute | solution.py:40
  25.3 2.1 %collective-permute-start.4 = (f32[256,128]{1,0:T(8,128)S(1)}, f32[256,128]{1,0:T(8,128)S(1)}, u32[]{:S(2)}, u32[]{:S(2)}) collective-permute-start(f32[256,128]{1,0:T(8,128)S(1)} %add.51), channel_id=1, source_target_pairs={{0,6},{1,7},{2,4},{3,5},{4,2},{5,3},{6,0},{7,1},{8,14},{9,15},{10,... | collective-permute-start | bytes 393224 | tf_op jit(solution)/shard_map/ppermute | solution.py:40
  27.4 1.6 %collective-permute-done.2 = f32[256,128]{1,0:T(8,128)S(1)} collective-permute-done((f32[256,128]{1,0:T(8,128)S(1)}, f32[256,128]{1,0:T(8,128)S(1)}, u32[]{:S(2)}, u32[]{:S(2)}) %collective-permute-start.2) | collective-permute-done | bytes 131104 | tf_op jit(solution)/shard_map/ppermute | solution.py:40
  29.0 2.7 %collective-permute-done.3 = f32[256,128]{1,0:T(8,128)S(1)} collective-permute-done((f32[256,128]{1,0:T(8,128)S(1)}, f32[256,128]{1,0:T(8,128)S(1)}, u32[]{:S(2)}, u32[]{:S(2)}) %collective-permute-start.3) | collective-permute-done | bytes 131104 | tf_op jit(solution)/shard_map/ppermute | solution.py:40
  31.8 2.2 %collective-permute-done.4 = f32[256,128]{1,0:T(8,128)S(1)} collective-permute-done((f32[256,128]{1,0:T(8,128)S(1)}, f32[256,128]{1,0:T(8,128)S(1)}, u32[]{:S(2)}, u32[]{:S(2)}) %collective-permute-start.4) | collective-permute-done | bytes 131104 | tf_op jit(solution)/shard_map/ppermute | solution.py:40
  34.1 1.4 %extra_term.1 = (f32[128,1024]{1,0:T(8,128)S(1)}, f32[128,1024]{1,0:T(8,128)S(1)}) custom-call(bf16[256,128]{1,0:T(8,128)(2,1)S(1)} %multiply_convert_fusion.weight_ref.refs_2_, f32[256,128]{1,0:T(8,128)S(1)} %get-tuple-element.25.slot_ref, bf16[1024,2048]{1,0:T(8,128)(2,1)S(1)} %copy-done.1), custom_call_target="tpu_custom_call" | custom-call | flops 1073741824 | bytes 4194304 | tf_op jit(solution)/shard_map/extra_term/pallas_call | solution.py:231
  35.4 1.7 %pack.1 = bf16[512,1408]{1,0:T(8,128)(2,1)} custom-call(s32[1,256]{1,0:T(1,128)S(1)} %get-tuple-element.36.place_ref, bf16[256,1024]{1,0:T(8,128)(2,1)S(1)} %bitcast.12, bf16[256,256]{1,0:T(8,128)(2,1)S(1)} %get-tuple-element.37.refs_1_, bf16[256,128]{1,0:T(8,128)(2,1)S(1)} %multiply_convert_fusion.weight_ref.refs_2_), custom_call_target="tpu_custom_call" | custom-call | flops 369098752 | bytes 2162688 | tf_op jit(solution)/shard_map/pack/pallas_call | solution.py:163
  37.1 11.2 %all-to-all-start.1 = ((bf16[32,16,1408]{2,1,0:T(8,128)(2,1)}), bf16[32,16,1408]{2,1,0:T(8,128)(2,1)}, u32[]{:S(2)}, u32[]{:S(2)}) async-start(bf16[32,16,1408]{2,1,0:T(8,128)(2,1)} %bitcast.3), calls=%async_computation.1 | async-start | bytes 2883584 | tf_op jit(solution)/shard_map/all_to_all | solution.py:327
  48.4 0.1 collective-permute-start.5
  48.5 0.5 collective-permute-start
  49.0 1.5 %collective-permute-done.pair_rows_ref = bf16[128,256]{1,0:T(8,128)(2,1)S(1)} collective-permute-done((bf16[128,256]{1,0:T(8,128)(2,1)S(1)}, bf16[128,256]{1,0:T(8,128)(2,1)S(1)}, u32[]{:S(2)}, u32[]{:S(2)}) %collective-permute-start) | collective-permute-done | bytes 65568 | tf_op jit(solution)/shard_map/ppermute | solution.py:40
  50.5 0.0 collective-permute-done.5.extra_pair_ref
  50.5 0.0 collective-permute-done.6.pair_frozen_ref
  50.5 2.2 %copy-done.2 = bf16[8192,256]{1,0:T(8,128)(2,1)S(1)} copy-done((bf16[8192,256]{1,0:T(8,128)(2,1)S(1)}, bf16[8192,256]{1,0:T(8,128)(2,1)}, u32[]{:S(2)}) %copy-start.2) | copy-done | bytes 4194328
  52.7 5.0 %pair_sum.1 = (f32[32,8192]{1,0:T(8,128)S(1)}, bf16[32,8192]{1,0:T(8,128)(2,1)S(1)}, bf16[32,8192]{1,0:T(8,128)(2,1)S(1)}, bf16[32,8192]{1,0:T(8,128)(2,1)S(1)}) custom-call(bf16[128,256]{1,0:T(8,128)(2,1)S(1)} %get-tuple-element.23.rows_ref, bf16[128,256]{1,0:T(8,128)(2,1)S(1)} %collective-permute-done.pair_rows_ref, ...), custom_call_target="tpu_custom_call" | custom-call | flops 1073741824 | bytes 12582912 | tf_op jit(solution)/shard_map/pair_sum/pallas_call | solution.py:267
  57.7 0.1 collective-permute-start.7
  57.8 3.5 %collective-permute-start.8 = (bf16[32,8192]{1,0:T(8,128)(2,1)S(1)}, bf16[32,8192]{1,0:T(8,128)(2,1)}, u32[]{:S(2)}, u32[]{:S(2)}) collective-permute-start(bf16[32,8192]{1,0:T(8,128)(2,1)S(1)} %get-tuple-element.34), channel_id=1, source_target_pairs={{0,4},{1,5},{2,6},{3,7},{4,0},{5,1},{6,2},{7,3},{8,12},{9,13},{10,... | collective-permute-start | bytes 1572872 | tf_op jit(solution)/shard_map/ppermute | solution.py:341
  61.4 0.0 collective-permute-start.9
  61.4 23.5 %all-to-all-done.1 = bf16[32,16,1408]{2,1,0:T(8,128)(2,1)} async-done(((bf16[32,16,1408]{2,1,0:T(8,128)(2,1)}), bf16[32,16,1408]{2,1,0:T(8,128)(2,1)}, u32[]{:S(2)}, u32[]{:S(2)}) %all-to-all-start.1) | async-done | bytes 1441824 | tf_op jit(solution)/shard_map/all_to_all | solution.py:327
  84.9 0.0 copy-done.10
  84.9 1.9 %multiply_subtract_fusion.1 = (f32[64,256]{1,0:T(8,128)}, f32[64,256]{1,0:T(8,128)}, f32[64,256]{1,0:T(8,128)}) fusion(f32[64,256]{1,0:T(8,128)S(1)} %copy-done.9, f32[64,256]{1,0:T(8,128)S(1)} %copy-done.10, f32[64,256]{1,0:T(8,128)} %param.25, bf16[512,1408]{1,0:T(8,128)(2,1)} %bitcast.4), kind=kOutput, calls=%fused_computation.12 | convolution fusion | flops 17039360 | bytes 786432 | tf_op jit(solution)/shard_map/dot_general | solution.py:34
  86.8 2.9 %multiply_subtract_fusion = (f32[1024,64]{0,1:T(8,128)}, f32[1024,64]{0,1:T(8,128)}, f32[1024,64]{0,1:T(8,128)}) fusion(f32[1024,64]{0,1:T(8,128)} %param.20, f32[1024,64]{0,1:T(8,128)} %param.21, f32[1024,64]{0,1:T(8,128)} %param.22, bf16[512,1408]{1,0:T(8,128)(2,1)} %bitcast.4), kind=kOutput, calls=%fused_computation.6 | convolution fusion | flops 68157440 | bytes 2752512 | tf_op jit(solution)/shard_map/dot_general | solution.py:34
  89.7 0.0 collective-permute-done.7
  89.7 0.0 collective-permute-done.8
  89.7 0.0 collective-permute-done.9
  89.8 2.2 %add_convert_fusion = bf16[32,8192]{1,0:T(8,128)(2,1)} fusion(bf16[32,8192]{1,0:T(8,128)(2,1)} %collective-permute-done.9, bf16[32,8192]{1,0:T(8,128)(2,1)} %collective-permute-done.8, f32[32,8192]{1,0:T(8,128)S(1)} %get-tuple-element.32, bf16[32,8192]{1,0:T(8,128)(2,1)S(1)} %collective-permute-done.7), kind=kLoop, calls=%fused_computation.2 | loop fusion | flops 1835008 | bytes 3145728 | tf_op jit(solution)/shard_map/convert_element_type | solution.py:345
  (9 shorter events, 0.1 us)
Async XLA Ops:
  0.6 6.6 %copy-start.5 = (s32[256,1]{0,1:T(1,128)S(1)}, s32[256,1]{0,1:T(1,128)}, u32[]{:S(2)}) copy-start(s32[256,1]{0,1:T(1,128)} %param.26) | copy-start | bytes 3076
  0.6 6.6 %copy-start.4 = (bf16[256,256]{1,0:T(8,128)(2,1)S(1)}, bf16[256,256]{1,0:T(8,128)(2,1)}, u32[]{:S(2)}) copy-start(bf16[256,256]{1,0:T(8,128)(2,1)} %cot_ref.1) | copy-start | bytes 393220
  0.7 6.6 %copy-start.3 = (bf16[2048,256]{1,0:T(8,128)(2,1)S(1)}, bf16[2048,256]{1,0:T(8,128)(2,1)}, u32[]{:S(2)}) copy-start(bf16[2048,256]{1,0:T(8,128)(2,1)} %up_ref.1) | copy-start | bytes 3145732
  0.7 6.6 %copy-start.7 = (s32[32]{0:T(128)S(1)}, s32[32]{0:T(128)}, u32[]{:S(2)}) copy-start(s32[32]{0:T(128)} %bucket_ref.1) | copy-start | bytes 388
  0.7 6.6 %copy-start.8 = (s32[32]{0:T(128)S(1)}, s32[32]{0:T(128)}, u32[]{:S(2)}) copy-start(s32[32]{0:T(128)} %owner_ref.1) | copy-start | bytes 388
  0.7 6.6 %copy-start.6 = (s32[32]{0:T(128)S(1)}, s32[32]{0:T(128)}, u32[]{:S(2)}) copy-start(s32[32]{0:T(128)} %live_ref.1) | copy-start | bytes 388
  0.7 49.8 %collective-permute-start.6 = (bf16[8192,256]{1,0:T(8,128)(2,1)}, bf16[8192,256]{1,0:T(8,128)(2,1)}, u32[]{:S(2)}, u32[]{:S(2)}) collective-permute-start(bf16[8192,256]{1,0:T(8,128)(2,1)} %frozen_ref.1), channel_id=1, source_target_pairs={{0,1},{1,0},{2,3},{3,2},{4,5},{5,4},{6,7},{7,6},{8,9},{9,8},{10,11... | collective-permute-start | bytes 12582920 | tf_op jit(solution)/shard_map/ppermute | solution.py:40
  2.8 14.8 %all-to-all-start = ((bf16[8,32,1024]{2,1,0:T(8,128)(2,1)}), bf16[8,32,1024]{2,1,0:T(8,128)(2,1)S(1)}, u32[]{:S(2)}, u32[]{:S(2)}) async-start(bf16[8,32,1024]{2,1,0:T(8,128)(2,1)} %bitcast.10), calls=%async_computation | async-start | bytes 1048576 | tf_op jit(solution)/shard_map/all_to_all | solution.py:303
  17.6 2.2 %copy-start = (bf16[1024,2048]{1,0:T(8,128)(2,1)S(1)}, bf16[1024,2048]{1,0:T(8,128)(2,1)}, u32[]{:S(2)}) copy-start(bf16[1024,2048]{1,0:T(8,128)(2,1)} %factors_ref.3) | copy-start | bytes 12582916
  19.8 14.2 %copy-start.1 = (bf16[1024,2048]{1,0:T(8,128)(2,1)S(1)}, bf16[1024,2048]{1,0:T(8,128)(2,1)}, u32[]{:S(2)}) copy-start(bf16[1024,2048]{1,0:T(8,128)(2,1)} %factors_ref.3) | copy-start | bytes 12582916
  21.2 1.4 %collective-permute-start.1 = (f32[256,128]{1,0:T(8,128)S(1)}, f32[256,128]{1,0:T(8,128)S(1)}, u32[]{:S(2)}, u32[]{:S(2)}) collective-permute-start(f32[256,128]{1,0:T(8,128)S(1)} %low_rank.1), channel_id=1, source_target_pairs={{0,1},{1,0},{2,3},{3,2},{4,5},{5,4},{6,7},{7,6},{8,9},{9,8},{10,11... | collective-permute-start | bytes 393224 | tf_op jit(solution)/shard_map/ppermute | solution.py:40
  22.6 6.4 %collective-permute-start.2 = (f32[256,128]{1,0:T(8,128)S(1)}, f32[256,128]{1,0:T(8,128)S(1)}, u32[]{:S(2)}, u32[]{:S(2)}) collective-permute-start(f32[256,128]{1,0:T(8,128)S(1)} %add.51), channel_id=1, source_target_pairs={{0,2},{1,3},{2,0},{3,1},{4,6},{5,7},{6,4},{7,5},{8,10},{9,11},{10,... | collective-permute-start | bytes 393224 | tf_op jit(solution)/shard_map/ppermute | solution.py:40
  23.3 8.5 %collective-permute-start.3 = (f32[256,128]{1,0:T(8,128)S(1)}, f32[256,128]{1,0:T(8,128)S(1)}, u32[]{:S(2)}, u32[]{:S(2)}) collective-permute-start(f32[256,128]{1,0:T(8,128)S(1)} %add.51), channel_id=1, source_target_pairs={{0,4},{1,5},{2,6},{3,7},{4,0},{5,1},{6,2},{7,3},{8,12},{9,13},{10,... | collective-permute-start | bytes 393224 | tf_op jit(solution)/shard_map/ppermute | solution.py:40
  25.3 8.7 %collective-permute-start.4 = (f32[256,128]{1,0:T(8,128)S(1)}, f32[256,128]{1,0:T(8,128)S(1)}, u32[]{:S(2)}, u32[]{:S(2)}) collective-permute-start(f32[256,128]{1,0:T(8,128)S(1)} %add.51), channel_id=1, source_target_pairs={{0,6},{1,7},{2,4},{3,5},{4,2},{5,3},{6,0},{7,1},{8,14},{9,15},{10,... | collective-permute-start | bytes 393224 | tf_op jit(solution)/shard_map/ppermute | solution.py:40
  37.1 47.8 %all-to-all-start.1 = ((bf16[32,16,1408]{2,1,0:T(8,128)(2,1)}), bf16[32,16,1408]{2,1,0:T(8,128)(2,1)}, u32[]{:S(2)}, u32[]{:S(2)}) async-start(bf16[32,16,1408]{2,1,0:T(8,128)(2,1)} %bitcast.3), calls=%async_computation.1 | async-start | bytes 2883584 | tf_op jit(solution)/shard_map/all_to_all | solution.py:327
  48.4 2.1 %collective-permute-start.5 = (f32[128,1024]{1,0:T(8,128)S(1)}, f32[128,1024]{1,0:T(8,128)S(1)}, u32[]{:S(2)}, u32[]{:S(2)}) collective-permute-start(f32[128,1024]{1,0:T(8,128)S(1)} %get-tuple-element.31), channel_id=1, source_target_pairs={{0,1},{1,0},{2,3},{3,2},{4,5},{5,4},{6,7},{7,6},{8,9},{9,8},{10,11... | collective-permute-start | bytes 1572872 | tf_op jit(solution)/shard_map/ppermute | solution.py:40
  48.5 2.0 %collective-permute-start = (bf16[128,256]{1,0:T(8,128)(2,1)S(1)}, bf16[128,256]{1,0:T(8,128)(2,1)S(1)}, u32[]{:S(2)}, u32[]{:S(2)}) collective-permute-start(bf16[128,256]{1,0:T(8,128)(2,1)S(1)} %get-tuple-element.24), channel_id=1, source_target_pairs={{0,1},{1,0},{2,3},{3,2},{4,5},{5,4},{6,7},{7,6},{8,9},{9,8},{10,11... | collective-permute-start | bytes 196616 | tf_op jit(solution)/shard_map/ppermute | solution.py:40
  50.5 2.2 %copy-start.2 = (bf16[8192,256]{1,0:T(8,128)(2,1)S(1)}, bf16[8192,256]{1,0:T(8,128)(2,1)}, u32[]{:S(2)}) copy-start(bf16[8192,256]{1,0:T(8,128)(2,1)} %frozen_ref.1) | copy-start | bytes 12582916
  52.7 32.2 %copy-start.9 = (f32[64,256]{1,0:T(8,128)S(1)}, f32[64,256]{1,0:T(8,128)}, u32[]{:S(2)}) copy-start(f32[64,256]{1,0:T(8,128)} %param.23) | copy-start | bytes 196612
  52.7 32.2 %copy-start.10 = (f32[64,256]{1,0:T(8,128)S(1)}, f32[64,256]{1,0:T(8,128)}, u32[]{:S(2)}) copy-start(f32[64,256]{1,0:T(8,128)} %param.24) | copy-start | bytes 196612
  57.7 32.0 %collective-permute-start.7 = (bf16[32,8192]{1,0:T(8,128)(2,1)S(1)}, bf16[32,8192]{1,0:T(8,128)(2,1)S(1)}, u32[]{:S(2)}, u32[]{:S(2)}) collective-permute-start(bf16[32,8192]{1,0:T(8,128)(2,1)S(1)} %get-tuple-element.33), channel_id=1, source_target_pairs={{0,2},{1,3},{2,4},{3,5},{4,6},{5,7},{6,0},{7,1},{8,10},{9,11},{10,... | collective-permute-start | bytes 1572872 | tf_op jit(solution)/shard_map/ppermute | solution.py:341
  57.8 31.9 %collective-permute-start.8 = (bf16[32,8192]{1,0:T(8,128)(2,1)S(1)}, bf16[32,8192]{1,0:T(8,128)(2,1)}, u32[]{:S(2)}, u32[]{:S(2)}) collective-permute-start(bf16[32,8192]{1,0:T(8,128)(2,1)S(1)} %get-tuple-element.34), channel_id=1, source_target_pairs={{0,4},{1,5},{2,6},{3,7},{4,0},{5,1},{6,2},{7,3},{8,12},{9,13},{10,... | collective-permute-start | bytes 1572872 | tf_op jit(solution)/shard_map/ppermute | solution.py:341
  61.4 28.4 %collective-permute-start.9 = (bf16[32,8192]{1,0:T(8,128)(2,1)S(1)}, bf16[32,8192]{1,0:T(8,128)(2,1)}, u32[]{:S(2)}, u32[]{:S(2)}) collective-permute-start(bf16[32,8192]{1,0:T(8,128)(2,1)S(1)} %get-tuple-element.35), channel_id=1, source_target_pairs={{0,6},{1,7},{2,0},{3,1},{4,2},{5,3},{6,4},{7,5},{8,14},{9,15},{10,... | collective-permute-start | bytes 1572872 | tf_op jit(solution)/shard_map/ppermute | solution.py:341

commit v9 on v8

--- a/solution.py
+++ b/solution.py
@@ -275,6 +275,31 @@
     )(rows, pair_rows, extra, extra_pair, frozen, pair_frozen)
 
 
+def adam_kernel(columns, kv, scale, owned_ref, *refs):
+    states, outs = refs[:6], refs[6:]
+    weights = owned_ref[:, columns + kv :].astype(jnp.float32)
+    turned = jnp.transpose(weights).astype(jnp.bfloat16)
+    grad_up = dot(turned[:PADDED_RANK], owned_ref[:, columns : columns + kv], NN) / scale
+    grad_down = dot(turned[PADDED_RANK:], owned_ref[:, :columns], NN) / scale
+    for first, grad in ((0, grad_down), (3, grad_up)):
+        state = [ref[...] for ref in states[first : first + 3]]
+        for out, value in zip(outs[first : first + 3], adamw(*state, grad), strict=True):
+            out[...] = value
+
+
+def owners_update(owned, columns, kv, scale, states):
+    shapes = tuple(jax.ShapeDtypeStruct(v.shape, v.dtype) for v in states)
+    return call(
+        functools.partial(adam_kernel, columns, kv, scale),
+        shapes,
+        2 * owned.size * PADDED_RANK,
+        2 * owned.size + 8 * sum(v.size for v in states),
+        in_specs=[VMEM_SPEC] * (1 + len(states)),
+        out_specs=(VMEM_SPEC,) * len(states),
+        name="owners_update",
+    )(owned, *states)
+
+
 def local(
     hidden,
     cotangent,
@@ -314,6 +339,7 @@
 
     pair_rows = swap(pair_rows, 1, n_tensor)
     pair_frozen = swap(frozen_key_value, 1, n_tensor)
+    slot_wide, pair_rows = lax.optimization_barrier((slot_wide, pair_rows))
 
     own = low_rank(hidden_columns, slot_wide, up_own, adapter_down_factors)
     own = own + swap(own, 1, n_tensor)
@@ -344,16 +370,14 @@
         total = total + arrived.astype(jnp.float32)
     hidden_gradient = total.astype(jnp.bfloat16)
 
-    kv = cotangent.shape[1]
-    owned_hidden, owned_cot = owned[:, :columns], owned[:, columns : columns + kv]
-    owned_down = owned[:, columns + kv : columns + kv + PADDED_RANK]
-    owned_up = owned[:, columns + kv + PADDED_RANK :]
-    grad_down = contract_helper(owned_hidden, owned_up, 0, 0) / tokens
-    grad_up = contract_helper(owned_down, owned_cot, 0, 0) / tokens
-    new_dm, new_dmo, new_ds = adamw(
-        down_master_copy, down_first_moment, down_second_moment, grad_down
-    )
-    new_um, new_umo, new_us = adamw(up_master_copy, up_first_moment, up_second_moment, grad_up)
+    owned, hidden_gradient = lax.optimization_barrier((owned, hidden_gradient))
+    down_states = (down_master_copy.T, down_first_moment.T, down_second_moment.T)
+    up_states = (up_master_copy, up_first_moment, up_second_moment)
+    updated = owners_update(
+        owned, columns, cotangent.shape[1], tokens, (*down_states, *up_states)
+    )
+    new_dm, new_dmo, new_ds = (value.T for value in updated[:3])
+    new_um, new_umo, new_us = updated[3:]
     return (hidden_gradient, new_dm, new_dmo, new_ds, new_um, new_umo, new_us)
 
 

time: 92.4 us -> 87.9 us (0.951)
  local copies, waits for them, and re-layouts: 6.39 us -> 11.9 us
  waiting for transfers between devices: 42.2 us -> 36.7 us
  matrix products: 4.83 us -> 0 us
  Pallas kernels: 10.6 us -> 12 us
  other arithmetic: 2.3 us -> 1.09 us
    ppermute x3, waiting for transfers between devices: 0.01 us -> 23.3 us  [local(): lax.ppermute(value, 'tensor', [(i, (i + 2 * step) % n_tensor) for i in ra...]
    all_to_all x1, waiting for transfers between devices: 23.5 us -> 1.55 us  [local(): lax.all_to_all(packed.reshape(n_slot, CAP, -1), 'dp', 0, 0, tiled=True)]
    all_to_all x1, waiting for transfers between devices: 9.16 us -> 2.97 us  [local(): lax.all_to_all(blocks, 'tensor', 0, 0, tiled=True).reshape(tokens, columns)]
    unnamed x22 -> x30, local copies, waits for them, and re-layouts: 4.41 us -> 10 us
    dot_general x2 -> x0, matrix products: 4.83 us -> none  [contract_helper(): lax.dot_general(left, right, (((left_dim,), (right_dim,)), ((), ())), pre...]
    pallas_call x0 -> x1, Pallas kernels: none -> 1.4 us  [owners_update(): call(functools.partial(adam_kernel, columns, kv, scale), shapes, 2 * owne...]
    convert_element_type x1, other arithmetic: 2.25 us -> 1.02 us  [local(): hidden_gradient = total.astype(jnp.bfloat16)]
  transfers between devices with their start and end apart: 12 -> 12, of which waited for: 7 -> 10; matrix products, arithmetic and copies ran while one was open for 7% -> 3% of each run, Pallas kernels for 12% -> 12%
where the time goes in v9:
time: 87.9 us; the launch traced here: 87.4 us
  waiting for transfers between devices  36.7 us (42%)
  starting transfers between devices  25 us (28%)
  Pallas kernels  12 us (14%)
  local copies, waits for them, and re-layouts  11.9 us (14%)
  other arithmetic  1.09 us (1%)
    ppermute x3, waiting for transfers between devices, local(): lax.ppermute(value, 'tensor', [(i, (i + 2 * step) % n_tensor) for i in ra...  23.3 us
    all_to_all x1, starting transfers between devices, local(): lax.all_to_all(packed.reshape(n_slot, CAP, -1), 'dp', 0, 0, tiled=True)  11.2 us
    unnamed x30, local copies, waits for them, and re-layouts  10 us
    ppermute x7, waiting for transfers between devices, swap(): return lax.ppermute(value, 'tensor', [(i, i ^ mask) for i in range(count)])  8.85 us
    ppermute x7, starting transfers between devices, swap(): return lax.ppermute(value, 'tensor', [(i, i ^ mask) for i in range(count)])  5.66 us
    pallas_call x1, Pallas kernels, pair_sum(): call(functools.partial(pair_kernel, rows_own), (jax.ShapeDtypeStruct((row...  5.07 us
    all_to_all x1, starting transfers between devices, local(): lax.all_to_all(blocks, 'tensor', 0, 0, tiled=True).reshape(tokens, columns)  4.57 us
    ppermute x3, starting transfers between devices, local(): lax.ppermute(value, 'tensor', [(i, (i + 2 * step) % n_tensor) for i in ra...  3.6 us
  transfers between devices with their start and end apart: 12, of which 10 were waited for; matrix products, arithmetic and copies ran while one was open for 3% of the time, Pallas kernels for 12%

profile of v9, /device:TPU:32, one launch (start us, length us, event | category | flops | bytes accessed | tf_op | source)
XLA Modules:
  0.0 87.4 jit_solution(2492406010584448770)
XLA Ops:
  0.6 0.1 collective-permute-start.6
  0.7 1.9 %copy.25 = bf16[4,8,8,1024]{3,2,0,1:T(8,128)(2,1)} copy(bf16[4,8,8,1024]{3,2,1,0:T(8,128)(2,1)} %bitcast.24) | data formatting | bytes 1048576 | tf_op jit(solution)/shard_map/reshape | solution.py:327
  2.6 4.6 %all-to-all-start = ((bf16[8,32,1024]{2,1,0:T(8,128)(2,1)}), bf16[8,32,1024]{2,1,0:T(8,128)(2,1)S(1)}, u32[]{:S(2)}, u32[]{:S(2)}) async-start(bf16[8,32,1024]{2,1,0:T(8,128)(2,1)} %bitcast.16), calls=%async_computation | async-start | bytes 1048576 | tf_op jit(solution)/shard_map/all_to_all | solution.py:328
  7.2 1.2 %copy-done.3 = bf16[2048,256]{1,0:T(8,128)(2,1)S(1)} copy-done((bf16[2048,256]{1,0:T(8,128)(2,1)S(1)}, bf16[2048,256]{1,0:T(8,128)(2,1)}, u32[]{:S(2)}) %copy-start.3) | copy-done | bytes 1048600
  8.4 0.9 %copy-done.7 = bf16[256,256]{1,0:T(8,128)(2,1)S(1)} copy-done((bf16[256,256]{1,0:T(8,128)(2,1)S(1)}, bf16[256,256]{1,0:T(8,128)(2,1)}, u32[]{:S(2)}) %copy-start.7) | copy-done | bytes 131096
  9.3 0.7 copy-done.11
  10.0 0.7 copy-done.12
  10.6 0.7 copy-done.13
  11.3 0.7 copy-done.14
  12.0 1.1 %prep.1 = (bf16[256,256]{1,0:T(8,128)(2,1)S(1)}, bf16[128,256]{1,0:T(8,128)(2,1)S(1)}, bf16[128,256]{1,0:T(8,128)(2,1)S(1)}, f32[256,128]{1,0:T(8,128)S(1)}, f32...) custom-call(s32[32]{0:T(128)S(1)} %copy-done.12, s32[32]{0:T(128)S(1)} %copy-done.13, ...), custom_call_target="tpu_custom_call" | custom-call | flops 268435456 | bytes 1048576 | tf_op jit(solution)/shard_map/prep/pallas_call | solution.py:138
  13.1 0.6 collective-permute-start
  13.7 0.9 %collective-permute-done.pair_rows_ref = bf16[128,256]{1,0:T(8,128)(2,1)S(1)} collective-permute-done((bf16[128,256]{1,0:T(8,128)(2,1)S(1)}, bf16[128,256]{1,0:T(8,128)(2,1)S(1)}, u32[]{:S(2)}, u32[]{:S(2)}) %collective-permute-start) | collective-permute-done | bytes 65568 | tf_op jit(solution)/shard_map/ppermute | solution.py:40
  14.6 3.0 %all-to-all-done = bf16[8,32,1024]{2,1,0:T(8,128)(2,1)S(1)} async-done(((bf16[8,32,1024]{2,1,0:T(8,128)(2,1)}), bf16[8,32,1024]{2,1,0:T(8,128)(2,1)S(1)}, u32[]{:S(2)}, u32[]{:S(2)}) %all-to-all-start) | async-done | bytes 524320 | tf_op jit(solution)/shard_map/all_to_all | solution.py:328
  17.5 2.2 %copy-done = bf16[1024,2048]{1,0:T(8,128)(2,1)S(1)} copy-done((bf16[1024,2048]{1,0:T(8,128)(2,1)S(1)}, bf16[1024,2048]{1,0:T(8,128)(2,1)}, u32[]{:S(2)}) %copy-start) | copy-done | bytes 4194328
  19.7 1.3 %low_rank.1 = f32[256,128]{1,0:T(8,128)S(1)} custom-call(bf16[256,1024]{1,0:T(8,128)(2,1)S(1)} %bitcast.18, f32[256,128]{1,0:T(8,128)S(1)} %get-tuple-element.37.slot_ref, f32[256,64]{1,0:T(8,128)S(1)} %get-tuple-element.38.up_own_ref, bf16[1024,2048]{1,0:T(8,128)(2,1)S(1)} %copy-done), custom_call_target="tpu_custom_call" | custom-call | flops 1073741824 | bytes 4194304 | tf_op jit(solution)/shard_map/low_rank/pallas_call | solution.py:191
  21.0 0.1 collective-permute-start.1
  21.1 1.3 %collective-permute-done.1 = f32[256,128]{1,0:T(8,128)S(1)} collective-permute-done((f32[256,128]{1,0:T(8,128)S(1)}, f32[256,128]{1,0:T(8,128)S(1)}, u32[]{:S(2)}, u32[]{:S(2)}) %collective-permute-start.1) | collective-permute-done | bytes 131104 | tf_op jit(solution)/shard_map/ppermute | solution.py:40
  22.5 0.7 collective-permute-start.2
  23.2 2.1 %collective-permute-start.3 = (f32[256,128]{1,0:T(8,128)S(1)}, f32[256,128]{1,0:T(8,128)S(1)}, u32[]{:S(2)}, u32[]{:S(2)}) collective-permute-start(f32[256,128]{1,0:T(8,128)S(1)} %add.21), channel_id=1, source_target_pairs={{0,4},{1,5},{2,6},{3,7},{4,0},{5,1},{6,2},{7,3},{8,12},{9,13},{10,... | collective-permute-start | bytes 393224 | tf_op jit(solution)/shard_map/ppermute | solution.py:40
  25.2 2.1 %collective-permute-start.4 = (f32[256,128]{1,0:T(8,128)S(1)}, f32[256,128]{1,0:T(8,128)S(1)}, u32[]{:S(2)}, u32[]{:S(2)}) collective-permute-start(f32[256,128]{1,0:T(8,128)S(1)} %add.21), channel_id=1, source_target_pairs={{0,6},{1,7},{2,4},{3,5},{4,2},{5,3},{6,0},{7,1},{8,14},{9,15},{10,... | collective-permute-start | bytes 393224 | tf_op jit(solution)/shard_map/ppermute | solution.py:40
  27.3 1.6 %collective-permute-done.2 = f32[256,128]{1,0:T(8,128)S(1)} collective-permute-done((f32[256,128]{1,0:T(8,128)S(1)}, f32[256,128]{1,0:T(8,128)S(1)}, u32[]{:S(2)}, u32[]{:S(2)}) %collective-permute-start.2) | collective-permute-done | bytes 131104 | tf_op jit(solution)/shard_map/ppermute | solution.py:40
  28.9 2.7 %collective-permute-done.3 = f32[256,128]{1,0:T(8,128)S(1)} collective-permute-done((f32[256,128]{1,0:T(8,128)S(1)}, f32[256,128]{1,0:T(8,128)S(1)}, u32[]{:S(2)}, u32[]{:S(2)}) %collective-permute-start.3) | collective-permute-done | bytes 131104 | tf_op jit(solution)/shard_map/ppermute | solution.py:40
  31.7 2.2 %collective-permute-done.4 = f32[256,128]{1,0:T(8,128)S(1)} collective-permute-done((f32[256,128]{1,0:T(8,128)S(1)}, f32[256,128]{1,0:T(8,128)S(1)}, u32[]{:S(2)}, u32[]{:S(2)}) %collective-permute-start.4) | collective-permute-done | bytes 131104 | tf_op jit(solution)/shard_map/ppermute | solution.py:40
  34.0 0.0 copy-done.1
  34.0 1.4 %extra_term.1 = (f32[128,1024]{1,0:T(8,128)S(1)}, f32[128,1024]{1,0:T(8,128)S(1)}) custom-call(bf16[256,128]{1,0:T(8,128)(2,1)S(1)} %multiply_convert_fusion.weight_ref.refs_2_, f32[256,128]{1,0:T(8,128)S(1)} %get-tuple-element.37.slot_ref, bf16[1024,2048]{1,0:T(8,128)(2,1)S(1)} %copy-done.1), custom_call_target="tpu_custom_call" | custom-call | flops 1073741824 | bytes 4194304 | tf_op jit(solution)/shard_map/extra_term/pallas_call | solution.py:231
  35.3 0.1 collective-permute-start.5
  35.4 1.7 %pack.1 = bf16[512,1408]{1,0:T(8,128)(2,1)} custom-call(s32[1,256]{1,0:T(1,128)S(1)} %get-tuple-element.33.place_ref, bf16[256,1024]{1,0:T(8,128)(2,1)S(1)} %bitcast.19, bf16[256,256]{1,0:T(8,128)(2,1)S(1)} %get-tuple-element.34.refs_1_, bf16[256,128]{1,0:T(8,128)(2,1)S(1)} %multiply_convert_fusion.weight_ref.refs_2_), custom_call_target="tpu_custom_call" | custom-call | flops 369098752 | bytes 2162688 | tf_op jit(solution)/shard_map/pack/pallas_call | solution.py:163
  37.2 11.2 %all-to-all-start.1 = ((bf16[32,16,1408]{2,1,0:T(8,128)(2,1)}), bf16[32,16,1408]{2,1,0:T(8,128)(2,1)S(1)}, u32[]{:S(2)}, u32[]{:S(2)}) async-start(bf16[32,16,1408]{2,1,0:T(8,128)(2,1)} %bitcast.3), calls=%async_computation.1 | async-start | bytes 2883584 | tf_op jit(solution)/shard_map/all_to_all | solution.py:353
  48.4 0.0 collective-permute-done.5.extra_pair_ref
  48.4 0.0 collective-permute-done.6.pair_frozen_ref
  48.4 0.0 copy-start.2
  48.4 2.2 %copy-done.2 = bf16[8192,256]{1,0:T(8,128)(2,1)S(1)} copy-done((bf16[8192,256]{1,0:T(8,128)(2,1)S(1)}, bf16[8192,256]{1,0:T(8,128)(2,1)}, u32[]{:S(2)}) %copy-start.2) | copy-done | bytes 4194328
  50.6 0.0 copy-start.9
  50.6 5.1 %pair_sum.1 = (f32[32,8192]{1,0:T(8,128)S(1)}, bf16[32,8192]{1,0:T(8,128)(2,1)S(1)}, bf16[32,8192]{1,0:T(8,128)(2,1)S(1)}, bf16[32,8192]{1,0:T(8,128)(2,1)S(1)}) custom-call(bf16[128,256]{1,0:T(8,128)(2,1)S(1)} %get-tuple-element.43.rows_ref, bf16[128,256]{1,0:T(8,128)(2,1)S(1)} %collective-permute-done.pair_rows_ref, ...), custom_call_target="tpu_custom_call" | custom-call | flops 1073741824 | bytes 12582912 | tf_op jit(solution)/shard_map/pair_sum/pallas_call | solution.py:267
  55.7 0.1 collective-permute-start.7
  55.8 3.5 %collective-permute-start.8 = (bf16[32,8192]{1,0:T(8,128)(2,1)S(1)}, bf16[32,8192]{1,0:T(8,128)(2,1)S(1)}, u32[]{:S(2)}, u32[]{:S(2)}) collective-permute-start(bf16[32,8192]{1,0:T(8,128)(2,1)S(1)} %get-tuple-element.49), channel_id=1, source_target_pairs={{0,4},{1,5},{2,6},{3,7},{4,0},{5,1},{6,2},{7,3},{8,12},{9,13},{10,... | collective-permute-start | bytes 1572872 | tf_op jit(solution)/shard_map/ppermute | solution.py:367
  59.3 0.0 collective-permute-start.9
  59.3 12.2 %collective-permute-done.7 = bf16[32,8192]{1,0:T(8,128)(2,1)S(1)} collective-permute-done((bf16[32,8192]{1,0:T(8,128)(2,1)S(1)}, bf16[32,8192]{1,0:T(8,128)(2,1)S(1)}, u32[]{:S(2)}, u32[]{:S(2)}) %collective-permute-start.7) | collective-permute-done | bytes 524320 | tf_op jit(solution)/shard_map/ppermute | solution.py:367
  71.4 10.8 %collective-permute-done.8 = bf16[32,8192]{1,0:T(8,128)(2,1)S(1)} collective-permute-done((bf16[32,8192]{1,0:T(8,128)(2,1)S(1)}, bf16[32,8192]{1,0:T(8,128)(2,1)S(1)}, u32[]{:S(2)}, u32[]{:S(2)}) %collective-permute-start.8) | collective-permute-done | bytes 524320 | tf_op jit(solution)/shard_map/ppermute | solution.py:367
  82.3 0.3 collective-permute-done.9
  82.6 1.0 %add_convert_fusion = bf16[32,8192]{1,0:T(8,128)(2,1)} fusion(bf16[32,8192]{1,0:T(8,128)(2,1)S(1)} %collective-permute-done.9, bf16[32,8192]{1,0:T(8,128)(2,1)S(1)} %collective-permute-done.8, f32[32,8192]{1,0:T(8,128)S(1)} %get-tuple-element.47, bf16[32,8192]{1,0:T(8,128)(2,1)S(1)} %collective-permute-done.7), kind=kLoop, calls=%fused_computation | loop fusion | flops 1835008 | bytes 3145728 | tf_op jit(solution)/shard_map/convert_element_type | solution.py:371
  83.6 1.5 %all-to-all-done.1 = bf16[32,16,1408]{2,1,0:T(8,128)(2,1)S(1)} async-done(((bf16[32,16,1408]{2,1,0:T(8,128)(2,1)}), bf16[32,16,1408]{2,1,0:T(8,128)(2,1)S(1)}, u32[]{:S(2)}, u32[]{:S(2)}) %all-to-all-start.1) | async-done | bytes 1441824 | tf_op jit(solution)/shard_map/all_to_all | solution.py:353
  85.1 0.0 copy-done.4
  85.2 0.0 copy-done.8
  85.2 0.0 copy-done.9
  85.2 0.0 copy-start.10
  85.2 0.8 copy-done.10
  86.0 1.4 %owners_update.1 = (f32[64,1024]{1,0:T(8,128)}, f32[64,1024]{1,0:T(8,128)}, f32[64,1024]{1,0:T(8,128)}, f32[64,256]{1,0:T(8,128)}, f32[64,256]{1,0:T(8,128)}, /*index=5*/f32[64,256]{1,0:T(8,128)}) custom-call(bf16[512,1408]{1,0:T(8,128)(2,1)S(1)} %bitcast.17, f32[64,1024]{1,0:T(8,128)S(1)} %bitcast.20, f32[64,1024]{1,0:T(8,128)S(1)} %bitcast.21, ...), custom_call_target="tpu_custom_call" | custom-call | flops 92274688 | bytes 3407872 | tf_op jit(solution)/shard_map/owners_update/pallas_call | solution.py:292
  (16 shorter events, 0.1 us)
Async XLA Ops:
  0.6 47.7 %collective-permute-start.6 = (bf16[8192,256]{1,0:T(8,128)(2,1)}, bf16[8192,256]{1,0:T(8,128)(2,1)}, u32[]{:S(2)}, u32[]{:S(2)}) collective-permute-start(bf16[8192,256]{1,0:T(8,128)(2,1)} %frozen_ref.1), channel_id=1, source_target_pairs={{0,1},{1,0},{2,3},{3,2},{4,5},{5,4},{6,7},{7,6},{8,9},{9,8},{10,11... | collective-permute-start | bytes 12582920 | tf_op jit(solution)/shard_map/ppermute | solution.py:40
  2.6 14.9 %all-to-all-start = ((bf16[8,32,1024]{2,1,0:T(8,128)(2,1)}), bf16[8,32,1024]{2,1,0:T(8,128)(2,1)S(1)}, u32[]{:S(2)}, u32[]{:S(2)}) async-start(bf16[8,32,1024]{2,1,0:T(8,128)(2,1)} %bitcast.16), calls=%async_computation | async-start | bytes 1048576 | tf_op jit(solution)/shard_map/all_to_all | solution.py:328
  7.2 1.2 %copy-start.3 = (bf16[2048,256]{1,0:T(8,128)(2,1)S(1)}, bf16[2048,256]{1,0:T(8,128)(2,1)}, u32[]{:S(2)}) copy-start(bf16[2048,256]{1,0:T(8,128)(2,1)} %up_ref.1) | copy-start | bytes 3145732
  8.4 0.9 %copy-start.7 = (bf16[256,256]{1,0:T(8,128)(2,1)S(1)}, bf16[256,256]{1,0:T(8,128)(2,1)}, u32[]{:S(2)}) copy-start(bf16[256,256]{1,0:T(8,128)(2,1)} %cot_ref.1) | copy-start | bytes 393220
  9.3 0.7 copy-start.11
  10.0 0.7 copy-start.12
  10.6 0.7 copy-start.13
  11.3 0.7 copy-start.14
  13.1 1.5 %collective-permute-start = (bf16[128,256]{1,0:T(8,128)(2,1)S(1)}, bf16[128,256]{1,0:T(8,128)(2,1)S(1)}, u32[]{:S(2)}, u32[]{:S(2)}) collective-permute-start(bf16[128,256]{1,0:T(8,128)(2,1)S(1)} %get-tuple-element.36), channel_id=1, source_target_pairs={{0,1},{1,0},{2,3},{3,2},{4,5},{5,4},{6,7},{7,6},{8,9},{9,8},{10,11... | collective-permute-start | bytes 196616 | tf_op jit(solution)/shard_map/ppermute | solution.py:40
  17.5 2.2 %copy-start = (bf16[1024,2048]{1,0:T(8,128)(2,1)S(1)}, bf16[1024,2048]{1,0:T(8,128)(2,1)}, u32[]{:S(2)}) copy-start(bf16[1024,2048]{1,0:T(8,128)(2,1)} %factors_ref.3) | copy-start | bytes 12582916
  19.7 14.2 %copy-start.1 = (bf16[1024,2048]{1,0:T(8,128)(2,1)S(1)}, bf16[1024,2048]{1,0:T(8,128)(2,1)}, u32[]{:S(2)}) copy-start(bf16[1024,2048]{1,0:T(8,128)(2,1)} %factors_ref.3) | copy-start | bytes 12582916
  21.0 1.4 %collective-permute-start.1 = (f32[256,128]{1,0:T(8,128)S(1)}, f32[256,128]{1,0:T(8,128)S(1)}, u32[]{:S(2)}, u32[]{:S(2)}) collective-permute-start(f32[256,128]{1,0:T(8,128)S(1)} %low_rank.1), channel_id=1, source_target_pairs={{0,1},{1,0},{2,3},{3,2},{4,5},{5,4},{6,7},{7,6},{8,9},{9,8},{10,11... | collective-permute-start | bytes 393224 | tf_op jit(solution)/shard_map/ppermute | solution.py:40
  22.5 6.4 %collective-permute-start.2 = (f32[256,128]{1,0:T(8,128)S(1)}, f32[256,128]{1,0:T(8,128)S(1)}, u32[]{:S(2)}, u32[]{:S(2)}) collective-permute-start(f32[256,128]{1,0:T(8,128)S(1)} %add.21), channel_id=1, source_target_pairs={{0,2},{1,3},{2,0},{3,1},{4,6},{5,7},{6,4},{7,5},{8,10},{9,11},{10,... | collective-permute-start | bytes 393224 | tf_op jit(solution)/shard_map/ppermute | solution.py:40
  23.2 8.5 %collective-permute-start.3 = (f32[256,128]{1,0:T(8,128)S(1)}, f32[256,128]{1,0:T(8,128)S(1)}, u32[]{:S(2)}, u32[]{:S(2)}) collective-permute-start(f32[256,128]{1,0:T(8,128)S(1)} %add.21), channel_id=1, source_target_pairs={{0,4},{1,5},{2,6},{3,7},{4,0},{5,1},{6,2},{7,3},{8,12},{9,13},{10,... | collective-permute-start | bytes 393224 | tf_op jit(solution)/shard_map/ppermute | solution.py:40
  25.2 8.7 %collective-permute-start.4 = (f32[256,128]{1,0:T(8,128)S(1)}, f32[256,128]{1,0:T(8,128)S(1)}, u32[]{:S(2)}, u32[]{:S(2)}) collective-permute-start(f32[256,128]{1,0:T(8,128)S(1)} %add.21), channel_id=1, source_target_pairs={{0,6},{1,7},{2,4},{3,5},{4,2},{5,3},{6,0},{7,1},{8,14},{9,15},{10,... | collective-permute-start | bytes 393224 | tf_op jit(solution)/shard_map/ppermute | solution.py:40
  35.3 13.0 %collective-permute-start.5 = (f32[128,1024]{1,0:T(8,128)S(1)}, f32[128,1024]{1,0:T(8,128)S(1)}, u32[]{:S(2)}, u32[]{:S(2)}) collective-permute-start(f32[128,1024]{1,0:T(8,128)S(1)} %get-tuple-element.46), channel_id=1, source_target_pairs={{0,1},{1,0},{2,3},{3,2},{4,5},{5,4},{6,7},{7,6},{8,9},{9,8},{10,11... | collective-permute-start | bytes 1572872 | tf_op jit(solution)/shard_map/ppermute | solution.py:40
  37.2 48.0 %all-to-all-start.1 = ((bf16[32,16,1408]{2,1,0:T(8,128)(2,1)}), bf16[32,16,1408]{2,1,0:T(8,128)(2,1)S(1)}, u32[]{:S(2)}, u32[]{:S(2)}) async-start(bf16[32,16,1408]{2,1,0:T(8,128)(2,1)} %bitcast.3), calls=%async_computation.1 | async-start | bytes 2883584 | tf_op jit(solution)/shard_map/all_to_all | solution.py:353
  48.4 2.2 %copy-start.2 = (bf16[8192,256]{1,0:T(8,128)(2,1)S(1)}, bf16[8192,256]{1,0:T(8,128)(2,1)}, u32[]{:S(2)}) copy-start(bf16[8192,256]{1,0:T(8,128)(2,1)} %frozen_ref.1) | copy-start | bytes 12582916
  50.6 34.6 %copy-start.4 = (f32[1024,64]{0,1:T(8,128)S(1)}, f32[1024,64]{0,1:T(8,128)}, u32[]{:S(2)}) copy-start(f32[1024,64]{0,1:T(8,128)} %param.20) | copy-start | bytes 786436
  50.6 34.6 %copy-start.5 = (f32[1024,64]{0,1:T(8,128)S(1)}, f32[1024,64]{0,1:T(8,128)}, u32[]{:S(2)}) copy-start(f32[1024,64]{0,1:T(8,128)} %param.21) | copy-start | bytes 786436
  50.6 34.6 %copy-start.6 = (f32[1024,64]{0,1:T(8,128)S(1)}, f32[1024,64]{0,1:T(8,128)}, u32[]{:S(2)}) copy-start(f32[1024,64]{0,1:T(8,128)} %param.22) | copy-start | bytes 786436
  50.6 34.6 %copy-start.8 = (f32[64,256]{1,0:T(8,128)S(1)}, f32[64,256]{1,0:T(8,128)}, u32[]{:S(2)}) copy-start(f32[64,256]{1,0:T(8,128)} %refs_3_.1) | copy-start | bytes 196612
  50.6 34.6 %copy-start.9 = (f32[64,256]{1,0:T(8,128)S(1)}, f32[64,256]{1,0:T(8,128)}, u32[]{:S(2)}) copy-start(f32[64,256]{1,0:T(8,128)} %refs_4_.1) | copy-start | bytes 196612
  55.7 15.8 %collective-permute-start.7 = (bf16[32,8192]{1,0:T(8,128)(2,1)S(1)}, bf16[32,8192]{1,0:T(8,128)(2,1)S(1)}, u32[]{:S(2)}, u32[]{:S(2)}) collective-permute-start(bf16[32,8192]{1,0:T(8,128)(2,1)S(1)} %get-tuple-element.48), channel_id=1, source_target_pairs={{0,2},{1,3},{2,4},{3,5},{4,6},{5,7},{6,0},{7,1},{8,10},{9,11},{10,... | collective-permute-start | bytes 1572872 | tf_op jit(solution)/shard_map/ppermute | solution.py:367
  55.8 26.5 %collective-permute-start.8 = (bf16[32,8192]{1,0:T(8,128)(2,1)S(1)}, bf16[32,8192]{1,0:T(8,128)(2,1)S(1)}, u32[]{:S(2)}, u32[]{:S(2)}) collective-permute-start(bf16[32,8192]{1,0:T(8,128)(2,1)S(1)} %get-tuple-element.49), channel_id=1, source_target_pairs={{0,4},{1,5},{2,6},{3,7},{4,0},{5,1},{6,2},{7,3},{8,12},{9,13},{10,... | collective-permute-start | bytes 1572872 | tf_op jit(solution)/shard_map/ppermute | solution.py:367
  59.3 23.3 %collective-permute-start.9 = (bf16[32,8192]{1,0:T(8,128)(2,1)S(1)}, bf16[32,8192]{1,0:T(8,128)(2,1)S(1)}, u32[]{:S(2)}, u32[]{:S(2)}) collective-permute-start(bf16[32,8192]{1,0:T(8,128)(2,1)S(1)} %get-tuple-element.50), channel_id=1, source_target_pairs={{0,6},{1,7},{2,0},{3,1},{4,2},{5,3},{6,4},{7,5},{8,14},{9,15},{10,... | collective-permute-start | bytes 1572872 | tf_op jit(solution)/shard_map/ppermute | solution.py:367
  85.2 0.8 copy-start.10

commit v10 on v9

--- a/solution.py
+++ b/solution.py
@@ -41,9 +41,10 @@
 
 
 def sum_over_chips(value, count):
-    near = value + swap(value, 2, count)
-    far = swap(value, 4, count) + swap(value, 6, count)
-    return near + far
+    value = value.astype(jnp.bfloat16)
+    terms = [value] + [swap(value, mask, count) for mask in (2, 4, 6)]
+    own, near, far, farther = (term.astype(jnp.float32) for term in terms)
+    return (own + near) + (far + farther)
 
 
 VMEM_LIMIT = 16 * 1024 * 1024
@@ -344,12 +345,9 @@
     own = low_rank(hidden_columns, slot_wide, up_own, adapter_down_factors)
     own = own + swap(own, 1, n_tensor)
     weights = (sum_over_chips(own, n_tensor) * factor_wide).astype(jnp.bfloat16)
+    packed = pack_rows(place, [hidden_columns, masked, weights], n_slot * CAP)
+    packed, weights = lax.optimization_barrier((packed, weights))
     extra_ours, extra_theirs = extra_term(rows_own, weights, slot_wide, adapter_down_factors)
-    weights, extra_ours, extra_theirs = lax.optimization_barrier(
-        (weights, extra_ours, extra_theirs)
-    )
-
-    packed = pack_rows(place, [hidden_columns, masked, weights], n_slot * CAP)
     owned = lax.all_to_all(
         packed.reshape(n_slot, CAP, -1), "dp", 0, 0, tiled=True
     ).reshape(n_slot * CAP, -1)

time: 87.9 us -> 84 us (0.956)
  waiting for transfers between devices: 36.7 us -> 32.5 us
    ppermute x7, waiting for transfers between devices: 8.85 us -> 5.48 us  [swap(): return lax.ppermute(value, 'tensor', [(i, i ^ mask) for i in range(count)])]
  transfers between devices with their start and end apart: 12 -> 12, of which waited for: 10 -> 10; matrix products, arithmetic and copies ran while one was open for 3% -> 4% of each run, Pallas kernels for 12% -> 13%
where the time goes in v10:
time: 84 us; the launch traced here: 83.4 us
  waiting for transfers between devices  32.5 us (39%)
  starting transfers between devices  25.2 us (30%)
  Pallas kernels  12 us (14%)
  local copies, waits for them, and re-layouts  11.9 us (14%)
  other arithmetic  1.08 us (1%)
    ppermute x3, waiting for transfers between devices, local(): lax.ppermute(value, 'tensor', [(i, (i + 2 * step) % n_tensor) for i in ra...  22.5 us
    all_to_all x1, starting transfers between devices, local(): lax.all_to_all(packed.reshape(n_slot, CAP, -1), 'dp', 0, 0, tiled=True)  11.2 us
    unnamed x30, local copies, waits for them, and re-layouts  10 us
    ppermute x7, waiting for transfers between devices, swap(): return lax.ppermute(value, 'tensor', [(i, i ^ mask) for i in range(count)])  5.48 us
    pallas_call x1, Pallas kernels, pair_sum(): call(functools.partial(pair_kernel, rows_own), (jax.ShapeDtypeStruct((row...  5.07 us
    ppermute x7, starting transfers between devices, swap(): return lax.ppermute(value, 'tensor', [(i, i ^ mask) for i in range(count)])  5.05 us
    all_to_all x1, starting transfers between devices, local(): lax.all_to_all(blocks, 'tensor', 0, 0, tiled=True).reshape(tokens, columns)  4.57 us
    ppermute x3, starting transfers between devices, local(): lax.ppermute(value, 'tensor', [(i, (i + 2 * step) % n_tensor) for i in ra...  4.4 us
  transfers between devices with their start and end apart: 12, of which 10 were waited for; matrix products, arithmetic and copies ran while one was open for 4% of the time, Pallas kernels for 13%

profile of v10, /device:TPU:32, one launch (start us, length us, event | category | flops | bytes accessed | tf_op | source)
XLA Modules:
  0.0 83.4 jit_solution(1391483167630300303)
XLA Ops:
  0.6 0.1 collective-permute-start.6
  0.7 1.9 %copy.25 = bf16[4,8,8,1024]{3,2,0,1:T(8,128)(2,1)} copy(bf16[4,8,8,1024]{3,2,1,0:T(8,128)(2,1)} %bitcast.24) | data formatting | bytes 1048576 | tf_op jit(solution)/shard_map/reshape | solution.py:328
  2.6 4.6 %all-to-all-start = ((bf16[8,32,1024]{2,1,0:T(8,128)(2,1)}), bf16[8,32,1024]{2,1,0:T(8,128)(2,1)S(1)}, u32[]{:S(2)}, u32[]{:S(2)}) async-start(bf16[8,32,1024]{2,1,0:T(8,128)(2,1)} %bitcast.16), calls=%async_computation | async-start | bytes 1048576 | tf_op jit(solution)/shard_map/all_to_all | solution.py:329
  7.2 1.2 %copy-done.3 = bf16[2048,256]{1,0:T(8,128)(2,1)S(1)} copy-done((bf16[2048,256]{1,0:T(8,128)(2,1)S(1)}, bf16[2048,256]{1,0:T(8,128)(2,1)}, u32[]{:S(2)}) %copy-start.3) | copy-done | bytes 1048600
  8.4 0.9 %copy-done.7 = bf16[256,256]{1,0:T(8,128)(2,1)S(1)} copy-done((bf16[256,256]{1,0:T(8,128)(2,1)S(1)}, bf16[256,256]{1,0:T(8,128)(2,1)}, u32[]{:S(2)}) %copy-start.7) | copy-done | bytes 131096
  9.3 0.7 copy-done.11
  10.0 0.7 copy-done.12
  10.6 0.7 copy-done.13
  11.3 0.7 copy-done.14
  12.0 1.1 %prep.1 = (bf16[256,256]{1,0:T(8,128)(2,1)S(1)}, bf16[128,256]{1,0:T(8,128)(2,1)S(1)}, bf16[128,256]{1,0:T(8,128)(2,1)S(1)}, f32[256,128]{1,0:T(8,128)S(1)}, f32...) custom-call(s32[32]{0:T(128)S(1)} %copy-done.12, s32[32]{0:T(128)S(1)} %copy-done.13, ...), custom_call_target="tpu_custom_call" | custom-call | flops 268435456 | bytes 1048576 | tf_op jit(solution)/shard_map/prep/pallas_call | solution.py:139
  13.1 0.6 collective-permute-start
  13.7 0.9 %collective-permute-done.pair_rows_ref = bf16[128,256]{1,0:T(8,128)(2,1)S(1)} collective-permute-done((bf16[128,256]{1,0:T(8,128)(2,1)S(1)}, bf16[128,256]{1,0:T(8,128)(2,1)S(1)}, u32[]{:S(2)}, u32[]{:S(2)}) %collective-permute-start) | collective-permute-done | bytes 65568 | tf_op jit(solution)/shard_map/ppermute | solution.py:40
  14.6 3.0 %all-to-all-done = bf16[8,32,1024]{2,1,0:T(8,128)(2,1)S(1)} async-done(((bf16[8,32,1024]{2,1,0:T(8,128)(2,1)}), bf16[8,32,1024]{2,1,0:T(8,128)(2,1)S(1)}, u32[]{:S(2)}, u32[]{:S(2)}) %all-to-all-start) | async-done | bytes 524320 | tf_op jit(solution)/shard_map/all_to_all | solution.py:329
  17.5 2.2 %copy-done = bf16[1024,2048]{1,0:T(8,128)(2,1)S(1)} copy-done((bf16[1024,2048]{1,0:T(8,128)(2,1)S(1)}, bf16[1024,2048]{1,0:T(8,128)(2,1)}, u32[]{:S(2)}) %copy-start) | copy-done | bytes 4194328
  19.7 1.3 %low_rank.1 = f32[256,128]{1,0:T(8,128)S(1)} custom-call(bf16[256,1024]{1,0:T(8,128)(2,1)S(1)} %bitcast.18, f32[256,128]{1,0:T(8,128)S(1)} %get-tuple-element.36.slot_ref, f32[256,64]{1,0:T(8,128)S(1)} %get-tuple-element.37.up_own_ref, bf16[1024,2048]{1,0:T(8,128)(2,1)S(1)} %copy-done), custom_call_target="tpu_custom_call" | custom-call | flops 1073741824 | bytes 4194304 | tf_op jit(solution)/shard_map/low_rank/pallas_call | solution.py:192
  21.0 0.1 collective-permute-start.1
  21.1 1.3 %collective-permute-done.1 = f32[256,128]{1,0:T(8,128)S(1)} collective-permute-done((f32[256,128]{1,0:T(8,128)S(1)}, f32[256,128]{1,0:T(8,128)S(1)}, u32[]{:S(2)}, u32[]{:S(2)}) %collective-permute-start.1) | collective-permute-done | bytes 131104 | tf_op jit(solution)/shard_map/ppermute | solution.py:40
  22.5 1.3 %collective-permute-start.4 = (bf16[256,128]{1,0:T(8,128)(2,1)S(1)}, bf16[256,128]{1,0:T(8,128)(2,1)S(1)}, u32[]{:S(2)}, u32[]{:S(2)}) collective-permute-start(bf16[256,128]{1,0:T(8,128)(2,1)S(1)} %add_convert_fusion.1), channel_id=1, source_target_pairs={{0,6},{1,7},{2,4},{3,5},{4,2},{5,3},{6,0},{7,1},{8,14},{9,15},{10,... | collective-permute-start | bytes 196616 | tf_op jit(solution)/shard_map/ppermute | solution.py:40
  23.8 1.5 %collective-permute-start.3 = (bf16[256,128]{1,0:T(8,128)(2,1)S(1)}, bf16[256,128]{1,0:T(8,128)(2,1)S(1)}, u32[]{:S(2)}, u32[]{:S(2)}) collective-permute-start(bf16[256,128]{1,0:T(8,128)(2,1)S(1)} %add_convert_fusion.1), channel_id=1, source_target_pairs={{0,4},{1,5},{2,6},{3,7},{4,0},{5,1},{6,2},{7,3},{8,12},{9,13},{10,... | collective-permute-start | bytes 196616 | tf_op jit(solution)/shard_map/ppermute | solution.py:40
  25.2 1.5 %collective-permute-start.2 = (bf16[256,128]{1,0:T(8,128)(2,1)S(1)}, bf16[256,128]{1,0:T(8,128)(2,1)S(1)}, u32[]{:S(2)}, u32[]{:S(2)}) collective-permute-start(bf16[256,128]{1,0:T(8,128)(2,1)S(1)} %add_convert_fusion.1), channel_id=1, source_target_pairs={{0,2},{1,3},{2,0},{3,1},{4,6},{5,7},{6,4},{7,5},{8,10},{9,11},{10,... | collective-permute-start | bytes 196616 | tf_op jit(solution)/shard_map/ppermute | solution.py:40
  26.7 2.1 %collective-permute-done.4 = bf16[256,128]{1,0:T(8,128)(2,1)S(1)} collective-permute-done((bf16[256,128]{1,0:T(8,128)(2,1)S(1)}, bf16[256,128]{1,0:T(8,128)(2,1)S(1)}, u32[]{:S(2)}, u32[]{:S(2)}) %collective-permute-start.4) | collective-permute-done | bytes 65568 | tf_op jit(solution)/shard_map/ppermute | solution.py:40
  28.8 1.1 %collective-permute-done.3 = bf16[256,128]{1,0:T(8,128)(2,1)S(1)} collective-permute-done((bf16[256,128]{1,0:T(8,128)(2,1)S(1)}, bf16[256,128]{1,0:T(8,128)(2,1)S(1)}, u32[]{:S(2)}, u32[]{:S(2)}) %collective-permute-start.3) | collective-permute-done | bytes 65568 | tf_op jit(solution)/shard_map/ppermute | solution.py:40
  29.8 0.1 collective-permute-done.2
  30.0 1.7 %pack.1 = bf16[512,1408]{1,0:T(8,128)(2,1)} custom-call(s32[1,256]{1,0:T(1,128)S(1)} %get-tuple-element.32.place_ref, bf16[256,1024]{1,0:T(8,128)(2,1)S(1)} %bitcast.19, bf16[256,256]{1,0:T(8,128)(2,1)S(1)} %get-tuple-element.33.refs_1_, bf16[256,128]{1,0:T(8,128)(2,1)S(1)} %multiply_convert_fusion.refs_2_.weight_ref), custom_call_target="tpu_custom_call" | custom-call | flops 369098752 | bytes 2162688 | tf_op jit(solution)/shard_map/pack/pallas_call | solution.py:164
  31.7 0.0 copy-done.1
  31.7 1.4 %extra_term.1 = (f32[128,1024]{1,0:T(8,128)S(1)}, f32[128,1024]{1,0:T(8,128)S(1)}) custom-call(bf16[256,128]{1,0:T(8,128)(2,1)S(1)} %multiply_convert_fusion.refs_2_.weight_ref, f32[256,128]{1,0:T(8,128)S(1)} %get-tuple-element.36.slot_ref, bf16[1024,2048]{1,0:T(8,128)(2,1)S(1)} %copy-done.1), custom_call_target="tpu_custom_call" | custom-call | flops 1073741824 | bytes 4194304 | tf_op jit(solution)/shard_map/extra_term/pallas_call | solution.py:232
  33.1 0.1 collective-permute-start.5
  33.2 11.2 %all-to-all-start.1 = ((bf16[32,16,1408]{2,1,0:T(8,128)(2,1)}), bf16[32,16,1408]{2,1,0:T(8,128)(2,1)S(1)}, u32[]{:S(2)}, u32[]{:S(2)}) async-start(bf16[32,16,1408]{2,1,0:T(8,128)(2,1)} %bitcast.3), calls=%async_computation.1 | async-start | bytes 2883584 | tf_op jit(solution)/shard_map/all_to_all | solution.py:351
  44.4 0.0 collective-permute-done.5.extra_pair_ref
  44.4 0.0 collective-permute-done.6.pair_frozen_ref
  44.4 0.0 copy-start.2
  44.4 2.2 %copy-done.2 = bf16[8192,256]{1,0:T(8,128)(2,1)S(1)} copy-done((bf16[8192,256]{1,0:T(8,128)(2,1)S(1)}, bf16[8192,256]{1,0:T(8,128)(2,1)}, u32[]{:S(2)}) %copy-start.2) | copy-done | bytes 4194328
  46.6 0.0 copy-start.9
  46.6 5.1 %pair_sum.1 = (f32[32,8192]{1,0:T(8,128)S(1)}, bf16[32,8192]{1,0:T(8,128)(2,1)S(1)}, bf16[32,8192]{1,0:T(8,128)(2,1)S(1)}, bf16[32,8192]{1,0:T(8,128)(2,1)S(1)}) custom-call(bf16[128,256]{1,0:T(8,128)(2,1)S(1)} %get-tuple-element.40.rows_ref, bf16[128,256]{1,0:T(8,128)(2,1)S(1)} %collective-permute-done.pair_rows_ref, ...), custom_call_target="tpu_custom_call" | custom-call | flops 1073741824 | bytes 12582912 | tf_op jit(solution)/shard_map/pair_sum/pallas_call | solution.py:268
  51.7 1.1 %collective-permute-start.7 = (bf16[32,8192]{1,0:T(8,128)(2,1)S(1)}, bf16[32,8192]{1,0:T(8,128)(2,1)S(1)}, u32[]{:S(2)}, u32[]{:S(2)}) collective-permute-start(bf16[32,8192]{1,0:T(8,128)(2,1)S(1)} %get-tuple-element.46), channel_id=1, source_target_pairs={{0,2},{1,3},{2,4},{3,5},{4,6},{5,7},{6,0},{7,1},{8,10},{9,11},{10,... | collective-permute-start | bytes 1572872 | tf_op jit(solution)/shard_map/ppermute | solution.py:365
  52.8 2.4 %collective-permute-start.8 = (bf16[32,8192]{1,0:T(8,128)(2,1)S(1)}, bf16[32,8192]{1,0:T(8,128)(2,1)S(1)}, u32[]{:S(2)}, u32[]{:S(2)}) collective-permute-start(bf16[32,8192]{1,0:T(8,128)(2,1)S(1)} %get-tuple-element.47), channel_id=1, source_target_pairs={{0,4},{1,5},{2,6},{3,7},{4,0},{5,1},{6,2},{7,3},{8,12},{9,13},{10,... | collective-permute-start | bytes 1572872 | tf_op jit(solution)/shard_map/ppermute | solution.py:365
  55.2 0.9 %collective-permute-start.9 = (bf16[32,8192]{1,0:T(8,128)(2,1)S(1)}, bf16[32,8192]{1,0:T(8,128)(2,1)S(1)}, u32[]{:S(2)}, u32[]{:S(2)}) collective-permute-start(bf16[32,8192]{1,0:T(8,128)(2,1)S(1)} %get-tuple-element.48), channel_id=1, source_target_pairs={{0,6},{1,7},{2,0},{3,1},{4,2},{5,3},{6,4},{7,5},{8,14},{9,15},{10,... | collective-permute-start | bytes 1572872 | tf_op jit(solution)/shard_map/ppermute | solution.py:365
  56.1 11.5 %collective-permute-done.7 = bf16[32,8192]{1,0:T(8,128)(2,1)S(1)} collective-permute-done((bf16[32,8192]{1,0:T(8,128)(2,1)S(1)}, bf16[32,8192]{1,0:T(8,128)(2,1)S(1)}, u32[]{:S(2)}, u32[]{:S(2)}) %collective-permute-start.7) | collective-permute-done | bytes 524320 | tf_op jit(solution)/shard_map/ppermute | solution.py:365
  67.6 10.6 %collective-permute-done.8 = bf16[32,8192]{1,0:T(8,128)(2,1)S(1)} collective-permute-done((bf16[32,8192]{1,0:T(8,128)(2,1)S(1)}, bf16[32,8192]{1,0:T(8,128)(2,1)S(1)}, u32[]{:S(2)}, u32[]{:S(2)}) %collective-permute-start.8) | collective-permute-done | bytes 524320 | tf_op jit(solution)/shard_map/ppermute | solution.py:365
  78.2 0.4 collective-permute-done.9
  78.6 1.0 %add_convert_fusion = bf16[32,8192]{1,0:T(8,128)(2,1)} fusion(bf16[32,8192]{1,0:T(8,128)(2,1)S(1)} %collective-permute-done.9, bf16[32,8192]{1,0:T(8,128)(2,1)S(1)} %collective-permute-done.8, f32[32,8192]{1,0:T(8,128)S(1)} %get-tuple-element.45, bf16[32,8192]{1,0:T(8,128)(2,1)S(1)} %collective-permute-done.7), kind=kLoop, calls=%fused_computation | loop fusion | flops 1835008 | bytes 3145728 | tf_op jit(solution)/shard_map/convert_element_type | solution.py:369
  79.6 1.5 %all-to-all-done.1 = bf16[32,16,1408]{2,1,0:T(8,128)(2,1)S(1)} async-done(((bf16[32,16,1408]{2,1,0:T(8,128)(2,1)}), bf16[32,16,1408]{2,1,0:T(8,128)(2,1)S(1)}, u32[]{:S(2)}, u32[]{:S(2)}) %all-to-all-start.1) | async-done | bytes 1441824 | tf_op jit(solution)/shard_map/all_to_all | solution.py:351
  81.1 0.0 copy-done.4
  81.2 0.0 copy-done.5
  81.2 0.0 copy-done.6
  81.2 0.0 copy-start.10
  81.2 0.8 copy-done.10
  82.0 1.4 %owners_update.1 = (f32[64,1024]{1,0:T(8,128)}, f32[64,1024]{1,0:T(8,128)}, f32[64,1024]{1,0:T(8,128)}, f32[64,256]{1,0:T(8,128)}, f32[64,256]{1,0:T(8,128)}, /*index=5*/f32[64,256]{1,0:T(8,128)}) custom-call(bf16[512,1408]{1,0:T(8,128)(2,1)S(1)} %bitcast.17, f32[64,1024]{1,0:T(8,128)S(1)} %bitcast.20, f32[64,1024]{1,0:T(8,128)S(1)} %bitcast.21, ...), custom_call_target="tpu_custom_call" | custom-call | flops 92274688 | bytes 3407872 | tf_op jit(solution)/shard_map/owners_update/pallas_call | solution.py:293
  (16 shorter events, 0.1 us)
Async XLA Ops:
  0.6 43.8 %collective-permute-start.6 = (bf16[8192,256]{1,0:T(8,128)(2,1)}, bf16[8192,256]{1,0:T(8,128)(2,1)}, u32[]{:S(2)}, u32[]{:S(2)}) collective-permute-start(bf16[8192,256]{1,0:T(8,128)(2,1)} %frozen_ref.1), channel_id=1, source_target_pairs={{0,1},{1,0},{2,3},{3,2},{4,5},{5,4},{6,7},{7,6},{8,9},{9,8},{10,11... | collective-permute-start | bytes 12582920 | tf_op jit(solution)/shard_map/ppermute | solution.py:40
  2.6 14.9 %all-to-all-start = ((bf16[8,32,1024]{2,1,0:T(8,128)(2,1)}), bf16[8,32,1024]{2,1,0:T(8,128)(2,1)S(1)}, u32[]{:S(2)}, u32[]{:S(2)}) async-start(bf16[8,32,1024]{2,1,0:T(8,128)(2,1)} %bitcast.16), calls=%async_computation | async-start | bytes 1048576 | tf_op jit(solution)/shard_map/all_to_all | solution.py:329
  7.2 1.2 %copy-start.3 = (bf16[2048,256]{1,0:T(8,128)(2,1)S(1)}, bf16[2048,256]{1,0:T(8,128)(2,1)}, u32[]{:S(2)}) copy-start(bf16[2048,256]{1,0:T(8,128)(2,1)} %up_ref.1) | copy-start | bytes 3145732
  8.4 0.9 %copy-start.7 = (bf16[256,256]{1,0:T(8,128)(2,1)S(1)}, bf16[256,256]{1,0:T(8,128)(2,1)}, u32[]{:S(2)}) copy-start(bf16[256,256]{1,0:T(8,128)(2,1)} %cot_ref.1) | copy-start | bytes 393220
  9.3 0.7 copy-start.11
  10.0 0.7 copy-start.12
  10.6 0.7 copy-start.13
  11.3 0.7 copy-start.14
  13.1 1.5 %collective-permute-start = (bf16[128,256]{1,0:T(8,128)(2,1)S(1)}, bf16[128,256]{1,0:T(8,128)(2,1)S(1)}, u32[]{:S(2)}, u32[]{:S(2)}) collective-permute-start(bf16[128,256]{1,0:T(8,128)(2,1)S(1)} %get-tuple-element.35), channel_id=1, source_target_pairs={{0,1},{1,0},{2,3},{3,2},{4,5},{5,4},{6,7},{7,6},{8,9},{9,8},{10,11... | collective-permute-start | bytes 196616 | tf_op jit(solution)/shard_map/ppermute | solution.py:40
  17.5 2.2 %copy-start = (bf16[1024,2048]{1,0:T(8,128)(2,1)S(1)}, bf16[1024,2048]{1,0:T(8,128)(2,1)}, u32[]{:S(2)}) copy-start(bf16[1024,2048]{1,0:T(8,128)(2,1)} %factors_ref.3) | copy-start | bytes 12582916
  19.7 12.0 %copy-start.1 = (bf16[1024,2048]{1,0:T(8,128)(2,1)S(1)}, bf16[1024,2048]{1,0:T(8,128)(2,1)}, u32[]{:S(2)}) copy-start(bf16[1024,2048]{1,0:T(8,128)(2,1)} %factors_ref.3) | copy-start | bytes 12582916
  21.0 1.4 %collective-permute-start.1 = (f32[256,128]{1,0:T(8,128)S(1)}, f32[256,128]{1,0:T(8,128)S(1)}, u32[]{:S(2)}, u32[]{:S(2)}) collective-permute-start(f32[256,128]{1,0:T(8,128)S(1)} %low_rank.1), channel_id=1, source_target_pairs={{0,1},{1,0},{2,3},{3,2},{4,5},{5,4},{6,7},{7,6},{8,9},{9,8},{10,11... | collective-permute-start | bytes 393224 | tf_op jit(solution)/shard_map/ppermute | solution.py:40
  22.5 6.3 %collective-permute-start.4 = (bf16[256,128]{1,0:T(8,128)(2,1)S(1)}, bf16[256,128]{1,0:T(8,128)(2,1)S(1)}, u32[]{:S(2)}, u32[]{:S(2)}) collective-permute-start(bf16[256,128]{1,0:T(8,128)(2,1)S(1)} %add_convert_fusion.1), channel_id=1, source_target_pairs={{0,6},{1,7},{2,4},{3,5},{4,2},{5,3},{6,0},{7,1},{8,14},{9,15},{10,... | collective-permute-start | bytes 196616 | tf_op jit(solution)/shard_map/ppermute | solution.py:40
  23.8 6.1 %collective-permute-start.3 = (bf16[256,128]{1,0:T(8,128)(2,1)S(1)}, bf16[256,128]{1,0:T(8,128)(2,1)S(1)}, u32[]{:S(2)}, u32[]{:S(2)}) collective-permute-start(bf16[256,128]{1,0:T(8,128)(2,1)S(1)} %add_convert_fusion.1), channel_id=1, source_target_pairs={{0,4},{1,5},{2,6},{3,7},{4,0},{5,1},{6,2},{7,3},{8,12},{9,13},{10,... | collective-permute-start | bytes 196616 | tf_op jit(solution)/shard_map/ppermute | solution.py:40
  25.2 4.7 %collective-permute-start.2 = (bf16[256,128]{1,0:T(8,128)(2,1)S(1)}, bf16[256,128]{1,0:T(8,128)(2,1)S(1)}, u32[]{:S(2)}, u32[]{:S(2)}) collective-permute-start(bf16[256,128]{1,0:T(8,128)(2,1)S(1)} %add_convert_fusion.1), channel_id=1, source_target_pairs={{0,2},{1,3},{2,0},{3,1},{4,6},{5,7},{6,4},{7,5},{8,10},{9,11},{10,... | collective-permute-start | bytes 196616 | tf_op jit(solution)/shard_map/ppermute | solution.py:40
  33.1 11.3 %collective-permute-start.5 = (f32[128,1024]{1,0:T(8,128)S(1)}, f32[128,1024]{1,0:T(8,128)S(1)}, u32[]{:S(2)}, u32[]{:S(2)}) collective-permute-start(f32[128,1024]{1,0:T(8,128)S(1)} %get-tuple-element.44), channel_id=1, source_target_pairs={{0,1},{1,0},{2,3},{3,2},{4,5},{5,4},{6,7},{7,6},{8,9},{9,8},{10,11... | collective-permute-start | bytes 1572872 | tf_op jit(solution)/shard_map/ppermute | solution.py:40
  33.2 48.0 %all-to-all-start.1 = ((bf16[32,16,1408]{2,1,0:T(8,128)(2,1)}), bf16[32,16,1408]{2,1,0:T(8,128)(2,1)S(1)}, u32[]{:S(2)}, u32[]{:S(2)}) async-start(bf16[32,16,1408]{2,1,0:T(8,128)(2,1)} %bitcast.3), calls=%async_computation.1 | async-start | bytes 2883584 | tf_op jit(solution)/shard_map/all_to_all | solution.py:351
  44.4 2.2 %copy-start.2 = (bf16[8192,256]{1,0:T(8,128)(2,1)S(1)}, bf16[8192,256]{1,0:T(8,128)(2,1)}, u32[]{:S(2)}) copy-start(bf16[8192,256]{1,0:T(8,128)(2,1)} %frozen_ref.1) | copy-start | bytes 12582916
  46.6 34.6 %copy-start.4 = (f32[1024,64]{0,1:T(8,128)S(1)}, f32[1024,64]{0,1:T(8,128)}, u32[]{:S(2)}) copy-start(f32[1024,64]{0,1:T(8,128)} %param.20) | copy-start | bytes 786436
  46.6 34.6 %copy-start.5 = (f32[1024,64]{0,1:T(8,128)S(1)}, f32[1024,64]{0,1:T(8,128)}, u32[]{:S(2)}) copy-start(f32[1024,64]{0,1:T(8,128)} %param.21) | copy-start | bytes 786436
  46.6 34.6 %copy-start.6 = (f32[1024,64]{0,1:T(8,128)S(1)}, f32[1024,64]{0,1:T(8,128)}, u32[]{:S(2)}) copy-start(f32[1024,64]{0,1:T(8,128)} %param.22) | copy-start | bytes 786436
  46.6 34.6 %copy-start.8 = (f32[64,256]{1,0:T(8,128)S(1)}, f32[64,256]{1,0:T(8,128)}, u32[]{:S(2)}) copy-start(f32[64,256]{1,0:T(8,128)} %refs_3_.1) | copy-start | bytes 196612
  46.6 34.6 %copy-start.9 = (f32[64,256]{1,0:T(8,128)S(1)}, f32[64,256]{1,0:T(8,128)}, u32[]{:S(2)}) copy-start(f32[64,256]{1,0:T(8,128)} %refs_4_.1) | copy-start | bytes 196612
  51.7 15.9 %collective-permute-start.7 = (bf16[32,8192]{1,0:T(8,128)(2,1)S(1)}, bf16[32,8192]{1,0:T(8,128)(2,1)S(1)}, u32[]{:S(2)}, u32[]{:S(2)}) collective-permute-start(bf16[32,8192]{1,0:T(8,128)(2,1)S(1)} %get-tuple-element.46), channel_id=1, source_target_pairs={{0,2},{1,3},{2,4},{3,5},{4,6},{5,7},{6,0},{7,1},{8,10},{9,11},{10,... | collective-permute-start | bytes 1572872 | tf_op jit(solution)/shard_map/ppermute | solution.py:365
  52.8 25.4 %collective-permute-start.8 = (bf16[32,8192]{1,0:T(8,128)(2,1)S(1)}, bf16[32,8192]{1,0:T(8,128)(2,1)S(1)}, u32[]{:S(2)}, u32[]{:S(2)}) collective-permute-start(bf16[32,8192]{1,0:T(8,128)(2,1)S(1)} %get-tuple-element.47), channel_id=1, source_target_pairs={{0,4},{1,5},{2,6},{3,7},{4,0},{5,1},{6,2},{7,3},{8,12},{9,13},{10,... | collective-permute-start | bytes 1572872 | tf_op jit(solution)/shard_map/ppermute | solution.py:365
  55.2 23.4 %collective-permute-start.9 = (bf16[32,8192]{1,0:T(8,128)(2,1)S(1)}, bf16[32,8192]{1,0:T(8,128)(2,1)S(1)}, u32[]{:S(2)}, u32[]{:S(2)}) collective-permute-start(bf16[32,8192]{1,0:T(8,128)(2,1)S(1)} %get-tuple-element.48), channel_id=1, source_target_pairs={{0,6},{1,7},{2,0},{3,1},{4,2},{5,3},{6,4},{7,5},{8,14},{9,15},{10,... | collective-permute-start | bytes 1572872 | tf_op jit(solution)/shard_map/ppermute | solution.py:365
  81.2 0.8 %copy-start.10 = (f32[64,256]{1,0:T(8,128)S(1)}, f32[64,256]{1,0:T(8,128)}, u32[]{:S(2)}) copy-start(f32[64,256]{1,0:T(8,128)} %refs_5_.1) | copy-start | bytes 196612

commit v11 on v9

--- a/solution.py
+++ b/solution.py
@@ -174,7 +174,7 @@
 CHUNK = 256
 
 
-def down_kernel(hidden_ref, slot_ref, up_own_ref, factors_ref, out_ref):
+def down_kernel(hidden_ref, slot_ref, up_own_ref, factors_ref, ours_ref, theirs_ref, both_ref):
     slot = slot_ref[...]
     acc = jnp.zeros(slot.shape, jnp.float32)
     for first in range(0, factors_ref.shape[1], CHUNK):
@@ -182,19 +182,24 @@
         for d in range(0, CHUNK, 128):
             hit = slot == lane_slot((1, 128), (first + d) // PADDED_RANK)
             acc = acc + jnp.where(hit, product[:, d : d + 128], 0.0)
-    out_ref[:, :PADDED_RANK] = acc[:, :PADDED_RANK] + acc[:, PADDED_RANK:]
-    out_ref[:, PADDED_RANK:] = up_own_ref[...]
+    both_ref[:, :PADDED_RANK] = acc[:, :PADDED_RANK] + acc[:, PADDED_RANK:]
+    both_ref[:, PADDED_RANK:] = up_own_ref[...]
+    half = ours_ref.shape[0]
+    core = lax.axis_index("tensor") % 2
+    ours_ref[...] = both_ref[pl.ds(pl.multiple_of(core * half, half), half), :]
+    theirs_ref[...] = both_ref[pl.ds(pl.multiple_of((1 - core) * half, half), half), :]
 
 
 def low_rank(hidden_columns, slot_wide, up_own, factors):
     tokens = hidden_columns.shape[0]
     return call(
         down_kernel,
-        jax.ShapeDtypeStruct((tokens, 2 * PADDED_RANK), jnp.float32),
+        (jax.ShapeDtypeStruct((tokens // 2, 2 * PADDED_RANK), jnp.float32),) * 2,
         2 * tokens * factors.size,
         2 * factors.size,
         in_specs=[VMEM_SPEC] * 4,
-        out_specs=VMEM_SPEC,
+        out_specs=(VMEM_SPEC,) * 2,
+        scratch_shapes=[pltpu.VMEM((tokens, 2 * PADDED_RANK), jnp.float32)],
         name="low_rank",
     )(hidden_columns, slot_wide, up_own, factors)
 
@@ -341,15 +346,18 @@
     pair_frozen = swap(frozen_key_value, 1, n_tensor)
     slot_wide, pair_rows = lax.optimization_barrier((slot_wide, pair_rows))
 
-    own = low_rank(hidden_columns, slot_wide, up_own, adapter_down_factors)
-    own = own + swap(own, 1, n_tensor)
-    weights = (sum_over_chips(own, n_tensor) * factor_wide).astype(jnp.bfloat16)
+    own, theirs = low_rank(hidden_columns, slot_wide, up_own, adapter_down_factors)
+    own = sum_over_chips(own + swap(theirs, 1, n_tensor), n_tensor)
+    other = swap(own, 1, n_tensor)
+    low_core = lax.axis_index("tensor") % 2 == 0
+    summed = jnp.concatenate(
+        [jnp.where(low_core, own, other), jnp.where(low_core, other, own)], axis=0
+    )
+    weights = (summed * factor_wide).astype(jnp.bfloat16)
+
+    packed = pack_rows(place, [hidden_columns, masked, weights], n_slot * CAP)
+    packed, weights = lax.optimization_barrier((packed, weights))
     extra_ours, extra_theirs = extra_term(rows_own, weights, slot_wide, adapter_down_factors)
-    weights, extra_ours, extra_theirs = lax.optimization_barrier(
-        (weights, extra_ours, extra_theirs)
-    )
-
-    packed = pack_rows(place, [hidden_columns, masked, weights], n_slot * CAP)
     owned = lax.all_to_all(
         packed.reshape(n_slot, CAP, -1), "dp", 0, 0, tiled=True
     ).reshape(n_slot * CAP, -1)

time: 87.9 us -> 87.6 us (level)
  waiting for transfers between devices: 36.7 us -> 33.4 us
  local copies, waits for them, and re-layouts: 11.9 us -> 14.1 us
    ppermute x7 -> x8, waiting for transfers between devices: 8.85 us -> 6.63 us  [swap(): return lax.ppermute(value, 'tensor', [(i, i ^ mask) for i in range(count)])]
    unnamed x30, local copies, waits for them, and re-layouts: 10 us -> 12.2 us
    ppermute x3, waiting for transfers between devices: 23.3 us -> 22.4 us  [local(): lax.ppermute(value, 'tensor', [(i, (i + 2 * step) % n_tensor) for i in ra...]
    ppermute x7 -> x8, starting transfers between devices: 5.66 us -> 5.3 us  [swap(): return lax.ppermute(value, 'tensor', [(i, i ^ mask) for i in range(count)])]
  transfers between devices with their start and end apart: 12 -> 13, of which waited for: 10 -> 11; matrix products, arithmetic and copies ran while one was open for 3% -> 3% of each run, Pallas kernels for 12% -> 12%
where the time goes in v11:
time: 87.6 us; the launch traced here: 86.8 us
  waiting for transfers between devices  33.4 us (38%)
  starting transfers between devices  25.4 us (29%)
  local copies, waits for them, and re-layouts  14.1 us (16%)
  Pallas kernels  12 us (14%)
  other arithmetic  1.08 us (1%)
    ppermute x3, waiting for transfers between devices, local(): lax.ppermute(value, 'tensor', [(i, (i + 2 * step) % n_tensor) for i in ra...  22.4 us
    unnamed x30, local copies, waits for them, and re-layouts  12.2 us
    all_to_all x1, starting transfers between devices, local(): lax.all_to_all(packed.reshape(n_slot, CAP, -1), 'dp', 0, 0, tiled=True)  11.2 us
    ppermute x8, waiting for transfers between devices, swap(): return lax.ppermute(value, 'tensor', [(i, i ^ mask) for i in range(count)])  6.63 us
    ppermute x8, starting transfers between devices, swap(): return lax.ppermute(value, 'tensor', [(i, i ^ mask) for i in range(count)])  5.3 us
    pallas_call x1, Pallas kernels, pair_sum(): call(functools.partial(pair_kernel, rows_own), (jax.ShapeDtypeStruct((row...  5.07 us
    all_to_all x1, starting transfers between devices, local(): lax.all_to_all(blocks, 'tensor', 0, 0, tiled=True).reshape(tokens, columns)  4.57 us
    ppermute x3, starting transfers between devices, local(): lax.ppermute(value, 'tensor', [(i, (i + 2 * step) % n_tensor) for i in ra...  4.39 us
  transfers between devices with their start and end apart: 13, of which 11 were waited for; matrix products, arithmetic and copies ran while one was open for 3% of the time, Pallas kernels for 12%

profile of v11, /device:TPU:32, one launch (start us, length us, event | category | flops | bytes accessed | tf_op | source)
XLA Modules:
  0.0 86.8 jit_solution(112047409357773878)
XLA Ops:
  0.6 0.1 collective-permute-start.7
  0.7 1.9 %copy.25 = bf16[4,8,8,1024]{3,2,0,1:T(8,128)(2,1)} copy(bf16[4,8,8,1024]{3,2,1,0:T(8,128)(2,1)} %bitcast.24) | data formatting | bytes 1048576 | tf_op jit(solution)/shard_map/reshape | solution.py:332
  2.6 4.6 %all-to-all-start = ((bf16[8,32,1024]{2,1,0:T(8,128)(2,1)}), bf16[8,32,1024]{2,1,0:T(8,128)(2,1)S(1)}, u32[]{:S(2)}, u32[]{:S(2)}) async-start(bf16[8,32,1024]{2,1,0:T(8,128)(2,1)} %bitcast.16), calls=%async_computation | async-start | bytes 1048576 | tf_op jit(solution)/shard_map/all_to_all | solution.py:333
  7.2 1.2 %copy-done.3 = bf16[2048,256]{1,0:T(8,128)(2,1)S(1)} copy-done((bf16[2048,256]{1,0:T(8,128)(2,1)S(1)}, bf16[2048,256]{1,0:T(8,128)(2,1)}, u32[]{:S(2)}) %copy-start.3) | copy-done | bytes 1048600
  8.4 0.9 %copy-done.7 = bf16[256,256]{1,0:T(8,128)(2,1)S(1)} copy-done((bf16[256,256]{1,0:T(8,128)(2,1)S(1)}, bf16[256,256]{1,0:T(8,128)(2,1)}, u32[]{:S(2)}) %copy-start.7) | copy-done | bytes 131096
  9.3 0.7 copy-done.11
  10.0 0.7 copy-done.12
  10.6 0.7 copy-done.13
  11.3 0.7 copy-done.14
  12.0 1.1 %prep.1 = (bf16[256,256]{1,0:T(8,128)(2,1)S(1)}, bf16[128,256]{1,0:T(8,128)(2,1)S(1)}, bf16[128,256]{1,0:T(8,128)(2,1)S(1)}, f32[256,128]{1,0:T(8,128)S(1)}, f32...) custom-call(s32[32]{0:T(128)S(1)} %copy-done.12, s32[32]{0:T(128)S(1)} %copy-done.13, ...), custom_call_target="tpu_custom_call" | custom-call | flops 268435456 | bytes 1048576 | tf_op jit(solution)/shard_map/prep/pallas_call | solution.py:138
  13.1 0.6 collective-permute-start
  13.7 0.9 %collective-permute-done.pair_rows_ref = bf16[128,256]{1,0:T(8,128)(2,1)S(1)} collective-permute-done((bf16[128,256]{1,0:T(8,128)(2,1)S(1)}, bf16[128,256]{1,0:T(8,128)(2,1)S(1)}, u32[]{:S(2)}, u32[]{:S(2)}) %collective-permute-start) | collective-permute-done | bytes 65568 | tf_op jit(solution)/shard_map/ppermute | solution.py:40
  14.6 3.0 %all-to-all-done = bf16[8,32,1024]{2,1,0:T(8,128)(2,1)S(1)} async-done(((bf16[8,32,1024]{2,1,0:T(8,128)(2,1)}), bf16[8,32,1024]{2,1,0:T(8,128)(2,1)S(1)}, u32[]{:S(2)}, u32[]{:S(2)}) %all-to-all-start) | async-done | bytes 524320 | tf_op jit(solution)/shard_map/all_to_all | solution.py:333
  17.5 2.2 %copy-done = bf16[1024,2048]{1,0:T(8,128)(2,1)S(1)} copy-done((bf16[1024,2048]{1,0:T(8,128)(2,1)S(1)}, bf16[1024,2048]{1,0:T(8,128)(2,1)}, u32[]{:S(2)}) %copy-start) | copy-done | bytes 4194328
  19.7 1.4 %low_rank.1 = (f32[128,128]{1,0:T(8,128)S(1)}, f32[128,128]{1,0:T(8,128)S(1)}) custom-call(bf16[256,1024]{1,0:T(8,128)(2,1)S(1)} %bitcast.18, f32[256,128]{1,0:T(8,128)S(1)} %get-tuple-element.38.slot_ref, f32[256,64]{1,0:T(8,128)S(1)} %get-tuple-element.39.up_own_ref, bf16[1024,2048]{1,0:T(8,128)(2,1)S(1)} %copy-done), custom_call_target="tpu_custom_call" | custom-call | flops 1073741824 | bytes 4194304 | tf_op jit(solution)/shard_map/low_rank/pallas_call | solution.py:195
  21.1 0.1 collective-permute-start.1
  21.2 1.2 %collective-permute-done.1 = f32[128,128]{1,0:T(8,128)S(1)} collective-permute-done((f32[128,128]{1,0:T(8,128)S(1)}, f32[128,128]{1,0:T(8,128)S(1)}, u32[]{:S(2)}, u32[]{:S(2)}) %collective-permute-start.1) | collective-permute-done | bytes 65568 | tf_op jit(solution)/shard_map/ppermute | solution.py:40
  22.4 1.3 %collective-permute-start.4 = (f32[128,128]{1,0:T(8,128)S(1)}, f32[128,128]{1,0:T(8,128)S(1)}, u32[]{:S(2)}, u32[]{:S(2)}) collective-permute-start(f32[128,128]{1,0:T(8,128)S(1)} %add.26), channel_id=1, source_target_pairs={{0,6},{1,7},{2,4},{3,5},{4,2},{5,3},{6,0},{7,1},{8,14},{9,15},{10,... | collective-permute-start | bytes 196616 | tf_op jit(solution)/shard_map/ppermute | solution.py:40
  23.7 1.5 %collective-permute-start.3 = (f32[128,128]{1,0:T(8,128)S(1)}, f32[128,128]{1,0:T(8,128)S(1)}, u32[]{:S(2)}, u32[]{:S(2)}) collective-permute-start(f32[128,128]{1,0:T(8,128)S(1)} %add.26), channel_id=1, source_target_pairs={{0,4},{1,5},{2,6},{3,7},{4,0},{5,1},{6,2},{7,3},{8,12},{9,13},{10,... | collective-permute-start | bytes 196616 | tf_op jit(solution)/shard_map/ppermute | solution.py:40
  25.1 1.5 %collective-permute-start.2 = (f32[128,128]{1,0:T(8,128)S(1)}, f32[128,128]{1,0:T(8,128)S(1)}, u32[]{:S(2)}, u32[]{:S(2)}) collective-permute-start(f32[128,128]{1,0:T(8,128)S(1)} %add.26), channel_id=1, source_target_pairs={{0,2},{1,3},{2,0},{3,1},{4,6},{5,7},{6,4},{7,5},{8,10},{9,11},{10,... | collective-permute-start | bytes 196616 | tf_op jit(solution)/shard_map/ppermute | solution.py:40
  26.6 2.1 %collective-permute-done.4 = f32[128,128]{1,0:T(8,128)S(1)} collective-permute-done((f32[128,128]{1,0:T(8,128)S(1)}, f32[128,128]{1,0:T(8,128)S(1)}, u32[]{:S(2)}, u32[]{:S(2)}) %collective-permute-start.4) | collective-permute-done | bytes 65568 | tf_op jit(solution)/shard_map/ppermute | solution.py:40
  28.7 1.1 %collective-permute-done.3 = f32[128,128]{1,0:T(8,128)S(1)} collective-permute-done((f32[128,128]{1,0:T(8,128)S(1)}, f32[128,128]{1,0:T(8,128)S(1)}, u32[]{:S(2)}, u32[]{:S(2)}) %collective-permute-start.3) | collective-permute-done | bytes 65568 | tf_op jit(solution)/shard_map/ppermute | solution.py:40
  29.8 0.1 collective-permute-done.2
  29.9 0.1 collective-permute-start.5
  30.0 1.2 %collective-permute-done.5 = f32[128,128]{1,0:T(8,128)S(1)} collective-permute-done((f32[128,128]{1,0:T(8,128)S(1)}, f32[128,128]{1,0:T(8,128)S(1)}, u32[]{:S(2)}, u32[]{:S(2)}) %collective-permute-start.5) | collective-permute-done | bytes 65568 | tf_op jit(solution)/shard_map/ppermute | solution.py:40
  31.3 1.7 %pack.1 = bf16[512,1408]{1,0:T(8,128)(2,1)} custom-call(s32[1,256]{1,0:T(1,128)S(1)} %get-tuple-element.34.place_ref, bf16[256,1024]{1,0:T(8,128)(2,1)S(1)} %bitcast.19, bf16[256,256]{1,0:T(8,128)(2,1)S(1)} %get-tuple-element.35.refs_1_, bf16[256,128]{1,0:T(8,128)(2,1)S(1)} %fusion.refs_2_.weight_ref), custom_call_target="tpu_custom_call" | custom-call | flops 369098752 | bytes 2162688 | tf_op jit(solution)/shard_map/pack/pallas_call | solution.py:163
  33.0 2.2 %copy-done.1 = bf16[1024,2048]{1,0:T(8,128)(2,1)S(1)} copy-done((bf16[1024,2048]{1,0:T(8,128)(2,1)S(1)}, bf16[1024,2048]{1,0:T(8,128)(2,1)}, u32[]{:S(2)}) %copy-start.1) | copy-done | bytes 4194328
  35.2 1.4 %extra_term.1 = (f32[128,1024]{1,0:T(8,128)S(1)}, f32[128,1024]{1,0:T(8,128)S(1)}) custom-call(bf16[256,128]{1,0:T(8,128)(2,1)S(1)} %fusion.refs_2_.weight_ref, f32[256,128]{1,0:T(8,128)S(1)} %get-tuple-element.38.slot_ref, bf16[1024,2048]{1,0:T(8,128)(2,1)S(1)} %copy-done.1), custom_call_target="tpu_custom_call" | custom-call | flops 1073741824 | bytes 4194304 | tf_op jit(solution)/shard_map/extra_term/pallas_call | solution.py:236
  36.5 0.3 collective-permute-start.6
  36.8 11.2 %all-to-all-start.1 = ((bf16[32,16,1408]{2,1,0:T(8,128)(2,1)}), bf16[32,16,1408]{2,1,0:T(8,128)(2,1)S(1)}, u32[]{:S(2)}, u32[]{:S(2)}) async-start(bf16[32,16,1408]{2,1,0:T(8,128)(2,1)} %bitcast.3), calls=%async_computation.1 | async-start | bytes 2883584 | tf_op jit(solution)/shard_map/all_to_all | solution.py:361
  48.0 0.0 collective-permute-done.6.extra_pair_ref
  48.0 0.0 collective-permute-done.7.pair_frozen_ref
  48.0 0.0 copy-start.2
  48.0 2.2 %copy-done.2 = bf16[8192,256]{1,0:T(8,128)(2,1)S(1)} copy-done((bf16[8192,256]{1,0:T(8,128)(2,1)S(1)}, bf16[8192,256]{1,0:T(8,128)(2,1)}, u32[]{:S(2)}) %copy-start.2) | copy-done | bytes 4194328
  50.2 0.0 copy-start.9
  50.2 5.1 %pair_sum.1 = (f32[32,8192]{1,0:T(8,128)S(1)}, bf16[32,8192]{1,0:T(8,128)(2,1)S(1)}, bf16[32,8192]{1,0:T(8,128)(2,1)S(1)}, bf16[32,8192]{1,0:T(8,128)(2,1)S(1)}) custom-call(bf16[128,256]{1,0:T(8,128)(2,1)S(1)} %get-tuple-element.44.rows_ref, bf16[128,256]{1,0:T(8,128)(2,1)S(1)} %collective-permute-done.pair_rows_ref, ...), custom_call_target="tpu_custom_call" | custom-call | flops 1073741824 | bytes 12582912 | tf_op jit(solution)/shard_map/pair_sum/pallas_call | solution.py:272
  55.3 1.1 %collective-permute-start.8 = (bf16[32,8192]{1,0:T(8,128)(2,1)S(1)}, bf16[32,8192]{1,0:T(8,128)(2,1)S(1)}, u32[]{:S(2)}, u32[]{:S(2)}) collective-permute-start(bf16[32,8192]{1,0:T(8,128)(2,1)S(1)} %get-tuple-element.50), channel_id=1, source_target_pairs={{0,2},{1,3},{2,4},{3,5},{4,6},{5,7},{6,0},{7,1},{8,10},{9,11},{10,... | collective-permute-start | bytes 1572872 | tf_op jit(solution)/shard_map/ppermute | solution.py:375
  56.4 2.4 %collective-permute-start.9 = (bf16[32,8192]{1,0:T(8,128)(2,1)S(1)}, bf16[32,8192]{1,0:T(8,128)(2,1)S(1)}, u32[]{:S(2)}, u32[]{:S(2)}) collective-permute-start(bf16[32,8192]{1,0:T(8,128)(2,1)S(1)} %get-tuple-element.51), channel_id=1, source_target_pairs={{0,4},{1,5},{2,6},{3,7},{4,0},{5,1},{6,2},{7,3},{8,12},{9,13},{10,... | collective-permute-start | bytes 1572872 | tf_op jit(solution)/shard_map/ppermute | solution.py:375
  58.8 0.9 %collective-permute-start.10 = (bf16[32,8192]{1,0:T(8,128)(2,1)S(1)}, bf16[32,8192]{1,0:T(8,128)(2,1)S(1)}, u32[]{:S(2)}, u32[]{:S(2)}) collective-permute-start(bf16[32,8192]{1,0:T(8,128)(2,1)S(1)} %get-tuple-element.52), channel_id=1, source_target_pairs={{0,6},{1,7},{2,0},{3,1},{4,2},{5,3},{6,4},{7,5},{8,14},{9,15},{10,... | collective-permute-start | bytes 1572872 | tf_op jit(solution)/shard_map/ppermute | solution.py:375
  59.7 11.5 %collective-permute-done.8 = bf16[32,8192]{1,0:T(8,128)(2,1)S(1)} collective-permute-done((bf16[32,8192]{1,0:T(8,128)(2,1)S(1)}, bf16[32,8192]{1,0:T(8,128)(2,1)S(1)}, u32[]{:S(2)}, u32[]{:S(2)}) %collective-permute-start.8) | collective-permute-done | bytes 524320 | tf_op jit(solution)/shard_map/ppermute | solution.py:375
  71.2 10.4 %collective-permute-done.9 = bf16[32,8192]{1,0:T(8,128)(2,1)S(1)} collective-permute-done((bf16[32,8192]{1,0:T(8,128)(2,1)S(1)}, bf16[32,8192]{1,0:T(8,128)(2,1)S(1)}, u32[]{:S(2)}, u32[]{:S(2)}) %collective-permute-start.9) | collective-permute-done | bytes 524320 | tf_op jit(solution)/shard_map/ppermute | solution.py:375
  81.6 0.4 collective-permute-done.10
  82.1 1.0 %add_convert_fusion = bf16[32,8192]{1,0:T(8,128)(2,1)} fusion(bf16[32,8192]{1,0:T(8,128)(2,1)S(1)} %collective-permute-done.10, bf16[32,8192]{1,0:T(8,128)(2,1)S(1)} %collective-permute-done.9, f32[32,8192]{1,0:T(8,128)S(1)} %get-tuple-element.49, bf16[32,8192]{1,0:T(8,128)(2,1)S(1)} %collective-permute-done.8), kind=kLoop, calls=%fused_computation | loop fusion | flops 1835008 | bytes 3145728 | tf_op jit(solution)/shard_map/convert_element_type | solution.py:379
  83.1 1.5 %all-to-all-done.1 = bf16[32,16,1408]{2,1,0:T(8,128)(2,1)S(1)} async-done(((bf16[32,16,1408]{2,1,0:T(8,128)(2,1)}), bf16[32,16,1408]{2,1,0:T(8,128)(2,1)S(1)}, u32[]{:S(2)}, u32[]{:S(2)}) %all-to-all-start.1) | async-done | bytes 1441824 | tf_op jit(solution)/shard_map/all_to_all | solution.py:361
  84.6 0.0 copy-done.5
  84.6 0.0 copy-start.10
  84.6 0.8 copy-done.10
  85.4 1.4 %owners_update.1 = (f32[64,1024]{1,0:T(8,128)}, f32[64,1024]{1,0:T(8,128)}, f32[64,1024]{1,0:T(8,128)}, f32[64,256]{1,0:T(8,128)}, f32[64,256]{1,0:T(8,128)}, /*index=5*/f32[64,256]{1,0:T(8,128)}) custom-call(bf16[512,1408]{1,0:T(8,128)(2,1)S(1)} %bitcast.17, f32[64,1024]{1,0:T(8,128)S(1)} %bitcast.20, f32[64,1024]{1,0:T(8,128)S(1)} %bitcast.21, ...), custom_call_target="tpu_custom_call" | custom-call | flops 92274688 | bytes 3407872 | tf_op jit(solution)/shard_map/owners_update/pallas_call | solution.py:297
  (20 shorter events, 0.1 us)
Async XLA Ops:
  0.6 47.4 %collective-permute-start.7 = (bf16[8192,256]{1,0:T(8,128)(2,1)}, bf16[8192,256]{1,0:T(8,128)(2,1)}, u32[]{:S(2)}, u32[]{:S(2)}) collective-permute-start(bf16[8192,256]{1,0:T(8,128)(2,1)} %frozen_ref.1), channel_id=1, source_target_pairs={{0,1},{1,0},{2,3},{3,2},{4,5},{5,4},{6,7},{7,6},{8,9},{9,8},{10,11... | collective-permute-start | bytes 12582920 | tf_op jit(solution)/shard_map/ppermute | solution.py:40
  2.6 14.9 %all-to-all-start = ((bf16[8,32,1024]{2,1,0:T(8,128)(2,1)}), bf16[8,32,1024]{2,1,0:T(8,128)(2,1)S(1)}, u32[]{:S(2)}, u32[]{:S(2)}) async-start(bf16[8,32,1024]{2,1,0:T(8,128)(2,1)} %bitcast.16), calls=%async_computation | async-start | bytes 1048576 | tf_op jit(solution)/shard_map/all_to_all | solution.py:333
  7.2 1.2 %copy-start.3 = (bf16[2048,256]{1,0:T(8,128)(2,1)S(1)}, bf16[2048,256]{1,0:T(8,128)(2,1)}, u32[]{:S(2)}) copy-start(bf16[2048,256]{1,0:T(8,128)(2,1)} %up_ref.1) | copy-start | bytes 3145732
  8.4 0.9 %copy-start.7 = (bf16[256,256]{1,0:T(8,128)(2,1)S(1)}, bf16[256,256]{1,0:T(8,128)(2,1)}, u32[]{:S(2)}) copy-start(bf16[256,256]{1,0:T(8,128)(2,1)} %cot_ref.1) | copy-start | bytes 393220
  9.3 0.7 copy-start.11
  10.0 0.7 copy-start.12
  10.6 0.7 copy-start.13
  11.3 0.7 copy-start.14
  13.1 1.5 %collective-permute-start = (bf16[128,256]{1,0:T(8,128)(2,1)S(1)}, bf16[128,256]{1,0:T(8,128)(2,1)S(1)}, u32[]{:S(2)}, u32[]{:S(2)}) collective-permute-start(bf16[128,256]{1,0:T(8,128)(2,1)S(1)} %get-tuple-element.37), channel_id=1, source_target_pairs={{0,1},{1,0},{2,3},{3,2},{4,5},{5,4},{6,7},{7,6},{8,9},{9,8},{10,11... | collective-permute-start | bytes 196616 | tf_op jit(solution)/shard_map/ppermute | solution.py:40
  17.5 2.2 %copy-start = (bf16[1024,2048]{1,0:T(8,128)(2,1)S(1)}, bf16[1024,2048]{1,0:T(8,128)(2,1)}, u32[]{:S(2)}) copy-start(bf16[1024,2048]{1,0:T(8,128)(2,1)} %factors_ref.3) | copy-start | bytes 12582916
  21.1 1.3 %collective-permute-start.1 = (f32[128,128]{1,0:T(8,128)S(1)}, f32[128,128]{1,0:T(8,128)S(1)}, u32[]{:S(2)}, u32[]{:S(2)}) collective-permute-start(f32[128,128]{1,0:T(8,128)S(1)} %get-tuple-element.41), channel_id=1, source_target_pairs={{0,1},{1,0},{2,3},{3,2},{4,5},{5,4},{6,7},{7,6},{8,9},{9,8},{10,11... | collective-permute-start | bytes 196616 | tf_op jit(solution)/shard_map/ppermute | solution.py:40
  22.4 6.3 %collective-permute-start.4 = (f32[128,128]{1,0:T(8,128)S(1)}, f32[128,128]{1,0:T(8,128)S(1)}, u32[]{:S(2)}, u32[]{:S(2)}) collective-permute-start(f32[128,128]{1,0:T(8,128)S(1)} %add.26), channel_id=1, source_target_pairs={{0,6},{1,7},{2,4},{3,5},{4,2},{5,3},{6,0},{7,1},{8,14},{9,15},{10,... | collective-permute-start | bytes 196616 | tf_op jit(solution)/shard_map/ppermute | solution.py:40
  23.7 6.1 %collective-permute-start.3 = (f32[128,128]{1,0:T(8,128)S(1)}, f32[128,128]{1,0:T(8,128)S(1)}, u32[]{:S(2)}, u32[]{:S(2)}) collective-permute-start(f32[128,128]{1,0:T(8,128)S(1)} %add.26), channel_id=1, source_target_pairs={{0,4},{1,5},{2,6},{3,7},{4,0},{5,1},{6,2},{7,3},{8,12},{9,13},{10,... | collective-permute-start | bytes 196616 | tf_op jit(solution)/shard_map/ppermute | solution.py:40
  25.1 4.7 %collective-permute-start.2 = (f32[128,128]{1,0:T(8,128)S(1)}, f32[128,128]{1,0:T(8,128)S(1)}, u32[]{:S(2)}, u32[]{:S(2)}) collective-permute-start(f32[128,128]{1,0:T(8,128)S(1)} %add.26), channel_id=1, source_target_pairs={{0,2},{1,3},{2,0},{3,1},{4,6},{5,7},{6,4},{7,5},{8,10},{9,11},{10,... | collective-permute-start | bytes 196616 | tf_op jit(solution)/shard_map/ppermute | solution.py:40
  29.9 1.3 %collective-permute-start.5 = (f32[128,128]{1,0:T(8,128)S(1)}, f32[128,128]{1,0:T(8,128)S(1)}, u32[]{:S(2)}, u32[]{:S(2)}) collective-permute-start(f32[128,128]{1,0:T(8,128)S(1)} %add_add_fusion), channel_id=1, source_target_pairs={{0,1},{1,0},{2,3},{3,2},{4,5},{5,4},{6,7},{7,6},{8,9},{9,8},{10,11... | collective-permute-start | bytes 196616 | tf_op jit(solution)/shard_map/ppermute | solution.py:40
  33.0 2.2 %copy-start.1 = (bf16[1024,2048]{1,0:T(8,128)(2,1)S(1)}, bf16[1024,2048]{1,0:T(8,128)(2,1)}, u32[]{:S(2)}) copy-start(bf16[1024,2048]{1,0:T(8,128)(2,1)} %factors_ref.3) | copy-start | bytes 12582916
  36.5 11.4 %collective-permute-start.6 = (f32[128,1024]{1,0:T(8,128)S(1)}, f32[128,1024]{1,0:T(8,128)S(1)}, u32[]{:S(2)}, u32[]{:S(2)}) collective-permute-start(f32[128,1024]{1,0:T(8,128)S(1)} %get-tuple-element.48), channel_id=1, source_target_pairs={{0,1},{1,0},{2,3},{3,2},{4,5},{5,4},{6,7},{7,6},{8,9},{9,8},{10,11... | collective-permute-start | bytes 1572872 | tf_op jit(solution)/shard_map/ppermute | solution.py:40
  36.8 47.8 %all-to-all-start.1 = ((bf16[32,16,1408]{2,1,0:T(8,128)(2,1)}), bf16[32,16,1408]{2,1,0:T(8,128)(2,1)S(1)}, u32[]{:S(2)}, u32[]{:S(2)}) async-start(bf16[32,16,1408]{2,1,0:T(8,128)(2,1)} %bitcast.3), calls=%async_computation.1 | async-start | bytes 2883584 | tf_op jit(solution)/shard_map/all_to_all | solution.py:361
  48.0 2.2 %copy-start.2 = (bf16[8192,256]{1,0:T(8,128)(2,1)S(1)}, bf16[8192,256]{1,0:T(8,128)(2,1)}, u32[]{:S(2)}) copy-start(bf16[8192,256]{1,0:T(8,128)(2,1)} %frozen_ref.1) | copy-start | bytes 12582916
  50.2 34.4 %copy-start.4 = (f32[1024,64]{0,1:T(8,128)S(1)}, f32[1024,64]{0,1:T(8,128)}, u32[]{:S(2)}) copy-start(f32[1024,64]{0,1:T(8,128)} %param.20) | copy-start | bytes 786436
  50.2 34.4 %copy-start.5 = (f32[1024,64]{0,1:T(8,128)S(1)}, f32[1024,64]{0,1:T(8,128)}, u32[]{:S(2)}) copy-start(f32[1024,64]{0,1:T(8,128)} %param.21) | copy-start | bytes 786436
  50.2 34.4 %copy-start.6 = (f32[1024,64]{0,1:T(8,128)S(1)}, f32[1024,64]{0,1:T(8,128)}, u32[]{:S(2)}) copy-start(f32[1024,64]{0,1:T(8,128)} %param.22) | copy-start | bytes 786436
  50.2 34.4 %copy-start.8 = (f32[64,256]{1,0:T(8,128)S(1)}, f32[64,256]{1,0:T(8,128)}, u32[]{:S(2)}) copy-start(f32[64,256]{1,0:T(8,128)} %refs_3_.1) | copy-start | bytes 196612
  50.2 34.4 %copy-start.9 = (f32[64,256]{1,0:T(8,128)S(1)}, f32[64,256]{1,0:T(8,128)}, u32[]{:S(2)}) copy-start(f32[64,256]{1,0:T(8,128)} %refs_4_.1) | copy-start | bytes 196612
  55.3 15.9 %collective-permute-start.8 = (bf16[32,8192]{1,0:T(8,128)(2,1)S(1)}, bf16[32,8192]{1,0:T(8,128)(2,1)S(1)}, u32[]{:S(2)}, u32[]{:S(2)}) collective-permute-start(bf16[32,8192]{1,0:T(8,128)(2,1)S(1)} %get-tuple-element.50), channel_id=1, source_target_pairs={{0,2},{1,3},{2,4},{3,5},{4,6},{5,7},{6,0},{7,1},{8,10},{9,11},{10,... | collective-permute-start | bytes 1572872 | tf_op jit(solution)/shard_map/ppermute | solution.py:375
  56.4 25.2 %collective-permute-start.9 = (bf16[32,8192]{1,0:T(8,128)(2,1)S(1)}, bf16[32,8192]{1,0:T(8,128)(2,1)S(1)}, u32[]{:S(2)}, u32[]{:S(2)}) collective-permute-start(bf16[32,8192]{1,0:T(8,128)(2,1)S(1)} %get-tuple-element.51), channel_id=1, source_target_pairs={{0,4},{1,5},{2,6},{3,7},{4,0},{5,1},{6,2},{7,3},{8,12},{9,13},{10,... | collective-permute-start | bytes 1572872 | tf_op jit(solution)/shard_map/ppermute | solution.py:375
  58.8 23.2 %collective-permute-start.10 = (bf16[32,8192]{1,0:T(8,128)(2,1)S(1)}, bf16[32,8192]{1,0:T(8,128)(2,1)S(1)}, u32[]{:S(2)}, u32[]{:S(2)}) collective-permute-start(bf16[32,8192]{1,0:T(8,128)(2,1)S(1)} %get-tuple-element.52), channel_id=1, source_target_pairs={{0,6},{1,7},{2,0},{3,1},{4,2},{5,3},{6,4},{7,5},{8,14},{9,15},{10,... | collective-permute-start | bytes 1572872 | tf_op jit(solution)/shard_map/ppermute | solution.py:375
  84.6 0.8 copy-start.10
